TPU v7x, 256 devices: a whole 4x4x8 slice. The times are simulated.
256 devices in a mesh: replica: 32 (over x, z), tensor: 8 (over y, core).
Axes of the slice: x: 4, y: 4, z: 8, core: 2. Of those that a mesh axis runs over, the one named last changes fastest.
Arguments:
- tokens: bfloat16 [96, 2048], P('replica'), may hold values from -0.8984375 to 0.8984375
- long_tokens: bfloat16 [32, 2048], P('replica'), may hold values from -0.8984375 to 0.8984375
- cache: bfloat16 [2, 2, 96, 2048, 8, 128], P(None, None, 'replica', None, 'tensor')
- long_request_cache: bfloat16 [2, 2, 32, 2, 2048, 8, 128], P(None, None, 'replica', None, None, 'tensor')
- lengths: int32 [96], replicated, may hold values from 1 to 2047, as said below
- long_lengths: int32 [32], replicated, may hold values from 2049 to 4095, as said below
- norm_gain: float32 [2, 2048], replicated, may hold values from 0.1 to 1.9
- q_gain: float32 [2, 128], replicated, may hold values from 0.1 to 1.9
- k_gain: float32 [2, 128], replicated, may hold values from 0.1 to 1.9
- w_query: bfloat16 [2, 2048, 2048], P(None, None, 'tensor'), may hold values from -0.125 to 0.125
- key_weight: bfloat16 [2, 2048, 1024], P(None, None, 'tensor'), may hold values from -0.125 to 0.125
- value_weight: bfloat16 [2, 2048, 1024], P(None, None, 'tensor'), may hold values from -0.125 to 0.125
- w_out: bfloat16 [2, 2048, 2048], P(None, 'tensor'), may hold values from -0.125 to 0.125
Outputs:
- out_hidden: float32 [96, 2048], P('replica')
- out_long: float32 [32, 2048], P('replica')
- moved_cache: bfloat16 [32, 2, 2, 2048, 8, 128], P('replica', None, None, None, 'tensor')
Inputs may be any that keep to these rules, and one draw needn't show every extreme that they name: `lengths`: cached length of each request; some request has 2047 in every draw. `long_lengths`: cached length of each long request, always past 2048; some long request has 4095 in every draw.
All inputs are finite; a program needn't handle non-finite values.
Results may differ from a plain program's by a relative error of at most 0.028.
Values may be sent and summed in bfloat16 or wider, within the bound.
No kernel may reach another device: no remote copies, remote signals or barrier semaphores. Data moves between devices by JAX's collectives and lax.ppermute only.
A program may use at most 64 MiB of HBM per device.

v0:
```python
import jax
import jax.numpy as jnp
from jax import lax
from jax.sharding import PartitionSpec as P

EPSILON = 1e-06
ROPE_BASE = 1000000.0
NEGATIVE = -1e30


def shifted(block, axis, distance):
    devices = range(lax.axis_size(axis))
    route = [((i - distance) % len(devices), i) for i in devices]
    return lax.ppermute(block, axis, route)


def partner_2(value, axis, apart):
    mask = 2**apart
    pairs = [(source, source ^ mask) for source in range(lax.axis_size(axis))]
    return lax.ppermute(value, axis, pairs)


def rms_scale(values, gain_row):
    return (
        values * lax.rsqrt(jnp.mean(values * values, axis=-1, keepdims=True) + EPSILON) * gain_row
    )


def rotate(values, places):
    head_width = values.shape[-1]
    halfway = head_width // 2
    inverse = ROPE_BASE ** (-2.0 * jnp.arange(halfway, dtype=jnp.float32) / head_width)
    angles = places.astype(jnp.float32)[:, None, None] * inverse
    cosine = jnp.cos(angles)
    sine_of = jnp.sin(angles)
    leading = values[..., :halfway]
    trailing = values[..., halfway:]
    return jnp.concatenate(
        [leading * cosine - trailing * sine_of, trailing * cosine + leading * sine_of], axis=-1
    )


def project(hidden, gain_row, w_query, key_weight, value_weight, query_gain, key_gain, places):
    head_width = query_gain.shape[-1]
    count_rows = hidden.shape[0]
    normed = rms_scale(hidden.astype(jnp.float32), gain_row).astype(jnp.bfloat16)
    queries = jnp.dot(normed, w_query, preferred_element_type=jnp.float32).reshape(
        count_rows, -1, head_width
    )
    keys_new = jnp.dot(normed, key_weight, preferred_element_type=jnp.float32).reshape(
        count_rows, -1, head_width
    )
    values_new = (
        jnp.dot(normed, value_weight, preferred_element_type=jnp.float32)
        .reshape(count_rows, -1, head_width)
        .astype(jnp.bfloat16)
    )
    queries = rotate(rms_scale(queries, query_gain), places).astype(jnp.bfloat16)
    keys_new = rotate(rms_scale(keys_new, key_gain), places).astype(jnp.bfloat16)
    return (queries, keys_new, values_new)


def own_terms(queries, key_new):
    head_width = queries.shape[-1]
    grouped = queries.reshape(key_new.shape[0], -1, head_width)
    return jnp.einsum(
        "kgd,kd->kg", grouped, key_new, preferred_element_type=jnp.float32
    ) * head_width ** (-0.5)


def masked_scores(queries, key_rows, visible):
    head_width = queries.shape[-1]
    grouped = queries.reshape(key_rows.shape[1], -1, head_width)
    scores = jnp.einsum(
        "kgd,tkd->kgt", grouped, key_rows, preferred_element_type=jnp.float32
    ) * head_width ** (-0.5)
    return jnp.where(visible[None, None, :], scores, NEGATIVE)


def attend(queries, key_rows, value_rows, visible, key_new, value_new):
    scores = masked_scores(queries, key_rows, visible)
    own_score = own_terms(queries, key_new)
    highest = jnp.maximum(jnp.max(scores, axis=-1), own_score)
    weights = jnp.exp(scores - highest[..., None])
    own_weight = jnp.exp(own_score - highest)
    denominator = jnp.sum(weights, axis=-1) + own_weight
    summed = jnp.einsum(
        "kgt,tkd->kgd", weights.astype(jnp.bfloat16), value_rows, preferred_element_type=jnp.float32
    )
    own_rounded = lax.optimization_barrier(own_weight.astype(jnp.bfloat16)).astype(jnp.float32)
    summed = summed + own_rounded[..., None] * value_new.astype(jnp.float32)[:, None, :]
    return (summed / denominator[..., None]).reshape(queries.shape).astype(jnp.bfloat16)


def partial_attend(queries, key_rows, value_rows, visible):
    scores = masked_scores(queries, key_rows, visible)
    highest = jnp.max(scores, axis=-1)
    weights = jnp.exp(scores - highest[..., None])
    summed = jnp.einsum(
        "kgt,tkd->kgd", weights.astype(jnp.bfloat16), value_rows, preferred_element_type=jnp.float32
    )
    return (highest, jnp.sum(weights, axis=-1), summed)


def combine(one_side, far_side):
    highest = jnp.maximum(one_side[0], far_side[0])
    factor_here = jnp.exp(one_side[0] - highest)
    factor_far = jnp.exp(far_side[0] - highest)
    totals = one_side[1] * factor_here + far_side[1] * factor_far
    summed = one_side[2] * factor_here[..., None] + far_side[2] * factor_far[..., None]
    return (highest, totals, summed)


def close_with_own(state_in, queries, key_new, value_new):
    own_score = own_terms(queries, key_new)
    highest = jnp.maximum(state_in[0], own_score)
    factor_here = jnp.exp(state_in[0] - highest)
    own_weight = jnp.exp(own_score - highest)
    denominator = state_in[1] * factor_here + own_weight
    own_rounded = lax.optimization_barrier(own_weight.astype(jnp.bfloat16)).astype(jnp.float32)
    summed = (
        state_in[2] * factor_here[..., None]
        + own_rounded[..., None] * value_new.astype(jnp.float32)[:, None, :]
    )
    return (summed / denominator[..., None]).reshape(queries.shape).astype(jnp.bfloat16)


def local(
    tokens,
    long_tokens,
    cache,
    long_request_cache,
    lengths,
    long_lengths,
    norm_gain,
    q_gain,
    k_gain,
    w_query,
    key_weight,
    value_weight,
    w_out,
):
    groups = lax.axis_size("replica")
    group_at = lax.axis_index("replica")
    per_group = tokens.shape[0]
    resident = per_group - 1
    layers = cache.shape[0]
    positions = jnp.arange(cache.shape[3])
    half_len = long_request_cache.shape[4]
    partner = (group_at + groups // 2) % groups
    local_len = lax.dynamic_slice_in_dim(lengths, group_at * per_group, per_group)
    arrived_len = lax.dynamic_index_in_dim(
        lengths, partner * per_group + resident, 0, keepdims=False
    )
    parity = group_at % 2
    pair_len = lax.dynamic_slice_in_dim(long_lengths, group_at - parity, 2)
    arrived_cache, arrived_token = shifted(
        (cache[:, :, resident], tokens[resident:]), "replica", groups // 2
    )
    hidden = jnp.concatenate([tokens[:resident], arrived_token], axis=0)
    places = jnp.concatenate([local_len[:resident], arrived_len[None]])
    visible = positions[None, :] < places[:, None]
    partner_token = partner_2(long_tokens, "replica", 0)
    long_hidden = jnp.where(
        parity == 0,
        jnp.concatenate([long_tokens, partner_token], axis=0),
        jnp.concatenate([partner_token, long_tokens], axis=0),
    )
    offsets = parity * half_len + jnp.arange(half_len)
    long_visible = offsets[None, :] < pair_len[:, None]
    main_rows = hidden.shape[0]
    fresh_rows = []
    for layer_at in range(layers):
        queries, keys_new, values_new = project(
            hidden,
            norm_gain[layer_at],
            w_query[layer_at],
            key_weight[layer_at],
            value_weight[layer_at],
            q_gain[layer_at],
            k_gain[layer_at],
            places,
        )
        staying = jax.vmap(attend)(
            queries[:resident],
            cache[layer_at, 0, :resident],
            cache[layer_at, 1, :resident],
            visible[:resident],
            keys_new[:resident],
            values_new[:resident],
        )
        incoming = attend(
            queries[resident],
            arrived_cache[layer_at, 0],
            arrived_cache[layer_at, 1],
            visible[resident],
            keys_new[resident],
            values_new[resident],
        )
        attended = jnp.concatenate([staying, incoming[None]], axis=0)
        fresh_rows.append(jnp.stack([keys_new[resident], values_new[resident]]))
        long_queries, long_keys, long_values = project(
            long_hidden,
            norm_gain[layer_at],
            w_query[layer_at],
            key_weight[layer_at],
            value_weight[layer_at],
            q_gain[layer_at],
            k_gain[layer_at],
            pair_len,
        )
        state_here = jax.vmap(partial_attend)(
            long_queries,
            long_request_cache[layer_at, 0, 0],
            long_request_cache[layer_at, 1, 0],
            long_visible,
        )
        state_far = partner_2(state_here, "replica", 0)
        merged = combine(state_here, state_far)
        long_attended = jax.vmap(close_with_own)(merged, long_queries, long_keys, long_values)
        stacked = jnp.concatenate([attended, long_attended], axis=0)
        heads_out = jnp.dot(
            stacked.reshape(stacked.shape[0], -1),
            w_out[layer_at],
            preferred_element_type=jnp.float32,
        )
        summed = lax.psum(heads_out, "tensor")
        carried = jnp.concatenate([hidden, long_hidden], axis=0).astype(jnp.float32) + summed
        if layer_at + 1 < layers:
            carried = carried.astype(jnp.bfloat16)
        hidden = carried[:main_rows]
        long_hidden = carried[main_rows:]
    fresh_all = jnp.stack(fresh_rows)
    moved_here = lax.dynamic_update_slice_in_dim(
        arrived_cache, fresh_all[:, :, None], arrived_len, axis=2
    )
    long_out = lax.dynamic_slice_in_dim(long_hidden, parity, 1)
    return (hidden, long_out, moved_here[None])


def solution(mesh):
    return jax.shard_map(
        local,
        mesh=mesh,
        in_specs=(
            P("replica", None),
            P("replica", None),
            P(None, None, "replica", None, "tensor", None),
            P(None, None, "replica", None, None, "tensor", None),
            P(),
            P(),
            P(),
            P(),
            P(),
            P(None, None, "tensor"),
            P(None, None, "tensor"),
            P(None, None, "tensor"),
            P(None, "tensor", None),
        ),
        out_specs=(
            P("replica", None),
            P("replica", None),
            P("replica", None, None, None, "tensor", None),
        ),
        check_vma=False,
    )
```

profile of v0, /device:TPU:64, one launch (start us, length us, event | category | flops | bytes accessed | tf_op | source)
XLA Modules:
  0.0 137.5 jit_solution(526159633632751661)
XLA Ops:
  1.4 3.1 %collective-permute-start = (bf16[1,2048]{1,0:T(2,128)(2,1)S(1)}, bf16[1,2048]{1,0:T(2,128)(2,1)S(1)}, u32[]{:S(2)}, u32[]{:S(2)}) collective-permute-start(bf16[1,2048]{1,0:T(2,128)(2,1)S(1)} %slice.220), channel_id=1, source_target_pairs={{128,0},{136,8},{144,16},{152,24},{160,32},{168,40},{176,48},{184,... | collective-permute-start | bytes 12296 | tf_op jit(solution)/shard_map/ppermute | solution.py:14
  4.5 1.9 %collective-permute-start.1 = (bf16[1,2048]{1,0:T(2,128)(2,1)}, bf16[1,2048]{1,0:T(2,128)(2,1)S(1)}, u32[]{:S(2)}, u32[]{:S(2)}) collective-permute-start(bf16[1,2048]{1,0:T(2,128)(2,1)} %param.14), channel_id=1, source_target_pairs={{0,8},{8,0},{16,24},{24,16},{32,40},{40,32},{48,56},{56,48},{64,72... | collective-permute-start | bytes 12296 | tf_op jit(solution)/shard_map/ppermute | solution.py:20
  6.5 3.0 %slice_bitcast_fusion = bf16[2,2,2048,1,128]{4,2,1,0,3:T(8,128)(2,1)} fusion(bf16[2,2,3,2048,1,128]{5,3,4,2,1,0:T(8,128)(2,1)} %param.15), kind=kLoop, calls=%fused_computation.12 | loop fusion | bytes 4194304 | tf_op jit(solution)/shard_map/squeeze | solution.py:158
  11.9 1.7 %slice_bitcast_fusion.18 = (bf16[256,2048]{0,1:T(8,128)(2,1)S(1)}, bf16[256,2048]{0,1:T(8,128)(2,1)S(1)}) fusion(bf16[2,2048,256]{2,1,0:T(8,128)(2,1)} %param.22), kind=kLoop, calls=%fused_computation.56 | loop fusion | bytes 4194304 | tf_op jit(solution)/shard_map/dot_general | solution.py:47
  17.2 1.4 %multiply_reduce_fusion.5 = (f32[3]{0:T(128)S(1)}, f32[3,128]{1,0:T(4,128)S(1)}) fusion(bf16[2,2048,128]{2,1,0:T(8,128)(2,1)} %param.23, f32[2048]{0:T(1024)S(1)} %bitcast.414, f32[3]{0:T(128)S(1)} %add_rsqrt_fusion.11, bf16[1,2048]{1,0:T(2,128)(2,1)S(1)} %collective-permute-done, bf16[2,2048]{1,0:T(2,128)(2,1)S(1)} %slice.219), kind=kOutput, calls=%fused_computation.200 | convolution fusion | flops 1616637 | bytes 546328 | tf_op jit(solution)/shard_map/dot_general | solution.py:50
  21.1 1.7 %fusion.203 = (f32[2,2]{1,0:T(2,128)S(1)}, f32[2,2,2048]{2,1,0:T(2,128)S(1)}) fusion(bf16[2,2,1,2,2048,1,128]{6,4,3,5,2,1,0:T(8,128)(2,1)} %bitcast.441, bf16[2,2,128]{2,0,1:T(2,128)(2,1)S(1)} %pad_maximum_fusion.4, pred[2,2048]{1,0:T(4,128)(4,1)S(1)} %broadcast_compare_fusion), kind=kOutput, calls=%fused_computation.350 | convolution fusion | flops 2121724 | bytes 1086480 | tf_op jit(solution)/shard_map/vmap(kgd,tkd->kgt)/dot_general | solution.py:74
  23.0 1.5 %fusion.23 = f32[2,2,128]{2,1,0:T(2,128)S(1)} fusion(bf16[2,2,1,2,2048,1,128]{6,4,3,5,2,1,0:T(8,128)(2,1)} %bitcast.442, f32[2,2,2048]{2,1,0:T(2,128)S(1)} %get-tuple-element.64, f32[2,2]{1,0:T(2,128)S(1)} %get-tuple-element.63), kind=kOutput, calls=%fused_computation.45 | convolution fusion | flops 2113536 | bytes 1083408 | tf_op jit(solution)/shard_map/vmap(kgt,tkd->kgd)/dot_general | solution.py:99
  25.7 1.8 %fusion.205 = (f32[2,2]{1,0:T(2,128)S(1)}, f32[2,2,2048]{2,1,0:T(2,128)S(1)}) fusion(bf16[2,2,3,2048,1,128]{5,3,2,4,1,0:T(8,128)(2,1)} %bitcast.404, bf16[2,2,128]{2,0,1:T(2,128)(2,1)S(1)} %fusion.143, pred[2,2048]{1,0:T(4,128)(4,1)S(1)} %bitcast.420), kind=kOutput, calls=%fused_computation.352 | convolution fusion | flops 2121724 | bytes 1086480 | tf_op jit(solution)/shard_map/vmap(kgd,tkd->kgt)/dot_general | solution.py:74
  27.7 1.5 %fusion.11 = bf16[1,2,2,128]{3,2,1,0:T(2,128)(2,1)S(1)} fusion(bf16[2,2,3,2048,1,128]{5,3,2,4,1,0:T(8,128)(2,1)} %bitcast.405, f32[2,2,2048]{2,1,0:T(2,128)S(1)} %get-tuple-element.72, f32[2,2]{1,0:T(2,128)S(1)} %multiply_maximum_fusion.1, f32[2,2]{1,0:T(2,128)S(1)} %get-tuple-element.42, f32[2,128]{1,0:T(2,128)S(1)} %slice_convert_fusion.1, ...), kind=kOutput, calls=%fused_computation.22 | convolution fusion | flops 2115584 | bytes 1083440 | tf_op jit(solution)/shard_map/vmap(kgt,tkd->kgd)/dot_general | solution.py:87
  29.5 1.9 %collective-permute-start.3 = (f32[2,1,2]{2,0,1:T(2,128)S(1)}, f32[2,1,2]{2,0,1:T(2,128)S(1)}, u32[]{:S(2)}, u32[]{:S(2)}) collective-permute-start(f32[2,1,2]{2,0,1:T(2,128)S(1)} %bitcast.428), channel_id=1, source_target_pairs={{0,8},{8,0},{16,24},{24,16},{32,40},{40,32},{48,56},{56,48},{64,72... | collective-permute-start | bytes 56 | tf_op jit(solution)/shard_map/ppermute | solution.py:20
  33.1 1.9 %collective-permute-done.4 = f32[2,1,2,128]{3,2,0,1:T(2,128)S(1)} collective-permute-done((f32[2,1,2,128]{3,2,0,1:T(2,128)S(1)}, f32[2,1,2,128]{3,2,0,1:T(2,128)S(1)}, u32[]{:S(2)}, u32[]{:S(2)}) %collective-permute-start.4) | collective-permute-done | bytes 2080 | tf_op jit(solution)/shard_map/ppermute | solution.py:20
  35.1 23.1 %collective-permute-done.2 = bf16[2,2,2048,1,128]{4,2,1,0,3:T(8,128)(2,1)} collective-permute-done((bf16[2,2,2048,1,128]{4,2,1,0,3:T(8,128)(2,1)}, bf16[2,2,2048,1,128]{4,2,1,0,3:T(8,128)(2,1)}, u32[]{:S(2)}, u32[]{:S(2)}) %collective-permute-start.2) | collective-permute-done | bytes 2097184 | tf_op jit(solution)/shard_map/ppermute | solution.py:14
  58.1 1.4 %fusion.204 = (f32[2]{0:T(128)S(1)}, f32[2,2048]{1,0:T(2,128)S(1)}) fusion(bf16[2,2,2048,1,128]{4,2,1,0,3:T(8,128)(2,1)} %collective-permute-done.2, bf16[1,2,128]{2,0,1:T(2,128)(2,1)S(1)} %pad_maximum_fusion.2, pred[2048]{0:T(1024)(128)(4,1)S(1)} %slice_reduce_fusion), kind=kOutput, calls=%fused_computation.351 | convolution fusion | flops 1060862 | bytes 543240 | tf_op jit(solution)/shard_map/kgd,tkd->kgt/dot_general | solution.py:74
  61.3 24.8 %psum.14 = f32[5,2048]{1,0:T(8,128)S(1)} all-reduce(f32[5,2048]{1,0:T(8,128)S(1)} %fusion.26), channel_id=1, replica_groups=mesh['replica'=32,'tensor'=8] {'tensor'}, use_global_device_ids=true, to_apply=%region_12.13 | all-reduce | flops 10240 | bytes 81920 | tf_op jit(solution)/shard_map/psum | solution.py:227
  86.5 1.4 %convolution_convert_fusion = bf16[3,128]{1,0:T(4,128)(2,1)S(1)} fusion(bf16[2,2048,128]{2,1,0:T(8,128)(2,1)} %param.24, f32[2048]{0:T(1024)S(1)} %bitcast.408, f32[3]{0:T(128)S(1)} %add_rsqrt_fusion.7, bf16[5,2048]{1,0:T(8,128)(2,1)S(1)} %add_convert_fusion), kind=kOutput, calls=%fused_computation.17 | convolution fusion | flops 1597824 | bytes 550144 | tf_op jit(solution)/shard_map/dot_general | solution.py:54
  89.2 1.4 %multiply_reduce_fusion.6 = (f32[2]{0:T(128)S(1)}, f32[2,128]{1,0:T(2,128)S(1)}) fusion(bf16[2,2048,128]{2,1,0:T(8,128)(2,1)} %param.23, f32[2]{0:T(128)S(1)} %add_rsqrt_fusion.5, f32[2048]{0:T(1024)S(1)} %bitcast.410, bf16[5,2048]{1,0:T(8,128)(2,1)S(1)} %add_convert_fusion), kind=kOutput, calls=%fused_computation.244 | convolution fusion | flops 1065470 | bytes 542216 | tf_op jit(solution)/shard_map/dot_general | solution.py:50
  91.5 1.4 %multiply_reduce_fusion.3 = (f32[3]{0:T(128)S(1)}, f32[3,128]{1,0:T(4,128)S(1)}) fusion(bf16[2,2048,128]{2,1,0:T(8,128)(2,1)} %param.23, f32[2048]{0:T(1024)S(1)} %bitcast.413, f32[3]{0:T(128)S(1)} %add_rsqrt_fusion.7, bf16[5,2048]{1,0:T(8,128)(2,1)S(1)} %add_convert_fusion), kind=kOutput, calls=%fused_computation.194 | convolution fusion | flops 1598205 | bytes 550924 | tf_op jit(solution)/shard_map/dot_general | solution.py:50
  95.3 1.7 %fusion.208 = (f32[2,2]{1,0:T(2,128)S(1)}, f32[2,2,2048]{2,1,0:T(2,128)S(1)}) fusion(bf16[2,2,3,2048,1,128]{5,3,2,4,1,0:T(8,128)(2,1)} %bitcast.406, bf16[2,2,128]{2,0,1:T(2,128)(2,1)S(1)} %fusion.142, pred[2,2048]{1,0:T(4,128)(4,1)S(1)} %bitcast.421), kind=kOutput, calls=%fused_computation.355 | convolution fusion | flops 2121724 | bytes 1086480 | tf_op jit(solution)/shard_map/vmap(kgd,tkd->kgt)/dot_general | solution.py:74
  97.2 1.4 %fusion.207 = (f32[2]{0:T(128)S(1)}, f32[2,2048]{1,0:T(2,128)S(1)}) fusion(bf16[2,2,2048,1,128]{4,2,1,0,3:T(8,128)(2,1)} %collective-permute-done.2, bf16[1,2,128]{2,0,1:T(2,128)(2,1)S(1)} %pad_maximum_fusion.1, pred[2048]{0:T(1024)(128)(4,1)S(1)} %slice_reduce_fusion), kind=kOutput, calls=%fused_computation.354 | convolution fusion | flops 1060862 | bytes 543240 | tf_op jit(solution)/shard_map/kgd,tkd->kgt/dot_general | solution.py:74
  101.6 1.5 %fusion.10 = bf16[1,2,2,128]{3,2,1,0:T(2,128)(2,1)S(1)} fusion(bf16[2,2,3,2048,1,128]{5,3,2,4,1,0:T(8,128)(2,1)} %bitcast.407, f32[2,2,2048]{2,1,0:T(2,128)S(1)} %get-tuple-element.86, f32[2,2]{1,0:T(2,128)S(1)} %multiply_maximum_fusion, f32[2,2]{1,0:T(2,128)S(1)} %get-tuple-element.36, f32[2,128]{1,0:T(2,128)S(1)} %slice_convert_fusion, ...), kind=kOutput, calls=%fused_computation.21 | convolution fusion | flops 2115584 | bytes 1083440 | tf_op jit(solution)/shard_map/vmap(kgt,tkd->kgd)/dot_general | solution.py:87
  103.7 1.6 %collective-permute-start.6 = (f32[2,1,2]{2,0,1:T(2,128)S(1)}, f32[2,1,2]{2,0,1:T(2,128)S(1)}, u32[]{:S(2)}, u32[]{:S(2)}) collective-permute-start(f32[2,1,2]{2,0,1:T(2,128)S(1)} %bitcast.426), channel_id=1, source_target_pairs={{0,8},{8,0},{16,24},{24,16},{32,40},{40,32},{48,56},{56,48},{64,72... | collective-permute-start | bytes 56 | tf_op jit(solution)/shard_map/ppermute | solution.py:20
  107.3 1.5 %collective-permute-done.7 = f32[2,1,2,128]{3,2,0,1:T(2,128)S(1)} collective-permute-done((f32[2,1,2,128]{3,2,0,1:T(2,128)S(1)}, f32[2,1,2,128]{3,2,0,1:T(2,128)S(1)}, u32[]{:S(2)}, u32[]{:S(2)}) %collective-permute-start.7) | collective-permute-done | bytes 2080 | tf_op jit(solution)/shard_map/ppermute | solution.py:20
  109.2 23.9 %psum.15 = f32[5,2048]{1,0:T(8,128)S(1)} all-reduce(f32[5,2048]{1,0:T(8,128)S(1)} %fusion.24), channel_id=1, replica_groups=mesh['replica'=32,'tensor'=8] {'tensor'}, use_global_device_ids=true, to_apply=%region_25.26 | all-reduce | flops 10240 | bytes 81920 | tf_op jit(solution)/shard_map/psum | solution.py:227
  134.4 3.0 %copy.125 = bf16[1,2,2,2048,1,128]{5,3,4,2,1,0:T(8,128)(2,1)} copy(bf16[1,2,2,2048,1,128]{5,3,4,2,1,0:T(8,128)(2,1)} %dynamic_update_slice.4) | data formatting | bytes 4194304
  (158 shorter events, 24.7 us)
Async XLA Ops:
  1.4 8.7 %copy-start.9 = (s32[96]{0:T(128)S(1)}, s32[96]{0:T(128)}, u32[]{:S(2)}) copy-start(s32[96]{0:T(128)} %param.17) | copy-start | bytes 1156
  1.4 9.3 %copy-start.4 = (f32[2,128]{1,0:T(2,128)S(1)}, f32[2,128]{1,0:T(2,128)}, u32[]{:S(2)}) copy-start(f32[2,128]{1,0:T(2,128)} %param.20) | copy-start | bytes 3076
  1.4 9.3 %copy-start.5 = (f32[2,128]{1,0:T(2,128)S(1)}, f32[2,128]{1,0:T(2,128)}, u32[]{:S(2)}) copy-start(f32[2,128]{1,0:T(2,128)} %param.21) | copy-start | bytes 3076
  1.4 10.0 %copy-start.6 = (s32[32]{0:T(128)S(1)}, s32[32]{0:T(128)}, u32[]{:S(2)}) copy-start(s32[32]{0:T(128)} %param.18) | copy-start | bytes 388
  1.4 10.4 %copy-start.1 = (f32[2,2048]{1,0:T(2,128)S(1)}, f32[2,2048]{1,0:T(2,128)}, u32[]{:S(2)}) copy-start(f32[2,2048]{1,0:T(2,128)} %param.19) | copy-start | bytes 49156
  1.4 15.6 %collective-permute-start = (bf16[1,2048]{1,0:T(2,128)(2,1)S(1)}, bf16[1,2048]{1,0:T(2,128)(2,1)S(1)}, u32[]{:S(2)}, u32[]{:S(2)}) collective-permute-start(bf16[1,2048]{1,0:T(2,128)(2,1)S(1)} %slice.220), channel_id=1, source_target_pairs={{128,0},{136,8},{144,16},{152,24},{160,32},{168,40},{176,48},{184,... | collective-permute-start | bytes 12296 | tf_op jit(solution)/shard_map/ppermute | solution.py:14
  4.5 14.3 %collective-permute-start.1 = (bf16[1,2048]{1,0:T(2,128)(2,1)}, bf16[1,2048]{1,0:T(2,128)(2,1)S(1)}, u32[]{:S(2)}, u32[]{:S(2)}) collective-permute-start(bf16[1,2048]{1,0:T(2,128)(2,1)} %param.14), channel_id=1, source_target_pairs={{0,8},{8,0},{16,24},{24,16},{32,40},{40,32},{48,56},{56,48},{64,72... | collective-permute-start | bytes 12296 | tf_op jit(solution)/shard_map/ppermute | solution.py:20
  9.5 48.6 %collective-permute-start.2 = (bf16[2,2,2048,1,128]{4,2,1,0,3:T(8,128)(2,1)}, bf16[2,2,2048,1,128]{4,2,1,0,3:T(8,128)(2,1)}, u32[]{:S(2)}, u32[]{:S(2)}) collective-permute-start(bf16[2,2,2048,1,128]{4,2,1,0,3:T(8,128)(2,1)} %slice_bitcast_fusion), channel_id=1, source_target_pairs={{128,0},{136,8},{144,16},{152,24},{160,32},{168,40},{176,48},{184,... | collective-permute-start | bytes 6291464 | tf_op jit(solution)/shard_map/ppermute | solution.py:14
  11.9 3.1 %copy-start.2 = (bf16[3,2048]{1,0:T(4,128)(2,1)S(1)}, bf16[3,2048]{1,0:T(4,128)(2,1)}, u32[]{:S(2)}) copy-start(bf16[3,2048]{1,0:T(4,128)(2,1)} %param.13) | copy-start | bytes 36868
  15.0 3.8 %copy-start.3 = (bf16[1,2048]{1,0:T(2,128)(2,1)S(1)}, bf16[1,2048]{1,0:T(2,128)(2,1)}, u32[]{:S(2)}) copy-start(bf16[1,2048]{1,0:T(2,128)(2,1)} %param.14) | copy-start | bytes 12292
  18.5 6.0 %copy-start.8 = (bf16[2,2048,128]{2,1,0:T(8,128)(2,1)S(1)}, bf16[2,2048,128]{2,1,0:T(8,128)(2,1)}, u32[]{:S(2)}) copy-start(bf16[2,2048,128]{2,1,0:T(8,128)(2,1)} %param.24) | copy-start | bytes 3145732
  25.7 35.4 %copy-start = (bf16[2,256,2048]{2,1,0:T(8,128)(2,1)S(1)}, bf16[2,256,2048]{2,1,0:T(8,128)(2,1)}, u32[]{:S(2)}) copy-start(bf16[2,256,2048]{2,1,0:T(8,128)(2,1)} %param.25) | copy-start | bytes 6291460
  29.3 3.7 %collective-permute-start.5 = (f32[2,1,2]{2,0,1:T(2,128)S(1)}, f32[2,1,2]{2,0,1:T(2,128)S(1)}, u32[]{:S(2)}, u32[]{:S(2)}) collective-permute-start(f32[2,1,2]{2,0,1:T(2,128)S(1)} %bitcast.429), channel_id=1, source_target_pairs={{0,8},{8,0},{16,24},{24,16},{32,40},{40,32},{48,56},{56,48},{64,72... | collective-permute-start | bytes 56 | tf_op jit(solution)/shard_map/ppermute | solution.py:20
  29.5 3.6 %collective-permute-start.3 = (f32[2,1,2]{2,0,1:T(2,128)S(1)}, f32[2,1,2]{2,0,1:T(2,128)S(1)}, u32[]{:S(2)}, u32[]{:S(2)}) collective-permute-start(f32[2,1,2]{2,0,1:T(2,128)S(1)} %bitcast.428), channel_id=1, source_target_pairs={{0,8},{8,0},{16,24},{24,16},{32,40},{40,32},{48,56},{56,48},{64,72... | collective-permute-start | bytes 56 | tf_op jit(solution)/shard_map/ppermute | solution.py:20
  31.4 3.6 %collective-permute-start.4 = (f32[2,1,2,128]{3,2,0,1:T(2,128)S(1)}, f32[2,1,2,128]{3,2,0,1:T(2,128)S(1)}, u32[]{:S(2)}, u32[]{:S(2)}) collective-permute-start(f32[2,1,2,128]{3,2,0,1:T(2,128)S(1)} %bitcast.435), channel_id=1, source_target_pairs={{0,8},{8,0},{16,24},{24,16},{32,40},{40,32},{48,56},{56,48},{64,72... | collective-permute-start | bytes 6152 | tf_op jit(solution)/shard_map/ppermute | solution.py:20
  86.5 7.4 %copy-start.7 = (bf16[2,2,1,2,2048,1,128]{6,4,5,3,2,1,0:T(8,128)(2,1)S(1)}, bf16[2,2,1,2,2048,1,128]{6,4,5,3,2,1,0:T(8,128)(2,1)}, u32[]{:S(2)}) copy-start(bf16[2,2,1,2,2048,1,128]{6,4,5,3,2,1,0:T(8,128)(2,1)} %param.16) | copy-start | bytes 12582916
  103.2 3.7 %collective-permute-start.8 = (f32[2,1,2]{2,0,1:T(2,128)S(1)}, f32[2,1,2]{2,0,1:T(2,128)S(1)}, u32[]{:S(2)}, u32[]{:S(2)}) collective-permute-start(f32[2,1,2]{2,0,1:T(2,128)S(1)} %bitcast.427), channel_id=1, source_target_pairs={{0,8},{8,0},{16,24},{24,16},{32,40},{40,32},{48,56},{56,48},{64,72... | collective-permute-start | bytes 56 | tf_op jit(solution)/shard_map/ppermute | solution.py:20
  103.7 3.6 %collective-permute-start.6 = (f32[2,1,2]{2,0,1:T(2,128)S(1)}, f32[2,1,2]{2,0,1:T(2,128)S(1)}, u32[]{:S(2)}, u32[]{:S(2)}) collective-permute-start(f32[2,1,2]{2,0,1:T(2,128)S(1)} %bitcast.426), channel_id=1, source_target_pairs={{0,8},{8,0},{16,24},{24,16},{32,40},{40,32},{48,56},{56,48},{64,72... | collective-permute-start | bytes 56 | tf_op jit(solution)/shard_map/ppermute | solution.py:20
  105.3 3.6 %collective-permute-start.7 = (f32[2,1,2,128]{3,2,0,1:T(2,128)S(1)}, f32[2,1,2,128]{3,2,0,1:T(2,128)S(1)}, u32[]{:S(2)}, u32[]{:S(2)}) collective-permute-start(f32[2,1,2,128]{3,2,0,1:T(2,128)S(1)} %bitcast.434), channel_id=1, source_target_pairs={{0,8},{8,0},{16,24},{24,16},{32,40},{40,32},{48,56},{56,48},{64,72... | collective-permute-start | bytes 6152 | tf_op jit(solution)/shard_map/ppermute | solution.py:20
where the time goes:
time: 138 us; the launch traced here: 137 us
  blocking collectives  48.8 us (35%)
  waiting for transfers between devices  28.8 us (21%)
  matrix products  27.8 us (20%)
  local copies, waits for them, and re-layouts  13.2 us (10%)
  starting transfers between devices  10.3 us (7%)
  other arithmetic  5.61 us (4%)
  between operations  3.04 us (2%)
    psum x2, blocking collectives, local(): summed = lax.psum(heads_out, 'tensor')  48.8 us
    ppermute x2, waiting for transfers between devices, shifted(): return lax.ppermute(block, axis, route)  23.1 us
    dot_general x6, matrix products, masked_scores(): jnp.einsum('kgd,tkd->kgt', grouped, key_rows, preferred_element_type=jnp....  8.49 us
    ppermute x7, starting transfers between devices, partner_2(): return lax.ppermute(value, axis, pairs)  6.72 us
    ppermute x7, waiting for transfers between devices, partner_2(): return lax.ppermute(value, axis, pairs)  5.72 us
    dot_general x4, matrix products, attend(): jnp.einsum('kgt,tkd->kgd', weights.astype(jnp.bfloat16), value_rows, pref...  5.64 us
    dot_general x4, matrix products, project(): jnp.dot(normed, key_weight, preferred_element_type=jnp.float32)  5.57 us
    ppermute x2, starting transfers between devices, shifted(): return lax.ppermute(block, axis, route)  3.62 us
  transfers between devices with their start and end apart: 9, of which 7 were waited for; matrix products, arithmetic and copies ran while one was open for 15% of the time, Pallas kernels for 0%

commit v1 on v0

v1 whole, which is shorter than its diff:
```python
import functools

import jax
import jax.numpy as jnp
import numpy as np
from jax import lax
from jax.experimental import pallas as pl
from jax.experimental.pallas import tpu as pltpu
from jax.sharding import PartitionSpec as P

EPSILON = 1e-06
ROPE_BASE = 1000000.0
NEGATIVE = -1e30
ROWS = 8
ANY = pl.BlockSpec(memory_space=pltpu.HBM)
VM = pl.BlockSpec(memory_space=pltpu.VMEM)
SM = pl.BlockSpec(memory_space=pltpu.SMEM)


def permute(value, axis, target):
    pairs = [(source, target(source)) for source in range(lax.axis_size(axis))]
    return lax.ppermute(value, axis, pairs)


def row_of(count):
    return lax.broadcasted_iota(jnp.int32, (count, 1), 0)


def attention_step(
    layer, group_ref, lengths_ref, long_lengths_ref, hidden, gain_ref, q_gain_ref, k_gain_ref,
    cosine_ref, sine_ref, cache_ref, long_ref, wq_ref, wk_ref, wv_ref,
    state_ref, side_ref, fresh_ref, buffers, semaphores,
):
    wq, wk, wv, keys, values, long_keys, long_values = buffers
    sources = (
        wq_ref.at[layer], wk_ref.at[layer], wv_ref.at[layer],
        cache_ref.at[layer, 0], long_ref.at[layer, 0, 0],
        cache_ref.at[layer, 1], long_ref.at[layer, 1, 0],
    )
    targets = (wq, wk, wv, keys, long_keys, values, long_values)
    copies = [
        pltpu.make_async_copy(source, target, semaphores.at[i])
        for i, (source, target) in enumerate(zip(sources, targets))
    ]
    for copy in copies:
        copy.start()
    rows = hidden()
    scale = lax.rsqrt(jnp.mean(rows * rows, axis=-1, keepdims=True) + EPSILON)
    normed = (rows * scale * gain_ref[layer : layer + 1, :]).astype(jnp.bfloat16)
    for copy in copies[:3]:
        copy.wait()
    queries = jnp.dot(normed, wq[...], preferred_element_type=jnp.float32)
    new_keys = jnp.dot(normed, wk[...], preferred_element_type=jnp.float32)
    new_values = jnp.dot(normed, wv[...], preferred_element_type=jnp.float32).astype(jnp.bfloat16)

    def finish(heads, gain, cosine, sine):
        heads = heads * lax.rsqrt(jnp.mean(heads * heads, axis=-1, keepdims=True) + EPSILON) * gain
        return (heads * cosine + pltpu.roll(heads, 64, 1) * sine).astype(jnp.bfloat16)

    cosine, sine = cosine_ref[...], sine_ref[...]
    q_gain = q_gain_ref[layer : layer + 1, :]
    q0 = finish(queries[:, :128], q_gain, cosine, sine).astype(jnp.float32)
    q1 = finish(queries[:, 128:], q_gain, cosine, sine).astype(jnp.float32)
    key_new = finish(new_keys, k_gain_ref[layer : layer + 1, :], cosine, sine).astype(jnp.float32)
    value_new = new_values.astype(jnp.float32)
    fresh_ref[0:1, :] = key_new[2:3, :]
    fresh_ref[1:2, :] = value_new[2:3, :]
    both = jnp.concatenate([q0, q1], axis=0)
    query = both.astype(jnp.bfloat16)
    keys_twice = jnp.concatenate([key_new, key_new], axis=0)
    values_twice = jnp.concatenate([value_new, value_new], axis=0)
    factor = 128 ** (-0.5)
    own = jnp.sum(both * keys_twice, axis=-1, keepdims=True) * factor

    group = group_ref[0]
    parity = lax.rem(group, 2)
    which = lax.rem(row_of(16), 8)
    limit = jnp.ones((16, 1), jnp.int32)
    for r in range(3):
        limit = jnp.where(which == r, lengths_ref[group * 3 + r], limit)
    for r in range(2):
        limit = jnp.where(
            which == 3 + r, long_lengths_ref[group - parity + r] - parity * 2048, limit
        )
    scores = jnp.zeros((16, 2048), jnp.float32)
    for r in range(5):
        if r == 0:
            copies[3].wait()
        if r == 3:
            copies[4].wait()
        block = keys[r] if r < 3 else long_keys[r - 3]
        product = lax.dot_general(
            query, block, (((1,), (1,)), ((), ())), preferred_element_type=jnp.float32
        )
        scores = jnp.where(which == r, product, scores)
    places = lax.broadcasted_iota(jnp.int32, (16, 2048), 1)
    scores = jnp.where(places < limit, scores * factor, NEGATIVE)
    is_main = which < 3
    highest = jnp.max(scores, axis=-1, keepdims=True)
    highest = jnp.where(is_main, jnp.maximum(highest, own), highest)
    weights = jnp.exp(scores - highest)
    own_weight = jnp.where(is_main, jnp.exp(own - highest), 0.0)
    total = jnp.sum(weights, axis=-1, keepdims=True) + own_weight
    rounded = weights.astype(jnp.bfloat16)
    summed = own_weight.astype(jnp.bfloat16).astype(jnp.float32) * values_twice
    for r in range(5):
        if r == 0:
            copies[5].wait()
        if r == 3:
            copies[6].wait()
        block = values[r] if r < 3 else long_values[r - 3]
        product = jnp.dot(rounded, block, preferred_element_type=jnp.float32)
        summed = summed + jnp.where(which == r, product, 0.0)
    state_ref[:, 0:128] = summed
    lanes = lax.broadcasted_iota(jnp.int32, (16, 128), 1)
    state_ref[:, 128:256] = jnp.where(lanes < 64, highest, total)
    side_ref[:, 0:128] = jnp.broadcast_to(own, (16, 128))
    side_ref[:, 128:256] = values_twice


def first_kernel(
    group_ref, lengths_ref, long_lengths_ref, tokens_ref, own_long_ref, far_long_ref, *rest
):
    *middle, state_ref, side_ref, fresh_ref, hidden_ref = rest[:14]
    buffers, semaphores = rest[14:21], rest[21]

    def hidden():
        own = own_long_ref[...].astype(jnp.float32)
        far = far_long_ref[...].astype(jnp.float32)
        even = lax.rem(group_ref[0], 2) == 0
        hidden_ref[...] = jnp.zeros((ROWS, 2048), jnp.float32)
        hidden_ref[0:3, :] = tokens_ref[...].astype(jnp.float32)
        hidden_ref[3:4, :] = jnp.where(even, own, far)
        hidden_ref[4:5, :] = jnp.where(even, far, own)
        return hidden_ref[...]

    attention_step(
        0, group_ref, lengths_ref, long_lengths_ref, hidden, *middle,
        state_ref, side_ref, fresh_ref, buffers, semaphores,
    )


def second_kernel(
    group_ref, lengths_ref, long_lengths_ref, before_ref, p_ref, r1_ref, r2_ref, r3_ref, *rest
):
    *middle, state_ref, side_ref, fresh_ref, hidden_ref = rest[:14]
    buffers, semaphores = rest[14:21], rest[21]

    def hidden():
        summed = (p_ref[...] + r1_ref[...]) + (r2_ref[...] + r3_ref[...])
        rows = (before_ref[...] + summed).astype(jnp.bfloat16).astype(jnp.float32)
        hidden_ref[...] = rows
        return rows

    attention_step(
        1, group_ref, lengths_ref, long_lengths_ref, hidden, *middle,
        state_ref, side_ref, fresh_ref, buffers, semaphores,
    )


def out_kernel(layer, state_ref, far_ref, side_ref, w_ref, out_ref, w, semaphore):
    copy = pltpu.make_async_copy(w_ref.at[layer], w, semaphore)
    copy.start()
    is_main = lax.rem(row_of(16), 8) < 3
    here, far = state_ref[...], far_ref[...]
    m_here, l_here, acc_here = here[:, 128:129], here[:, 192:193], here[:, :128]
    m_far, l_far, acc_far = far[:, 128:129], far[:, 192:193], far[:, :128]
    own, value = side_ref[:, 0:1], side_ref[:, 128:256]
    highest = jnp.maximum(jnp.maximum(m_here, m_far), own)
    f_here, f_far = jnp.exp(m_here - highest), jnp.exp(m_far - highest)
    own_weight = jnp.exp(own - highest)
    total = (l_here * f_here + l_far * f_far) + own_weight
    own_rounded = own_weight.astype(jnp.bfloat16).astype(jnp.float32)
    summed = (acc_here * f_here + acc_far * f_far) + own_rounded * value
    total = jnp.where(is_main, l_here, total)
    summed = jnp.where(is_main, acc_here, summed)
    attended = summed / total
    attended = jnp.concatenate([attended[:8], attended[8:]], axis=1).astype(jnp.bfloat16)
    copy.wait()
    out_ref[...] = jnp.dot(attended, w[...], preferred_element_type=jnp.float32)


def final_kernel(
    group_ref, before_ref, p_ref, r1_ref, r2_ref, r3_ref, fresh0_ref, fresh1_ref,
    stay_ref, long_ref, leave_ref, scratch,
):
    summed = (p_ref[...] + r1_ref[...]) + (r2_ref[...] + r3_ref[...])
    scratch[...] = before_ref[...] + summed
    stay_ref[...] = scratch[0:2, :]
    odd = lax.rem(group_ref[0], 2) == 1
    long_ref[...] = jnp.where(odd, scratch[4:5, :], scratch[3:4, :])
    leave_ref[0:1, 0:2048] = scratch[2:3, :]
    for i, ref in enumerate((fresh0_ref, fresh1_ref)):
        for j in range(2):
            leave_ref[0:1, 2048 + 128 * (2 * i + j) : 2176 + 128 * (2 * i + j)] = ref[j : j + 1, :]


def local(
    tokens, long_tokens, cache, long_cache, lengths, long_lengths, norm_gain, q_gain, k_gain,
    w_query, key_weight, value_weight, w_out,
):
    groups = lax.axis_size("replica")
    group = lax.axis_index("replica")
    parity = group % 2
    group_1 = group[None]
    cache = cache.reshape(2, 2, 3, 2048, 128)
    long_cache = long_cache.reshape(2, 2, 1, 2, 2048, 128)

    far_token = permute(long_tokens, "replica", lambda i: i ^ 1)
    moving = permute(cache[:, :, 2], "replica", lambda i: (i + groups // 2) % groups)

    places = jnp.concatenate(
        [
            lax.dynamic_slice_in_dim(lengths, group * 3, 3),
            lax.dynamic_slice_in_dim(long_lengths, group - parity, 2),
            jnp.zeros((3,), jnp.int32),
        ]
    ).astype(jnp.float32)
    inverse = np.float64(ROPE_BASE) ** (-2.0 * np.arange(64) / 128)
    inverse = jnp.asarray(np.concatenate([inverse, inverse]).astype(np.float32))
    sign = jnp.asarray(np.where(np.arange(128) < 64, -1.0, 1.0).astype(np.float32))
    angles = places[:, None] * inverse[None, :]
    cosine, sine = jnp.cos(angles), jnp.sin(angles) * sign

    out_shape = (
        jax.ShapeDtypeStruct((16, 256), jnp.float32),
        jax.ShapeDtypeStruct((16, 256), jnp.float32),
        jax.ShapeDtypeStruct((2, 128), jnp.float32),
        jax.ShapeDtypeStruct((ROWS, 2048), jnp.float32),
    )
    scratch = [
        pltpu.VMEM((2048, 256), jnp.bfloat16),
        pltpu.VMEM((2048, 128), jnp.bfloat16),
        pltpu.VMEM((2048, 128), jnp.bfloat16),
        pltpu.VMEM((3, 2048, 128), jnp.bfloat16),
        pltpu.VMEM((3, 2048, 128), jnp.bfloat16),
        pltpu.VMEM((2, 2048, 128), jnp.bfloat16),
        pltpu.VMEM((2, 2048, 128), jnp.bfloat16),
        pltpu.SemaphoreType.DMA((7,)),
    ]
    params = pltpu.CompilerParams(vmem_limit_bytes=24 * 2**20)
    middle = (norm_gain, q_gain, k_gain, cosine, sine, cache, long_cache, w_query, key_weight, value_weight)
    middle_specs = [VM] * 5 + [ANY] * 5

    def project_out(layer, state, side):
        far = permute(state, "replica", lambda i: i ^ 1)
        part = pl.pallas_call(
            functools.partial(out_kernel, layer),
            out_shape=jax.ShapeDtypeStruct((ROWS, 2048), jnp.float32),
            in_specs=[VM, VM, VM, ANY],
            out_specs=VM,
            scratch_shapes=[pltpu.VMEM((256, 2048), jnp.bfloat16), pltpu.SemaphoreType.DMA(())],
            compiler_params=params,
            name=f"out_projection_{layer}",
        )(state, far, side, w_out)
        part = part + permute(part, "tensor", lambda i: i ^ 1)
        received = [permute(part, "tensor", lambda i, k=k: i ^ k) for k in (2, 4, 6)]
        return (part, *received)

    state, side, fresh_0, hidden = pl.pallas_call(
        first_kernel,
        out_shape=out_shape,
        in_specs=[SM] * 3 + [VM] * 3 + middle_specs,
        out_specs=(VM,) * 4,
        scratch_shapes=scratch,
        compiler_params=params,
        name="attention_0",
    )(group_1, lengths, long_lengths, tokens, long_tokens, far_token, *middle)
    terms = project_out(0, state, side)
    state, side, fresh_1, hidden = pl.pallas_call(
        second_kernel,
        out_shape=out_shape,
        in_specs=[SM] * 3 + [VM] * 5 + middle_specs,
        out_specs=(VM,) * 4,
        scratch_shapes=scratch,
        compiler_params=params,
        name="attention_1",
    )(group_1, lengths, long_lengths, hidden, *terms, *middle)
    terms = project_out(1, state, side)
    stay, long_out, leave = pl.pallas_call(
        final_kernel,
        out_shape=(
            jax.ShapeDtypeStruct((2, 2048), jnp.float32),
            jax.ShapeDtypeStruct((1, 2048), jnp.float32),
            jax.ShapeDtypeStruct((1, 2560), jnp.float32),
        ),
        in_specs=[SM] + [VM] * 7,
        out_specs=(VM,) * 3,
        scratch_shapes=[pltpu.VMEM((ROWS, 2048), jnp.float32)],
        name="final_rows",
    )(group_1, hidden, *terms, fresh_0, fresh_1)
    arrived = permute(leave, "replica", lambda i: (i + groups // 2) % groups)
    out_hidden = jnp.concatenate([stay, arrived[:, :2048]], axis=0)
    fresh = arrived[0, 2048:].reshape(2, 2, 1, 128).astype(jnp.bfloat16)
    partner = (group + groups // 2) % groups
    arrived_len = lax.dynamic_index_in_dim(lengths, partner * 3 + 2, 0, keepdims=False)
    at = lax.broadcasted_iota(jnp.int32, (1, 1, 2048, 1), 2) == arrived_len
    moved = jnp.where(at, fresh, moving)
    return (out_hidden, long_out, moved[None, :, :, :, None, :])


def solution(mesh):
    return jax.shard_map(
        local,
        mesh=mesh,
        in_specs=(
            P("replica", None),
            P("replica", None),
            P(None, None, "replica", None, "tensor", None),
            P(None, None, "replica", None, None, "tensor", None),
            P(),
            P(),
            P(),
            P(),
            P(),
            P(None, None, "tensor"),
            P(None, None, "tensor"),
            P(None, None, "tensor"),
            P(None, "tensor", None),
        ),
        out_specs=(
            P("replica", None),
            P("replica", None),
            P("replica", None, None, None, "tensor", None),
        ),
        check_vma=False,
    )
```

time: 138 us -> 67.7 us (0.49)
  blocking collectives: 48.8 us -> 0 us
  matrix products: 27.8 us -> 0 us
  Pallas kernels: 0 us -> 9.68 us
  waiting for transfers between devices: 28.8 us -> 19.5 us
  starting transfers between devices: 10.3 us -> 19.1 us
  between operations: 3.04 us -> 0.91 us
    psum x2 -> x0, blocking collectives: 48.8 us -> none  [local(): summed = lax.psum(heads_out, 'tensor')]
    dot_general x32 -> x0, matrix products: 27.8 us -> none  [the longest x6 8.49 us: masked_scores(): jnp.einsum('kgd,tkd->kgt', grouped, key_rows, preferred_element_type=jnp....]
    pallas_call x0 -> x5, Pallas kernels: none -> 9.68 us  [the longest x1 3.55 us: local(): pl.pallas_call(second_kernel, out_shape=out_shape, in_specs=[SM] * 3 + [V...]
    ppermute x9 -> x13, waiting for transfers between devices: 28.8 us -> 19.5 us  [permute(): return lax.ppermute(value, axis, pairs)]
    ppermute x9 -> x13, starting transfers between devices: 10.3 us -> 19.1 us  [permute(): return lax.ppermute(value, axis, pairs)]
    unnamed x27 -> x52, local copies, waits for them, and re-layouts: 3.14 us -> 9.05 us
    dot_general x3 -> x0, local copies, waits for them, and re-layouts: 2.97 us -> none  [project(): jnp.dot(normed, w_query, preferred_element_type=jnp.float32)]
    unnamed x2, other arithmetic: 0.16 us -> 2.75 us
  transfers between devices with their start and end apart: 9 -> 13, of which waited for: 7 -> 10; matrix products, arithmetic and copies ran while one was open for 15% -> 5% of each run, Pallas kernels for 0% -> 14%
where the time goes in v1:
time: 67.7 us; the launch traced here: 67.3 us
  waiting for transfers between devices  19.5 us (29%)
  starting transfers between devices  19.1 us (28%)
  local copies, waits for them, and re-layouts  13.1 us (19%)
  Pallas kernels  9.68 us (14%)
  other arithmetic  5 us (7%)
  between operations  0.91 us (1%)
    ppermute x13, waiting for transfers between devices, permute(): return lax.ppermute(value, axis, pairs)  19.5 us
    ppermute x13, starting transfers between devices, permute(): return lax.ppermute(value, axis, pairs)  19.1 us
    unnamed x52, local copies, waits for them, and re-layouts  9.05 us
    pallas_call x1, Pallas kernels, local(): pl.pallas_call(second_kernel, out_shape=out_shape, in_specs=[SM] * 3 + [V...  3.55 us
    pallas_call x1, Pallas kernels, local(): pl.pallas_call(first_kernel, out_shape=out_shape, in_specs=[SM] * 3 + [VM...  3.54 us
    squeeze x1, local copies, waits for them, and re-layouts, local(): cache[:, :, 2]  3.2 us
    unnamed x2, other arithmetic  2.75 us
    pallas_call x1, Pallas kernels, local(): pl.pallas_call(final_kernel, out_shape=(jax.ShapeDtypeStruct((2, 2048), j...  1.61 us
  transfers between devices with their start and end apart: 13, of which 10 were waited for; matrix products, arithmetic and copies ran while one was open for 5% of the time, Pallas kernels for 14%

profile of v1, /device:TPU:64, one launch (start us, length us, event | category | flops | bytes accessed | tf_op | source)
XLA Modules:
  0.0 67.3 jit_solution(12422246357206955863)
XLA Ops:
  0.8 3.2 %slice_bitcast_fusion = bf16[2,2,2048,128]{3,2,1,0:T(8,128)(2,1)} fusion(bf16[2,2,3,2048,128]{4,3,2,1,0:T(8,128)(2,1)} %bitcast.11), kind=kLoop, calls=%fused_computation | loop fusion | bytes 4194304 | tf_op jit(solution)/shard_map/squeeze | solution.py:210
  4.0 3.0 %collective-permute-start.12 = (bf16[2,2,2048,128]{3,2,1,0:T(8,128)(2,1)}, bf16[2,2,2048,128]{3,2,1,0:T(8,128)(2,1)}, u32[]{:S(2)}, u32[]{:S(2)}) collective-permute-start(bf16[2,2,2048,128]{3,2,1,0:T(8,128)(2,1)} %slice_bitcast_fusion), channel_id=1, source_target_pairs={{0,128},{8,136},{16,144},{24,152},{32,160},{40,168},{48,176},{56,1... | collective-permute-start | bytes 6291464 | tf_op jit(solution)/shard_map/ppermute | solution.py:22
  7.0 1.9 %collective-permute-start = (bf16[1,2048]{1,0:T(2,128)(2,1)S(1)}, bf16[1,2048]{1,0:T(2,128)(2,1)S(1)}, u32[]{:S(2)}, u32[]{:S(2)}) collective-permute-start(bf16[1,2048]{1,0:T(2,128)(2,1)S(1)} %copy-done.11), channel_id=1, source_target_pairs={{0,8},{8,0},{16,24},{24,16},{32,40},{40,32},{48,56},{56,48},{64,72... | collective-permute-start | bytes 12296 | tf_op jit(solution)/shard_map/ppermute | solution.py:22
  9.2 1.4 %collective-permute-done.far_long_ref = bf16[1,2048]{1,0:T(2,128)(2,1)S(1)} collective-permute-done((bf16[1,2048]{1,0:T(2,128)(2,1)S(1)}, bf16[1,2048]{1,0:T(2,128)(2,1)S(1)}, u32[]{:S(2)}, u32[]{:S(2)}) %collective-permute-start) | collective-permute-done | bytes 4128 | tf_op jit(solution)/shard_map/ppermute | solution.py:22
  10.7 2.8 %copy-done = bf16[2,2,3,2048,1,128]{5,3,4,2,1,0:T(8,128)(2,1)S(1)} copy-done((bf16[2,2,3,2048,1,128]{5,3,4,2,1,0:T(8,128)(2,1)S(1)}, bf16[2,2,3,2048,1,128]{5,3,4,2,1,0:T(8,128)(2,1)}, u32[]{:S(2)}) %copy-start) | copy-done | bytes 6291480
  13.5 2.2 %copy-done.1 = bf16[2,2,1,2,2048,1,128]{6,4,5,3,2,1,0:T(8,128)(2,1)S(1)} copy-done((bf16[2,2,1,2,2048,1,128]{6,4,5,3,2,1,0:T(8,128)(2,1)S(1)}, bf16[2,2,1,2,2048,1,128]{6,4,5,3,2,1,0:T(8,128)(2,1)}, u32[]{:S(2)}) %copy-start.1) | copy-done | bytes 4194328
  15.6 1.6 %copy-done.4 = bf16[2,2048,256]{2,1,0:T(8,128)(2,1)S(1)} copy-done((bf16[2,2048,256]{2,1,0:T(8,128)(2,1)S(1)}, bf16[2,2048,256]{2,1,0:T(8,128)(2,1)}, u32[]{:S(2)}) %copy-start.4) | copy-done | bytes 2097176
  18.5 3.5 %attention_0.1 = (f32[16,256]{1,0:T(8,128)S(1)}, f32[16,256]{1,0:T(8,128)S(1)}, f32[2,128]{1,0:T(2,128)S(1)}, f32[8,2048]{1,0:T(8,128)S(1)}) custom-call(s32[1]{0:T(128)} %bitcast.group_ref, s32[96]{0:T(128)S(1)} %copy-done.15, s32[32]{0:T(128)S(1)} %copy-done.14, bf16[3,2048]{1,0:T(4,128)(2,1)S(1)} %copy-done.10, bf16[1,2048]{1,0:T(2,128)(2,1)S(1)} %copy-done.11, ...), custom_call_target="tpu_custom_call" | custom-call | tf_op jit(solution)/shard_map/attention_0/pallas_call | solution.py:260
  22.6 1.9 %collective-permute-start.1 = (f32[16,256]{1,0:T(8,128)S(1)}, f32[16,256]{1,0:T(8,128)S(1)}, u32[]{:S(2)}, u32[]{:S(2)}) collective-permute-start(f32[16,256]{1,0:T(8,128)S(1)} %get-tuple-element.15.state_ref), channel_id=1, source_target_pairs={{0,8},{8,0},{16,24},{24,16},{32,40},{40,32},{48,56},{56,48},{64,72... | collective-permute-start | bytes 49160 | tf_op jit(solution)/shard_map/ppermute | solution.py:22
  24.5 1.8 %collective-permute-done.1.far_ref = f32[16,256]{1,0:T(8,128)S(1)} collective-permute-done((f32[16,256]{1,0:T(8,128)S(1)}, f32[16,256]{1,0:T(8,128)S(1)}, u32[]{:S(2)}, u32[]{:S(2)}) %collective-permute-start.1) | collective-permute-done | bytes 16416 | tf_op jit(solution)/shard_map/ppermute | solution.py:22
  26.9 1.2 %collective-permute-done.2 = f32[8,2048]{1,0:T(8,128)S(1)} collective-permute-done((f32[8,2048]{1,0:T(8,128)S(1)}, f32[8,2048]{1,0:T(8,128)S(1)}, u32[]{:S(2)}, u32[]{:S(2)}) %collective-permute-start.2) | collective-permute-done | bytes 65568 | tf_op jit(solution)/shard_map/ppermute | solution.py:22
  28.2 1.7 %collective-permute-start.3 = (f32[8,2048]{1,0:T(8,128)S(1)}, f32[8,2048]{1,0:T(8,128)S(1)}, u32[]{:S(2)}, u32[]{:S(2)}) collective-permute-start(f32[8,2048]{1,0:T(8,128)S(1)} %add.34.p_ref), channel_id=1, source_target_pairs={{0,2},{1,3},{2,0},{3,1},{4,6},{5,7},{6,4},{7,5},{8,10},{9,11},{10,... | collective-permute-start | bytes 196616 | tf_op jit(solution)/shard_map/ppermute | solution.py:22
  29.8 2.9 %collective-permute-start.4 = (f32[8,2048]{1,0:T(8,128)S(1)}, f32[8,2048]{1,0:T(8,128)S(1)}, u32[]{:S(2)}, u32[]{:S(2)}) collective-permute-start(f32[8,2048]{1,0:T(8,128)S(1)} %add.34.p_ref), channel_id=1, source_target_pairs={{0,4},{1,5},{2,6},{3,7},{4,0},{5,1},{6,2},{7,3},{8,12},{9,13},{10,... | collective-permute-start | bytes 196616 | tf_op jit(solution)/shard_map/ppermute | solution.py:22
  33.0 3.3 %collective-permute-done.4.r2_ref = f32[8,2048]{1,0:T(8,128)S(1)} collective-permute-done((f32[8,2048]{1,0:T(8,128)S(1)}, f32[8,2048]{1,0:T(8,128)S(1)}, u32[]{:S(2)}, u32[]{:S(2)}) %collective-permute-start.4) | collective-permute-done | bytes 65568 | tf_op jit(solution)/shard_map/ppermute | solution.py:22
  36.3 1.9 %collective-permute-done.5.r3_ref = f32[8,2048]{1,0:T(8,128)S(1)} collective-permute-done((f32[8,2048]{1,0:T(8,128)S(1)}, f32[8,2048]{1,0:T(8,128)S(1)}, u32[]{:S(2)}, u32[]{:S(2)}) %collective-permute-start.5) | collective-permute-done | bytes 65568 | tf_op jit(solution)/shard_map/ppermute | solution.py:22
  38.3 3.6 %attention_1.1 = (f32[16,256]{1,0:T(8,128)S(1)}, f32[16,256]{1,0:T(8,128)S(1)}, f32[2,128]{1,0:T(2,128)S(1)}, f32[8,2048]{1,0:T(8,128)S(1)}) custom-call(s32[1]{0:T(128)} %bitcast.group_ref, s32[96]{0:T(128)S(1)} %copy-done.15, s32[32]{0:T(128)S(1)} %copy-done.14, f32[8,2048]{1,0:T(8,128)S(1)} %get-tuple-element.14.before_ref, f32[8,2048]{1,0:T(8,128)S(1)} %add.34.p_ref, ...), custom_call_target="tpu_custom_call" | custom-call | tf_op jit(solution)/shard_map/attention_1/pallas_call | solution.py:270
  41.8 2.0 %collective-permute-start.6 = (f32[16,256]{1,0:T(8,128)S(1)}, f32[16,256]{1,0:T(8,128)S(1)}, u32[]{:S(2)}, u32[]{:S(2)}) collective-permute-start(f32[16,256]{1,0:T(8,128)S(1)} %get-tuple-element.18.state_ref), channel_id=1, source_target_pairs={{0,8},{8,0},{16,24},{24,16},{32,40},{40,32},{48,56},{56,48},{64,72... | collective-permute-start | bytes 49160 | tf_op jit(solution)/shard_map/ppermute | solution.py:22
  43.8 1.8 %collective-permute-done.6.far_ref = f32[16,256]{1,0:T(8,128)S(1)} collective-permute-done((f32[16,256]{1,0:T(8,128)S(1)}, f32[16,256]{1,0:T(8,128)S(1)}, u32[]{:S(2)}, u32[]{:S(2)}) %collective-permute-start.6) | collective-permute-done | bytes 16416 | tf_op jit(solution)/shard_map/ppermute | solution.py:22
  48.2 4.1 %collective-permute-start.9 = (f32[8,2048]{1,0:T(8,128)S(1)}, f32[8,2048]{1,0:T(8,128)S(1)}, u32[]{:S(2)}, u32[]{:S(2)}) collective-permute-start(f32[8,2048]{1,0:T(8,128)S(1)} %add.35.p_ref), channel_id=1, source_target_pairs={{0,4},{1,5},{2,6},{3,7},{4,0},{5,1},{6,2},{7,3},{8,12},{9,13},{10,... | collective-permute-start | bytes 196616 | tf_op jit(solution)/shard_map/ppermute | solution.py:22
  53.1 2.5 %collective-permute-done.9.r2_ref = f32[8,2048]{1,0:T(8,128)S(1)} collective-permute-done((f32[8,2048]{1,0:T(8,128)S(1)}, f32[8,2048]{1,0:T(8,128)S(1)}, u32[]{:S(2)}, u32[]{:S(2)}) %collective-permute-start.9) | collective-permute-done | bytes 65568 | tf_op jit(solution)/shard_map/ppermute | solution.py:22
  56.2 1.6 %final_rows.1 = (f32[2,2048]{1,0:T(2,128)}, f32[1,2048]{1,0:T(1,128)}, f32[1,2560]{1,0:T(1,128)}) custom-call(s32[1]{0:T(128)} %bitcast.group_ref, f32[8,2048]{1,0:T(8,128)} %copy-done.8, f32[8,2048]{1,0:T(8,128)} %copy-done.18, f32[8,2048]{1,0:T(8,128)} %copy-done.20, f32[8,2048]{1,0:T(8,128)} %copy-done.21, f32[8,2048]{1,0:T(8,128)} %copy-done.19, ...), custom_call_target="tpu_custom_call" | custom-call | tf_op jit(solution)/shard_map/final_rows/pallas_call | solution.py:280
  59.0 4.2 %collective-permute-done.11 = f32[1,2560]{1,0:T(1,128)S(1)} collective-permute-done((f32[1,2560]{1,0:T(1,128)}, f32[1,2560]{1,0:T(1,128)S(1)}, u32[]{:S(2)}, u32[]{:S(2)}) %collective-permute-start.11) | collective-permute-done | bytes 10272 | tf_op jit(solution)/shard_map/ppermute | solution.py:22
  63.2 1.3 %pad_maximum_fusion = f32[3,2048]{1,0:T(4,128)} fusion(f32[1,2048]{1,0:T(1,128)S(1)} %slice.13, f32[2,2048]{1,0:T(2,128)} %get-tuple-element.22), kind=kLoop, calls=%fused_computation.2 | loop fusion | flops 6144 | bytes 49152 | tf_op jit(solution)/shard_map/concatenate | solution.py:293
  64.6 2.7 %select_bitcast_fusion = bf16[1,2,2,2048,1,128]{5,3,4,2,1,0:T(8,128)(2,1)} fusion(bf16[2,2,2048,128]{3,2,1,0:T(8,128)(2,1)} %collective-permute-done.12, pred[2048]{0:T(1024)(128)(4,1)S(1)} %iota_compare_fusion, bf16[2,2,128]{2,1,0:T(2,128)(2,1)S(1)} %bitcast.18), kind=kLoop, calls=%fused_computation.1 | loop fusion | flops 1048576 | bytes 4197376
  (74 shorter events, 8.2 us)
Async XLA Ops:
  0.7 8.5 %copy-start.22 = (f32[128]{0:T(128)S(1)}, f32[128]{0:T(128)}, u32[]{:S(2)}) copy-start(f32[128]{0:T(128)} %constant.47.clone) | copy-start | bytes 1540
  0.7 9.9 %copy-start.6 = (bf16[2,2048,128]{2,1,0:T(8,128)(2,1)S(1)}, bf16[2,2048,128]{2,1,0:T(8,128)(2,1)}, u32[]{:S(2)}) copy-start(bf16[2,2048,128]{2,1,0:T(8,128)(2,1)} %rest_8_.3) | copy-start | bytes 3145732
  0.7 9.9 %copy-start.9 = (f32[2,2048]{1,0:T(2,128)S(1)}, f32[2,2048]{1,0:T(2,128)}, u32[]{:S(2)}) copy-start(f32[2,2048]{1,0:T(2,128)} %rest_0_.3) | copy-start | bytes 49156
  0.7 9.9 %copy-start.10 = (bf16[3,2048]{1,0:T(4,128)(2,1)S(1)}, bf16[3,2048]{1,0:T(4,128)(2,1)}, u32[]{:S(2)}) copy-start(bf16[3,2048]{1,0:T(4,128)(2,1)} %tokens_ref.1) | copy-start | bytes 36868
  0.7 9.9 %copy-start.12 = (f32[2,128]{1,0:T(2,128)S(1)}, f32[2,128]{1,0:T(2,128)}, u32[]{:S(2)}) copy-start(f32[2,128]{1,0:T(2,128)} %rest_1_.3) | copy-start | bytes 3076
  0.7 9.9 %copy-start.13 = (f32[2,128]{1,0:T(2,128)S(1)}, f32[2,128]{1,0:T(2,128)}, u32[]{:S(2)}) copy-start(f32[2,128]{1,0:T(2,128)} %rest_2_.3) | copy-start | bytes 3076
  0.7 37.5 %slice-start = ((s8[6291456]{0:T(1024)(128)(4,1)}), s8[2097152]{0:T(1024)(128)(4,1)S(1)}, s32[]{:S(2)}) async-start(s8[6291456]{0:T(1024)(128)(4,1)} %bitcast.13), calls=%async_computation | async-start | bytes 4194304
  4.0 60.6 %collective-permute-start.12 = (bf16[2,2,2048,128]{3,2,1,0:T(8,128)(2,1)}, bf16[2,2,2048,128]{3,2,1,0:T(8,128)(2,1)}, u32[]{:S(2)}, u32[]{:S(2)}) collective-permute-start(bf16[2,2,2048,128]{3,2,1,0:T(8,128)(2,1)} %slice_bitcast_fusion), channel_id=1, source_target_pairs={{0,128},{8,136},{16,144},{24,152},{32,160},{40,168},{48,176},{56,1... | collective-permute-start | bytes 6291464 | tf_op jit(solution)/shard_map/ppermute | solution.py:22
  7.0 3.7 %collective-permute-start = (bf16[1,2048]{1,0:T(2,128)(2,1)S(1)}, bf16[1,2048]{1,0:T(2,128)(2,1)S(1)}, u32[]{:S(2)}, u32[]{:S(2)}) collective-permute-start(bf16[1,2048]{1,0:T(2,128)(2,1)S(1)} %copy-done.11), channel_id=1, source_target_pairs={{0,8},{8,0},{16,24},{24,16},{32,40},{40,32},{48,56},{56,48},{64,72... | collective-permute-start | bytes 12296 | tf_op jit(solution)/shard_map/ppermute | solution.py:22
  18.5 19.8 %slice-start.1 = ((s8[6291456]{0:T(1024)(128)(4,1)}), s8[4194304]{0:T(1024)(128)(4,1)S(1)}, s32[]{:S(2)}) async-start(s8[6291456]{0:T(1024)(128)(4,1)} %bitcast.13), calls=%async_computation.1 | async-start | bytes 8388608
  18.5 19.8 %copy-start.2 = (bf16[2,2,1,2,2048,1,128]{6,4,5,3,2,1,0:T(8,128)(2,1)S(1)}, bf16[2,2,1,2,2048,1,128]{6,4,5,3,2,1,0:T(8,128)(2,1)}, u32[]{:S(2)}) copy-start(bf16[2,2,1,2,2048,1,128]{6,4,5,3,2,1,0:T(8,128)(2,1)} %param.18) | copy-start | bytes 12582916
  22.6 15.7 %copy-start.5 = (bf16[2,2048,256]{2,1,0:T(8,128)(2,1)S(1)}, bf16[2,2048,256]{2,1,0:T(8,128)(2,1)}, u32[]{:S(2)}) copy-start(bf16[2,2048,256]{2,1,0:T(8,128)(2,1)} %rest_7_.3) | copy-start | bytes 6291460
  22.6 3.7 %collective-permute-start.1 = (f32[16,256]{1,0:T(8,128)S(1)}, f32[16,256]{1,0:T(8,128)S(1)}, u32[]{:S(2)}, u32[]{:S(2)}) collective-permute-start(f32[16,256]{1,0:T(8,128)S(1)} %get-tuple-element.15.state_ref), channel_id=1, source_target_pairs={{0,8},{8,0},{16,24},{24,16},{32,40},{40,32},{48,56},{56,48},{64,72... | collective-permute-start | bytes 49160 | tf_op jit(solution)/shard_map/ppermute | solution.py:22
  26.8 1.3 %collective-permute-start.2 = (f32[8,2048]{1,0:T(8,128)S(1)}, f32[8,2048]{1,0:T(8,128)S(1)}, u32[]{:S(2)}, u32[]{:S(2)}) collective-permute-start(f32[8,2048]{1,0:T(8,128)S(1)} %out_projection_0.1), channel_id=1, source_target_pairs={{0,1},{1,0},{2,3},{3,2},{4,5},{5,4},{6,7},{7,6},{8,9},{9,8},{10,11... | collective-permute-start | bytes 196616 | tf_op jit(solution)/shard_map/ppermute | solution.py:22
  28.2 4.8 %collective-permute-start.3 = (f32[8,2048]{1,0:T(8,128)S(1)}, f32[8,2048]{1,0:T(8,128)S(1)}, u32[]{:S(2)}, u32[]{:S(2)}) collective-permute-start(f32[8,2048]{1,0:T(8,128)S(1)} %add.34.p_ref), channel_id=1, source_target_pairs={{0,2},{1,3},{2,0},{3,1},{4,6},{5,7},{6,4},{7,5},{8,10},{9,11},{10,... | collective-permute-start | bytes 196616 | tf_op jit(solution)/shard_map/ppermute | solution.py:22
  29.8 6.4 %collective-permute-start.4 = (f32[8,2048]{1,0:T(8,128)S(1)}, f32[8,2048]{1,0:T(8,128)S(1)}, u32[]{:S(2)}, u32[]{:S(2)}) collective-permute-start(f32[8,2048]{1,0:T(8,128)S(1)} %add.34.p_ref), channel_id=1, source_target_pairs={{0,4},{1,5},{2,6},{3,7},{4,0},{5,1},{6,2},{7,3},{8,12},{9,13},{10,... | collective-permute-start | bytes 196616 | tf_op jit(solution)/shard_map/ppermute | solution.py:22
  32.7 5.5 %collective-permute-start.5 = (f32[8,2048]{1,0:T(8,128)S(1)}, f32[8,2048]{1,0:T(8,128)S(1)}, u32[]{:S(2)}, u32[]{:S(2)}) collective-permute-start(f32[8,2048]{1,0:T(8,128)S(1)} %add.34.p_ref), channel_id=1, source_target_pairs={{0,6},{1,7},{2,4},{3,5},{4,2},{5,3},{6,0},{7,1},{8,14},{9,15},{10,... | collective-permute-start | bytes 196616 | tf_op jit(solution)/shard_map/ppermute | solution.py:22
  41.8 13.8 %copy-start.17 = (f32[2,128]{1,0:T(2,128)}, f32[2,128]{1,0:T(2,128)S(1)}, u32[]{:S(2)}) copy-start(f32[2,128]{1,0:T(2,128)S(1)} %get-tuple-element.21.fresh1_ref) | copy-start | bytes 3076
  41.8 3.8 %collective-permute-start.6 = (f32[16,256]{1,0:T(8,128)S(1)}, f32[16,256]{1,0:T(8,128)S(1)}, u32[]{:S(2)}, u32[]{:S(2)}) collective-permute-start(f32[16,256]{1,0:T(8,128)S(1)} %get-tuple-element.18.state_ref), channel_id=1, source_target_pairs={{0,8},{8,0},{16,24},{24,16},{32,40},{40,32},{48,56},{56,48},{64,72... | collective-permute-start | bytes 49160 | tf_op jit(solution)/shard_map/ppermute | solution.py:22
  46.2 1.3 %collective-permute-start.7 = (f32[8,2048]{1,0:T(8,128)S(1)}, f32[8,2048]{1,0:T(8,128)S(1)}, u32[]{:S(2)}, u32[]{:S(2)}) collective-permute-start(f32[8,2048]{1,0:T(8,128)S(1)} %out_projection_1.1), channel_id=1, source_target_pairs={{0,1},{1,0},{2,3},{3,2},{4,5},{5,4},{6,7},{7,6},{8,9},{9,8},{10,11... | collective-permute-start | bytes 196616 | tf_op jit(solution)/shard_map/ppermute | solution.py:22
  47.5 5.6 %collective-permute-start.10 = (f32[8,2048]{1,0:T(8,128)S(1)}, f32[8,2048]{1,0:T(8,128)S(1)}, u32[]{:S(2)}, u32[]{:S(2)}) collective-permute-start(f32[8,2048]{1,0:T(8,128)S(1)} %add.35.p_ref), channel_id=1, source_target_pairs={{0,6},{1,7},{2,4},{3,5},{4,2},{5,3},{6,0},{7,1},{8,14},{9,15},{10,... | collective-permute-start | bytes 196616 | tf_op jit(solution)/shard_map/ppermute | solution.py:22
  48.2 4.9 %collective-permute-start.8 = (f32[8,2048]{1,0:T(8,128)S(1)}, f32[8,2048]{1,0:T(8,128)S(1)}, u32[]{:S(2)}, u32[]{:S(2)}) collective-permute-start(f32[8,2048]{1,0:T(8,128)S(1)} %add.35.p_ref), channel_id=1, source_target_pairs={{0,2},{1,3},{2,0},{3,1},{4,6},{5,7},{6,4},{7,5},{8,10},{9,11},{10,... | collective-permute-start | bytes 196616 | tf_op jit(solution)/shard_map/ppermute | solution.py:22
  48.2 7.4 %collective-permute-start.9 = (f32[8,2048]{1,0:T(8,128)S(1)}, f32[8,2048]{1,0:T(8,128)S(1)}, u32[]{:S(2)}, u32[]{:S(2)}) collective-permute-start(f32[8,2048]{1,0:T(8,128)S(1)} %add.35.p_ref), channel_id=1, source_target_pairs={{0,4},{1,5},{2,6},{3,7},{4,0},{5,1},{6,2},{7,3},{8,12},{9,13},{10,... | collective-permute-start | bytes 196616 | tf_op jit(solution)/shard_map/ppermute | solution.py:22
  57.8 5.4 %collective-permute-start.11 = (f32[1,2560]{1,0:T(1,128)}, f32[1,2560]{1,0:T(1,128)S(1)}, u32[]{:S(2)}, u32[]{:S(2)}) collective-permute-start(f32[1,2560]{1,0:T(1,128)} %get-tuple-element.23), channel_id=1, source_target_pairs={{0,128},{8,136},{16,144},{24,152},{32,160},{40,168},{48,176},{56,1... | collective-permute-start | bytes 30728 | tf_op jit(solution)/shard_map/ppermute | solution.py:22
  (15 other events, 67.0 us)

commit v2 on v1

--- a/solution.py
+++ b/solution.py
@@ -12,7 +12,7 @@
 ROPE_BASE = 1000000.0
 NEGATIVE = -1e30
 ROWS = 8
-ANY = pl.BlockSpec(memory_space=pltpu.HBM)
+ANY = pl.BlockSpec(memory_space=pl.ANY)
 VM = pl.BlockSpec(memory_space=pltpu.VMEM)
 SM = pl.BlockSpec(memory_space=pltpu.SMEM)
 
@@ -22,33 +22,23 @@
     return lax.ppermute(value, axis, pairs)
 
 
+def in_hbm(value):
+    return pltpu.with_memory_space_constraint(value, pltpu.HBM)
+
+
 def row_of(count):
     return lax.broadcasted_iota(jnp.int32, (count, 1), 0)
 
 
 def attention_step(
     layer, group_ref, lengths_ref, long_lengths_ref, hidden, gain_ref, q_gain_ref, k_gain_ref,
-    cosine_ref, sine_ref, cache_ref, long_ref, wq_ref, wk_ref, wv_ref,
-    state_ref, side_ref, fresh_ref, buffers, semaphores,
-):
-    wq, wk, wv, keys, values, long_keys, long_values = buffers
-    sources = (
-        wq_ref.at[layer], wk_ref.at[layer], wv_ref.at[layer],
-        cache_ref.at[layer, 0], long_ref.at[layer, 0, 0],
-        cache_ref.at[layer, 1], long_ref.at[layer, 1, 0],
-    )
-    targets = (wq, wk, wv, keys, long_keys, values, long_values)
-    copies = [
-        pltpu.make_async_copy(source, target, semaphores.at[i])
-        for i, (source, target) in enumerate(zip(sources, targets))
-    ]
-    for copy in copies:
-        copy.start()
+    cosine_ref, sine_ref, stored, state_ref, side_ref, fresh_ref, ready,
+):
+    wq, wk, wv, keys, long_keys, values, long_values = stored
     rows = hidden()
     scale = lax.rsqrt(jnp.mean(rows * rows, axis=-1, keepdims=True) + EPSILON)
     normed = (rows * scale * gain_ref[layer : layer + 1, :]).astype(jnp.bfloat16)
-    for copy in copies[:3]:
-        copy.wait()
+    ready(0, 1, 2)
     queries = jnp.dot(normed, wq[...], preferred_element_type=jnp.float32)
     new_keys = jnp.dot(normed, wk[...], preferred_element_type=jnp.float32)
     new_values = jnp.dot(normed, wv[...], preferred_element_type=jnp.float32).astype(jnp.bfloat16)
@@ -85,9 +75,9 @@
     scores = jnp.zeros((16, 2048), jnp.float32)
     for r in range(5):
         if r == 0:
-            copies[3].wait()
+            ready(3)
         if r == 3:
-            copies[4].wait()
+            ready(4)
         block = keys[r] if r < 3 else long_keys[r - 3]
         product = lax.dot_general(
             query, block, (((1,), (1,)), ((), ())), preferred_element_type=jnp.float32
@@ -105,9 +95,9 @@
     summed = own_weight.astype(jnp.bfloat16).astype(jnp.float32) * values_twice
     for r in range(5):
         if r == 0:
-            copies[5].wait()
+            ready(5)
         if r == 3:
-            copies[6].wait()
+            ready(6)
         block = values[r] if r < 3 else long_values[r - 3]
         product = jnp.dot(rounded, block, preferred_element_type=jnp.float32)
         summed = summed + jnp.where(which == r, product, 0.0)
@@ -118,11 +108,30 @@
     side_ref[:, 128:256] = values_twice
 
 
+def parts_of(layer, cache_ref, long_ref, wq_ref, wk_ref, wv_ref):
+    return (
+        wq_ref.at[layer], wk_ref.at[layer], wv_ref.at[layer],
+        cache_ref.at[layer, 0], long_ref.at[layer, 0, 0],
+        cache_ref.at[layer, 1], long_ref.at[layer, 1, 0],
+    )
+
+
 def first_kernel(
     group_ref, lengths_ref, long_lengths_ref, tokens_ref, own_long_ref, far_long_ref, *rest
 ):
-    *middle, state_ref, side_ref, fresh_ref, hidden_ref = rest[:14]
+    tables, held = rest[:5], rest[5:10]
+    state_ref, side_ref, fresh_ref, hidden_ref = rest[10:14]
     buffers, semaphores = rest[14:21], rest[21]
+    copies = [
+        pltpu.make_async_copy(source, target, semaphores.at[i])
+        for i, (source, target) in enumerate(zip(parts_of(0, *held), buffers))
+    ]
+    for copy in copies:
+        copy.start()
+
+    def ready(*which):
+        for i in which:
+            copies[i].wait()
 
     def hidden():
         own = own_long_ref[...].astype(jnp.float32)
@@ -135,27 +144,94 @@
         return hidden_ref[...]
 
     attention_step(
-        0, group_ref, lengths_ref, long_lengths_ref, hidden, *middle,
-        state_ref, side_ref, fresh_ref, buffers, semaphores,
+        0, group_ref, lengths_ref, long_lengths_ref, hidden, *tables, buffers,
+        state_ref, side_ref, fresh_ref, ready,
     )
+
+
+def total_of(p_ref, r1_ref, r2_ref, r3_ref):
+    p, r1, r2, r3 = (ref[...].astype(jnp.float32) for ref in (p_ref, r1_ref, r2_ref, r3_ref))
+    return (p + r1) + (r2 + r3)
 
 
 def second_kernel(
     group_ref, lengths_ref, long_lengths_ref, before_ref, p_ref, r1_ref, r2_ref, r3_ref, *rest
 ):
-    *middle, state_ref, side_ref, fresh_ref, hidden_ref = rest[:14]
-    buffers, semaphores = rest[14:21], rest[21]
+    tables, stored = rest[:5], rest[5:12]
+    state_ref, side_ref, fresh_ref, hidden_ref = rest[12:16]
 
     def hidden():
-        summed = (p_ref[...] + r1_ref[...]) + (r2_ref[...] + r3_ref[...])
+        summed = total_of(p_ref, r1_ref, r2_ref, r3_ref)
         rows = (before_ref[...] + summed).astype(jnp.bfloat16).astype(jnp.float32)
         hidden_ref[...] = rows
         return rows
 
     attention_step(
-        1, group_ref, lengths_ref, long_lengths_ref, hidden, *middle,
-        state_ref, side_ref, fresh_ref, buffers, semaphores,
+        1, group_ref, lengths_ref, long_lengths_ref, hidden, *tables, stored,
+        state_ref, side_ref, fresh_ref, lambda *which: None,
     )
+
+
+def leaving_kernel(cache_ref, out_ref, semaphores):
+    copies = [
+        pltpu.make_async_copy(cache_ref.at[i, j, 2], out_ref.at[i, j], semaphores.at[2 * i + j])
+        for i in range(2)
+        for j in range(2)
+    ]
+    for copy in copies:
+        copy.start()
+    for copy in copies:
+        copy.wait()
+
+
+def arrival_kernel(
+    length_ref, stay_ref, arrived_ref, moving_ref, out_ref, moved_ref, blocks, semaphores
+):
+    start = pl.multiple_of(length_ref[0] // 16 * 16, 16)
+    places = [(i, j) for i in range(2) for j in range(2)]
+    bodies = [
+        pltpu.make_async_copy(moving_ref.at[i, j], moved_ref.at[i, j], semaphores.at[0, i, j])
+        for i, j in places
+    ]
+    reads = [
+        pltpu.make_async_copy(
+            moving_ref.at[i, j, pl.ds(start, 16)], blocks.at[i, j], semaphores.at[1, i, j]
+        )
+        for i, j in places
+    ]
+    for copy in (*reads, *bodies):
+        copy.start()
+    out_ref[0:2, :] = stay_ref[...]
+    out_ref[2:3, :] = arrived_ref[0:1, 0:2048]
+    hit = row_of(16) == length_ref[0] - start
+    for n, (i, j) in enumerate(places):
+        fresh = arrived_ref[0:1, 2048 + 128 * n : 2176 + 128 * n]
+        reads[n].wait()
+        block = jnp.where(hit, fresh, blocks[i, j].astype(jnp.float32))
+        blocks[i, j] = block.astype(jnp.bfloat16)
+    writes = []
+    for n, (i, j) in enumerate(places):
+        bodies[n].wait()
+        writes.append(
+            pltpu.make_async_copy(
+                blocks.at[i, j], moved_ref.at[i, j, pl.ds(start, 16)], semaphores.at[2, i, j]
+            )
+        )
+        writes[-1].start()
+    for copy in writes:
+        copy.wait()
+
+
+def fetch_kernel(*refs):
+    held, outputs, semaphores = refs[:5], refs[5:12], refs[12]
+    copies = [
+        pltpu.make_async_copy(source, target, semaphores.at[i])
+        for i, (source, target) in enumerate(zip(parts_of(1, *held), outputs))
+    ]
+    for copy in copies:
+        copy.start()
+    for copy in copies:
+        copy.wait()
 
 
 def out_kernel(layer, state_ref, far_ref, side_ref, w_ref, out_ref, w, semaphore):
@@ -184,8 +260,7 @@
     group_ref, before_ref, p_ref, r1_ref, r2_ref, r3_ref, fresh0_ref, fresh1_ref,
     stay_ref, long_ref, leave_ref, scratch,
 ):
-    summed = (p_ref[...] + r1_ref[...]) + (r2_ref[...] + r3_ref[...])
-    scratch[...] = before_ref[...] + summed
+    scratch[...] = before_ref[...] + total_of(p_ref, r1_ref, r2_ref, r3_ref)
     stay_ref[...] = scratch[0:2, :]
     odd = lax.rem(group_ref[0], 2) == 1
     long_ref[...] = jnp.where(odd, scratch[4:5, :], scratch[3:4, :])
@@ -207,7 +282,19 @@
     long_cache = long_cache.reshape(2, 2, 1, 2, 2048, 128)
 
     far_token = permute(long_tokens, "replica", lambda i: i ^ 1)
-    moving = permute(cache[:, :, 2], "replica", lambda i: (i + groups // 2) % groups)
+    params = pltpu.CompilerParams(vmem_limit_bytes=16 * 2**20)
+    small = pltpu.CompilerParams(vmem_limit_bytes=2 * 2**20)
+    held = in_hbm(cache)
+    leaving = pl.pallas_call(
+        leaving_kernel,
+        out_shape=jax.ShapeDtypeStruct((2, 2, 2048, 128), jnp.bfloat16),
+        in_specs=[ANY],
+        out_specs=ANY,
+        scratch_shapes=[pltpu.SemaphoreType.DMA((4,))],
+        compiler_params=small,
+        name="leaving_cache",
+    )(held)
+    moving = permute(leaving, "replica", lambda i: (i + groups // 2) % groups)
 
     places = jnp.concatenate(
         [
@@ -233,14 +320,13 @@
         pltpu.VMEM((2048, 128), jnp.bfloat16),
         pltpu.VMEM((2048, 128), jnp.bfloat16),
         pltpu.VMEM((3, 2048, 128), jnp.bfloat16),
+        pltpu.VMEM((2, 2048, 128), jnp.bfloat16),
         pltpu.VMEM((3, 2048, 128), jnp.bfloat16),
         pltpu.VMEM((2, 2048, 128), jnp.bfloat16),
-        pltpu.VMEM((2, 2048, 128), jnp.bfloat16),
         pltpu.SemaphoreType.DMA((7,)),
     ]
-    params = pltpu.CompilerParams(vmem_limit_bytes=24 * 2**20)
-    middle = (norm_gain, q_gain, k_gain, cosine, sine, cache, long_cache, w_query, key_weight, value_weight)
-    middle_specs = [VM] * 5 + [ANY] * 5
+    stored = (cache, long_cache, w_query, key_weight, value_weight)
+    tables = (norm_gain, q_gain, k_gain, cosine, sine)
 
     def project_out(layer, state, side):
         far = permute(state, "replica", lambda i: i ^ 1)
@@ -253,29 +339,40 @@
             compiler_params=params,
             name=f"out_projection_{layer}",
         )(state, far, side, w_out)
-        part = part + permute(part, "tensor", lambda i: i ^ 1)
+        part = (part + permute(part, "tensor", lambda i: i ^ 1)).astype(jnp.bfloat16)
         received = [permute(part, "tensor", lambda i, k=k: i ^ k) for k in (2, 4, 6)]
         return (part, *received)
 
     state, side, fresh_0, hidden = pl.pallas_call(
         first_kernel,
         out_shape=out_shape,
-        in_specs=[SM] * 3 + [VM] * 3 + middle_specs,
+        in_specs=[SM] * 3 + [VM] * 8 + [ANY] * 5,
         out_specs=(VM,) * 4,
         scratch_shapes=scratch,
         compiler_params=params,
         name="attention_0",
-    )(group_1, lengths, long_lengths, tokens, long_tokens, far_token, *middle)
+    )(group_1, lengths, long_lengths, tokens, long_tokens, far_token, *tables, *map(in_hbm, stored))
     terms = project_out(0, state, side)
+    buffers = ((2048, 256), (2048, 128), (2048, 128)) + ((3, 2048, 128), (2, 2048, 128)) * 2
+    gate, *stored = lax.optimization_barrier((terms[0], *stored))
+    terms = (gate, *terms[1:])
+    stored = pl.pallas_call(
+        fetch_kernel,
+        out_shape=tuple(pltpu.VMEM(shape, jnp.bfloat16) for shape in buffers),
+        in_specs=[ANY] * 5,
+        out_specs=(ANY,) * 7,
+        scratch_shapes=[pltpu.SemaphoreType.DMA((7,))],
+        compiler_params=small,
+        name="fetch_1",
+    )(*map(in_hbm, stored))
     state, side, fresh_1, hidden = pl.pallas_call(
         second_kernel,
         out_shape=out_shape,
-        in_specs=[SM] * 3 + [VM] * 5 + middle_specs,
+        in_specs=[SM] * 3 + [VM] * 17,
         out_specs=(VM,) * 4,
-        scratch_shapes=scratch,
         compiler_params=params,
         name="attention_1",
-    )(group_1, lengths, long_lengths, hidden, *terms, *middle)
+    )(group_1, lengths, long_lengths, hidden, *terms, *tables, *stored)
     terms = project_out(1, state, side)
     stay, long_out, leave = pl.pallas_call(
         final_kernel,
@@ -287,15 +384,27 @@
         in_specs=[SM] + [VM] * 7,
         out_specs=(VM,) * 3,
         scratch_shapes=[pltpu.VMEM((ROWS, 2048), jnp.float32)],
+        compiler_params=params,
         name="final_rows",
     )(group_1, hidden, *terms, fresh_0, fresh_1)
     arrived = permute(leave, "replica", lambda i: (i + groups // 2) % groups)
-    out_hidden = jnp.concatenate([stay, arrived[:, :2048]], axis=0)
-    fresh = arrived[0, 2048:].reshape(2, 2, 1, 128).astype(jnp.bfloat16)
     partner = (group + groups // 2) % groups
-    arrived_len = lax.dynamic_index_in_dim(lengths, partner * 3 + 2, 0, keepdims=False)
-    at = lax.broadcasted_iota(jnp.int32, (1, 1, 2048, 1), 2) == arrived_len
-    moved = jnp.where(at, fresh, moving)
+    arrived_len = lax.dynamic_slice_in_dim(lengths, partner * 3 + 2, 1)
+    out_hidden, moved = pl.pallas_call(
+        arrival_kernel,
+        out_shape=(
+            jax.ShapeDtypeStruct((3, 2048), jnp.float32),
+            jax.ShapeDtypeStruct((2, 2, 2048, 128), jnp.bfloat16),
+        ),
+        in_specs=[SM, VM, VM, ANY],
+        out_specs=(VM, ANY),
+        scratch_shapes=[
+            pltpu.VMEM((2, 2, 16, 128), jnp.bfloat16),
+            pltpu.SemaphoreType.DMA((3, 2, 2)),
+        ],
+        compiler_params=small,
+        name="arrival",
+    )(arrived_len, stay, arrived, moving)
     return (out_hidden, long_out, moved[None, :, :, :, None, :])
 
 

time: 67.7 us -> 118 us (1.74)
  Pallas kernels: 9.68 us -> 79.9 us
  local copies, waits for them, and re-layouts: 13.1 us -> 0.86 us
  other arithmetic: 5 us -> 0.21 us
  waiting for transfers between devices: 19.5 us -> 17 us
    pallas_call x0 -> x3, Pallas kernels: none -> 71.4 us  [the longest x1 64.7 us: local(): pl.pallas_call(leaving_kernel, out_shape=jax.ShapeDtypeStruct((2, 2, 2048...]
    unnamed x52 -> x20, local copies, waits for them, and re-layouts: 9.05 us -> 0.05 us
    squeeze x1 -> x0, local copies, waits for them, and re-layouts: 3.2 us -> none  [local(): cache[:, :, 2]]
    unnamed x2 -> x0, other arithmetic: 2.75 us -> none
    ppermute x13, waiting for transfers between devices: 19.5 us -> 17 us  [permute(): return lax.ppermute(value, axis, pairs)]
    concatenate x1 -> x0, other arithmetic: 1.35 us -> none  [local(): out_hidden = jnp.concatenate([stay, arrived[:, :2048]], axis=0)]
  transfers between devices with their start and end apart: 13 -> 13, of which waited for: 10 -> 10; matrix products, arithmetic and copies ran while one was open for 5% -> 1% of each run, Pallas kernels for 14% -> 10%
where the time goes in v2:
time: 118 us
  Pallas kernels  79.9 us (68%)
  starting transfers between devices  19.3 us (16%)
  waiting for transfers between devices  17 us (14%)
    pallas_call x1, Pallas kernels, local(): pl.pallas_call(leaving_kernel, out_shape=jax.ShapeDtypeStruct((2, 2, 2048...  64.7 us
    ppermute x13, starting transfers between devices, permute(): return lax.ppermute(value, axis, pairs)  19.3 us
    ppermute x13, waiting for transfers between devices, permute(): return lax.ppermute(value, axis, pairs)  17 us
    pallas_call x1, Pallas kernels, local(): pl.pallas_call(first_kernel, out_shape=out_shape, in_specs=[SM] * 3 + [VM...  4.51 us
    pallas_call x1, Pallas kernels, local(): pl.pallas_call(fetch_kernel, out_shape=tuple((pltpu.VMEM(shape, jnp.bfloa...  3.35 us
    pallas_call x1, Pallas kernels, local(): pl.pallas_call(arrival_kernel, out_shape=(jax.ShapeDtypeStruct((3, 2048),...  3.34 us
    pallas_call x1, Pallas kernels, local(): pl.pallas_call(second_kernel, out_shape=out_shape, in_specs=[SM] * 3 + [V...  2.47 us
  transfers between devices with their start and end apart: 13, of which 10 were waited for; matrix products, arithmetic and copies ran while one was open for 1% of the time, Pallas kernels for 10%

profile of v2, /device:TPU:64, one launch (start us, length us, event | category | flops | bytes accessed | tf_op | source)
XLA Modules:
  0.0 118.1 jit_solution(2085996418579219308)
XLA Ops:
  0.7 64.7 %leaving_cache.1 = bf16[2,2,2048,128]{3,2,1,0:T(8,128)(2,1)} custom-call(bf16[2,2,3,2048,128]{4,3,2,1,0:T(8,128)(2,1)} %bitcast.6), custom_call_target="tpu_custom_call" | custom-call | tf_op jit(solution)/shard_map/leaving_cache/pallas_call | solution.py:288
  65.4 3.1 %collective-permute-start.12 = (bf16[2,2,2048,128]{3,2,1,0:T(8,128)(2,1)}, bf16[2,2,2048,128]{3,2,1,0:T(8,128)(2,1)S(1)}, u32[]{:S(2)}, u32[]{:S(2)}) collective-permute-start(bf16[2,2,2048,128]{3,2,1,0:T(8,128)(2,1)} %leaving_cache.1), channel_id=1, source_target_pairs={{0,128},{8,136},{16,144},{24,152},{32,160},{40,168},{48,176},{56,1... | collective-permute-start | bytes 6291464 | tf_op jit(solution)/shard_map/ppermute | solution.py:22
  68.5 1.9 %collective-permute-start = (bf16[1,2048]{1,0:T(2,128)(2,1)S(1)}, bf16[1,2048]{1,0:T(2,128)(2,1)S(1)}, u32[]{:S(2)}, u32[]{:S(2)}) collective-permute-start(bf16[1,2048]{1,0:T(2,128)(2,1)S(1)} %copy-done.3), channel_id=1, source_target_pairs={{0,8},{8,0},{16,24},{24,16},{32,40},{40,32},{48,56},{56,48},{64,72... | collective-permute-start | bytes 12296 | tf_op jit(solution)/shard_map/ppermute | solution.py:22
  70.8 1.4 %collective-permute-done.far_long_ref = bf16[1,2048]{1,0:T(2,128)(2,1)S(1)} collective-permute-done((bf16[1,2048]{1,0:T(2,128)(2,1)S(1)}, bf16[1,2048]{1,0:T(2,128)(2,1)S(1)}, u32[]{:S(2)}, u32[]{:S(2)}) %collective-permute-start) | collective-permute-done | bytes 4128 | tf_op jit(solution)/shard_map/ppermute | solution.py:22
  72.2 4.5 %attention_0.1 = (f32[16,256]{1,0:T(8,128)S(1)}, f32[16,256]{1,0:T(8,128)S(1)}, f32[2,128]{1,0:T(2,128)S(1)}, f32[8,2048]{1,0:T(8,128)S(1)}) custom-call(s32[1]{0:T(128)} %bitcast.group_ref, s32[96]{0:T(128)S(1)} %copy-done.7, s32[32]{0:T(128)S(1)} %copy-done.6, bf16[3,2048]{1,0:T(4,128)(2,1)S(1)} %copy-done.2, bf16[1,2048]{1,0:T(2,128)(2,1)S(1)} %copy-done.3, ...), custom_call_target="tpu_custom_call" | custom-call | tf_op jit(solution)/shard_map/attention_0/pallas_call | solution.py:346
  76.7 2.0 %collective-permute-start.1 = (f32[16,256]{1,0:T(8,128)S(1)}, f32[16,256]{1,0:T(8,128)S(1)}, u32[]{:S(2)}, u32[]{:S(2)}) collective-permute-start(f32[16,256]{1,0:T(8,128)S(1)} %get-tuple-element.30.state_ref), channel_id=1, source_target_pairs={{0,8},{8,0},{16,24},{24,16},{32,40},{40,32},{48,56},{56,48},{64,72... | collective-permute-start | bytes 49160 | tf_op jit(solution)/shard_map/ppermute | solution.py:22
  78.7 1.8 %collective-permute-done.1.far_ref = f32[16,256]{1,0:T(8,128)S(1)} collective-permute-done((f32[16,256]{1,0:T(8,128)S(1)}, f32[16,256]{1,0:T(8,128)S(1)}, u32[]{:S(2)}, u32[]{:S(2)}) %collective-permute-start.1) | collective-permute-done | bytes 16416 | tf_op jit(solution)/shard_map/ppermute | solution.py:22
  81.1 1.2 %collective-permute-done.2 = f32[8,2048]{1,0:T(8,128)S(1)} collective-permute-done((f32[8,2048]{1,0:T(8,128)S(1)}, f32[8,2048]{1,0:T(8,128)S(1)}, u32[]{:S(2)}, u32[]{:S(2)}) %collective-permute-start.2) | collective-permute-done | bytes 65568 | tf_op jit(solution)/shard_map/ppermute | solution.py:22
  82.4 1.7 %collective-permute-start.3 = (bf16[8,2048]{1,0:T(8,128)(2,1)S(1)}, bf16[8,2048]{1,0:T(8,128)(2,1)S(1)}, u32[]{:S(2)}, u32[]{:S(2)}) collective-permute-start(bf16[8,2048]{1,0:T(8,128)(2,1)S(1)} %add_convert_fusion.1.p_ref), channel_id=1, source_target_pairs={{0,2},{1,3},{2,0},{3,1},{4,6},{5,7},{6,4},{7,5},{8,10},{9,11},{10,... | collective-permute-start | bytes 98312 | tf_op jit(solution)/shard_map/ppermute | solution.py:22
  84.1 2.9 %collective-permute-start.4 = (bf16[8,2048]{1,0:T(8,128)(2,1)S(1)}, bf16[8,2048]{1,0:T(8,128)(2,1)S(1)}, u32[]{:S(2)}, u32[]{:S(2)}) collective-permute-start(bf16[8,2048]{1,0:T(8,128)(2,1)S(1)} %add_convert_fusion.1.p_ref), channel_id=1, source_target_pairs={{0,4},{1,5},{2,6},{3,7},{4,0},{5,1},{6,2},{7,3},{8,12},{9,13},{10,... | collective-permute-start | bytes 98312 | tf_op jit(solution)/shard_map/ppermute | solution.py:22
  87.2 3.4 %fetch_1.1 = (bf16[2048,256]{1,0:T(8,128)(2,1)S(1)}, bf16[2048,128]{1,0:T(8,128)(2,1)S(1)}, bf16[2048,128]{1,0:T(8,128)(2,1)S(1)}, bf16[3,2048,128]{2,1,0:T(8,12...) custom-call(bf16[2,2,3,2048,128]{4,3,2,1,0:T(8,128)(2,1)} %bitcast.8, ...), custom_call_target="tpu_custom_call" | custom-call | tf_op jit(solution)/shard_map/fetch_1/pallas_call | solution.py:359
  90.6 1.5 %collective-permute-done.5.r3_ref = bf16[8,2048]{1,0:T(8,128)(2,1)S(1)} collective-permute-done((bf16[8,2048]{1,0:T(8,128)(2,1)S(1)}, bf16[8,2048]{1,0:T(8,128)(2,1)S(1)}, u32[]{:S(2)}, u32[]{:S(2)}) %collective-permute-start.5) | collective-permute-done | bytes 32800 | tf_op jit(solution)/shard_map/ppermute | solution.py:22
  92.1 2.5 %attention_1.1 = (f32[16,256]{1,0:T(8,128)S(1)}, f32[16,256]{1,0:T(8,128)S(1)}, f32[2,128]{1,0:T(2,128)S(1)}, f32[8,2048]{1,0:T(8,128)S(1)}) custom-call(s32[1]{0:T(128)} %bitcast.group_ref, s32[96]{0:T(128)S(1)} %copy-done.7, s32[32]{0:T(128)S(1)} %copy-done.6, f32[8,2048]{1,0:T(8,128)S(1)} %get-tuple-element.29.before_ref, ...), custom_call_target="tpu_custom_call" | custom-call | tf_op jit(solution)/shard_map/attention_1/pallas_call | solution.py:368
  94.6 2.0 %collective-permute-start.6 = (f32[16,256]{1,0:T(8,128)S(1)}, f32[16,256]{1,0:T(8,128)S(1)}, u32[]{:S(2)}, u32[]{:S(2)}) collective-permute-start(f32[16,256]{1,0:T(8,128)S(1)} %get-tuple-element.46.state_ref), channel_id=1, source_target_pairs={{0,8},{8,0},{16,24},{24,16},{32,40},{40,32},{48,56},{56,48},{64,72... | collective-permute-start | bytes 49160 | tf_op jit(solution)/shard_map/ppermute | solution.py:22
  96.6 1.8 %collective-permute-done.6.far_ref = f32[16,256]{1,0:T(8,128)S(1)} collective-permute-done((f32[16,256]{1,0:T(8,128)S(1)}, f32[16,256]{1,0:T(8,128)S(1)}, u32[]{:S(2)}, u32[]{:S(2)}) %collective-permute-start.6) | collective-permute-done | bytes 16416 | tf_op jit(solution)/shard_map/ppermute | solution.py:22
  99.0 1.2 %collective-permute-done.7 = f32[8,2048]{1,0:T(8,128)S(1)} collective-permute-done((f32[8,2048]{1,0:T(8,128)S(1)}, f32[8,2048]{1,0:T(8,128)S(1)}, u32[]{:S(2)}, u32[]{:S(2)}) %collective-permute-start.7) | collective-permute-done | bytes 65568 | tf_op jit(solution)/shard_map/ppermute | solution.py:22
  100.2 1.6 %collective-permute-start.10 = (bf16[8,2048]{1,0:T(8,128)(2,1)S(1)}, bf16[8,2048]{1,0:T(8,128)(2,1)S(1)}, u32[]{:S(2)}, u32[]{:S(2)}) collective-permute-start(bf16[8,2048]{1,0:T(8,128)(2,1)S(1)} %add_convert_fusion.p_ref), channel_id=1, source_target_pairs={{0,6},{1,7},{2,4},{3,5},{4,2},{5,3},{6,0},{7,1},{8,14},{9,15},{10,... | collective-permute-start | bytes 98312 | tf_op jit(solution)/shard_map/ppermute | solution.py:22
  101.9 3.2 %collective-permute-start.9 = (bf16[8,2048]{1,0:T(8,128)(2,1)S(1)}, bf16[8,2048]{1,0:T(8,128)(2,1)S(1)}, u32[]{:S(2)}, u32[]{:S(2)}) collective-permute-start(bf16[8,2048]{1,0:T(8,128)(2,1)S(1)} %add_convert_fusion.p_ref), channel_id=1, source_target_pairs={{0,4},{1,5},{2,6},{3,7},{4,0},{5,1},{6,2},{7,3},{8,12},{9,13},{10,... | collective-permute-start | bytes 98312 | tf_op jit(solution)/shard_map/ppermute | solution.py:22
  105.8 1.5 %collective-permute-done.9.r2_ref = bf16[8,2048]{1,0:T(8,128)(2,1)S(1)} collective-permute-done((bf16[8,2048]{1,0:T(8,128)(2,1)S(1)}, bf16[8,2048]{1,0:T(8,128)(2,1)S(1)}, u32[]{:S(2)}, u32[]{:S(2)}) %collective-permute-start.9) | collective-permute-done | bytes 32800 | tf_op jit(solution)/shard_map/ppermute | solution.py:22
  107.3 0.6 final_rows.1
  107.9 0.5 collective-permute-start.11
  108.4 0.7 dynamic_slice.9.length_ref
  109.1 5.7 %collective-permute-done.11.arrived_ref = f32[1,2560]{1,0:T(1,128)S(1)} collective-permute-done((f32[1,2560]{1,0:T(1,128)S(1)}, f32[1,2560]{1,0:T(1,128)S(1)}, u32[]{:S(2)}, u32[]{:S(2)}) %collective-permute-start.11) | collective-permute-done | bytes 10272 | tf_op jit(solution)/shard_map/ppermute | solution.py:22
  114.8 3.3 %arrival.1 = (f32[3,2048]{1,0:T(4,128)}, bf16[2,2,2048,128]{3,2,1,0:T(8,128)(2,1)}) custom-call(s32[1]{0:T(128)} %dynamic_slice.9.length_ref, f32[2,2048]{1,0:T(2,128)S(1)} %get-tuple-element.50.stay_ref, f32[1,2560]{1,0:T(1,128)S(1)} %collective-permute-done.11.arrived_ref, bf16[2,2,2048,128]{3,2,1,0:T(8,128)(2,1)S(1)} %collective-permute-done.12.moving_ref), custom_call_target="tpu_custom_call" | custom-call | tf_op jit(solution)/shard_map/arrival/pallas_call | solution.py:393
  (38 shorter events, 2.5 us)
Async XLA Ops:
  0.6 67.9 %copy-start.3 = (bf16[1,2048]{1,0:T(2,128)(2,1)S(1)}, bf16[1,2048]{1,0:T(2,128)(2,1)}, u32[]{:S(2)}) copy-start(bf16[1,2048]{1,0:T(2,128)(2,1)} %own_long_ref.1) | copy-start | bytes 12292
  0.6 69.8 %copy-start.6 = (s32[32]{0:T(128)S(1)}, s32[32]{0:T(128)}, u32[]{:S(2)}) copy-start(s32[32]{0:T(128)} %long_lengths_ref.3) | copy-start | bytes 388
  0.7 69.9 %copy-start.7 = (s32[96]{0:T(128)S(1)}, s32[96]{0:T(128)}, u32[]{:S(2)}) copy-start(s32[96]{0:T(128)} %lengths_ref.3) | copy-start | bytes 1156
  0.7 70.0 %copy-start.8 = (f32[128]{0:T(128)S(1)}, f32[128]{0:T(128)}, u32[]{:S(2)}) copy-start(f32[128]{0:T(128)} %constant.43.clone) | copy-start | bytes 1540
  0.7 70.0 %copy-start.9 = (f32[128]{0:T(128)S(1)}, f32[128]{0:T(128)}, u32[]{:S(2)}) copy-start(f32[128]{0:T(128)} %constant.44.clone) | copy-start | bytes 1540
  0.7 71.5 %copy-start.1 = (f32[2,2048]{1,0:T(2,128)S(1)}, f32[2,2048]{1,0:T(2,128)}, u32[]{:S(2)}) copy-start(f32[2,2048]{1,0:T(2,128)} %rest_0_.3) | copy-start | bytes 49156
  0.7 71.5 %copy-start.2 = (bf16[3,2048]{1,0:T(4,128)(2,1)S(1)}, bf16[3,2048]{1,0:T(4,128)(2,1)}, u32[]{:S(2)}) copy-start(bf16[3,2048]{1,0:T(4,128)(2,1)} %tokens_ref.1) | copy-start | bytes 36868
  0.7 71.5 %copy-start.4 = (f32[2,128]{1,0:T(2,128)S(1)}, f32[2,128]{1,0:T(2,128)}, u32[]{:S(2)}) copy-start(f32[2,128]{1,0:T(2,128)} %rest_1_.3) | copy-start | bytes 3076
  0.7 71.5 %copy-start.5 = (f32[2,128]{1,0:T(2,128)S(1)}, f32[2,128]{1,0:T(2,128)}, u32[]{:S(2)}) copy-start(f32[2,128]{1,0:T(2,128)} %rest_2_.3) | copy-start | bytes 3076
  65.4 49.4 %collective-permute-start.12 = (bf16[2,2,2048,128]{3,2,1,0:T(8,128)(2,1)}, bf16[2,2,2048,128]{3,2,1,0:T(8,128)(2,1)S(1)}, u32[]{:S(2)}, u32[]{:S(2)}) collective-permute-start(bf16[2,2,2048,128]{3,2,1,0:T(8,128)(2,1)} %leaving_cache.1), channel_id=1, source_target_pairs={{0,128},{8,136},{16,144},{24,152},{32,160},{40,168},{48,176},{56,1... | collective-permute-start | bytes 6291464 | tf_op jit(solution)/shard_map/ppermute | solution.py:22
  68.5 3.7 %collective-permute-start = (bf16[1,2048]{1,0:T(2,128)(2,1)S(1)}, bf16[1,2048]{1,0:T(2,128)(2,1)S(1)}, u32[]{:S(2)}, u32[]{:S(2)}) collective-permute-start(bf16[1,2048]{1,0:T(2,128)(2,1)S(1)} %copy-done.3), channel_id=1, source_target_pairs={{0,8},{8,0},{16,24},{24,16},{32,40},{40,32},{48,56},{56,48},{64,72... | collective-permute-start | bytes 12296 | tf_op jit(solution)/shard_map/ppermute | solution.py:22
  72.2 8.4 %copy-start = (bf16[2,256,2048]{2,1,0:T(8,128)(2,1)S(1)}, bf16[2,256,2048]{2,1,0:T(8,128)(2,1)}, u32[]{:S(2)}) copy-start(bf16[2,256,2048]{2,1,0:T(8,128)(2,1)} %w_ref.3) | copy-start | bytes 6291460
  76.7 3.8 %collective-permute-start.1 = (f32[16,256]{1,0:T(8,128)S(1)}, f32[16,256]{1,0:T(8,128)S(1)}, u32[]{:S(2)}, u32[]{:S(2)}) collective-permute-start(f32[16,256]{1,0:T(8,128)S(1)} %get-tuple-element.30.state_ref), channel_id=1, source_target_pairs={{0,8},{8,0},{16,24},{24,16},{32,40},{40,32},{48,56},{56,48},{64,72... | collective-permute-start | bytes 49160 | tf_op jit(solution)/shard_map/ppermute | solution.py:22
  81.0 1.3 %collective-permute-start.2 = (f32[8,2048]{1,0:T(8,128)S(1)}, f32[8,2048]{1,0:T(8,128)S(1)}, u32[]{:S(2)}, u32[]{:S(2)}) collective-permute-start(f32[8,2048]{1,0:T(8,128)S(1)} %out_projection_0.1), channel_id=1, source_target_pairs={{0,1},{1,0},{2,3},{3,2},{4,5},{5,4},{6,7},{7,6},{8,9},{9,8},{10,11... | collective-permute-start | bytes 196616 | tf_op jit(solution)/shard_map/ppermute | solution.py:22
  82.4 8.1 %collective-permute-start.3 = (bf16[8,2048]{1,0:T(8,128)(2,1)S(1)}, bf16[8,2048]{1,0:T(8,128)(2,1)S(1)}, u32[]{:S(2)}, u32[]{:S(2)}) collective-permute-start(bf16[8,2048]{1,0:T(8,128)(2,1)S(1)} %add_convert_fusion.1.p_ref), channel_id=1, source_target_pairs={{0,2},{1,3},{2,0},{3,1},{4,6},{5,7},{6,4},{7,5},{8,10},{9,11},{10,... | collective-permute-start | bytes 98312 | tf_op jit(solution)/shard_map/ppermute | solution.py:22
  84.1 6.5 %collective-permute-start.4 = (bf16[8,2048]{1,0:T(8,128)(2,1)S(1)}, bf16[8,2048]{1,0:T(8,128)(2,1)S(1)}, u32[]{:S(2)}, u32[]{:S(2)}) collective-permute-start(bf16[8,2048]{1,0:T(8,128)(2,1)S(1)} %add_convert_fusion.1.p_ref), channel_id=1, source_target_pairs={{0,4},{1,5},{2,6},{3,7},{4,0},{5,1},{6,2},{7,3},{8,12},{9,13},{10,... | collective-permute-start | bytes 98312 | tf_op jit(solution)/shard_map/ppermute | solution.py:22
  87.0 5.1 %collective-permute-start.5 = (bf16[8,2048]{1,0:T(8,128)(2,1)S(1)}, bf16[8,2048]{1,0:T(8,128)(2,1)S(1)}, u32[]{:S(2)}, u32[]{:S(2)}) collective-permute-start(bf16[8,2048]{1,0:T(8,128)(2,1)S(1)} %add_convert_fusion.1.p_ref), channel_id=1, source_target_pairs={{0,6},{1,7},{2,4},{3,5},{4,2},{5,3},{6,0},{7,1},{8,14},{9,15},{10,... | collective-permute-start | bytes 98312 | tf_op jit(solution)/shard_map/ppermute | solution.py:22
  94.6 3.8 %collective-permute-start.6 = (f32[16,256]{1,0:T(8,128)S(1)}, f32[16,256]{1,0:T(8,128)S(1)}, u32[]{:S(2)}, u32[]{:S(2)}) collective-permute-start(f32[16,256]{1,0:T(8,128)S(1)} %get-tuple-element.46.state_ref), channel_id=1, source_target_pairs={{0,8},{8,0},{16,24},{24,16},{32,40},{40,32},{48,56},{56,48},{64,72... | collective-permute-start | bytes 49160 | tf_op jit(solution)/shard_map/ppermute | solution.py:22
  98.9 1.3 %collective-permute-start.7 = (f32[8,2048]{1,0:T(8,128)S(1)}, f32[8,2048]{1,0:T(8,128)S(1)}, u32[]{:S(2)}, u32[]{:S(2)}) collective-permute-start(f32[8,2048]{1,0:T(8,128)S(1)} %out_projection_1.1), channel_id=1, source_target_pairs={{0,1},{1,0},{2,3},{3,2},{4,5},{5,4},{6,7},{7,6},{8,9},{9,8},{10,11... | collective-permute-start | bytes 196616 | tf_op jit(solution)/shard_map/ppermute | solution.py:22
  100.2 5.2 %collective-permute-start.10 = (bf16[8,2048]{1,0:T(8,128)(2,1)S(1)}, bf16[8,2048]{1,0:T(8,128)(2,1)S(1)}, u32[]{:S(2)}, u32[]{:S(2)}) collective-permute-start(bf16[8,2048]{1,0:T(8,128)(2,1)S(1)} %add_convert_fusion.p_ref), channel_id=1, source_target_pairs={{0,6},{1,7},{2,4},{3,5},{4,2},{5,3},{6,0},{7,1},{8,14},{9,15},{10,... | collective-permute-start | bytes 98312 | tf_op jit(solution)/shard_map/ppermute | solution.py:22
  101.8 3.9 %collective-permute-start.8 = (bf16[8,2048]{1,0:T(8,128)(2,1)S(1)}, bf16[8,2048]{1,0:T(8,128)(2,1)S(1)}, u32[]{:S(2)}, u32[]{:S(2)}) collective-permute-start(bf16[8,2048]{1,0:T(8,128)(2,1)S(1)} %add_convert_fusion.p_ref), channel_id=1, source_target_pairs={{0,2},{1,3},{2,0},{3,1},{4,6},{5,7},{6,4},{7,5},{8,10},{9,11},{10,... | collective-permute-start | bytes 98312 | tf_op jit(solution)/shard_map/ppermute | solution.py:22
  101.9 5.4 %collective-permute-start.9 = (bf16[8,2048]{1,0:T(8,128)(2,1)S(1)}, bf16[8,2048]{1,0:T(8,128)(2,1)S(1)}, u32[]{:S(2)}, u32[]{:S(2)}) collective-permute-start(bf16[8,2048]{1,0:T(8,128)(2,1)S(1)} %add_convert_fusion.p_ref), channel_id=1, source_target_pairs={{0,4},{1,5},{2,6},{3,7},{4,0},{5,1},{6,2},{7,3},{8,12},{9,13},{10,... | collective-permute-start | bytes 98312 | tf_op jit(solution)/shard_map/ppermute | solution.py:22
  107.9 6.9 %collective-permute-start.11 = (f32[1,2560]{1,0:T(1,128)S(1)}, f32[1,2560]{1,0:T(1,128)S(1)}, u32[]{:S(2)}, u32[]{:S(2)}) collective-permute-start(f32[1,2560]{1,0:T(1,128)S(1)} %get-tuple-element.51), channel_id=1, source_target_pairs={{0,128},{8,136},{16,144},{24,152},{32,160},{40,168},{48,176},{56,1... | collective-permute-start | bytes 30728 | tf_op jit(solution)/shard_map/ppermute | solution.py:22

commit v3 on v2

--- a/solution.py
+++ b/solution.py
@@ -24,6 +24,10 @@
 
 def in_hbm(value):
     return pltpu.with_memory_space_constraint(value, pltpu.HBM)
+
+
+def in_vmem(value):
+    return pltpu.with_memory_space_constraint(value, pltpu.VMEM)
 
 
 def row_of(count):
@@ -185,41 +189,37 @@
 
 
 def arrival_kernel(
-    length_ref, stay_ref, arrived_ref, moving_ref, out_ref, moved_ref, blocks, semaphores
-):
-    start = pl.multiple_of(length_ref[0] // 16 * 16, 16)
+    length_ref, stay_ref, arrived_ref, moving_ref, out_ref, moved_ref, rows, blocks, semaphores
+):
     places = [(i, j) for i in range(2) for j in range(2)]
     bodies = [
-        pltpu.make_async_copy(moving_ref.at[i, j], moved_ref.at[i, j], semaphores.at[0, i, j])
+        pltpu.make_async_copy(moving_ref.at[i, j], moved_ref.at[i, j], semaphores.at[2 * i + j])
         for i, j in places
     ]
-    reads = [
-        pltpu.make_async_copy(
-            moving_ref.at[i, j, pl.ds(start, 16)], blocks.at[i, j], semaphores.at[1, i, j]
-        )
-        for i, j in places
-    ]
-    for copy in (*reads, *bodies):
+    for copy in bodies:
         copy.start()
-    out_ref[0:2, :] = stay_ref[...]
-    out_ref[2:3, :] = arrived_ref[0:1, 0:2048]
+    rows[0:2, :] = stay_ref[...]
+    rows[2:3, :] = arrived_ref[0:1, 0:2048]
+    out = pltpu.make_async_copy(rows, out_ref, semaphores.at[8])
+    out.start()
+    start = pl.multiple_of(length_ref[0] // 16 * 16, 16)
     hit = row_of(16) == length_ref[0] - start
     for n, (i, j) in enumerate(places):
         fresh = arrived_ref[0:1, 2048 + 128 * n : 2176 + 128 * n]
-        reads[n].wait()
-        block = jnp.where(hit, fresh, blocks[i, j].astype(jnp.float32))
-        blocks[i, j] = block.astype(jnp.bfloat16)
-    writes = []
-    for n, (i, j) in enumerate(places):
-        bodies[n].wait()
-        writes.append(
-            pltpu.make_async_copy(
-                blocks.at[i, j], moved_ref.at[i, j, pl.ds(start, 16)], semaphores.at[2, i, j]
-            )
+        block = moving_ref[i, j, pl.ds(start, 16), :].astype(jnp.float32)
+        blocks[i, j] = jnp.where(hit, fresh, block).astype(jnp.bfloat16)
+    writes = [
+        pltpu.make_async_copy(
+            blocks.at[i, j], moved_ref.at[i, j, pl.ds(start, 16)], semaphores.at[4 + 2 * i + j]
         )
-        writes[-1].start()
-    for copy in writes:
-        copy.wait()
+        for i, j in places
+    ]
+    for body, write in zip(bodies, writes):
+        body.wait()
+        write.start()
+    for write in writes:
+        write.wait()
+    out.wait()
 
 
 def fetch_kernel(*refs):
@@ -287,7 +287,7 @@
     held = in_hbm(cache)
     leaving = pl.pallas_call(
         leaving_kernel,
-        out_shape=jax.ShapeDtypeStruct((2, 2, 2048, 128), jnp.bfloat16),
+        out_shape=pltpu.VMEM((2, 2, 2048, 128), jnp.bfloat16),
         in_specs=[ANY],
         out_specs=ANY,
         scratch_shapes=[pltpu.SemaphoreType.DMA((4,))],
@@ -393,18 +393,19 @@
     out_hidden, moved = pl.pallas_call(
         arrival_kernel,
         out_shape=(
-            jax.ShapeDtypeStruct((3, 2048), jnp.float32),
-            jax.ShapeDtypeStruct((2, 2, 2048, 128), jnp.bfloat16),
+            pltpu.HBM((3, 2048), jnp.float32),
+            pltpu.HBM((2, 2, 2048, 128), jnp.bfloat16),
         ),
-        in_specs=[SM, VM, VM, ANY],
-        out_specs=(VM, ANY),
+        in_specs=[SM, VM, VM, VM],
+        out_specs=(ANY, ANY),
         scratch_shapes=[
+            pltpu.VMEM((3, 2048), jnp.float32),
             pltpu.VMEM((2, 2, 16, 128), jnp.bfloat16),
-            pltpu.SemaphoreType.DMA((3, 2, 2)),
+            pltpu.SemaphoreType.DMA((9,)),
         ],
         compiler_params=small,
         name="arrival",
-    )(arrived_len, stay, arrived, moving)
+    )(arrived_len, stay, arrived, in_vmem(moving))
     return (out_hidden, long_out, moved[None, :, :, :, None, :])
 
 

time: 118 us -> 118 us (level)
  no operation moved by 1% of the time
where the time goes in v3:
time: 118 us; the launch traced here: 117 us
  Pallas kernels  79.3 us (67%)
  starting transfers between devices  19.3 us (16%)
  waiting for transfers between devices  17 us (14%)
    pallas_call x1, Pallas kernels, local(): pl.pallas_call(leaving_kernel, out_shape=pltpu.VMEM((2, 2, 2048, 128), jn...  64.7 us
    ppermute x13, starting transfers between devices, permute(): return lax.ppermute(value, axis, pairs)  19.3 us
    ppermute x13, waiting for transfers between devices, permute(): return lax.ppermute(value, axis, pairs)  17 us
    pallas_call x1, Pallas kernels, local(): pl.pallas_call(first_kernel, out_shape=out_shape, in_specs=[SM] * 3 + [VM...  4.51 us
    pallas_call x1, Pallas kernels, local(): pl.pallas_call(fetch_kernel, out_shape=tuple((pltpu.VMEM(shape, jnp.bfloa...  3.35 us
    pallas_call x1, Pallas kernels, local(): pl.pallas_call(arrival_kernel, out_shape=(pltpu.HBM((3, 2048), jnp.float3...  2.67 us
    pallas_call x1, Pallas kernels, local(): pl.pallas_call(second_kernel, out_shape=out_shape, in_specs=[SM] * 3 + [V...  2.47 us
  transfers between devices with their start and end apart: 13, of which 10 were waited for; matrix products, arithmetic and copies ran while one was open for 1% of the time, Pallas kernels for 10%

profile of v3, /device:TPU:64, one launch (start us, length us, event | category | flops | bytes accessed | tf_op | source)
XLA Modules:
  0.0 117.5 jit_solution(134172100093772891)
XLA Ops:
  0.7 64.7 %leaving_cache.1 = bf16[2,2,2048,128]{3,2,1,0:T(8,128)(2,1)} custom-call(bf16[2,2,3,2048,128]{4,3,2,1,0:T(8,128)(2,1)} %bitcast.6), custom_call_target="tpu_custom_call" | custom-call | tf_op jit(solution)/shard_map/leaving_cache/pallas_call | solution.py:288
  65.4 3.1 %collective-permute-start.12 = (bf16[2,2,2048,128]{3,2,1,0:T(8,128)(2,1)}, bf16[2,2,2048,128]{3,2,1,0:T(8,128)(2,1)S(1)}, u32[]{:S(2)}, u32[]{:S(2)}) collective-permute-start(bf16[2,2,2048,128]{3,2,1,0:T(8,128)(2,1)} %leaving_cache.1), channel_id=1, source_target_pairs={{0,128},{8,136},{16,144},{24,152},{32,160},{40,168},{48,176},{56,1... | collective-permute-start | bytes 6291464 | tf_op jit(solution)/shard_map/ppermute | solution.py:22
  68.5 1.9 %collective-permute-start = (bf16[1,2048]{1,0:T(2,128)(2,1)S(1)}, bf16[1,2048]{1,0:T(2,128)(2,1)S(1)}, u32[]{:S(2)}, u32[]{:S(2)}) collective-permute-start(bf16[1,2048]{1,0:T(2,128)(2,1)S(1)} %copy-done.3), channel_id=1, source_target_pairs={{0,8},{8,0},{16,24},{24,16},{32,40},{40,32},{48,56},{56,48},{64,72... | collective-permute-start | bytes 12296 | tf_op jit(solution)/shard_map/ppermute | solution.py:22
  70.8 1.4 %collective-permute-done.far_long_ref = bf16[1,2048]{1,0:T(2,128)(2,1)S(1)} collective-permute-done((bf16[1,2048]{1,0:T(2,128)(2,1)S(1)}, bf16[1,2048]{1,0:T(2,128)(2,1)S(1)}, u32[]{:S(2)}, u32[]{:S(2)}) %collective-permute-start) | collective-permute-done | bytes 4128 | tf_op jit(solution)/shard_map/ppermute | solution.py:22
  72.2 4.5 %attention_0.1 = (f32[16,256]{1,0:T(8,128)S(1)}, f32[16,256]{1,0:T(8,128)S(1)}, f32[2,128]{1,0:T(2,128)S(1)}, f32[8,2048]{1,0:T(8,128)S(1)}) custom-call(s32[1]{0:T(128)} %bitcast.group_ref, s32[96]{0:T(128)S(1)} %copy-done.7, s32[32]{0:T(128)S(1)} %copy-done.6, bf16[3,2048]{1,0:T(4,128)(2,1)S(1)} %copy-done.2, bf16[1,2048]{1,0:T(2,128)(2,1)S(1)} %copy-done.3, ...), custom_call_target="tpu_custom_call" | custom-call | tf_op jit(solution)/shard_map/attention_0/pallas_call | solution.py:346
  76.7 2.0 %collective-permute-start.1 = (f32[16,256]{1,0:T(8,128)S(1)}, f32[16,256]{1,0:T(8,128)S(1)}, u32[]{:S(2)}, u32[]{:S(2)}) collective-permute-start(f32[16,256]{1,0:T(8,128)S(1)} %get-tuple-element.30.state_ref), channel_id=1, source_target_pairs={{0,8},{8,0},{16,24},{24,16},{32,40},{40,32},{48,56},{56,48},{64,72... | collective-permute-start | bytes 49160 | tf_op jit(solution)/shard_map/ppermute | solution.py:22
  78.7 1.8 %collective-permute-done.1.far_ref = f32[16,256]{1,0:T(8,128)S(1)} collective-permute-done((f32[16,256]{1,0:T(8,128)S(1)}, f32[16,256]{1,0:T(8,128)S(1)}, u32[]{:S(2)}, u32[]{:S(2)}) %collective-permute-start.1) | collective-permute-done | bytes 16416 | tf_op jit(solution)/shard_map/ppermute | solution.py:22
  81.1 1.2 %collective-permute-done.2 = f32[8,2048]{1,0:T(8,128)S(1)} collective-permute-done((f32[8,2048]{1,0:T(8,128)S(1)}, f32[8,2048]{1,0:T(8,128)S(1)}, u32[]{:S(2)}, u32[]{:S(2)}) %collective-permute-start.2) | collective-permute-done | bytes 65568 | tf_op jit(solution)/shard_map/ppermute | solution.py:22
  82.4 1.7 %collective-permute-start.3 = (bf16[8,2048]{1,0:T(8,128)(2,1)S(1)}, bf16[8,2048]{1,0:T(8,128)(2,1)S(1)}, u32[]{:S(2)}, u32[]{:S(2)}) collective-permute-start(bf16[8,2048]{1,0:T(8,128)(2,1)S(1)} %add_convert_fusion.1.p_ref), channel_id=1, source_target_pairs={{0,2},{1,3},{2,0},{3,1},{4,6},{5,7},{6,4},{7,5},{8,10},{9,11},{10,... | collective-permute-start | bytes 98312 | tf_op jit(solution)/shard_map/ppermute | solution.py:22
  84.1 2.9 %collective-permute-start.4 = (bf16[8,2048]{1,0:T(8,128)(2,1)S(1)}, bf16[8,2048]{1,0:T(8,128)(2,1)S(1)}, u32[]{:S(2)}, u32[]{:S(2)}) collective-permute-start(bf16[8,2048]{1,0:T(8,128)(2,1)S(1)} %add_convert_fusion.1.p_ref), channel_id=1, source_target_pairs={{0,4},{1,5},{2,6},{3,7},{4,0},{5,1},{6,2},{7,3},{8,12},{9,13},{10,... | collective-permute-start | bytes 98312 | tf_op jit(solution)/shard_map/ppermute | solution.py:22
  87.2 3.4 %fetch_1.1 = (bf16[2048,256]{1,0:T(8,128)(2,1)S(1)}, bf16[2048,128]{1,0:T(8,128)(2,1)S(1)}, bf16[2048,128]{1,0:T(8,128)(2,1)S(1)}, bf16[3,2048,128]{2,1,0:T(8,12...) custom-call(bf16[2,2,3,2048,128]{4,3,2,1,0:T(8,128)(2,1)} %bitcast.8, ...), custom_call_target="tpu_custom_call" | custom-call | tf_op jit(solution)/shard_map/fetch_1/pallas_call | solution.py:359
  90.6 1.5 %collective-permute-done.5.r3_ref = bf16[8,2048]{1,0:T(8,128)(2,1)S(1)} collective-permute-done((bf16[8,2048]{1,0:T(8,128)(2,1)S(1)}, bf16[8,2048]{1,0:T(8,128)(2,1)S(1)}, u32[]{:S(2)}, u32[]{:S(2)}) %collective-permute-start.5) | collective-permute-done | bytes 32800 | tf_op jit(solution)/shard_map/ppermute | solution.py:22
  92.1 2.5 %attention_1.1 = (f32[16,256]{1,0:T(8,128)S(1)}, f32[16,256]{1,0:T(8,128)S(1)}, f32[2,128]{1,0:T(2,128)S(1)}, f32[8,2048]{1,0:T(8,128)S(1)}) custom-call(s32[1]{0:T(128)} %bitcast.group_ref, s32[96]{0:T(128)S(1)} %copy-done.7, s32[32]{0:T(128)S(1)} %copy-done.6, f32[8,2048]{1,0:T(8,128)S(1)} %get-tuple-element.29.before_ref, ...), custom_call_target="tpu_custom_call" | custom-call | tf_op jit(solution)/shard_map/attention_1/pallas_call | solution.py:368
  94.6 2.0 %collective-permute-start.6 = (f32[16,256]{1,0:T(8,128)S(1)}, f32[16,256]{1,0:T(8,128)S(1)}, u32[]{:S(2)}, u32[]{:S(2)}) collective-permute-start(f32[16,256]{1,0:T(8,128)S(1)} %get-tuple-element.46.state_ref), channel_id=1, source_target_pairs={{0,8},{8,0},{16,24},{24,16},{32,40},{40,32},{48,56},{56,48},{64,72... | collective-permute-start | bytes 49160 | tf_op jit(solution)/shard_map/ppermute | solution.py:22
  96.6 1.8 %collective-permute-done.6.far_ref = f32[16,256]{1,0:T(8,128)S(1)} collective-permute-done((f32[16,256]{1,0:T(8,128)S(1)}, f32[16,256]{1,0:T(8,128)S(1)}, u32[]{:S(2)}, u32[]{:S(2)}) %collective-permute-start.6) | collective-permute-done | bytes 16416 | tf_op jit(solution)/shard_map/ppermute | solution.py:22
  99.0 1.2 %collective-permute-done.7 = f32[8,2048]{1,0:T(8,128)S(1)} collective-permute-done((f32[8,2048]{1,0:T(8,128)S(1)}, f32[8,2048]{1,0:T(8,128)S(1)}, u32[]{:S(2)}, u32[]{:S(2)}) %collective-permute-start.7) | collective-permute-done | bytes 65568 | tf_op jit(solution)/shard_map/ppermute | solution.py:22
  100.2 1.6 %collective-permute-start.10 = (bf16[8,2048]{1,0:T(8,128)(2,1)S(1)}, bf16[8,2048]{1,0:T(8,128)(2,1)S(1)}, u32[]{:S(2)}, u32[]{:S(2)}) collective-permute-start(bf16[8,2048]{1,0:T(8,128)(2,1)S(1)} %add_convert_fusion.p_ref), channel_id=1, source_target_pairs={{0,6},{1,7},{2,4},{3,5},{4,2},{5,3},{6,0},{7,1},{8,14},{9,15},{10,... | collective-permute-start | bytes 98312 | tf_op jit(solution)/shard_map/ppermute | solution.py:22
  101.9 3.2 %collective-permute-start.9 = (bf16[8,2048]{1,0:T(8,128)(2,1)S(1)}, bf16[8,2048]{1,0:T(8,128)(2,1)S(1)}, u32[]{:S(2)}, u32[]{:S(2)}) collective-permute-start(bf16[8,2048]{1,0:T(8,128)(2,1)S(1)} %add_convert_fusion.p_ref), channel_id=1, source_target_pairs={{0,4},{1,5},{2,6},{3,7},{4,0},{5,1},{6,2},{7,3},{8,12},{9,13},{10,... | collective-permute-start | bytes 98312 | tf_op jit(solution)/shard_map/ppermute | solution.py:22
  105.8 1.5 %collective-permute-done.9.r2_ref = bf16[8,2048]{1,0:T(8,128)(2,1)S(1)} collective-permute-done((bf16[8,2048]{1,0:T(8,128)(2,1)S(1)}, bf16[8,2048]{1,0:T(8,128)(2,1)S(1)}, u32[]{:S(2)}, u32[]{:S(2)}) %collective-permute-start.9) | collective-permute-done | bytes 32800 | tf_op jit(solution)/shard_map/ppermute | solution.py:22
  107.3 0.6 final_rows.1
  107.9 0.5 collective-permute-start.11
  108.4 0.7 dynamic_slice.9.length_ref
  109.1 5.7 %collective-permute-done.11.arrived_ref = f32[1,2560]{1,0:T(1,128)S(1)} collective-permute-done((f32[1,2560]{1,0:T(1,128)S(1)}, f32[1,2560]{1,0:T(1,128)S(1)}, u32[]{:S(2)}, u32[]{:S(2)}) %collective-permute-start.11) | collective-permute-done | bytes 10272 | tf_op jit(solution)/shard_map/ppermute | solution.py:22
  114.8 2.7 %arrival.1 = (f32[3,2048]{1,0:T(4,128)}, bf16[2,2,2048,128]{3,2,1,0:T(8,128)(2,1)}) custom-call(s32[1]{0:T(128)} %dynamic_slice.9.length_ref, f32[2,2048]{1,0:T(2,128)S(1)} %get-tuple-element.50.stay_ref, f32[1,2560]{1,0:T(1,128)S(1)} %collective-permute-done.11.arrived_ref, bf16[2,2,2048,128]{3,2,1,0:T(8,128)(2,1)S(1)} %collective-permute-done.12.moving_ref), custom_call_target="tpu_custom_call" | custom-call | tf_op jit(solution)/shard_map/arrival/pallas_call | solution.py:393
  (38 shorter events, 2.5 us)
Async XLA Ops:
  0.6 67.9 %copy-start.3 = (bf16[1,2048]{1,0:T(2,128)(2,1)S(1)}, bf16[1,2048]{1,0:T(2,128)(2,1)}, u32[]{:S(2)}) copy-start(bf16[1,2048]{1,0:T(2,128)(2,1)} %own_long_ref.1) | copy-start | bytes 12292
  0.6 69.8 %copy-start.6 = (s32[32]{0:T(128)S(1)}, s32[32]{0:T(128)}, u32[]{:S(2)}) copy-start(s32[32]{0:T(128)} %long_lengths_ref.3) | copy-start | bytes 388
  0.7 69.9 %copy-start.7 = (s32[96]{0:T(128)S(1)}, s32[96]{0:T(128)}, u32[]{:S(2)}) copy-start(s32[96]{0:T(128)} %lengths_ref.3) | copy-start | bytes 1156
  0.7 70.0 %copy-start.8 = (f32[128]{0:T(128)S(1)}, f32[128]{0:T(128)}, u32[]{:S(2)}) copy-start(f32[128]{0:T(128)} %constant.43.clone) | copy-start | bytes 1540
  0.7 70.0 %copy-start.9 = (f32[128]{0:T(128)S(1)}, f32[128]{0:T(128)}, u32[]{:S(2)}) copy-start(f32[128]{0:T(128)} %constant.44.clone) | copy-start | bytes 1540
  0.7 71.5 %copy-start.1 = (f32[2,2048]{1,0:T(2,128)S(1)}, f32[2,2048]{1,0:T(2,128)}, u32[]{:S(2)}) copy-start(f32[2,2048]{1,0:T(2,128)} %rest_0_.3) | copy-start | bytes 49156
  0.7 71.5 %copy-start.2 = (bf16[3,2048]{1,0:T(4,128)(2,1)S(1)}, bf16[3,2048]{1,0:T(4,128)(2,1)}, u32[]{:S(2)}) copy-start(bf16[3,2048]{1,0:T(4,128)(2,1)} %tokens_ref.1) | copy-start | bytes 36868
  0.7 71.5 %copy-start.4 = (f32[2,128]{1,0:T(2,128)S(1)}, f32[2,128]{1,0:T(2,128)}, u32[]{:S(2)}) copy-start(f32[2,128]{1,0:T(2,128)} %rest_1_.3) | copy-start | bytes 3076
  0.7 71.5 %copy-start.5 = (f32[2,128]{1,0:T(2,128)S(1)}, f32[2,128]{1,0:T(2,128)}, u32[]{:S(2)}) copy-start(f32[2,128]{1,0:T(2,128)} %rest_2_.3) | copy-start | bytes 3076
  65.4 49.4 %collective-permute-start.12 = (bf16[2,2,2048,128]{3,2,1,0:T(8,128)(2,1)}, bf16[2,2,2048,128]{3,2,1,0:T(8,128)(2,1)S(1)}, u32[]{:S(2)}, u32[]{:S(2)}) collective-permute-start(bf16[2,2,2048,128]{3,2,1,0:T(8,128)(2,1)} %leaving_cache.1), channel_id=1, source_target_pairs={{0,128},{8,136},{16,144},{24,152},{32,160},{40,168},{48,176},{56,1... | collective-permute-start | bytes 6291464 | tf_op jit(solution)/shard_map/ppermute | solution.py:22
  68.5 3.7 %collective-permute-start = (bf16[1,2048]{1,0:T(2,128)(2,1)S(1)}, bf16[1,2048]{1,0:T(2,128)(2,1)S(1)}, u32[]{:S(2)}, u32[]{:S(2)}) collective-permute-start(bf16[1,2048]{1,0:T(2,128)(2,1)S(1)} %copy-done.3), channel_id=1, source_target_pairs={{0,8},{8,0},{16,24},{24,16},{32,40},{40,32},{48,56},{56,48},{64,72... | collective-permute-start | bytes 12296 | tf_op jit(solution)/shard_map/ppermute | solution.py:22
  72.2 8.4 %copy-start = (bf16[2,256,2048]{2,1,0:T(8,128)(2,1)S(1)}, bf16[2,256,2048]{2,1,0:T(8,128)(2,1)}, u32[]{:S(2)}) copy-start(bf16[2,256,2048]{2,1,0:T(8,128)(2,1)} %w_ref.3) | copy-start | bytes 6291460
  76.7 3.8 %collective-permute-start.1 = (f32[16,256]{1,0:T(8,128)S(1)}, f32[16,256]{1,0:T(8,128)S(1)}, u32[]{:S(2)}, u32[]{:S(2)}) collective-permute-start(f32[16,256]{1,0:T(8,128)S(1)} %get-tuple-element.30.state_ref), channel_id=1, source_target_pairs={{0,8},{8,0},{16,24},{24,16},{32,40},{40,32},{48,56},{56,48},{64,72... | collective-permute-start | bytes 49160 | tf_op jit(solution)/shard_map/ppermute | solution.py:22
  81.0 1.3 %collective-permute-start.2 = (f32[8,2048]{1,0:T(8,128)S(1)}, f32[8,2048]{1,0:T(8,128)S(1)}, u32[]{:S(2)}, u32[]{:S(2)}) collective-permute-start(f32[8,2048]{1,0:T(8,128)S(1)} %out_projection_0.1), channel_id=1, source_target_pairs={{0,1},{1,0},{2,3},{3,2},{4,5},{5,4},{6,7},{7,6},{8,9},{9,8},{10,11... | collective-permute-start | bytes 196616 | tf_op jit(solution)/shard_map/ppermute | solution.py:22
  82.4 8.1 %collective-permute-start.3 = (bf16[8,2048]{1,0:T(8,128)(2,1)S(1)}, bf16[8,2048]{1,0:T(8,128)(2,1)S(1)}, u32[]{:S(2)}, u32[]{:S(2)}) collective-permute-start(bf16[8,2048]{1,0:T(8,128)(2,1)S(1)} %add_convert_fusion.1.p_ref), channel_id=1, source_target_pairs={{0,2},{1,3},{2,0},{3,1},{4,6},{5,7},{6,4},{7,5},{8,10},{9,11},{10,... | collective-permute-start | bytes 98312 | tf_op jit(solution)/shard_map/ppermute | solution.py:22
  84.1 6.5 %collective-permute-start.4 = (bf16[8,2048]{1,0:T(8,128)(2,1)S(1)}, bf16[8,2048]{1,0:T(8,128)(2,1)S(1)}, u32[]{:S(2)}, u32[]{:S(2)}) collective-permute-start(bf16[8,2048]{1,0:T(8,128)(2,1)S(1)} %add_convert_fusion.1.p_ref), channel_id=1, source_target_pairs={{0,4},{1,5},{2,6},{3,7},{4,0},{5,1},{6,2},{7,3},{8,12},{9,13},{10,... | collective-permute-start | bytes 98312 | tf_op jit(solution)/shard_map/ppermute | solution.py:22
  87.0 5.1 %collective-permute-start.5 = (bf16[8,2048]{1,0:T(8,128)(2,1)S(1)}, bf16[8,2048]{1,0:T(8,128)(2,1)S(1)}, u32[]{:S(2)}, u32[]{:S(2)}) collective-permute-start(bf16[8,2048]{1,0:T(8,128)(2,1)S(1)} %add_convert_fusion.1.p_ref), channel_id=1, source_target_pairs={{0,6},{1,7},{2,4},{3,5},{4,2},{5,3},{6,0},{7,1},{8,14},{9,15},{10,... | collective-permute-start | bytes 98312 | tf_op jit(solution)/shard_map/ppermute | solution.py:22
  94.6 3.8 %collective-permute-start.6 = (f32[16,256]{1,0:T(8,128)S(1)}, f32[16,256]{1,0:T(8,128)S(1)}, u32[]{:S(2)}, u32[]{:S(2)}) collective-permute-start(f32[16,256]{1,0:T(8,128)S(1)} %get-tuple-element.46.state_ref), channel_id=1, source_target_pairs={{0,8},{8,0},{16,24},{24,16},{32,40},{40,32},{48,56},{56,48},{64,72... | collective-permute-start | bytes 49160 | tf_op jit(solution)/shard_map/ppermute | solution.py:22
  98.9 1.3 %collective-permute-start.7 = (f32[8,2048]{1,0:T(8,128)S(1)}, f32[8,2048]{1,0:T(8,128)S(1)}, u32[]{:S(2)}, u32[]{:S(2)}) collective-permute-start(f32[8,2048]{1,0:T(8,128)S(1)} %out_projection_1.1), channel_id=1, source_target_pairs={{0,1},{1,0},{2,3},{3,2},{4,5},{5,4},{6,7},{7,6},{8,9},{9,8},{10,11... | collective-permute-start | bytes 196616 | tf_op jit(solution)/shard_map/ppermute | solution.py:22
  100.2 5.2 %collective-permute-start.10 = (bf16[8,2048]{1,0:T(8,128)(2,1)S(1)}, bf16[8,2048]{1,0:T(8,128)(2,1)S(1)}, u32[]{:S(2)}, u32[]{:S(2)}) collective-permute-start(bf16[8,2048]{1,0:T(8,128)(2,1)S(1)} %add_convert_fusion.p_ref), channel_id=1, source_target_pairs={{0,6},{1,7},{2,4},{3,5},{4,2},{5,3},{6,0},{7,1},{8,14},{9,15},{10,... | collective-permute-start | bytes 98312 | tf_op jit(solution)/shard_map/ppermute | solution.py:22
  101.8 3.9 %collective-permute-start.8 = (bf16[8,2048]{1,0:T(8,128)(2,1)S(1)}, bf16[8,2048]{1,0:T(8,128)(2,1)S(1)}, u32[]{:S(2)}, u32[]{:S(2)}) collective-permute-start(bf16[8,2048]{1,0:T(8,128)(2,1)S(1)} %add_convert_fusion.p_ref), channel_id=1, source_target_pairs={{0,2},{1,3},{2,0},{3,1},{4,6},{5,7},{6,4},{7,5},{8,10},{9,11},{10,... | collective-permute-start | bytes 98312 | tf_op jit(solution)/shard_map/ppermute | solution.py:22
  101.9 5.4 %collective-permute-start.9 = (bf16[8,2048]{1,0:T(8,128)(2,1)S(1)}, bf16[8,2048]{1,0:T(8,128)(2,1)S(1)}, u32[]{:S(2)}, u32[]{:S(2)}) collective-permute-start(bf16[8,2048]{1,0:T(8,128)(2,1)S(1)} %add_convert_fusion.p_ref), channel_id=1, source_target_pairs={{0,4},{1,5},{2,6},{3,7},{4,0},{5,1},{6,2},{7,3},{8,12},{9,13},{10,... | collective-permute-start | bytes 98312 | tf_op jit(solution)/shard_map/ppermute | solution.py:22
  107.9 6.9 %collective-permute-start.11 = (f32[1,2560]{1,0:T(1,128)S(1)}, f32[1,2560]{1,0:T(1,128)S(1)}, u32[]{:S(2)}, u32[]{:S(2)}) collective-permute-start(f32[1,2560]{1,0:T(1,128)S(1)} %get-tuple-element.51), channel_id=1, source_target_pairs={{0,128},{8,136},{16,144},{24,152},{32,160},{40,168},{48,176},{56,1... | collective-permute-start | bytes 30728 | tf_op jit(solution)/shard_map/ppermute | solution.py:22

commit v4 on v3

--- a/solution.py
+++ b/solution.py
@@ -176,7 +176,8 @@
     )
 
 
-def leaving_kernel(cache_ref, out_ref, semaphores):
+def leaving_kernel(cache_ref, out_ref, unused_ref, semaphores):
+    unused_ref[...] = jnp.zeros_like(unused_ref)
     copies = [
         pltpu.make_async_copy(cache_ref.at[i, j, 2], out_ref.at[i, j], semaphores.at[2 * i + j])
         for i in range(2)
@@ -285,11 +286,14 @@
     params = pltpu.CompilerParams(vmem_limit_bytes=16 * 2**20)
     small = pltpu.CompilerParams(vmem_limit_bytes=2 * 2**20)
     held = in_hbm(cache)
-    leaving = pl.pallas_call(
+    leaving, _ = pl.pallas_call(
         leaving_kernel,
-        out_shape=pltpu.VMEM((2, 2, 2048, 128), jnp.bfloat16),
+        out_shape=(
+            pltpu.VMEM((2, 2, 2048, 128), jnp.bfloat16),
+            pltpu.VMEM((8, 128), jnp.float32),
+        ),
         in_specs=[ANY],
-        out_specs=ANY,
+        out_specs=(ANY, VM),
         scratch_shapes=[pltpu.SemaphoreType.DMA((4,))],
         compiler_params=small,
         name="leaving_cache",

time: 118 us -> 118 us (level)
  no operation moved by 1% of the time
where the time goes in v4:
time: 118 us
  Pallas kernels  79.8 us (68%)
  starting transfers between devices  19.3 us (16%)
  waiting for transfers between devices  17.1 us (14%)
    pallas_call x1, Pallas kernels, local(): pl.pallas_call(leaving_kernel, out_shape=(pltpu.VMEM((2, 2, 2048, 128), j...  65.3 us
    ppermute x13, starting transfers between devices, permute(): return lax.ppermute(value, axis, pairs)  19.3 us
    ppermute x13, waiting for transfers between devices, permute(): return lax.ppermute(value, axis, pairs)  17.1 us
    pallas_call x1, Pallas kernels, local(): pl.pallas_call(first_kernel, out_shape=out_shape, in_specs=[SM] * 3 + [VM...  4.51 us
    pallas_call x1, Pallas kernels, local(): pl.pallas_call(fetch_kernel, out_shape=tuple((pltpu.VMEM(shape, jnp.bfloa...  3.35 us
    pallas_call x1, Pallas kernels, local(): pl.pallas_call(arrival_kernel, out_shape=(pltpu.HBM((3, 2048), jnp.float3...  2.61 us
    pallas_call x1, Pallas kernels, local(): pl.pallas_call(second_kernel, out_shape=out_shape, in_specs=[SM] * 3 + [V...  2.47 us
  transfers between devices with their start and end apart: 13, of which 10 were waited for; matrix products, arithmetic and copies ran while one was open for 1% of the time, Pallas kernels for 10%

profile of v4, /device:TPU:64, one launch (start us, length us, event | category | flops | bytes accessed | tf_op | source)
XLA Modules:
  0.0 118.0 jit_solution(10975871581451365544)
XLA Ops:
  0.7 65.3 %leaving_cache.1 = (bf16[2,2,2048,128]{3,2,1,0:T(8,128)(2,1)}, f32[8,128]{1,0:T(8,128)}) custom-call(bf16[2,2,3,2048,128]{4,3,2,1,0:T(8,128)(2,1)} %bitcast.6), custom_call_target="tpu_custom_call" | custom-call | tf_op jit(solution)/shard_map/leaving_cache/pallas_call | solution.py:289
  66.0 3.1 %collective-permute-start.12 = (bf16[2,2,2048,128]{3,2,1,0:T(8,128)(2,1)}, bf16[2,2,2048,128]{3,2,1,0:T(8,128)(2,1)S(1)}, u32[]{:S(2)}, u32[]{:S(2)}) collective-permute-start(bf16[2,2,2048,128]{3,2,1,0:T(8,128)(2,1)} %get-tuple-element.53), channel_id=1, source_target_pairs={{0,128},{8,136},{16,144},{24,152},{32,160},{40,168},{48,176},{56,1... | collective-permute-start | bytes 6291464 | tf_op jit(solution)/shard_map/ppermute | solution.py:22
  69.1 1.9 %collective-permute-start = (bf16[1,2048]{1,0:T(2,128)(2,1)S(1)}, bf16[1,2048]{1,0:T(2,128)(2,1)S(1)}, u32[]{:S(2)}, u32[]{:S(2)}) collective-permute-start(bf16[1,2048]{1,0:T(2,128)(2,1)S(1)} %copy-done.3), channel_id=1, source_target_pairs={{0,8},{8,0},{16,24},{24,16},{32,40},{40,32},{48,56},{56,48},{64,72... | collective-permute-start | bytes 12296 | tf_op jit(solution)/shard_map/ppermute | solution.py:22
  71.4 1.4 %collective-permute-done.far_long_ref = bf16[1,2048]{1,0:T(2,128)(2,1)S(1)} collective-permute-done((bf16[1,2048]{1,0:T(2,128)(2,1)S(1)}, bf16[1,2048]{1,0:T(2,128)(2,1)S(1)}, u32[]{:S(2)}, u32[]{:S(2)}) %collective-permute-start) | collective-permute-done | bytes 4128 | tf_op jit(solution)/shard_map/ppermute | solution.py:22
  72.8 4.5 %attention_0.1 = (f32[16,256]{1,0:T(8,128)S(1)}, f32[16,256]{1,0:T(8,128)S(1)}, f32[2,128]{1,0:T(2,128)S(1)}, f32[8,2048]{1,0:T(8,128)S(1)}) custom-call(s32[1]{0:T(128)} %bitcast.group_ref, s32[96]{0:T(128)S(1)} %copy-done.7, s32[32]{0:T(128)S(1)} %copy-done.6, bf16[3,2048]{1,0:T(4,128)(2,1)S(1)} %copy-done.2, bf16[1,2048]{1,0:T(2,128)(2,1)S(1)} %copy-done.3, ...), custom_call_target="tpu_custom_call" | custom-call | tf_op jit(solution)/shard_map/attention_0/pallas_call | solution.py:350
  77.3 2.0 %collective-permute-start.1 = (f32[16,256]{1,0:T(8,128)S(1)}, f32[16,256]{1,0:T(8,128)S(1)}, u32[]{:S(2)}, u32[]{:S(2)}) collective-permute-start(f32[16,256]{1,0:T(8,128)S(1)} %get-tuple-element.31.state_ref), channel_id=1, source_target_pairs={{0,8},{8,0},{16,24},{24,16},{32,40},{40,32},{48,56},{56,48},{64,72... | collective-permute-start | bytes 49160 | tf_op jit(solution)/shard_map/ppermute | solution.py:22
  79.3 1.8 %collective-permute-done.1.far_ref = f32[16,256]{1,0:T(8,128)S(1)} collective-permute-done((f32[16,256]{1,0:T(8,128)S(1)}, f32[16,256]{1,0:T(8,128)S(1)}, u32[]{:S(2)}, u32[]{:S(2)}) %collective-permute-start.1) | collective-permute-done | bytes 16416 | tf_op jit(solution)/shard_map/ppermute | solution.py:22
  81.7 1.2 %collective-permute-done.2 = f32[8,2048]{1,0:T(8,128)S(1)} collective-permute-done((f32[8,2048]{1,0:T(8,128)S(1)}, f32[8,2048]{1,0:T(8,128)S(1)}, u32[]{:S(2)}, u32[]{:S(2)}) %collective-permute-start.2) | collective-permute-done | bytes 65568 | tf_op jit(solution)/shard_map/ppermute | solution.py:22
  83.0 1.7 %collective-permute-start.3 = (bf16[8,2048]{1,0:T(8,128)(2,1)S(1)}, bf16[8,2048]{1,0:T(8,128)(2,1)S(1)}, u32[]{:S(2)}, u32[]{:S(2)}) collective-permute-start(bf16[8,2048]{1,0:T(8,128)(2,1)S(1)} %add_convert_fusion.1.p_ref), channel_id=1, source_target_pairs={{0,2},{1,3},{2,0},{3,1},{4,6},{5,7},{6,4},{7,5},{8,10},{9,11},{10,... | collective-permute-start | bytes 98312 | tf_op jit(solution)/shard_map/ppermute | solution.py:22
  84.7 2.9 %collective-permute-start.4 = (bf16[8,2048]{1,0:T(8,128)(2,1)S(1)}, bf16[8,2048]{1,0:T(8,128)(2,1)S(1)}, u32[]{:S(2)}, u32[]{:S(2)}) collective-permute-start(bf16[8,2048]{1,0:T(8,128)(2,1)S(1)} %add_convert_fusion.1.p_ref), channel_id=1, source_target_pairs={{0,4},{1,5},{2,6},{3,7},{4,0},{5,1},{6,2},{7,3},{8,12},{9,13},{10,... | collective-permute-start | bytes 98312 | tf_op jit(solution)/shard_map/ppermute | solution.py:22
  87.8 3.4 %fetch_1.1 = (bf16[2048,256]{1,0:T(8,128)(2,1)S(1)}, bf16[2048,128]{1,0:T(8,128)(2,1)S(1)}, bf16[2048,128]{1,0:T(8,128)(2,1)S(1)}, bf16[3,2048,128]{2,1,0:T(8,12...) custom-call(bf16[2,2,3,2048,128]{4,3,2,1,0:T(8,128)(2,1)} %bitcast.8, ...), custom_call_target="tpu_custom_call" | custom-call | tf_op jit(solution)/shard_map/fetch_1/pallas_call | solution.py:363
  91.2 1.5 %collective-permute-done.5.r3_ref = bf16[8,2048]{1,0:T(8,128)(2,1)S(1)} collective-permute-done((bf16[8,2048]{1,0:T(8,128)(2,1)S(1)}, bf16[8,2048]{1,0:T(8,128)(2,1)S(1)}, u32[]{:S(2)}, u32[]{:S(2)}) %collective-permute-start.5) | collective-permute-done | bytes 32800 | tf_op jit(solution)/shard_map/ppermute | solution.py:22
  92.7 2.5 %attention_1.1 = (f32[16,256]{1,0:T(8,128)S(1)}, f32[16,256]{1,0:T(8,128)S(1)}, f32[2,128]{1,0:T(2,128)S(1)}, f32[8,2048]{1,0:T(8,128)S(1)}) custom-call(s32[1]{0:T(128)} %bitcast.group_ref, s32[96]{0:T(128)S(1)} %copy-done.7, s32[32]{0:T(128)S(1)} %copy-done.6, f32[8,2048]{1,0:T(8,128)S(1)} %get-tuple-element.30.before_ref, ...), custom_call_target="tpu_custom_call" | custom-call | tf_op jit(solution)/shard_map/attention_1/pallas_call | solution.py:372
  95.2 2.0 %collective-permute-start.6 = (f32[16,256]{1,0:T(8,128)S(1)}, f32[16,256]{1,0:T(8,128)S(1)}, u32[]{:S(2)}, u32[]{:S(2)}) collective-permute-start(f32[16,256]{1,0:T(8,128)S(1)} %get-tuple-element.47.state_ref), channel_id=1, source_target_pairs={{0,8},{8,0},{16,24},{24,16},{32,40},{40,32},{48,56},{56,48},{64,72... | collective-permute-start | bytes 49160 | tf_op jit(solution)/shard_map/ppermute | solution.py:22
  97.2 1.8 %collective-permute-done.6.far_ref = f32[16,256]{1,0:T(8,128)S(1)} collective-permute-done((f32[16,256]{1,0:T(8,128)S(1)}, f32[16,256]{1,0:T(8,128)S(1)}, u32[]{:S(2)}, u32[]{:S(2)}) %collective-permute-start.6) | collective-permute-done | bytes 16416 | tf_op jit(solution)/shard_map/ppermute | solution.py:22
  99.6 1.2 %collective-permute-done.7 = f32[8,2048]{1,0:T(8,128)S(1)} collective-permute-done((f32[8,2048]{1,0:T(8,128)S(1)}, f32[8,2048]{1,0:T(8,128)S(1)}, u32[]{:S(2)}, u32[]{:S(2)}) %collective-permute-start.7) | collective-permute-done | bytes 65568 | tf_op jit(solution)/shard_map/ppermute | solution.py:22
  100.8 1.6 %collective-permute-start.10 = (bf16[8,2048]{1,0:T(8,128)(2,1)S(1)}, bf16[8,2048]{1,0:T(8,128)(2,1)S(1)}, u32[]{:S(2)}, u32[]{:S(2)}) collective-permute-start(bf16[8,2048]{1,0:T(8,128)(2,1)S(1)} %add_convert_fusion.p_ref), channel_id=1, source_target_pairs={{0,6},{1,7},{2,4},{3,5},{4,2},{5,3},{6,0},{7,1},{8,14},{9,15},{10,... | collective-permute-start | bytes 98312 | tf_op jit(solution)/shard_map/ppermute | solution.py:22
  102.4 3.2 %collective-permute-start.9 = (bf16[8,2048]{1,0:T(8,128)(2,1)S(1)}, bf16[8,2048]{1,0:T(8,128)(2,1)S(1)}, u32[]{:S(2)}, u32[]{:S(2)}) collective-permute-start(bf16[8,2048]{1,0:T(8,128)(2,1)S(1)} %add_convert_fusion.p_ref), channel_id=1, source_target_pairs={{0,4},{1,5},{2,6},{3,7},{4,0},{5,1},{6,2},{7,3},{8,12},{9,13},{10,... | collective-permute-start | bytes 98312 | tf_op jit(solution)/shard_map/ppermute | solution.py:22
  106.4 1.5 %collective-permute-done.9.r2_ref = bf16[8,2048]{1,0:T(8,128)(2,1)S(1)} collective-permute-done((bf16[8,2048]{1,0:T(8,128)(2,1)S(1)}, bf16[8,2048]{1,0:T(8,128)(2,1)S(1)}, u32[]{:S(2)}, u32[]{:S(2)}) %collective-permute-start.9) | collective-permute-done | bytes 32800 | tf_op jit(solution)/shard_map/ppermute | solution.py:22
  107.9 0.6 final_rows.1
  108.5 0.5 collective-permute-start.11
  109.0 0.6 dynamic_slice.9.length_ref
  109.6 5.8 %collective-permute-done.11.arrived_ref = f32[1,2560]{1,0:T(1,128)S(1)} collective-permute-done((f32[1,2560]{1,0:T(1,128)S(1)}, f32[1,2560]{1,0:T(1,128)S(1)}, u32[]{:S(2)}, u32[]{:S(2)}) %collective-permute-start.11) | collective-permute-done | bytes 10272 | tf_op jit(solution)/shard_map/ppermute | solution.py:22
  115.4 2.6 %arrival.1 = (f32[3,2048]{1,0:T(4,128)}, bf16[2,2,2048,128]{3,2,1,0:T(8,128)(2,1)}) custom-call(s32[1]{0:T(128)} %dynamic_slice.9.length_ref, f32[2,2048]{1,0:T(2,128)S(1)} %get-tuple-element.51.stay_ref, f32[1,2560]{1,0:T(1,128)S(1)} %collective-permute-done.11.arrived_ref, bf16[2,2,2048,128]{3,2,1,0:T(8,128)(2,1)S(1)} %collective-permute-done.12.moving_ref), custom_call_target="tpu_custom_call" | custom-call | tf_op jit(solution)/shard_map/arrival/pallas_call | solution.py:397
  (38 shorter events, 2.5 us)
Async XLA Ops:
  0.6 68.5 %copy-start.3 = (bf16[1,2048]{1,0:T(2,128)(2,1)S(1)}, bf16[1,2048]{1,0:T(2,128)(2,1)}, u32[]{:S(2)}) copy-start(bf16[1,2048]{1,0:T(2,128)(2,1)} %own_long_ref.1) | copy-start | bytes 12292
  0.6 70.4 %copy-start.6 = (s32[32]{0:T(128)S(1)}, s32[32]{0:T(128)}, u32[]{:S(2)}) copy-start(s32[32]{0:T(128)} %long_lengths_ref.3) | copy-start | bytes 388
  0.7 70.5 %copy-start.7 = (s32[96]{0:T(128)S(1)}, s32[96]{0:T(128)}, u32[]{:S(2)}) copy-start(s32[96]{0:T(128)} %lengths_ref.3) | copy-start | bytes 1156
  0.7 70.6 %copy-start.8 = (f32[128]{0:T(128)S(1)}, f32[128]{0:T(128)}, u32[]{:S(2)}) copy-start(f32[128]{0:T(128)} %constant.43.clone) | copy-start | bytes 1540
  0.7 70.6 %copy-start.9 = (f32[128]{0:T(128)S(1)}, f32[128]{0:T(128)}, u32[]{:S(2)}) copy-start(f32[128]{0:T(128)} %constant.44.clone) | copy-start | bytes 1540
  0.7 72.1 %copy-start.1 = (f32[2,2048]{1,0:T(2,128)S(1)}, f32[2,2048]{1,0:T(2,128)}, u32[]{:S(2)}) copy-start(f32[2,2048]{1,0:T(2,128)} %rest_0_.3) | copy-start | bytes 49156
  0.7 72.1 %copy-start.2 = (bf16[3,2048]{1,0:T(4,128)(2,1)S(1)}, bf16[3,2048]{1,0:T(4,128)(2,1)}, u32[]{:S(2)}) copy-start(bf16[3,2048]{1,0:T(4,128)(2,1)} %tokens_ref.1) | copy-start | bytes 36868
  0.7 72.1 %copy-start.4 = (f32[2,128]{1,0:T(2,128)S(1)}, f32[2,128]{1,0:T(2,128)}, u32[]{:S(2)}) copy-start(f32[2,128]{1,0:T(2,128)} %rest_1_.3) | copy-start | bytes 3076
  0.7 72.1 %copy-start.5 = (f32[2,128]{1,0:T(2,128)S(1)}, f32[2,128]{1,0:T(2,128)}, u32[]{:S(2)}) copy-start(f32[2,128]{1,0:T(2,128)} %rest_2_.3) | copy-start | bytes 3076
  66.0 49.4 %collective-permute-start.12 = (bf16[2,2,2048,128]{3,2,1,0:T(8,128)(2,1)}, bf16[2,2,2048,128]{3,2,1,0:T(8,128)(2,1)S(1)}, u32[]{:S(2)}, u32[]{:S(2)}) collective-permute-start(bf16[2,2,2048,128]{3,2,1,0:T(8,128)(2,1)} %get-tuple-element.53), channel_id=1, source_target_pairs={{0,128},{8,136},{16,144},{24,152},{32,160},{40,168},{48,176},{56,1... | collective-permute-start | bytes 6291464 | tf_op jit(solution)/shard_map/ppermute | solution.py:22
  69.1 3.7 %collective-permute-start = (bf16[1,2048]{1,0:T(2,128)(2,1)S(1)}, bf16[1,2048]{1,0:T(2,128)(2,1)S(1)}, u32[]{:S(2)}, u32[]{:S(2)}) collective-permute-start(bf16[1,2048]{1,0:T(2,128)(2,1)S(1)} %copy-done.3), channel_id=1, source_target_pairs={{0,8},{8,0},{16,24},{24,16},{32,40},{40,32},{48,56},{56,48},{64,72... | collective-permute-start | bytes 12296 | tf_op jit(solution)/shard_map/ppermute | solution.py:22
  72.8 8.4 %copy-start = (bf16[2,256,2048]{2,1,0:T(8,128)(2,1)S(1)}, bf16[2,256,2048]{2,1,0:T(8,128)(2,1)}, u32[]{:S(2)}) copy-start(bf16[2,256,2048]{2,1,0:T(8,128)(2,1)} %w_ref.3) | copy-start | bytes 6291460
  77.3 3.8 %collective-permute-start.1 = (f32[16,256]{1,0:T(8,128)S(1)}, f32[16,256]{1,0:T(8,128)S(1)}, u32[]{:S(2)}, u32[]{:S(2)}) collective-permute-start(f32[16,256]{1,0:T(8,128)S(1)} %get-tuple-element.31.state_ref), channel_id=1, source_target_pairs={{0,8},{8,0},{16,24},{24,16},{32,40},{40,32},{48,56},{56,48},{64,72... | collective-permute-start | bytes 49160 | tf_op jit(solution)/shard_map/ppermute | solution.py:22
  81.6 1.3 %collective-permute-start.2 = (f32[8,2048]{1,0:T(8,128)S(1)}, f32[8,2048]{1,0:T(8,128)S(1)}, u32[]{:S(2)}, u32[]{:S(2)}) collective-permute-start(f32[8,2048]{1,0:T(8,128)S(1)} %out_projection_0.1), channel_id=1, source_target_pairs={{0,1},{1,0},{2,3},{3,2},{4,5},{5,4},{6,7},{7,6},{8,9},{9,8},{10,11... | collective-permute-start | bytes 196616 | tf_op jit(solution)/shard_map/ppermute | solution.py:22
  83.0 8.1 %collective-permute-start.3 = (bf16[8,2048]{1,0:T(8,128)(2,1)S(1)}, bf16[8,2048]{1,0:T(8,128)(2,1)S(1)}, u32[]{:S(2)}, u32[]{:S(2)}) collective-permute-start(bf16[8,2048]{1,0:T(8,128)(2,1)S(1)} %add_convert_fusion.1.p_ref), channel_id=1, source_target_pairs={{0,2},{1,3},{2,0},{3,1},{4,6},{5,7},{6,4},{7,5},{8,10},{9,11},{10,... | collective-permute-start | bytes 98312 | tf_op jit(solution)/shard_map/ppermute | solution.py:22
  84.7 6.5 %collective-permute-start.4 = (bf16[8,2048]{1,0:T(8,128)(2,1)S(1)}, bf16[8,2048]{1,0:T(8,128)(2,1)S(1)}, u32[]{:S(2)}, u32[]{:S(2)}) collective-permute-start(bf16[8,2048]{1,0:T(8,128)(2,1)S(1)} %add_convert_fusion.1.p_ref), channel_id=1, source_target_pairs={{0,4},{1,5},{2,6},{3,7},{4,0},{5,1},{6,2},{7,3},{8,12},{9,13},{10,... | collective-permute-start | bytes 98312 | tf_op jit(solution)/shard_map/ppermute | solution.py:22
  87.6 5.1 %collective-permute-start.5 = (bf16[8,2048]{1,0:T(8,128)(2,1)S(1)}, bf16[8,2048]{1,0:T(8,128)(2,1)S(1)}, u32[]{:S(2)}, u32[]{:S(2)}) collective-permute-start(bf16[8,2048]{1,0:T(8,128)(2,1)S(1)} %add_convert_fusion.1.p_ref), channel_id=1, source_target_pairs={{0,6},{1,7},{2,4},{3,5},{4,2},{5,3},{6,0},{7,1},{8,14},{9,15},{10,... | collective-permute-start | bytes 98312 | tf_op jit(solution)/shard_map/ppermute | solution.py:22
  95.2 3.8 %collective-permute-start.6 = (f32[16,256]{1,0:T(8,128)S(1)}, f32[16,256]{1,0:T(8,128)S(1)}, u32[]{:S(2)}, u32[]{:S(2)}) collective-permute-start(f32[16,256]{1,0:T(8,128)S(1)} %get-tuple-element.47.state_ref), channel_id=1, source_target_pairs={{0,8},{8,0},{16,24},{24,16},{32,40},{40,32},{48,56},{56,48},{64,72... | collective-permute-start | bytes 49160 | tf_op jit(solution)/shard_map/ppermute | solution.py:22
  99.5 1.3 %collective-permute-start.7 = (f32[8,2048]{1,0:T(8,128)S(1)}, f32[8,2048]{1,0:T(8,128)S(1)}, u32[]{:S(2)}, u32[]{:S(2)}) collective-permute-start(f32[8,2048]{1,0:T(8,128)S(1)} %out_projection_1.1), channel_id=1, source_target_pairs={{0,1},{1,0},{2,3},{3,2},{4,5},{5,4},{6,7},{7,6},{8,9},{9,8},{10,11... | collective-permute-start | bytes 196616 | tf_op jit(solution)/shard_map/ppermute | solution.py:22
  100.8 5.2 %collective-permute-start.10 = (bf16[8,2048]{1,0:T(8,128)(2,1)S(1)}, bf16[8,2048]{1,0:T(8,128)(2,1)S(1)}, u32[]{:S(2)}, u32[]{:S(2)}) collective-permute-start(bf16[8,2048]{1,0:T(8,128)(2,1)S(1)} %add_convert_fusion.p_ref), channel_id=1, source_target_pairs={{0,6},{1,7},{2,4},{3,5},{4,2},{5,3},{6,0},{7,1},{8,14},{9,15},{10,... | collective-permute-start | bytes 98312 | tf_op jit(solution)/shard_map/ppermute | solution.py:22
  102.4 3.9 %collective-permute-start.8 = (bf16[8,2048]{1,0:T(8,128)(2,1)S(1)}, bf16[8,2048]{1,0:T(8,128)(2,1)S(1)}, u32[]{:S(2)}, u32[]{:S(2)}) collective-permute-start(bf16[8,2048]{1,0:T(8,128)(2,1)S(1)} %add_convert_fusion.p_ref), channel_id=1, source_target_pairs={{0,2},{1,3},{2,0},{3,1},{4,6},{5,7},{6,4},{7,5},{8,10},{9,11},{10,... | collective-permute-start | bytes 98312 | tf_op jit(solution)/shard_map/ppermute | solution.py:22
  102.4 5.4 %collective-permute-start.9 = (bf16[8,2048]{1,0:T(8,128)(2,1)S(1)}, bf16[8,2048]{1,0:T(8,128)(2,1)S(1)}, u32[]{:S(2)}, u32[]{:S(2)}) collective-permute-start(bf16[8,2048]{1,0:T(8,128)(2,1)S(1)} %add_convert_fusion.p_ref), channel_id=1, source_target_pairs={{0,4},{1,5},{2,6},{3,7},{4,0},{5,1},{6,2},{7,3},{8,12},{9,13},{10,... | collective-permute-start | bytes 98312 | tf_op jit(solution)/shard_map/ppermute | solution.py:22
  108.5 6.9 %collective-permute-start.11 = (f32[1,2560]{1,0:T(1,128)S(1)}, f32[1,2560]{1,0:T(1,128)S(1)}, u32[]{:S(2)}, u32[]{:S(2)}) collective-permute-start(f32[1,2560]{1,0:T(1,128)S(1)} %get-tuple-element.52), channel_id=1, source_target_pairs={{0,128},{8,136},{16,144},{24,152},{32,160},{40,168},{48,176},{56,1... | collective-permute-start | bytes 30728 | tf_op jit(solution)/shard_map/ppermute | solution.py:22

commit v5 on v3

--- a/solution.py
+++ b/solution.py
@@ -176,15 +176,22 @@
     )
 
 
-def leaving_kernel(cache_ref, out_ref, semaphores):
-    copies = [
-        pltpu.make_async_copy(cache_ref.at[i, j, 2], out_ref.at[i, j], semaphores.at[2 * i + j])
-        for i in range(2)
-        for j in range(2)
-    ]
-    for copy in copies:
+def leaving_kernel(cache_ref, out_ref, blocks, semaphores):
+    places = [(i, j) for i in range(2) for j in range(2)]
+    reads = [
+        pltpu.make_async_copy(cache_ref.at[i, j, 2], blocks.at[i, j], semaphores.at[0, i, j])
+        for i, j in places
+    ]
+    writes = [
+        pltpu.make_async_copy(blocks.at[i, j], out_ref.at[i, j], semaphores.at[1, i, j])
+        for i, j in places
+    ]
+    for copy in reads:
         copy.start()
-    for copy in copies:
+    for read, write in zip(reads, writes):
+        read.wait()
+        write.start()
+    for copy in writes:
         copy.wait()
 
 
@@ -287,11 +294,14 @@
     held = in_hbm(cache)
     leaving = pl.pallas_call(
         leaving_kernel,
-        out_shape=pltpu.VMEM((2, 2, 2048, 128), jnp.bfloat16),
+        out_shape=pltpu.HBM((2, 2, 2048, 128), jnp.bfloat16),
         in_specs=[ANY],
         out_specs=ANY,
-        scratch_shapes=[pltpu.SemaphoreType.DMA((4,))],
-        compiler_params=small,
+        scratch_shapes=[
+            pltpu.VMEM((2, 2, 2048, 128), jnp.bfloat16),
+            pltpu.SemaphoreType.DMA((2, 2, 2)),
+        ],
+        compiler_params=pltpu.CompilerParams(vmem_limit_bytes=4 * 2**20),
         name="leaving_cache",
     )(held)
     moving = permute(leaving, "replica", lambda i: (i + groups // 2) % groups)

time: 118 us -> 55.4 us (0.47)
  Pallas kernels: 79.3 us -> 17.1 us
    pallas_call x1, Pallas kernels: 64.7 us -> 2.47 us  [local(): pl.pallas_call(leaving_kernel, out_shape=pltpu.HBM((2, 2, 2048, 128), jnp...]
  transfers between devices with their start and end apart: 13 -> 13, of which waited for: 10 -> 10; matrix products, arithmetic and copies ran while one was open for 1% -> 2% of each run, Pallas kernels for 10% -> 22%
where the time goes in v5:
time: 55.4 us; the launch traced here: 55.3 us
  starting transfers between devices  19.3 us (35%)
  Pallas kernels  17.1 us (31%)
  waiting for transfers between devices  17 us (31%)
  local copies, waits for them, and re-layouts  0.86 us (2%)
  between operations  0.83 us (1%)
    ppermute x13, starting transfers between devices, permute(): return lax.ppermute(value, axis, pairs)  19.3 us
    ppermute x13, waiting for transfers between devices, permute(): return lax.ppermute(value, axis, pairs)  17 us
    pallas_call x1, Pallas kernels, local(): pl.pallas_call(first_kernel, out_shape=out_shape, in_specs=[SM] * 3 + [VM...  4.51 us
    pallas_call x1, Pallas kernels, local(): pl.pallas_call(fetch_kernel, out_shape=tuple((pltpu.VMEM(shape, jnp.bfloa...  3.35 us
    pallas_call x1, Pallas kernels, local(): pl.pallas_call(arrival_kernel, out_shape=(pltpu.HBM((3, 2048), jnp.float3...  2.67 us
    pallas_call x1, Pallas kernels, local(): pl.pallas_call(second_kernel, out_shape=out_shape, in_specs=[SM] * 3 + [V...  2.47 us
    pallas_call x1, Pallas kernels, local(): pl.pallas_call(leaving_kernel, out_shape=pltpu.HBM((2, 2, 2048, 128), jnp...  2.47 us
  transfers between devices with their start and end apart: 13, of which 10 were waited for; matrix products, arithmetic and copies ran while one was open for 2% of the time, Pallas kernels for 22%

profile of v5, /device:TPU:64, one launch (start us, length us, event | category | flops | bytes accessed | tf_op | source)
XLA Modules:
  0.0 55.3 jit_solution(1154247291440177344)
XLA Ops:
  0.7 2.5 %leaving_cache.1 = bf16[2,2,2048,128]{3,2,1,0:T(8,128)(2,1)} custom-call(bf16[2,2,3,2048,128]{4,3,2,1,0:T(8,128)(2,1)} %bitcast.6), custom_call_target="tpu_custom_call" | custom-call | tf_op jit(solution)/shard_map/leaving_cache/pallas_call | solution.py:295
  3.2 3.1 %collective-permute-start.12 = (bf16[2,2,2048,128]{3,2,1,0:T(8,128)(2,1)}, bf16[2,2,2048,128]{3,2,1,0:T(8,128)(2,1)S(1)}, u32[]{:S(2)}, u32[]{:S(2)}) collective-permute-start(bf16[2,2,2048,128]{3,2,1,0:T(8,128)(2,1)} %leaving_cache.1), channel_id=1, source_target_pairs={{0,128},{8,136},{16,144},{24,152},{32,160},{40,168},{48,176},{56,1... | collective-permute-start | bytes 6291464 | tf_op jit(solution)/shard_map/ppermute | solution.py:22
  6.3 1.9 %collective-permute-start = (bf16[1,2048]{1,0:T(2,128)(2,1)S(1)}, bf16[1,2048]{1,0:T(2,128)(2,1)S(1)}, u32[]{:S(2)}, u32[]{:S(2)}) collective-permute-start(bf16[1,2048]{1,0:T(2,128)(2,1)S(1)} %copy-done.3), channel_id=1, source_target_pairs={{0,8},{8,0},{16,24},{24,16},{32,40},{40,32},{48,56},{56,48},{64,72... | collective-permute-start | bytes 12296 | tf_op jit(solution)/shard_map/ppermute | solution.py:22
  8.6 1.4 %collective-permute-done.far_long_ref = bf16[1,2048]{1,0:T(2,128)(2,1)S(1)} collective-permute-done((bf16[1,2048]{1,0:T(2,128)(2,1)S(1)}, bf16[1,2048]{1,0:T(2,128)(2,1)S(1)}, u32[]{:S(2)}, u32[]{:S(2)}) %collective-permute-start) | collective-permute-done | bytes 4128 | tf_op jit(solution)/shard_map/ppermute | solution.py:22
  10.0 4.5 %attention_0.1 = (f32[16,256]{1,0:T(8,128)S(1)}, f32[16,256]{1,0:T(8,128)S(1)}, f32[2,128]{1,0:T(2,128)S(1)}, f32[8,2048]{1,0:T(8,128)S(1)}) custom-call(s32[1]{0:T(128)} %bitcast.group_ref, s32[96]{0:T(128)S(1)} %copy-done.7, s32[32]{0:T(128)S(1)} %copy-done.6, bf16[3,2048]{1,0:T(4,128)(2,1)S(1)} %copy-done.2, bf16[1,2048]{1,0:T(2,128)(2,1)S(1)} %copy-done.3, ...), custom_call_target="tpu_custom_call" | custom-call | tf_op jit(solution)/shard_map/attention_0/pallas_call | solution.py:356
  14.5 2.0 %collective-permute-start.1 = (f32[16,256]{1,0:T(8,128)S(1)}, f32[16,256]{1,0:T(8,128)S(1)}, u32[]{:S(2)}, u32[]{:S(2)}) collective-permute-start(f32[16,256]{1,0:T(8,128)S(1)} %get-tuple-element.30.state_ref), channel_id=1, source_target_pairs={{0,8},{8,0},{16,24},{24,16},{32,40},{40,32},{48,56},{56,48},{64,72... | collective-permute-start | bytes 49160 | tf_op jit(solution)/shard_map/ppermute | solution.py:22
  16.5 1.8 %collective-permute-done.1.far_ref = f32[16,256]{1,0:T(8,128)S(1)} collective-permute-done((f32[16,256]{1,0:T(8,128)S(1)}, f32[16,256]{1,0:T(8,128)S(1)}, u32[]{:S(2)}, u32[]{:S(2)}) %collective-permute-start.1) | collective-permute-done | bytes 16416 | tf_op jit(solution)/shard_map/ppermute | solution.py:22
  18.9 1.2 %collective-permute-done.2 = f32[8,2048]{1,0:T(8,128)S(1)} collective-permute-done((f32[8,2048]{1,0:T(8,128)S(1)}, f32[8,2048]{1,0:T(8,128)S(1)}, u32[]{:S(2)}, u32[]{:S(2)}) %collective-permute-start.2) | collective-permute-done | bytes 65568 | tf_op jit(solution)/shard_map/ppermute | solution.py:22
  20.2 1.7 %collective-permute-start.3 = (bf16[8,2048]{1,0:T(8,128)(2,1)S(1)}, bf16[8,2048]{1,0:T(8,128)(2,1)S(1)}, u32[]{:S(2)}, u32[]{:S(2)}) collective-permute-start(bf16[8,2048]{1,0:T(8,128)(2,1)S(1)} %add_convert_fusion.1.p_ref), channel_id=1, source_target_pairs={{0,2},{1,3},{2,0},{3,1},{4,6},{5,7},{6,4},{7,5},{8,10},{9,11},{10,... | collective-permute-start | bytes 98312 | tf_op jit(solution)/shard_map/ppermute | solution.py:22
  21.9 2.9 %collective-permute-start.4 = (bf16[8,2048]{1,0:T(8,128)(2,1)S(1)}, bf16[8,2048]{1,0:T(8,128)(2,1)S(1)}, u32[]{:S(2)}, u32[]{:S(2)}) collective-permute-start(bf16[8,2048]{1,0:T(8,128)(2,1)S(1)} %add_convert_fusion.1.p_ref), channel_id=1, source_target_pairs={{0,4},{1,5},{2,6},{3,7},{4,0},{5,1},{6,2},{7,3},{8,12},{9,13},{10,... | collective-permute-start | bytes 98312 | tf_op jit(solution)/shard_map/ppermute | solution.py:22
  25.0 3.4 %fetch_1.1 = (bf16[2048,256]{1,0:T(8,128)(2,1)S(1)}, bf16[2048,128]{1,0:T(8,128)(2,1)S(1)}, bf16[2048,128]{1,0:T(8,128)(2,1)S(1)}, bf16[3,2048,128]{2,1,0:T(8,12...) custom-call(bf16[2,2,3,2048,128]{4,3,2,1,0:T(8,128)(2,1)} %bitcast.8, ...), custom_call_target="tpu_custom_call" | custom-call | tf_op jit(solution)/shard_map/fetch_1/pallas_call | solution.py:369
  28.4 1.5 %collective-permute-done.5.r3_ref = bf16[8,2048]{1,0:T(8,128)(2,1)S(1)} collective-permute-done((bf16[8,2048]{1,0:T(8,128)(2,1)S(1)}, bf16[8,2048]{1,0:T(8,128)(2,1)S(1)}, u32[]{:S(2)}, u32[]{:S(2)}) %collective-permute-start.5) | collective-permute-done | bytes 32800 | tf_op jit(solution)/shard_map/ppermute | solution.py:22
  29.9 2.5 %attention_1.1 = (f32[16,256]{1,0:T(8,128)S(1)}, f32[16,256]{1,0:T(8,128)S(1)}, f32[2,128]{1,0:T(2,128)S(1)}, f32[8,2048]{1,0:T(8,128)S(1)}) custom-call(s32[1]{0:T(128)} %bitcast.group_ref, s32[96]{0:T(128)S(1)} %copy-done.7, s32[32]{0:T(128)S(1)} %copy-done.6, f32[8,2048]{1,0:T(8,128)S(1)} %get-tuple-element.29.before_ref, ...), custom_call_target="tpu_custom_call" | custom-call | tf_op jit(solution)/shard_map/attention_1/pallas_call | solution.py:378
  32.4 2.0 %collective-permute-start.6 = (f32[16,256]{1,0:T(8,128)S(1)}, f32[16,256]{1,0:T(8,128)S(1)}, u32[]{:S(2)}, u32[]{:S(2)}) collective-permute-start(f32[16,256]{1,0:T(8,128)S(1)} %get-tuple-element.46.state_ref), channel_id=1, source_target_pairs={{0,8},{8,0},{16,24},{24,16},{32,40},{40,32},{48,56},{56,48},{64,72... | collective-permute-start | bytes 49160 | tf_op jit(solution)/shard_map/ppermute | solution.py:22
  34.4 1.8 %collective-permute-done.6.far_ref = f32[16,256]{1,0:T(8,128)S(1)} collective-permute-done((f32[16,256]{1,0:T(8,128)S(1)}, f32[16,256]{1,0:T(8,128)S(1)}, u32[]{:S(2)}, u32[]{:S(2)}) %collective-permute-start.6) | collective-permute-done | bytes 16416 | tf_op jit(solution)/shard_map/ppermute | solution.py:22
  36.8 1.2 %collective-permute-done.7 = f32[8,2048]{1,0:T(8,128)S(1)} collective-permute-done((f32[8,2048]{1,0:T(8,128)S(1)}, f32[8,2048]{1,0:T(8,128)S(1)}, u32[]{:S(2)}, u32[]{:S(2)}) %collective-permute-start.7) | collective-permute-done | bytes 65568 | tf_op jit(solution)/shard_map/ppermute | solution.py:22
  38.0 1.6 %collective-permute-start.10 = (bf16[8,2048]{1,0:T(8,128)(2,1)S(1)}, bf16[8,2048]{1,0:T(8,128)(2,1)S(1)}, u32[]{:S(2)}, u32[]{:S(2)}) collective-permute-start(bf16[8,2048]{1,0:T(8,128)(2,1)S(1)} %add_convert_fusion.p_ref), channel_id=1, source_target_pairs={{0,6},{1,7},{2,4},{3,5},{4,2},{5,3},{6,0},{7,1},{8,14},{9,15},{10,... | collective-permute-start | bytes 98312 | tf_op jit(solution)/shard_map/ppermute | solution.py:22
  39.7 3.2 %collective-permute-start.9 = (bf16[8,2048]{1,0:T(8,128)(2,1)S(1)}, bf16[8,2048]{1,0:T(8,128)(2,1)S(1)}, u32[]{:S(2)}, u32[]{:S(2)}) collective-permute-start(bf16[8,2048]{1,0:T(8,128)(2,1)S(1)} %add_convert_fusion.p_ref), channel_id=1, source_target_pairs={{0,4},{1,5},{2,6},{3,7},{4,0},{5,1},{6,2},{7,3},{8,12},{9,13},{10,... | collective-permute-start | bytes 98312 | tf_op jit(solution)/shard_map/ppermute | solution.py:22
  43.6 1.5 %collective-permute-done.9.r2_ref = bf16[8,2048]{1,0:T(8,128)(2,1)S(1)} collective-permute-done((bf16[8,2048]{1,0:T(8,128)(2,1)S(1)}, bf16[8,2048]{1,0:T(8,128)(2,1)S(1)}, u32[]{:S(2)}, u32[]{:S(2)}) %collective-permute-start.9) | collective-permute-done | bytes 32800 | tf_op jit(solution)/shard_map/ppermute | solution.py:22
  45.1 0.6 %final_rows.1 = (f32[2,2048]{1,0:T(2,128)S(1)}, f32[1,2048]{1,0:T(1,128)}, f32[1,2560]{1,0:T(1,128)S(1)}) custom-call(s32[1]{0:T(128)} %bitcast.group_ref, f32[8,2048]{1,0:T(8,128)S(1)} %get-tuple-element.45.before_ref, bf16[8,2048]{1,0:T(8,128)(2,1)S(1)} %add_convert_fusion.p_ref, bf16[8,2048]{1,0:T(8,128)(2,1)S(1)} %collective-permute-done.8.r1_ref, ...), custom_call_target="tpu_custom_call" | custom-call | tf_op jit(solution)/shard_map/final_rows/pallas_call | solution.py:387
  45.7 0.5 collective-permute-start.11
  46.2 0.7 %dynamic_slice.9.length_ref = s32[1]{0:T(128)} dynamic-slice(s32[96]{0:T(128)S(1)} %copy-done.7, s32[]{:T(128)S(6)} %select_n.21), dynamic_slice_sizes={1} | dynamic-slice | bytes 12 | tf_op jit(solution)/shard_map/dynamic_slice | solution.py:402
  46.9 5.7 %collective-permute-done.11.arrived_ref = f32[1,2560]{1,0:T(1,128)S(1)} collective-permute-done((f32[1,2560]{1,0:T(1,128)S(1)}, f32[1,2560]{1,0:T(1,128)S(1)}, u32[]{:S(2)}, u32[]{:S(2)}) %collective-permute-start.11) | collective-permute-done | bytes 10272 | tf_op jit(solution)/shard_map/ppermute | solution.py:22
  52.6 2.7 %arrival.1 = (f32[3,2048]{1,0:T(4,128)}, bf16[2,2,2048,128]{3,2,1,0:T(8,128)(2,1)}) custom-call(s32[1]{0:T(128)} %dynamic_slice.9.length_ref, f32[2,2048]{1,0:T(2,128)S(1)} %get-tuple-element.50.stay_ref, f32[1,2560]{1,0:T(1,128)S(1)} %collective-permute-done.11.arrived_ref, bf16[2,2,2048,128]{3,2,1,0:T(8,128)(2,1)S(1)} %collective-permute-done.12.moving_ref), custom_call_target="tpu_custom_call" | custom-call | tf_op jit(solution)/shard_map/arrival/pallas_call | solution.py:403
  (38 shorter events, 2.5 us)
Async XLA Ops:
  0.6 5.7 %copy-start.3 = (bf16[1,2048]{1,0:T(2,128)(2,1)S(1)}, bf16[1,2048]{1,0:T(2,128)(2,1)}, u32[]{:S(2)}) copy-start(bf16[1,2048]{1,0:T(2,128)(2,1)} %own_long_ref.1) | copy-start | bytes 12292
  0.6 7.6 %copy-start.6 = (s32[32]{0:T(128)S(1)}, s32[32]{0:T(128)}, u32[]{:S(2)}) copy-start(s32[32]{0:T(128)} %long_lengths_ref.3) | copy-start | bytes 388
  0.7 7.7 %copy-start.7 = (s32[96]{0:T(128)S(1)}, s32[96]{0:T(128)}, u32[]{:S(2)}) copy-start(s32[96]{0:T(128)} %lengths_ref.3) | copy-start | bytes 1156
  0.7 7.8 %copy-start.8 = (f32[128]{0:T(128)S(1)}, f32[128]{0:T(128)}, u32[]{:S(2)}) copy-start(f32[128]{0:T(128)} %constant.43.clone) | copy-start | bytes 1540
  0.7 7.8 %copy-start.9 = (f32[128]{0:T(128)S(1)}, f32[128]{0:T(128)}, u32[]{:S(2)}) copy-start(f32[128]{0:T(128)} %constant.44.clone) | copy-start | bytes 1540
  0.7 9.3 %copy-start.1 = (f32[2,2048]{1,0:T(2,128)S(1)}, f32[2,2048]{1,0:T(2,128)}, u32[]{:S(2)}) copy-start(f32[2,2048]{1,0:T(2,128)} %rest_0_.3) | copy-start | bytes 49156
  0.7 9.3 %copy-start.2 = (bf16[3,2048]{1,0:T(4,128)(2,1)S(1)}, bf16[3,2048]{1,0:T(4,128)(2,1)}, u32[]{:S(2)}) copy-start(bf16[3,2048]{1,0:T(4,128)(2,1)} %tokens_ref.1) | copy-start | bytes 36868
  0.7 9.3 %copy-start.4 = (f32[2,128]{1,0:T(2,128)S(1)}, f32[2,128]{1,0:T(2,128)}, u32[]{:S(2)}) copy-start(f32[2,128]{1,0:T(2,128)} %rest_1_.3) | copy-start | bytes 3076
  0.7 9.3 %copy-start.5 = (f32[2,128]{1,0:T(2,128)S(1)}, f32[2,128]{1,0:T(2,128)}, u32[]{:S(2)}) copy-start(f32[2,128]{1,0:T(2,128)} %rest_2_.3) | copy-start | bytes 3076
  3.2 49.4 %collective-permute-start.12 = (bf16[2,2,2048,128]{3,2,1,0:T(8,128)(2,1)}, bf16[2,2,2048,128]{3,2,1,0:T(8,128)(2,1)S(1)}, u32[]{:S(2)}, u32[]{:S(2)}) collective-permute-start(bf16[2,2,2048,128]{3,2,1,0:T(8,128)(2,1)} %leaving_cache.1), channel_id=1, source_target_pairs={{0,128},{8,136},{16,144},{24,152},{32,160},{40,168},{48,176},{56,1... | collective-permute-start | bytes 6291464 | tf_op jit(solution)/shard_map/ppermute | solution.py:22
  6.3 3.7 %collective-permute-start = (bf16[1,2048]{1,0:T(2,128)(2,1)S(1)}, bf16[1,2048]{1,0:T(2,128)(2,1)S(1)}, u32[]{:S(2)}, u32[]{:S(2)}) collective-permute-start(bf16[1,2048]{1,0:T(2,128)(2,1)S(1)} %copy-done.3), channel_id=1, source_target_pairs={{0,8},{8,0},{16,24},{24,16},{32,40},{40,32},{48,56},{56,48},{64,72... | collective-permute-start | bytes 12296 | tf_op jit(solution)/shard_map/ppermute | solution.py:22
  10.0 8.4 %copy-start = (bf16[2,256,2048]{2,1,0:T(8,128)(2,1)S(1)}, bf16[2,256,2048]{2,1,0:T(8,128)(2,1)}, u32[]{:S(2)}) copy-start(bf16[2,256,2048]{2,1,0:T(8,128)(2,1)} %w_ref.3) | copy-start | bytes 6291460
  14.5 3.8 %collective-permute-start.1 = (f32[16,256]{1,0:T(8,128)S(1)}, f32[16,256]{1,0:T(8,128)S(1)}, u32[]{:S(2)}, u32[]{:S(2)}) collective-permute-start(f32[16,256]{1,0:T(8,128)S(1)} %get-tuple-element.30.state_ref), channel_id=1, source_target_pairs={{0,8},{8,0},{16,24},{24,16},{32,40},{40,32},{48,56},{56,48},{64,72... | collective-permute-start | bytes 49160 | tf_op jit(solution)/shard_map/ppermute | solution.py:22
  18.8 1.3 %collective-permute-start.2 = (f32[8,2048]{1,0:T(8,128)S(1)}, f32[8,2048]{1,0:T(8,128)S(1)}, u32[]{:S(2)}, u32[]{:S(2)}) collective-permute-start(f32[8,2048]{1,0:T(8,128)S(1)} %out_projection_0.1), channel_id=1, source_target_pairs={{0,1},{1,0},{2,3},{3,2},{4,5},{5,4},{6,7},{7,6},{8,9},{9,8},{10,11... | collective-permute-start | bytes 196616 | tf_op jit(solution)/shard_map/ppermute | solution.py:22
  20.2 8.1 %collective-permute-start.3 = (bf16[8,2048]{1,0:T(8,128)(2,1)S(1)}, bf16[8,2048]{1,0:T(8,128)(2,1)S(1)}, u32[]{:S(2)}, u32[]{:S(2)}) collective-permute-start(bf16[8,2048]{1,0:T(8,128)(2,1)S(1)} %add_convert_fusion.1.p_ref), channel_id=1, source_target_pairs={{0,2},{1,3},{2,0},{3,1},{4,6},{5,7},{6,4},{7,5},{8,10},{9,11},{10,... | collective-permute-start | bytes 98312 | tf_op jit(solution)/shard_map/ppermute | solution.py:22
  21.9 6.5 %collective-permute-start.4 = (bf16[8,2048]{1,0:T(8,128)(2,1)S(1)}, bf16[8,2048]{1,0:T(8,128)(2,1)S(1)}, u32[]{:S(2)}, u32[]{:S(2)}) collective-permute-start(bf16[8,2048]{1,0:T(8,128)(2,1)S(1)} %add_convert_fusion.1.p_ref), channel_id=1, source_target_pairs={{0,4},{1,5},{2,6},{3,7},{4,0},{5,1},{6,2},{7,3},{8,12},{9,13},{10,... | collective-permute-start | bytes 98312 | tf_op jit(solution)/shard_map/ppermute | solution.py:22
  24.8 5.1 %collective-permute-start.5 = (bf16[8,2048]{1,0:T(8,128)(2,1)S(1)}, bf16[8,2048]{1,0:T(8,128)(2,1)S(1)}, u32[]{:S(2)}, u32[]{:S(2)}) collective-permute-start(bf16[8,2048]{1,0:T(8,128)(2,1)S(1)} %add_convert_fusion.1.p_ref), channel_id=1, source_target_pairs={{0,6},{1,7},{2,4},{3,5},{4,2},{5,3},{6,0},{7,1},{8,14},{9,15},{10,... | collective-permute-start | bytes 98312 | tf_op jit(solution)/shard_map/ppermute | solution.py:22
  32.4 3.8 %collective-permute-start.6 = (f32[16,256]{1,0:T(8,128)S(1)}, f32[16,256]{1,0:T(8,128)S(1)}, u32[]{:S(2)}, u32[]{:S(2)}) collective-permute-start(f32[16,256]{1,0:T(8,128)S(1)} %get-tuple-element.46.state_ref), channel_id=1, source_target_pairs={{0,8},{8,0},{16,24},{24,16},{32,40},{40,32},{48,56},{56,48},{64,72... | collective-permute-start | bytes 49160 | tf_op jit(solution)/shard_map/ppermute | solution.py:22
  36.7 1.3 %collective-permute-start.7 = (f32[8,2048]{1,0:T(8,128)S(1)}, f32[8,2048]{1,0:T(8,128)S(1)}, u32[]{:S(2)}, u32[]{:S(2)}) collective-permute-start(f32[8,2048]{1,0:T(8,128)S(1)} %out_projection_1.1), channel_id=1, source_target_pairs={{0,1},{1,0},{2,3},{3,2},{4,5},{5,4},{6,7},{7,6},{8,9},{9,8},{10,11... | collective-permute-start | bytes 196616 | tf_op jit(solution)/shard_map/ppermute | solution.py:22
  38.0 5.2 %collective-permute-start.10 = (bf16[8,2048]{1,0:T(8,128)(2,1)S(1)}, bf16[8,2048]{1,0:T(8,128)(2,1)S(1)}, u32[]{:S(2)}, u32[]{:S(2)}) collective-permute-start(bf16[8,2048]{1,0:T(8,128)(2,1)S(1)} %add_convert_fusion.p_ref), channel_id=1, source_target_pairs={{0,6},{1,7},{2,4},{3,5},{4,2},{5,3},{6,0},{7,1},{8,14},{9,15},{10,... | collective-permute-start | bytes 98312 | tf_op jit(solution)/shard_map/ppermute | solution.py:22
  39.6 3.9 %collective-permute-start.8 = (bf16[8,2048]{1,0:T(8,128)(2,1)S(1)}, bf16[8,2048]{1,0:T(8,128)(2,1)S(1)}, u32[]{:S(2)}, u32[]{:S(2)}) collective-permute-start(bf16[8,2048]{1,0:T(8,128)(2,1)S(1)} %add_convert_fusion.p_ref), channel_id=1, source_target_pairs={{0,2},{1,3},{2,0},{3,1},{4,6},{5,7},{6,4},{7,5},{8,10},{9,11},{10,... | collective-permute-start | bytes 98312 | tf_op jit(solution)/shard_map/ppermute | solution.py:22
  39.7 5.4 %collective-permute-start.9 = (bf16[8,2048]{1,0:T(8,128)(2,1)S(1)}, bf16[8,2048]{1,0:T(8,128)(2,1)S(1)}, u32[]{:S(2)}, u32[]{:S(2)}) collective-permute-start(bf16[8,2048]{1,0:T(8,128)(2,1)S(1)} %add_convert_fusion.p_ref), channel_id=1, source_target_pairs={{0,4},{1,5},{2,6},{3,7},{4,0},{5,1},{6,2},{7,3},{8,12},{9,13},{10,... | collective-permute-start | bytes 98312 | tf_op jit(solution)/shard_map/ppermute | solution.py:22
  45.7 6.9 %collective-permute-start.11 = (f32[1,2560]{1,0:T(1,128)S(1)}, f32[1,2560]{1,0:T(1,128)S(1)}, u32[]{:S(2)}, u32[]{:S(2)}) collective-permute-start(f32[1,2560]{1,0:T(1,128)S(1)} %get-tuple-element.51), channel_id=1, source_target_pairs={{0,128},{8,136},{16,144},{24,152},{32,160},{40,168},{48,176},{56,1... | collective-permute-start | bytes 30728 | tf_op jit(solution)/shard_map/ppermute | solution.py:22

commit v6 on v5

--- a/solution.py
+++ b/solution.py
@@ -176,15 +176,19 @@
     )
 
 
-def leaving_kernel(cache_ref, out_ref, blocks, semaphores):
-    places = [(i, j) for i in range(2) for j in range(2)]
+PLANES = ((0, 0), (0, 1), (1, 0), (1, 1))
+FIRST = 3
+
+
+def leaving_kernel(planes, cache_ref, out_ref, blocks, semaphores):
+    pieces = [(n, i, j, pl.ds(at, 512)) for n, (i, j) in enumerate(planes) for at in range(0, 2048, 512)]
     reads = [
-        pltpu.make_async_copy(cache_ref.at[i, j, 2], blocks.at[i, j], semaphores.at[0, i, j])
-        for i, j in places
+        pltpu.make_async_copy(cache_ref.at[i, j, 2, at], blocks.at[n, at], semaphores.at[0, m])
+        for m, (n, i, j, at) in enumerate(pieces)
     ]
     writes = [
-        pltpu.make_async_copy(blocks.at[i, j], out_ref.at[i, j], semaphores.at[1, i, j])
-        for i, j in places
+        pltpu.make_async_copy(blocks.at[n, at], out_ref.at[n, at], semaphores.at[1, m])
+        for m, (n, i, j, at) in enumerate(pieces)
     ]
     for copy in reads:
         copy.start()
@@ -195,33 +199,48 @@
         copy.wait()
 
 
+def store_kernel(moving_ref, moved_ref, semaphores):
+    copies = [
+        pltpu.make_async_copy(moving_ref.at[n], moved_ref.at[i, j], semaphores.at[n])
+        for n, (i, j) in enumerate(PLANES[:FIRST])
+    ]
+    for copy in copies:
+        copy.start()
+    for copy in copies:
+        copy.wait()
+
+
 def arrival_kernel(
-    length_ref, stay_ref, arrived_ref, moving_ref, out_ref, moved_ref, rows, blocks, semaphores
-):
-    places = [(i, j) for i in range(2) for j in range(2)]
+    length_ref, stay_ref, arrived_ref, first_ref, second_ref, stored_ref, out_ref, moved_ref,
+    rows, blocks, semaphores,
+):
+    del stored_ref
     bodies = [
-        pltpu.make_async_copy(moving_ref.at[i, j], moved_ref.at[i, j], semaphores.at[2 * i + j])
-        for i, j in places
+        pltpu.make_async_copy(second_ref.at[n], moved_ref.at[i, j], semaphores.at[n])
+        for n, (i, j) in enumerate(PLANES[FIRST:])
     ]
     for copy in bodies:
         copy.start()
+    start = pl.multiple_of(length_ref[0] // 16 * 16, 16)
+    hit = row_of(16) == length_ref[0] - start
+    writes = []
+    for n, (i, j) in enumerate(PLANES):
+        fresh = arrived_ref[0:1, 2048 + 128 * n : 2176 + 128 * n]
+        plane = first_ref.at[n] if n < FIRST else second_ref.at[n - FIRST]
+        block = plane[pl.ds(start, 16), :].astype(jnp.float32)
+        blocks[n] = jnp.where(hit, fresh, block).astype(jnp.bfloat16)
+        writes.append(
+            pltpu.make_async_copy(
+                blocks.at[n], moved_ref.at[i, j, pl.ds(start, 16)], semaphores.at[4 + n]
+            )
+        )
+        if n < FIRST:
+            writes[-1].start()
     rows[0:2, :] = stay_ref[...]
     rows[2:3, :] = arrived_ref[0:1, 0:2048]
     out = pltpu.make_async_copy(rows, out_ref, semaphores.at[8])
     out.start()
-    start = pl.multiple_of(length_ref[0] // 16 * 16, 16)
-    hit = row_of(16) == length_ref[0] - start
-    for n, (i, j) in enumerate(places):
-        fresh = arrived_ref[0:1, 2048 + 128 * n : 2176 + 128 * n]
-        block = moving_ref[i, j, pl.ds(start, 16), :].astype(jnp.float32)
-        blocks[i, j] = jnp.where(hit, fresh, block).astype(jnp.bfloat16)
-    writes = [
-        pltpu.make_async_copy(
-            blocks.at[i, j], moved_ref.at[i, j, pl.ds(start, 16)], semaphores.at[4 + 2 * i + j]
-        )
-        for i, j in places
-    ]
-    for body, write in zip(bodies, writes):
+    for body, write in zip(bodies, writes[FIRST:]):
         body.wait()
         write.start()
     for write in writes:
@@ -292,19 +311,26 @@
     params = pltpu.CompilerParams(vmem_limit_bytes=16 * 2**20)
     small = pltpu.CompilerParams(vmem_limit_bytes=2 * 2**20)
     held = in_hbm(cache)
-    leaving = pl.pallas_call(
-        leaving_kernel,
-        out_shape=pltpu.HBM((2, 2, 2048, 128), jnp.bfloat16),
-        in_specs=[ANY],
-        out_specs=ANY,
-        scratch_shapes=[
-            pltpu.VMEM((2, 2, 2048, 128), jnp.bfloat16),
-            pltpu.SemaphoreType.DMA((2, 2, 2)),
-        ],
-        compiler_params=pltpu.CompilerParams(vmem_limit_bytes=4 * 2**20),
-        name="leaving_cache",
-    )(held)
-    moving = permute(leaving, "replica", lambda i: (i + groups // 2) % groups)
+
+    def leaving(planes, name):
+        count = len(planes)
+        return pl.pallas_call(
+            functools.partial(leaving_kernel, planes),
+            out_shape=pltpu.HBM((count, 2048, 128), jnp.bfloat16),
+            in_specs=[ANY],
+            out_specs=ANY,
+            scratch_shapes=[
+                pltpu.VMEM((count, 2048, 128), jnp.bfloat16),
+                pltpu.SemaphoreType.DMA((2, 4 * count)),
+            ],
+            compiler_params=pltpu.CompilerParams(vmem_limit_bytes=4 * 2**20),
+            name=name,
+        )(held)
+
+    first, second = (
+        permute(leaving(planes, name), "replica", lambda i: (i + groups // 2) % groups)
+        for planes, name in ((PLANES[:FIRST], "leaving_first"), (PLANES[FIRST:], "leaving_last"))
+    )
 
     places = jnp.concatenate(
         [
@@ -400,22 +426,33 @@
     arrived = permute(leave, "replica", lambda i: (i + groups // 2) % groups)
     partner = (group + groups // 2) % groups
     arrived_len = lax.dynamic_slice_in_dim(lengths, partner * 3 + 2, 1)
+    first, second = in_vmem(first), in_vmem(second)
+    stored = pl.pallas_call(
+        store_kernel,
+        out_shape=pltpu.HBM((2, 2, 2048, 128), jnp.bfloat16),
+        in_specs=[ANY],
+        out_specs=ANY,
+        scratch_shapes=[pltpu.SemaphoreType.DMA((FIRST,))],
+        compiler_params=small,
+        name="store_first",
+    )(first)
     out_hidden, moved = pl.pallas_call(
         arrival_kernel,
         out_shape=(
             pltpu.HBM((3, 2048), jnp.float32),
             pltpu.HBM((2, 2, 2048, 128), jnp.bfloat16),
         ),
-        in_specs=[SM, VM, VM, VM],
+        in_specs=[SM, VM, VM, VM, VM, ANY],
         out_specs=(ANY, ANY),
+        input_output_aliases={5: 1},
         scratch_shapes=[
             pltpu.VMEM((3, 2048), jnp.float32),
-            pltpu.VMEM((2, 2, 16, 128), jnp.bfloat16),
+            pltpu.VMEM((4, 16, 128), jnp.bfloat16),
             pltpu.SemaphoreType.DMA((9,)),
         ],
         compiler_params=small,
         name="arrival",
-    )(arrived_len, stay, arrived, in_vmem(moving))
+    )(arrived_len, stay, arrived, first, second, stored)
     return (out_hidden, long_out, moved[None, :, :, :, None, :])
 
 

time: 55.4 us -> 57.7 us (1.042); the launches traced: 55.3 us -> 56.9 us
  waiting for transfers between devices: 17 us -> 13.3 us
  starting transfers between devices: 19.3 us -> 22.4 us
  Pallas kernels: 17.1 us -> 19.3 us
    ppermute x13 -> x14, waiting for transfers between devices: 17 us -> 13.3 us  [permute(): return lax.ppermute(value, axis, pairs)]
    ppermute x13 -> x14, starting transfers between devices: 19.3 us -> 22.4 us  [permute(): return lax.ppermute(value, axis, pairs)]
    pallas_call x1 -> x3, Pallas kernels: 2.47 us -> 5.35 us  [the longest x2 4.19 us: leaving(): pl.pallas_call(functools.partial(leaving_kernel, planes), out_shape=pltpu...]
    pallas_call x1, Pallas kernels: 2.67 us -> 2.02 us  [local(): pl.pallas_call(arrival_kernel, out_shape=(pltpu.HBM((3, 2048), jnp.float3...]
  transfers between devices with their start and end apart: 13 -> 14, of which waited for: 10 -> 9; matrix products, arithmetic and copies ran while one was open for 2% -> 2% of each run, Pallas kernels for 22% -> 26%
where the time goes in v6:
time: 57.7 us; the launch traced here: 56.9 us
  starting transfers between devices  22.4 us (39%)
  Pallas kernels  19.3 us (33%)
  waiting for transfers between devices  13.3 us (23%)
  between operations  0.84 us (1%)
  local copies, waits for them, and re-layouts  0.78 us (1%)
    ppermute x14, starting transfers between devices, permute(): return lax.ppermute(value, axis, pairs)  22.4 us
    ppermute x14, waiting for transfers between devices, permute(): return lax.ppermute(value, axis, pairs)  13.3 us
    pallas_call x1, Pallas kernels, local(): pl.pallas_call(first_kernel, out_shape=out_shape, in_specs=[SM] * 3 + [VM...  4.51 us
    pallas_call x2, Pallas kernels, leaving(): pl.pallas_call(functools.partial(leaving_kernel, planes), out_shape=pltpu...  4.19 us
    pallas_call x1, Pallas kernels, local(): pl.pallas_call(fetch_kernel, out_shape=tuple((pltpu.VMEM(shape, jnp.bfloa...  3.35 us
    pallas_call x1, Pallas kernels, local(): pl.pallas_call(second_kernel, out_shape=out_shape, in_specs=[SM] * 3 + [V...  2.47 us
    pallas_call x1, Pallas kernels, local(): pl.pallas_call(arrival_kernel, out_shape=(pltpu.HBM((3, 2048), jnp.float3...  2.02 us
    pallas_call x1, Pallas kernels, local(): pl.pallas_call(store_kernel, out_shape=pltpu.HBM((2, 2, 2048, 128), jnp.b...  1.16 us
  transfers between devices with their start and end apart: 14, of which 9 were waited for; matrix products, arithmetic and copies ran while one was open for 2% of the time, Pallas kernels for 26%

profile of v6, /device:TPU:64, one launch (start us, length us, event | category | flops | bytes accessed | tf_op | source)
XLA Modules:
  0.0 56.9 jit_solution(17985873241894536517)
XLA Ops:
  0.7 2.4 %leaving_first.1 = bf16[3,2048,128]{2,1,0:T(8,128)(2,1)} custom-call(bf16[2,2,3,2048,128]{4,3,2,1,0:T(8,128)(2,1)} %bitcast.6), custom_call_target="tpu_custom_call" | custom-call | tf_op jit(solution)/shard_map/leaving_first/pallas_call | solution.py:317
  3.1 3.1 %collective-permute-start.12 = (bf16[3,2048,128]{2,1,0:T(8,128)(2,1)}, bf16[3,2048,128]{2,1,0:T(8,128)(2,1)S(1)}, u32[]{:S(2)}, u32[]{:S(2)}) collective-permute-start(bf16[3,2048,128]{2,1,0:T(8,128)(2,1)} %leaving_first.1), channel_id=1, source_target_pairs={{0,128},{8,136},{16,144},{24,152},{32,160},{40,168},{48,176},{56,1... | collective-permute-start | bytes 4718600 | tf_op jit(solution)/shard_map/ppermute | solution.py:22
  6.2 1.9 %collective-permute-start = (bf16[1,2048]{1,0:T(2,128)(2,1)S(1)}, bf16[1,2048]{1,0:T(2,128)(2,1)S(1)}, u32[]{:S(2)}, u32[]{:S(2)}) collective-permute-start(bf16[1,2048]{1,0:T(2,128)(2,1)S(1)} %copy-done.3), channel_id=1, source_target_pairs={{0,8},{8,0},{16,24},{24,16},{32,40},{40,32},{48,56},{56,48},{64,72... | collective-permute-start | bytes 12296 | tf_op jit(solution)/shard_map/ppermute | solution.py:22
  8.5 1.4 %collective-permute-done.far_long_ref = bf16[1,2048]{1,0:T(2,128)(2,1)S(1)} collective-permute-done((bf16[1,2048]{1,0:T(2,128)(2,1)S(1)}, bf16[1,2048]{1,0:T(2,128)(2,1)S(1)}, u32[]{:S(2)}, u32[]{:S(2)}) %collective-permute-start) | collective-permute-done | bytes 4128 | tf_op jit(solution)/shard_map/ppermute | solution.py:22
  9.9 4.5 %attention_0.1 = (f32[16,256]{1,0:T(8,128)S(1)}, f32[16,256]{1,0:T(8,128)S(1)}, f32[2,128]{1,0:T(2,128)S(1)}, f32[8,2048]{1,0:T(8,128)S(1)}) custom-call(s32[1]{0:T(128)} %bitcast.group_ref, s32[96]{0:T(128)S(1)} %copy-done.7, s32[32]{0:T(128)S(1)} %copy-done.6, bf16[3,2048]{1,0:T(4,128)(2,1)S(1)} %copy-done.2, bf16[1,2048]{1,0:T(2,128)(2,1)S(1)} %copy-done.3, ...), custom_call_target="tpu_custom_call" | custom-call | tf_op jit(solution)/shard_map/attention_0/pallas_call | solution.py:382
  14.4 2.0 %collective-permute-start.1 = (f32[16,256]{1,0:T(8,128)S(1)}, f32[16,256]{1,0:T(8,128)S(1)}, u32[]{:S(2)}, u32[]{:S(2)}) collective-permute-start(f32[16,256]{1,0:T(8,128)S(1)} %get-tuple-element.30.state_ref), channel_id=1, source_target_pairs={{0,8},{8,0},{16,24},{24,16},{32,40},{40,32},{48,56},{56,48},{64,72... | collective-permute-start | bytes 49160 | tf_op jit(solution)/shard_map/ppermute | solution.py:22
  16.4 1.8 %collective-permute-done.1.far_ref = f32[16,256]{1,0:T(8,128)S(1)} collective-permute-done((f32[16,256]{1,0:T(8,128)S(1)}, f32[16,256]{1,0:T(8,128)S(1)}, u32[]{:S(2)}, u32[]{:S(2)}) %collective-permute-start.1) | collective-permute-done | bytes 16416 | tf_op jit(solution)/shard_map/ppermute | solution.py:22
  18.8 1.2 %collective-permute-done.2 = f32[8,2048]{1,0:T(8,128)S(1)} collective-permute-done((f32[8,2048]{1,0:T(8,128)S(1)}, f32[8,2048]{1,0:T(8,128)S(1)}, u32[]{:S(2)}, u32[]{:S(2)}) %collective-permute-start.2) | collective-permute-done | bytes 65568 | tf_op jit(solution)/shard_map/ppermute | solution.py:22
  20.1 1.7 %collective-permute-start.3 = (bf16[8,2048]{1,0:T(8,128)(2,1)S(1)}, bf16[8,2048]{1,0:T(8,128)(2,1)S(1)}, u32[]{:S(2)}, u32[]{:S(2)}) collective-permute-start(bf16[8,2048]{1,0:T(8,128)(2,1)S(1)} %add_convert_fusion.1.p_ref), channel_id=1, source_target_pairs={{0,2},{1,3},{2,0},{3,1},{4,6},{5,7},{6,4},{7,5},{8,10},{9,11},{10,... | collective-permute-start | bytes 98312 | tf_op jit(solution)/shard_map/ppermute | solution.py:22
  21.8 2.9 %collective-permute-start.4 = (bf16[8,2048]{1,0:T(8,128)(2,1)S(1)}, bf16[8,2048]{1,0:T(8,128)(2,1)S(1)}, u32[]{:S(2)}, u32[]{:S(2)}) collective-permute-start(bf16[8,2048]{1,0:T(8,128)(2,1)S(1)} %add_convert_fusion.1.p_ref), channel_id=1, source_target_pairs={{0,4},{1,5},{2,6},{3,7},{4,0},{5,1},{6,2},{7,3},{8,12},{9,13},{10,... | collective-permute-start | bytes 98312 | tf_op jit(solution)/shard_map/ppermute | solution.py:22
  24.9 3.4 %fetch_1.1 = (bf16[2048,256]{1,0:T(8,128)(2,1)S(1)}, bf16[2048,128]{1,0:T(8,128)(2,1)S(1)}, bf16[2048,128]{1,0:T(8,128)(2,1)S(1)}, bf16[3,2048,128]{2,1,0:T(8,12...) custom-call(bf16[2,2,3,2048,128]{4,3,2,1,0:T(8,128)(2,1)} %bitcast.8, ...), custom_call_target="tpu_custom_call" | custom-call | tf_op jit(solution)/shard_map/fetch_1/pallas_call | solution.py:395
  28.3 1.5 %collective-permute-done.5.r3_ref = bf16[8,2048]{1,0:T(8,128)(2,1)S(1)} collective-permute-done((bf16[8,2048]{1,0:T(8,128)(2,1)S(1)}, bf16[8,2048]{1,0:T(8,128)(2,1)S(1)}, u32[]{:S(2)}, u32[]{:S(2)}) %collective-permute-start.5) | collective-permute-done | bytes 32800 | tf_op jit(solution)/shard_map/ppermute | solution.py:22
  29.8 2.5 %attention_1.1 = (f32[16,256]{1,0:T(8,128)S(1)}, f32[16,256]{1,0:T(8,128)S(1)}, f32[2,128]{1,0:T(2,128)S(1)}, f32[8,2048]{1,0:T(8,128)S(1)}) custom-call(s32[1]{0:T(128)} %bitcast.group_ref, s32[96]{0:T(128)S(1)} %copy-done.7, s32[32]{0:T(128)S(1)} %copy-done.6, f32[8,2048]{1,0:T(8,128)S(1)} %get-tuple-element.29.before_ref, ...), custom_call_target="tpu_custom_call" | custom-call | tf_op jit(solution)/shard_map/attention_1/pallas_call | solution.py:404
  32.3 2.0 %collective-permute-start.6 = (f32[16,256]{1,0:T(8,128)S(1)}, f32[16,256]{1,0:T(8,128)S(1)}, u32[]{:S(2)}, u32[]{:S(2)}) collective-permute-start(f32[16,256]{1,0:T(8,128)S(1)} %get-tuple-element.46.state_ref), channel_id=1, source_target_pairs={{0,8},{8,0},{16,24},{24,16},{32,40},{40,32},{48,56},{56,48},{64,72... | collective-permute-start | bytes 49160 | tf_op jit(solution)/shard_map/ppermute | solution.py:22
  34.3 1.8 %collective-permute-done.6.far_ref = f32[16,256]{1,0:T(8,128)S(1)} collective-permute-done((f32[16,256]{1,0:T(8,128)S(1)}, f32[16,256]{1,0:T(8,128)S(1)}, u32[]{:S(2)}, u32[]{:S(2)}) %collective-permute-start.6) | collective-permute-done | bytes 16416 | tf_op jit(solution)/shard_map/ppermute | solution.py:22
  36.7 1.8 %leaving_last.1 = bf16[1,2048,128]{2,1,0:T(8,128)(2,1)} custom-call(bf16[2,2,3,2048,128]{4,3,2,1,0:T(8,128)(2,1)} %bitcast.9), custom_call_target="tpu_custom_call" | custom-call | tf_op jit(solution)/shard_map/leaving_last/pallas_call | solution.py:317
  39.1 1.6 %collective-permute-start.10 = (bf16[8,2048]{1,0:T(8,128)(2,1)S(1)}, bf16[8,2048]{1,0:T(8,128)(2,1)S(1)}, u32[]{:S(2)}, u32[]{:S(2)}) collective-permute-start(bf16[8,2048]{1,0:T(8,128)(2,1)S(1)} %add_convert_fusion.p_ref), channel_id=1, source_target_pairs={{0,6},{1,7},{2,4},{3,5},{4,2},{5,3},{6,0},{7,1},{8,14},{9,15},{10,... | collective-permute-start | bytes 98312 | tf_op jit(solution)/shard_map/ppermute | solution.py:22
  40.7 3.2 %collective-permute-start.9 = (bf16[8,2048]{1,0:T(8,128)(2,1)S(1)}, bf16[8,2048]{1,0:T(8,128)(2,1)S(1)}, u32[]{:S(2)}, u32[]{:S(2)}) collective-permute-start(bf16[8,2048]{1,0:T(8,128)(2,1)S(1)} %add_convert_fusion.p_ref), channel_id=1, source_target_pairs={{0,4},{1,5},{2,6},{3,7},{4,0},{5,1},{6,2},{7,3},{8,12},{9,13},{10,... | collective-permute-start | bytes 98312 | tf_op jit(solution)/shard_map/ppermute | solution.py:22
  44.6 1.5 %collective-permute-done.9.r2_ref = bf16[8,2048]{1,0:T(8,128)(2,1)S(1)} collective-permute-done((bf16[8,2048]{1,0:T(8,128)(2,1)S(1)}, bf16[8,2048]{1,0:T(8,128)(2,1)S(1)}, u32[]{:S(2)}, u32[]{:S(2)}) %collective-permute-start.9) | collective-permute-done | bytes 32800 | tf_op jit(solution)/shard_map/ppermute | solution.py:22
  46.2 0.6 %final_rows.1 = (f32[2,2048]{1,0:T(2,128)S(1)}, f32[1,2048]{1,0:T(1,128)}, f32[1,2560]{1,0:T(1,128)S(1)}) custom-call(s32[1]{0:T(128)} %bitcast.group_ref, f32[8,2048]{1,0:T(8,128)S(1)} %get-tuple-element.45.before_ref, bf16[8,2048]{1,0:T(8,128)(2,1)S(1)} %add_convert_fusion.p_ref, bf16[8,2048]{1,0:T(8,128)(2,1)S(1)} %collective-permute-done.8.r1_ref, ...), custom_call_target="tpu_custom_call" | custom-call | tf_op jit(solution)/shard_map/final_rows/pallas_call | solution.py:413
  46.8 3.0 %collective-permute-start.11 = (f32[1,2560]{1,0:T(1,128)S(1)}, f32[1,2560]{1,0:T(1,128)S(1)}, u32[]{:S(2)}, u32[]{:S(2)}) collective-permute-start(f32[1,2560]{1,0:T(1,128)S(1)} %get-tuple-element.51), channel_id=1, source_target_pairs={{0,128},{8,136},{16,144},{24,152},{32,160},{40,168},{48,176},{56,1... | collective-permute-start | bytes 30728 | tf_op jit(solution)/shard_map/ppermute | solution.py:22
  50.4 1.2 %store_first.1.stored_ref = bf16[2,2,2048,128]{3,2,1,0:T(8,128)(2,1)} custom-call(bf16[3,2048,128]{2,1,0:T(8,128)(2,1)S(1)} %collective-permute-done.12.moving_ref.first_ref), custom_call_target="tpu_custom_call" | custom-call | tf_op jit(solution)/shard_map/store_first/pallas_call | solution.py:430
  51.6 3.3 %collective-permute-done.11.arrived_ref = f32[1,2560]{1,0:T(1,128)S(1)} collective-permute-done((f32[1,2560]{1,0:T(1,128)S(1)}, f32[1,2560]{1,0:T(1,128)S(1)}, u32[]{:S(2)}, u32[]{:S(2)}) %collective-permute-start.11) | collective-permute-done | bytes 10272 | tf_op jit(solution)/shard_map/ppermute | solution.py:22
  54.9 2.0 %arrival.1 = (f32[3,2048]{1,0:T(4,128)}, bf16[2,2,2048,128]{3,2,1,0:T(8,128)(2,1)}) custom-call(s32[1]{0:T(128)} %dynamic_slice.9.length_ref, f32[2,2048]{1,0:T(2,128)S(1)} %get-tuple-element.50.stay_ref, f32[1,2560]{1,0:T(1,128)S(1)} %collective-permute-done.11.arrived_ref, ...), custom_call_target="tpu_custom_call", output_to_operand_aliasing={{1}: (5, {})} | custom-call | tf_op jit(solution)/shard_map/arrival/pallas_call | solution.py:439
  (42 shorter events, 3.7 us)
Async XLA Ops:
  0.6 5.6 %copy-start.3 = (bf16[1,2048]{1,0:T(2,128)(2,1)S(1)}, bf16[1,2048]{1,0:T(2,128)(2,1)}, u32[]{:S(2)}) copy-start(bf16[1,2048]{1,0:T(2,128)(2,1)} %own_long_ref.1) | copy-start | bytes 12292
  0.6 7.5 %copy-start.6 = (s32[32]{0:T(128)S(1)}, s32[32]{0:T(128)}, u32[]{:S(2)}) copy-start(s32[32]{0:T(128)} %long_lengths_ref.3) | copy-start | bytes 388
  0.7 7.6 %copy-start.7 = (s32[96]{0:T(128)S(1)}, s32[96]{0:T(128)}, u32[]{:S(2)}) copy-start(s32[96]{0:T(128)} %lengths_ref.3) | copy-start | bytes 1156
  0.7 7.7 %copy-start.8 = (f32[128]{0:T(128)S(1)}, f32[128]{0:T(128)}, u32[]{:S(2)}) copy-start(f32[128]{0:T(128)} %constant.43.clone) | copy-start | bytes 1540
  0.7 7.7 %copy-start.9 = (f32[128]{0:T(128)S(1)}, f32[128]{0:T(128)}, u32[]{:S(2)}) copy-start(f32[128]{0:T(128)} %constant.44.clone) | copy-start | bytes 1540
  0.7 9.2 %copy-start.1 = (f32[2,2048]{1,0:T(2,128)S(1)}, f32[2,2048]{1,0:T(2,128)}, u32[]{:S(2)}) copy-start(f32[2,2048]{1,0:T(2,128)} %rest_0_.3) | copy-start | bytes 49156
  0.7 9.2 %copy-start.2 = (bf16[3,2048]{1,0:T(4,128)(2,1)S(1)}, bf16[3,2048]{1,0:T(4,128)(2,1)}, u32[]{:S(2)}) copy-start(bf16[3,2048]{1,0:T(4,128)(2,1)} %tokens_ref.1) | copy-start | bytes 36868
  0.7 9.2 %copy-start.4 = (f32[2,128]{1,0:T(2,128)S(1)}, f32[2,128]{1,0:T(2,128)}, u32[]{:S(2)}) copy-start(f32[2,128]{1,0:T(2,128)} %rest_1_.3) | copy-start | bytes 3076
  0.7 9.2 %copy-start.5 = (f32[2,128]{1,0:T(2,128)S(1)}, f32[2,128]{1,0:T(2,128)}, u32[]{:S(2)}) copy-start(f32[2,128]{1,0:T(2,128)} %rest_2_.3) | copy-start | bytes 3076
  3.1 47.3 %collective-permute-start.12 = (bf16[3,2048,128]{2,1,0:T(8,128)(2,1)}, bf16[3,2048,128]{2,1,0:T(8,128)(2,1)S(1)}, u32[]{:S(2)}, u32[]{:S(2)}) collective-permute-start(bf16[3,2048,128]{2,1,0:T(8,128)(2,1)} %leaving_first.1), channel_id=1, source_target_pairs={{0,128},{8,136},{16,144},{24,152},{32,160},{40,168},{48,176},{56,1... | collective-permute-start | bytes 4718600 | tf_op jit(solution)/shard_map/ppermute | solution.py:22
  6.2 3.7 %collective-permute-start = (bf16[1,2048]{1,0:T(2,128)(2,1)S(1)}, bf16[1,2048]{1,0:T(2,128)(2,1)S(1)}, u32[]{:S(2)}, u32[]{:S(2)}) collective-permute-start(bf16[1,2048]{1,0:T(2,128)(2,1)S(1)} %copy-done.3), channel_id=1, source_target_pairs={{0,8},{8,0},{16,24},{24,16},{32,40},{40,32},{48,56},{56,48},{64,72... | collective-permute-start | bytes 12296 | tf_op jit(solution)/shard_map/ppermute | solution.py:22
  9.9 8.4 %copy-start = (bf16[2,256,2048]{2,1,0:T(8,128)(2,1)S(1)}, bf16[2,256,2048]{2,1,0:T(8,128)(2,1)}, u32[]{:S(2)}) copy-start(bf16[2,256,2048]{2,1,0:T(8,128)(2,1)} %w_ref.3) | copy-start | bytes 6291460
  14.4 3.8 %collective-permute-start.1 = (f32[16,256]{1,0:T(8,128)S(1)}, f32[16,256]{1,0:T(8,128)S(1)}, u32[]{:S(2)}, u32[]{:S(2)}) collective-permute-start(f32[16,256]{1,0:T(8,128)S(1)} %get-tuple-element.30.state_ref), channel_id=1, source_target_pairs={{0,8},{8,0},{16,24},{24,16},{32,40},{40,32},{48,56},{56,48},{64,72... | collective-permute-start | bytes 49160 | tf_op jit(solution)/shard_map/ppermute | solution.py:22
  18.7 1.3 %collective-permute-start.2 = (f32[8,2048]{1,0:T(8,128)S(1)}, f32[8,2048]{1,0:T(8,128)S(1)}, u32[]{:S(2)}, u32[]{:S(2)}) collective-permute-start(f32[8,2048]{1,0:T(8,128)S(1)} %out_projection_0.1), channel_id=1, source_target_pairs={{0,1},{1,0},{2,3},{3,2},{4,5},{5,4},{6,7},{7,6},{8,9},{9,8},{10,11... | collective-permute-start | bytes 196616 | tf_op jit(solution)/shard_map/ppermute | solution.py:22
  20.1 8.1 %collective-permute-start.3 = (bf16[8,2048]{1,0:T(8,128)(2,1)S(1)}, bf16[8,2048]{1,0:T(8,128)(2,1)S(1)}, u32[]{:S(2)}, u32[]{:S(2)}) collective-permute-start(bf16[8,2048]{1,0:T(8,128)(2,1)S(1)} %add_convert_fusion.1.p_ref), channel_id=1, source_target_pairs={{0,2},{1,3},{2,0},{3,1},{4,6},{5,7},{6,4},{7,5},{8,10},{9,11},{10,... | collective-permute-start | bytes 98312 | tf_op jit(solution)/shard_map/ppermute | solution.py:22
  21.8 6.5 %collective-permute-start.4 = (bf16[8,2048]{1,0:T(8,128)(2,1)S(1)}, bf16[8,2048]{1,0:T(8,128)(2,1)S(1)}, u32[]{:S(2)}, u32[]{:S(2)}) collective-permute-start(bf16[8,2048]{1,0:T(8,128)(2,1)S(1)} %add_convert_fusion.1.p_ref), channel_id=1, source_target_pairs={{0,4},{1,5},{2,6},{3,7},{4,0},{5,1},{6,2},{7,3},{8,12},{9,13},{10,... | collective-permute-start | bytes 98312 | tf_op jit(solution)/shard_map/ppermute | solution.py:22
  24.7 5.1 %collective-permute-start.5 = (bf16[8,2048]{1,0:T(8,128)(2,1)S(1)}, bf16[8,2048]{1,0:T(8,128)(2,1)S(1)}, u32[]{:S(2)}, u32[]{:S(2)}) collective-permute-start(bf16[8,2048]{1,0:T(8,128)(2,1)S(1)} %add_convert_fusion.1.p_ref), channel_id=1, source_target_pairs={{0,6},{1,7},{2,4},{3,5},{4,2},{5,3},{6,0},{7,1},{8,14},{9,15},{10,... | collective-permute-start | bytes 98312 | tf_op jit(solution)/shard_map/ppermute | solution.py:22
  32.3 3.8 %collective-permute-start.6 = (f32[16,256]{1,0:T(8,128)S(1)}, f32[16,256]{1,0:T(8,128)S(1)}, u32[]{:S(2)}, u32[]{:S(2)}) collective-permute-start(f32[16,256]{1,0:T(8,128)S(1)} %get-tuple-element.46.state_ref), channel_id=1, source_target_pairs={{0,8},{8,0},{16,24},{24,16},{32,40},{40,32},{48,56},{56,48},{64,72... | collective-permute-start | bytes 49160 | tf_op jit(solution)/shard_map/ppermute | solution.py:22
  36.6 2.5 %collective-permute-start.7 = (f32[8,2048]{1,0:T(8,128)S(1)}, f32[8,2048]{1,0:T(8,128)S(1)}, u32[]{:S(2)}, u32[]{:S(2)}) collective-permute-start(f32[8,2048]{1,0:T(8,128)S(1)} %out_projection_1.1), channel_id=1, source_target_pairs={{0,1},{1,0},{2,3},{3,2},{4,5},{5,4},{6,7},{7,6},{8,9},{9,8},{10,11... | collective-permute-start | bytes 196616 | tf_op jit(solution)/shard_map/ppermute | solution.py:22
  38.5 16.3 %collective-permute-start.13 = (bf16[1,2048,128]{2,1,0:T(8,128)(2,1)}, bf16[1,2048,128]{2,1,0:T(8,128)(2,1)S(1)}, u32[]{:S(2)}, u32[]{:S(2)}) collective-permute-start(bf16[1,2048,128]{2,1,0:T(8,128)(2,1)} %leaving_last.1), channel_id=1, source_target_pairs={{0,128},{8,136},{16,144},{24,152},{32,160},{40,168},{48,176},{56,1... | collective-permute-start | bytes 1572872 | tf_op jit(solution)/shard_map/ppermute | solution.py:22
  39.1 5.2 %collective-permute-start.10 = (bf16[8,2048]{1,0:T(8,128)(2,1)S(1)}, bf16[8,2048]{1,0:T(8,128)(2,1)S(1)}, u32[]{:S(2)}, u32[]{:S(2)}) collective-permute-start(bf16[8,2048]{1,0:T(8,128)(2,1)S(1)} %add_convert_fusion.p_ref), channel_id=1, source_target_pairs={{0,6},{1,7},{2,4},{3,5},{4,2},{5,3},{6,0},{7,1},{8,14},{9,15},{10,... | collective-permute-start | bytes 98312 | tf_op jit(solution)/shard_map/ppermute | solution.py:22
  40.7 3.9 %collective-permute-start.8 = (bf16[8,2048]{1,0:T(8,128)(2,1)S(1)}, bf16[8,2048]{1,0:T(8,128)(2,1)S(1)}, u32[]{:S(2)}, u32[]{:S(2)}) collective-permute-start(bf16[8,2048]{1,0:T(8,128)(2,1)S(1)} %add_convert_fusion.p_ref), channel_id=1, source_target_pairs={{0,2},{1,3},{2,0},{3,1},{4,6},{5,7},{6,4},{7,5},{8,10},{9,11},{10,... | collective-permute-start | bytes 98312 | tf_op jit(solution)/shard_map/ppermute | solution.py:22
  40.7 5.4 %collective-permute-start.9 = (bf16[8,2048]{1,0:T(8,128)(2,1)S(1)}, bf16[8,2048]{1,0:T(8,128)(2,1)S(1)}, u32[]{:S(2)}, u32[]{:S(2)}) collective-permute-start(bf16[8,2048]{1,0:T(8,128)(2,1)S(1)} %add_convert_fusion.p_ref), channel_id=1, source_target_pairs={{0,4},{1,5},{2,6},{3,7},{4,0},{5,1},{6,2},{7,3},{8,12},{9,13},{10,... | collective-permute-start | bytes 98312 | tf_op jit(solution)/shard_map/ppermute | solution.py:22
  46.8 8.1 %collective-permute-start.11 = (f32[1,2560]{1,0:T(1,128)S(1)}, f32[1,2560]{1,0:T(1,128)S(1)}, u32[]{:S(2)}, u32[]{:S(2)}) collective-permute-start(f32[1,2560]{1,0:T(1,128)S(1)} %get-tuple-element.51), channel_id=1, source_target_pairs={{0,128},{8,136},{16,144},{24,152},{32,160},{40,168},{48,176},{56,1... | collective-permute-start | bytes 30728 | tf_op jit(solution)/shard_map/ppermute | solution.py:22

commit v7 on v3

--- a/solution.py
+++ b/solution.py
@@ -176,49 +176,127 @@
     )
 
 
-def leaving_kernel(cache_ref, out_ref, semaphores):
-    copies = [
-        pltpu.make_async_copy(cache_ref.at[i, j, 2], out_ref.at[i, j], semaphores.at[2 * i + j])
-        for i in range(2)
-        for j in range(2)
-    ]
+UNIT = 256
+FIRST = 23
+PER = 2048 // UNIT
+SECOND = 4 * PER - FIRST
+
+
+def plane_of(unit):
+    return unit // (2 * PER), unit // PER % 2, pl.ds(unit % PER * UNIT, UNIT)
+
+
+def runs(begin, end):
+    out, at = [], begin
+    while at < end:
+        stop = min(end, at // PER * PER + PER)
+        i, j, _ = plane_of(at)
+        out.append((i, j, at % PER * UNIT, (stop - at) * UNIT, (at - begin) * UNIT))
+        at = stop
+    return out
+
+
+def leaving_kernel(begin, end, cache_ref, out_ref, unused_ref, semaphores):
+    del unused_ref
+    copies = []
+    for n, (i, j, place, size, at) in enumerate(runs(begin, end)):
+        copies.append(
+            pltpu.make_async_copy(
+                cache_ref.at[i, j, 2, pl.ds(place, size)], out_ref.at[pl.ds(at, size)],
+                semaphores.at[n],
+            )
+        )
     for copy in copies:
         copy.start()
     for copy in copies:
         copy.wait()
 
 
+def store_kernel(length_ref, first_ref, stored_ref, blocks_ref, buffer, semaphores):
+    reads, writes = [], []
+    for n in range(FIRST):
+        i, j, rows = plane_of(n)
+        piece = pl.ds(n * UNIT, UNIT)
+        reads.append(
+            pltpu.make_async_copy(first_ref.at[piece], buffer.at[piece], semaphores.at[0, n])
+        )
+        writes.append(
+            pltpu.make_async_copy(buffer.at[piece], stored_ref.at[i, j, rows], semaphores.at[1, n])
+        )
+    for copy in reads:
+        copy.start()
+    for read, write in zip(reads, writes):
+        read.wait()
+        write.start()
+    start = length_ref[0] // 16 * 16
+    for plane in range(4):
+        at = jnp.minimum(plane * 2048 + start, FIRST * UNIT - 16)
+        blocks_ref[plane] = buffer[pl.ds(pl.multiple_of(at, 16), 16), :]
+    for copy in writes:
+        copy.wait()
+
+
 def arrival_kernel(
-    length_ref, stay_ref, arrived_ref, moving_ref, out_ref, moved_ref, rows, blocks, semaphores
+    length_ref, stay_ref, arrived_ref, blocks_ref, second_ref, stored_ref, out_ref, moved_ref,
+    rows, blocks, patched, semaphores,
 ):
-    places = [(i, j) for i in range(2) for j in range(2)]
-    bodies = [
-        pltpu.make_async_copy(moving_ref.at[i, j], moved_ref.at[i, j], semaphores.at[2 * i + j])
-        for i, j in places
-    ]
-    for copy in bodies:
-        copy.start()
+    del stored_ref
+    length = length_ref[0]
+    hit_unit = length // UNIT
+    units = [(unit, *plane_of(unit)) for unit in range(FIRST, 4 * PER)]
+
+    def straight(unit, i, j, place):
+        return pltpu.make_async_copy(
+            second_ref.at[pl.ds((unit - FIRST) * UNIT, UNIT)], moved_ref.at[i, j, place],
+            semaphores.at[unit - FIRST],
+        )
+
+    def changed(unit, i, j, place):
+        return pltpu.make_async_copy(
+            patched.at[unit // PER], moved_ref.at[i, j, place], semaphores.at[unit - FIRST]
+        )
+
+    for unit in units:
+
+        @pl.when(hit_unit != unit[0] % PER)
+        def _():
+            straight(*unit).start()
+
+    fresh = [arrived_ref[0:1, 2048 + 128 * n : 2176 + 128 * n] for n in range(4)]
+    start = pl.multiple_of(length // 16 * 16, 16)
+    early = []
+    for plane in range((FIRST + PER - 1) // PER):
+        block = blocks_ref[plane].astype(jnp.float32)
+        blocks[plane] = jnp.where(row_of(16) == length - start, fresh[plane], block).astype(
+            jnp.bfloat16
+        )
+        write = pltpu.make_async_copy(
+            blocks.at[plane], moved_ref.at[plane // 2, plane % 2, pl.ds(start, 16)],
+            semaphores.at[SECOND + plane],
+        )
+        early.append((plane * PER + hit_unit < FIRST, write))
+    for inside, write in early:
+        pl.when(inside)(write.start)
+    for plane in range(FIRST // PER, 4):
+        at = jnp.maximum(plane * PER + hit_unit - FIRST, 0) * UNIT
+        whole = second_ref[pl.ds(pl.multiple_of(at, UNIT), UNIT), :].astype(jnp.float32)
+        patched[plane] = jnp.where(
+            row_of(UNIT) == length - hit_unit * UNIT, fresh[plane], whole
+        ).astype(jnp.bfloat16)
+    for unit in units:
+
+        @pl.when(hit_unit == unit[0] % PER)
+        def _():
+            changed(*unit).start()
+
     rows[0:2, :] = stay_ref[...]
     rows[2:3, :] = arrived_ref[0:1, 0:2048]
-    out = pltpu.make_async_copy(rows, out_ref, semaphores.at[8])
+    out = pltpu.make_async_copy(rows, out_ref, semaphores.at[SECOND + 4])
     out.start()
-    start = pl.multiple_of(length_ref[0] // 16 * 16, 16)
-    hit = row_of(16) == length_ref[0] - start
-    for n, (i, j) in enumerate(places):
-        fresh = arrived_ref[0:1, 2048 + 128 * n : 2176 + 128 * n]
-        block = moving_ref[i, j, pl.ds(start, 16), :].astype(jnp.float32)
-        blocks[i, j] = jnp.where(hit, fresh, block).astype(jnp.bfloat16)
-    writes = [
-        pltpu.make_async_copy(
-            blocks.at[i, j], moved_ref.at[i, j, pl.ds(start, 16)], semaphores.at[4 + 2 * i + j]
-        )
-        for i, j in places
-    ]
-    for body, write in zip(bodies, writes):
-        body.wait()
-        write.start()
-    for write in writes:
-        write.wait()
+    for unit in units:
+        straight(*unit).wait()
+    for inside, write in early:
+        pl.when(inside)(write.wait)
     out.wait()
 
 
@@ -281,20 +359,30 @@
     cache = cache.reshape(2, 2, 3, 2048, 128)
     long_cache = long_cache.reshape(2, 2, 1, 2, 2048, 128)
 
-    far_token = permute(long_tokens, "replica", lambda i: i ^ 1)
     params = pltpu.CompilerParams(vmem_limit_bytes=16 * 2**20)
     small = pltpu.CompilerParams(vmem_limit_bytes=2 * 2**20)
     held = in_hbm(cache)
-    leaving = pl.pallas_call(
-        leaving_kernel,
-        out_shape=pltpu.VMEM((2, 2, 2048, 128), jnp.bfloat16),
-        in_specs=[ANY],
-        out_specs=ANY,
-        scratch_shapes=[pltpu.SemaphoreType.DMA((4,))],
-        compiler_params=small,
-        name="leaving_cache",
-    )(held)
-    moving = permute(leaving, "replica", lambda i: (i + groups // 2) % groups)
+
+    def leaving(begin, count, name):
+        return pl.pallas_call(
+            functools.partial(leaving_kernel, begin, begin + count),
+            out_shape=(
+                pltpu.VMEM((count * UNIT, 128), jnp.bfloat16),
+                pltpu.VMEM((8, 128), jnp.float32),
+            ),
+            in_specs=[ANY],
+            out_specs=(ANY, ANY),
+            scratch_shapes=[pltpu.SemaphoreType.DMA((4,))],
+            compiler_params=small,
+            name=name,
+        )(held)
+
+    first, _ = leaving(0, FIRST, "leaving_first")
+    second, _ = leaving(FIRST, SECOND, "leaving_second")
+    first, second = (
+        permute(piece, "replica", lambda i: (i + groups // 2) % groups) for piece in (first, second)
+    )
+    far_token = permute(long_tokens, "replica", lambda i: i ^ 1)
 
     places = jnp.concatenate(
         [
@@ -390,22 +478,39 @@
     arrived = permute(leave, "replica", lambda i: (i + groups // 2) % groups)
     partner = (group + groups // 2) % groups
     arrived_len = lax.dynamic_slice_in_dim(lengths, partner * 3 + 2, 1)
+    stored, blocks = pl.pallas_call(
+        store_kernel,
+        out_shape=(
+            pltpu.HBM((2, 2, 2048, 128), jnp.bfloat16),
+            pltpu.VMEM((4, 16, 128), jnp.bfloat16),
+        ),
+        in_specs=[SM, ANY],
+        out_specs=(ANY, VM),
+        scratch_shapes=[
+            pltpu.VMEM((FIRST * UNIT, 128), jnp.bfloat16),
+            pltpu.SemaphoreType.DMA((2, FIRST)),
+        ],
+        compiler_params=pltpu.CompilerParams(vmem_limit_bytes=4 * 2**20),
+        name="store_first",
+    )(arrived_len, in_hbm(first))
     out_hidden, moved = pl.pallas_call(
         arrival_kernel,
         out_shape=(
             pltpu.HBM((3, 2048), jnp.float32),
             pltpu.HBM((2, 2, 2048, 128), jnp.bfloat16),
         ),
-        in_specs=[SM, VM, VM, VM],
+        in_specs=[SM, VM, VM, VM, VM, ANY],
         out_specs=(ANY, ANY),
+        input_output_aliases={5: 1},
         scratch_shapes=[
             pltpu.VMEM((3, 2048), jnp.float32),
-            pltpu.VMEM((2, 2, 16, 128), jnp.bfloat16),
-            pltpu.SemaphoreType.DMA((9,)),
+            pltpu.VMEM((4, 16, 128), jnp.bfloat16),
+            pltpu.VMEM((4, UNIT, 128), jnp.bfloat16),
+            pltpu.SemaphoreType.DMA((SECOND + 5,)),
         ],
         compiler_params=small,
         name="arrival",
-    )(arrived_len, stay, arrived, in_vmem(moving))
+    )(arrived_len, stay, arrived, blocks, in_vmem(second), stored)
     return (out_hidden, long_out, moved[None, :, :, :, None, :])
 
 

time: 118 us -> 55.1 us (0.47)
  Pallas kernels: 79.3 us -> 19 us
  waiting for transfers between devices: 17 us -> 11.3 us
  starting transfers between devices: 19.3 us -> 22.4 us
    pallas_call x1 -> x3, Pallas kernels: 64.7 us -> 5.5 us  [the longest x1 2.97 us: local(): pl.pallas_call(store_kernel, out_shape=(pltpu.HBM((2, 2, 2048, 128), jnp....]
    ppermute x13 -> x14, waiting for transfers between devices: 17 us -> 11.3 us  [permute(): return lax.ppermute(value, axis, pairs)]
    ppermute x13 -> x14, starting transfers between devices: 19.3 us -> 22.4 us  [permute(): return lax.ppermute(value, axis, pairs)]
  transfers between devices with their start and end apart: 13 -> 14, of which waited for: 10 -> 8; matrix products, arithmetic and copies ran while one was open for 1% -> 2% of each run, Pallas kernels for 10% -> 29%
where the time goes in v7:
time: 55.1 us; the launch traced here: 54.4 us
  starting transfers between devices  22.4 us (41%)
  Pallas kernels  19 us (34%)
  waiting for transfers between devices  11.3 us (21%)
  between operations  0.86 us (2%)
  local copies, waits for them, and re-layouts  0.75 us (1%)
    ppermute x14, starting transfers between devices, permute(): return lax.ppermute(value, axis, pairs)  22.4 us
    ppermute x14, waiting for transfers between devices, permute(): return lax.ppermute(value, axis, pairs)  11.3 us
    pallas_call x1, Pallas kernels, local(): pl.pallas_call(first_kernel, out_shape=out_shape, in_specs=[SM] * 3 + [VM...  4.51 us
    pallas_call x1, Pallas kernels, local(): pl.pallas_call(fetch_kernel, out_shape=tuple((pltpu.VMEM(shape, jnp.bfloa...  3.35 us
    pallas_call x1, Pallas kernels, local(): pl.pallas_call(store_kernel, out_shape=(pltpu.HBM((2, 2, 2048, 128), jnp....  2.97 us
    pallas_call x2, Pallas kernels, leaving(): pl.pallas_call(functools.partial(leaving_kernel, begin, begin + count), o...  2.53 us
    pallas_call x1, Pallas kernels, local(): pl.pallas_call(second_kernel, out_shape=out_shape, in_specs=[SM] * 3 + [V...  2.49 us
    pallas_call x1, Pallas kernels, local(): pl.pallas_call(arrival_kernel, out_shape=(pltpu.HBM((3, 2048), jnp.float3...  1.5 us
  transfers between devices with their start and end apart: 14, of which 8 were waited for; matrix products, arithmetic and copies ran while one was open for 2% of the time, Pallas kernels for 29%

profile of v7, /device:TPU:64, one launch (start us, length us, event | category | flops | bytes accessed | tf_op | source)
XLA Modules:
  0.0 54.4 jit_solution(2765071472818973922)
XLA Ops:
  0.7 1.4 %leaving_first.1 = (bf16[5888,128]{1,0:T(8,128)(2,1)S(1)}, f32[8,128]{1,0:T(8,128)}) custom-call(bf16[2,2,3,2048,128]{4,3,2,1,0:T(8,128)(2,1)} %bitcast.6), custom_call_target="tpu_custom_call" | custom-call | tf_op jit(solution)/shard_map/leaving_first/pallas_call | solution.py:367
  2.2 3.1 %collective-permute-start.12 = (bf16[5888,128]{1,0:T(8,128)(2,1)S(1)}, bf16[5888,128]{1,0:T(8,128)(2,1)}, u32[]{:S(2)}, u32[]{:S(2)}) collective-permute-start(bf16[5888,128]{1,0:T(8,128)(2,1)S(1)} %get-tuple-element.56), channel_id=1, source_target_pairs={{0,128},{8,136},{16,144},{24,152},{32,160},{40,168},{48,176},{56,1... | collective-permute-start | bytes 4521992 | tf_op jit(solution)/shard_map/ppermute | solution.py:22
  5.3 1.9 %collective-permute-start = (bf16[1,2048]{1,0:T(2,128)(2,1)S(1)}, bf16[1,2048]{1,0:T(2,128)(2,1)S(1)}, u32[]{:S(2)}, u32[]{:S(2)}) collective-permute-start(bf16[1,2048]{1,0:T(2,128)(2,1)S(1)} %copy-done.3), channel_id=1, source_target_pairs={{0,8},{8,0},{16,24},{24,16},{32,40},{40,32},{48,56},{56,48},{64,72... | collective-permute-start | bytes 12296 | tf_op jit(solution)/shard_map/ppermute | solution.py:22
  7.5 1.4 %collective-permute-done.far_long_ref = bf16[1,2048]{1,0:T(2,128)(2,1)S(1)} collective-permute-done((bf16[1,2048]{1,0:T(2,128)(2,1)S(1)}, bf16[1,2048]{1,0:T(2,128)(2,1)S(1)}, u32[]{:S(2)}, u32[]{:S(2)}) %collective-permute-start) | collective-permute-done | bytes 4128 | tf_op jit(solution)/shard_map/ppermute | solution.py:22
  8.9 4.5 %attention_0.1 = (f32[16,256]{1,0:T(8,128)S(1)}, f32[16,256]{1,0:T(8,128)S(1)}, f32[2,128]{1,0:T(2,128)S(1)}, f32[8,2048]{1,0:T(8,128)S(1)}) custom-call(s32[1]{0:T(128)} %bitcast.group_ref, s32[96]{0:T(128)S(1)} %copy-done.7, s32[32]{0:T(128)S(1)} %copy-done.6, bf16[3,2048]{1,0:T(4,128)(2,1)S(1)} %copy-done.2, bf16[1,2048]{1,0:T(2,128)(2,1)S(1)} %copy-done.3, ...), custom_call_target="tpu_custom_call" | custom-call | tf_op jit(solution)/shard_map/attention_0/pallas_call | solution.py:434
  13.5 2.0 %collective-permute-start.1 = (f32[16,256]{1,0:T(8,128)S(1)}, f32[16,256]{1,0:T(8,128)S(1)}, u32[]{:S(2)}, u32[]{:S(2)}) collective-permute-start(f32[16,256]{1,0:T(8,128)S(1)} %get-tuple-element.34.state_ref), channel_id=1, source_target_pairs={{0,8},{8,0},{16,24},{24,16},{32,40},{40,32},{48,56},{56,48},{64,72... | collective-permute-start | bytes 49160 | tf_op jit(solution)/shard_map/ppermute | solution.py:22
  15.5 1.8 %collective-permute-done.1.far_ref = f32[16,256]{1,0:T(8,128)S(1)} collective-permute-done((f32[16,256]{1,0:T(8,128)S(1)}, f32[16,256]{1,0:T(8,128)S(1)}, u32[]{:S(2)}, u32[]{:S(2)}) %collective-permute-start.1) | collective-permute-done | bytes 16416 | tf_op jit(solution)/shard_map/ppermute | solution.py:22
  17.9 1.2 %collective-permute-done.2 = f32[8,2048]{1,0:T(8,128)S(1)} collective-permute-done((f32[8,2048]{1,0:T(8,128)S(1)}, f32[8,2048]{1,0:T(8,128)S(1)}, u32[]{:S(2)}, u32[]{:S(2)}) %collective-permute-start.2) | collective-permute-done | bytes 65568 | tf_op jit(solution)/shard_map/ppermute | solution.py:22
  19.1 1.7 %collective-permute-start.3 = (bf16[8,2048]{1,0:T(8,128)(2,1)S(1)}, bf16[8,2048]{1,0:T(8,128)(2,1)S(1)}, u32[]{:S(2)}, u32[]{:S(2)}) collective-permute-start(bf16[8,2048]{1,0:T(8,128)(2,1)S(1)} %add_convert_fusion.1.p_ref), channel_id=1, source_target_pairs={{0,2},{1,3},{2,0},{3,1},{4,6},{5,7},{6,4},{7,5},{8,10},{9,11},{10,... | collective-permute-start | bytes 98312 | tf_op jit(solution)/shard_map/ppermute | solution.py:22
  20.8 2.9 %collective-permute-start.4 = (bf16[8,2048]{1,0:T(8,128)(2,1)S(1)}, bf16[8,2048]{1,0:T(8,128)(2,1)S(1)}, u32[]{:S(2)}, u32[]{:S(2)}) collective-permute-start(bf16[8,2048]{1,0:T(8,128)(2,1)S(1)} %add_convert_fusion.1.p_ref), channel_id=1, source_target_pairs={{0,4},{1,5},{2,6},{3,7},{4,0},{5,1},{6,2},{7,3},{8,12},{9,13},{10,... | collective-permute-start | bytes 98312 | tf_op jit(solution)/shard_map/ppermute | solution.py:22
  23.9 1.1 %leaving_second.1 = (bf16[2304,128]{1,0:T(8,128)(2,1)S(1)}, f32[8,128]{1,0:T(8,128)}) custom-call(bf16[2,2,3,2048,128]{4,3,2,1,0:T(8,128)(2,1)} %bitcast.8), custom_call_target="tpu_custom_call" | custom-call | tf_op jit(solution)/shard_map/leaving_second/pallas_call | solution.py:367
  25.6 3.4 %fetch_1.1 = (bf16[2048,256]{1,0:T(8,128)(2,1)S(1)}, bf16[2048,128]{1,0:T(8,128)(2,1)S(1)}, bf16[2048,128]{1,0:T(8,128)(2,1)S(1)}, bf16[3,2048,128]{2,1,0:T(8,12...) custom-call(bf16[2,2,3,2048,128]{4,3,2,1,0:T(8,128)(2,1)} %bitcast.9, ...), custom_call_target="tpu_custom_call" | custom-call | tf_op jit(solution)/shard_map/fetch_1/pallas_call | solution.py:447
  29.0 2.5 %attention_1.1 = (f32[16,256]{1,0:T(8,128)S(1)}, f32[16,256]{1,0:T(8,128)S(1)}, f32[2,128]{1,0:T(2,128)S(1)}, f32[8,2048]{1,0:T(8,128)S(1)}) custom-call(s32[1]{0:T(128)} %bitcast.group_ref, s32[96]{0:T(128)S(1)} %copy-done.7, s32[32]{0:T(128)S(1)} %copy-done.6, f32[8,2048]{1,0:T(8,128)S(1)} %get-tuple-element.33.before_ref, ...), custom_call_target="tpu_custom_call" | custom-call | tf_op jit(solution)/shard_map/attention_1/pallas_call | solution.py:456
  31.5 2.0 %collective-permute-start.6 = (f32[16,256]{1,0:T(8,128)S(1)}, f32[16,256]{1,0:T(8,128)S(1)}, u32[]{:S(2)}, u32[]{:S(2)}) collective-permute-start(f32[16,256]{1,0:T(8,128)S(1)} %get-tuple-element.50.state_ref), channel_id=1, source_target_pairs={{0,8},{8,0},{16,24},{24,16},{32,40},{40,32},{48,56},{56,48},{64,72... | collective-permute-start | bytes 49160 | tf_op jit(solution)/shard_map/ppermute | solution.py:22
  33.5 1.8 %collective-permute-done.6.far_ref = f32[16,256]{1,0:T(8,128)S(1)} collective-permute-done((f32[16,256]{1,0:T(8,128)S(1)}, f32[16,256]{1,0:T(8,128)S(1)}, u32[]{:S(2)}, u32[]{:S(2)}) %collective-permute-start.6) | collective-permute-done | bytes 16416 | tf_op jit(solution)/shard_map/ppermute | solution.py:22
  36.0 1.2 %collective-permute-done.7 = f32[8,2048]{1,0:T(8,128)S(1)} collective-permute-done((f32[8,2048]{1,0:T(8,128)S(1)}, f32[8,2048]{1,0:T(8,128)S(1)}, u32[]{:S(2)}, u32[]{:S(2)}) %collective-permute-start.7) | collective-permute-done | bytes 65568 | tf_op jit(solution)/shard_map/ppermute | solution.py:22
  37.2 3.1 %collective-permute-start.10 = (bf16[8,2048]{1,0:T(8,128)(2,1)S(1)}, bf16[8,2048]{1,0:T(8,128)(2,1)S(1)}, u32[]{:S(2)}, u32[]{:S(2)}) collective-permute-start(bf16[8,2048]{1,0:T(8,128)(2,1)S(1)} %add_convert_fusion.p_ref), channel_id=1, source_target_pairs={{0,6},{1,7},{2,4},{3,5},{4,2},{5,3},{6,0},{7,1},{8,14},{9,15},{10,... | collective-permute-start | bytes 98312 | tf_op jit(solution)/shard_map/ppermute | solution.py:22
  40.3 1.7 %collective-permute-start.9 = (bf16[8,2048]{1,0:T(8,128)(2,1)S(1)}, bf16[8,2048]{1,0:T(8,128)(2,1)S(1)}, u32[]{:S(2)}, u32[]{:S(2)}) collective-permute-start(bf16[8,2048]{1,0:T(8,128)(2,1)S(1)} %add_convert_fusion.p_ref), channel_id=1, source_target_pairs={{0,4},{1,5},{2,6},{3,7},{4,0},{5,1},{6,2},{7,3},{8,12},{9,13},{10,... | collective-permute-start | bytes 98312 | tf_op jit(solution)/shard_map/ppermute | solution.py:22
  42.4 1.8 %collective-permute-done.8.r1_ref = bf16[8,2048]{1,0:T(8,128)(2,1)S(1)} collective-permute-done((bf16[8,2048]{1,0:T(8,128)(2,1)S(1)}, bf16[8,2048]{1,0:T(8,128)(2,1)S(1)}, u32[]{:S(2)}, u32[]{:S(2)}) %collective-permute-start.8) | collective-permute-done | bytes 32800 | tf_op jit(solution)/shard_map/ppermute | solution.py:22
  44.2 1.5 %collective-permute-done.9.r2_ref = bf16[8,2048]{1,0:T(8,128)(2,1)S(1)} collective-permute-done((bf16[8,2048]{1,0:T(8,128)(2,1)S(1)}, bf16[8,2048]{1,0:T(8,128)(2,1)S(1)}, u32[]{:S(2)}, u32[]{:S(2)}) %collective-permute-start.9) | collective-permute-done | bytes 32800 | tf_op jit(solution)/shard_map/ppermute | solution.py:22
  45.7 0.6 %final_rows.1 = (f32[2,2048]{1,0:T(2,128)S(1)}, f32[1,2048]{1,0:T(1,128)}, f32[1,2560]{1,0:T(1,128)S(1)}) custom-call(s32[1]{0:T(128)} %bitcast.group_ref, f32[8,2048]{1,0:T(8,128)S(1)} %get-tuple-element.49.before_ref, bf16[8,2048]{1,0:T(8,128)(2,1)S(1)} %add_convert_fusion.p_ref, bf16[8,2048]{1,0:T(8,128)(2,1)S(1)} %collective-permute-done.8.r1_ref, ...), custom_call_target="tpu_custom_call" | custom-call | tf_op jit(solution)/shard_map/final_rows/pallas_call | solution.py:465
  46.4 3.0 %collective-permute-start.11 = (f32[1,2560]{1,0:T(1,128)S(1)}, f32[1,2560]{1,0:T(1,128)S(1)}, u32[]{:S(2)}, u32[]{:S(2)}) collective-permute-start(f32[1,2560]{1,0:T(1,128)S(1)} %get-tuple-element.55), channel_id=1, source_target_pairs={{0,128},{8,136},{16,144},{24,152},{32,160},{40,168},{48,176},{56,1... | collective-permute-start | bytes 30728 | tf_op jit(solution)/shard_map/ppermute | solution.py:22
  49.9 3.0 %store_first.1 = (bf16[2,2,2048,128]{3,2,1,0:T(8,128)(2,1)}, bf16[4,16,128]{2,1,0:T(8,128)(2,1)S(1)}) custom-call(s32[1]{0:T(128)} %dynamic_slice.9.length_ref, bf16[5888,128]{1,0:T(8,128)(2,1)} %collective-permute-done.12.first_ref), custom_call_target="tpu_custom_call" | custom-call | tf_op jit(solution)/shard_map/store_first/pallas_call | solution.py:481
  52.9 1.5 %arrival.1 = (f32[3,2048]{1,0:T(4,128)}, bf16[2,2,2048,128]{3,2,1,0:T(8,128)(2,1)}) custom-call(s32[1]{0:T(128)} %dynamic_slice.9.length_ref, f32[2,2048]{1,0:T(2,128)S(1)} %get-tuple-element.54.stay_ref, f32[1,2560]{1,0:T(1,128)S(1)} %collective-permute-done.11.arrived_ref, ...), custom_call_target="tpu_custom_call", output_to_operand_aliasing={{1}: (5, {})} | custom-call | tf_op jit(solution)/shard_map/arrival/pallas_call | solution.py:496
  (42 shorter events, 3.4 us)
Async XLA Ops:
  0.6 4.6 %copy-start.3 = (bf16[1,2048]{1,0:T(2,128)(2,1)S(1)}, bf16[1,2048]{1,0:T(2,128)(2,1)}, u32[]{:S(2)}) copy-start(bf16[1,2048]{1,0:T(2,128)(2,1)} %own_long_ref.1) | copy-start | bytes 12292
  0.6 6.5 %copy-start.6 = (s32[32]{0:T(128)S(1)}, s32[32]{0:T(128)}, u32[]{:S(2)}) copy-start(s32[32]{0:T(128)} %long_lengths_ref.3) | copy-start | bytes 388
  0.7 6.6 %copy-start.7 = (s32[96]{0:T(128)S(1)}, s32[96]{0:T(128)}, u32[]{:S(2)}) copy-start(s32[96]{0:T(128)} %lengths_ref.3) | copy-start | bytes 1156
  0.7 6.8 %copy-start.8 = (f32[128]{0:T(128)S(1)}, f32[128]{0:T(128)}, u32[]{:S(2)}) copy-start(f32[128]{0:T(128)} %constant.43.clone) | copy-start | bytes 1540
  0.7 6.7 %copy-start.9 = (f32[128]{0:T(128)S(1)}, f32[128]{0:T(128)}, u32[]{:S(2)}) copy-start(f32[128]{0:T(128)} %constant.44.clone) | copy-start | bytes 1540
  0.7 8.2 %copy-start.1 = (f32[2,2048]{1,0:T(2,128)S(1)}, f32[2,2048]{1,0:T(2,128)}, u32[]{:S(2)}) copy-start(f32[2,2048]{1,0:T(2,128)} %rest_0_.3) | copy-start | bytes 49156
  0.7 8.2 %copy-start.2 = (bf16[3,2048]{1,0:T(4,128)(2,1)S(1)}, bf16[3,2048]{1,0:T(4,128)(2,1)}, u32[]{:S(2)}) copy-start(bf16[3,2048]{1,0:T(4,128)(2,1)} %tokens_ref.1) | copy-start | bytes 36868
  0.7 8.2 %copy-start.4 = (f32[2,128]{1,0:T(2,128)S(1)}, f32[2,128]{1,0:T(2,128)}, u32[]{:S(2)}) copy-start(f32[2,128]{1,0:T(2,128)} %rest_1_.3) | copy-start | bytes 3076
  0.7 8.2 %copy-start.5 = (f32[2,128]{1,0:T(2,128)S(1)}, f32[2,128]{1,0:T(2,128)}, u32[]{:S(2)}) copy-start(f32[2,128]{1,0:T(2,128)} %rest_2_.3) | copy-start | bytes 3076
  2.2 47.8 %collective-permute-start.12 = (bf16[5888,128]{1,0:T(8,128)(2,1)S(1)}, bf16[5888,128]{1,0:T(8,128)(2,1)}, u32[]{:S(2)}, u32[]{:S(2)}) collective-permute-start(bf16[5888,128]{1,0:T(8,128)(2,1)S(1)} %get-tuple-element.56), channel_id=1, source_target_pairs={{0,128},{8,136},{16,144},{24,152},{32,160},{40,168},{48,176},{56,1... | collective-permute-start | bytes 4521992 | tf_op jit(solution)/shard_map/ppermute | solution.py:22
  5.3 3.7 %collective-permute-start = (bf16[1,2048]{1,0:T(2,128)(2,1)S(1)}, bf16[1,2048]{1,0:T(2,128)(2,1)S(1)}, u32[]{:S(2)}, u32[]{:S(2)}) collective-permute-start(bf16[1,2048]{1,0:T(2,128)(2,1)S(1)} %copy-done.3), channel_id=1, source_target_pairs={{0,8},{8,0},{16,24},{24,16},{32,40},{40,32},{48,56},{56,48},{64,72... | collective-permute-start | bytes 12296 | tf_op jit(solution)/shard_map/ppermute | solution.py:22
  8.9 8.4 %copy-start = (bf16[2,256,2048]{2,1,0:T(8,128)(2,1)S(1)}, bf16[2,256,2048]{2,1,0:T(8,128)(2,1)}, u32[]{:S(2)}) copy-start(bf16[2,256,2048]{2,1,0:T(8,128)(2,1)} %w_ref.3) | copy-start | bytes 6291460
  13.5 3.8 %collective-permute-start.1 = (f32[16,256]{1,0:T(8,128)S(1)}, f32[16,256]{1,0:T(8,128)S(1)}, u32[]{:S(2)}, u32[]{:S(2)}) collective-permute-start(f32[16,256]{1,0:T(8,128)S(1)} %get-tuple-element.34.state_ref), channel_id=1, source_target_pairs={{0,8},{8,0},{16,24},{24,16},{32,40},{40,32},{48,56},{56,48},{64,72... | collective-permute-start | bytes 49160 | tf_op jit(solution)/shard_map/ppermute | solution.py:22
  17.8 1.3 %collective-permute-start.2 = (f32[8,2048]{1,0:T(8,128)S(1)}, f32[8,2048]{1,0:T(8,128)S(1)}, u32[]{:S(2)}, u32[]{:S(2)}) collective-permute-start(f32[8,2048]{1,0:T(8,128)S(1)} %out_projection_0.1), channel_id=1, source_target_pairs={{0,1},{1,0},{2,3},{3,2},{4,5},{5,4},{6,7},{7,6},{8,9},{9,8},{10,11... | collective-permute-start | bytes 196616 | tf_op jit(solution)/shard_map/ppermute | solution.py:22
  19.1 9.9 %collective-permute-start.3 = (bf16[8,2048]{1,0:T(8,128)(2,1)S(1)}, bf16[8,2048]{1,0:T(8,128)(2,1)S(1)}, u32[]{:S(2)}, u32[]{:S(2)}) collective-permute-start(bf16[8,2048]{1,0:T(8,128)(2,1)S(1)} %add_convert_fusion.1.p_ref), channel_id=1, source_target_pairs={{0,2},{1,3},{2,0},{3,1},{4,6},{5,7},{6,4},{7,5},{8,10},{9,11},{10,... | collective-permute-start | bytes 98312 | tf_op jit(solution)/shard_map/ppermute | solution.py:22
  20.8 8.2 %collective-permute-start.4 = (bf16[8,2048]{1,0:T(8,128)(2,1)S(1)}, bf16[8,2048]{1,0:T(8,128)(2,1)S(1)}, u32[]{:S(2)}, u32[]{:S(2)}) collective-permute-start(bf16[8,2048]{1,0:T(8,128)(2,1)S(1)} %add_convert_fusion.1.p_ref), channel_id=1, source_target_pairs={{0,4},{1,5},{2,6},{3,7},{4,0},{5,1},{6,2},{7,3},{8,12},{9,13},{10,... | collective-permute-start | bytes 98312 | tf_op jit(solution)/shard_map/ppermute | solution.py:22
  23.7 5.3 %collective-permute-start.5 = (bf16[8,2048]{1,0:T(8,128)(2,1)S(1)}, bf16[8,2048]{1,0:T(8,128)(2,1)S(1)}, u32[]{:S(2)}, u32[]{:S(2)}) collective-permute-start(bf16[8,2048]{1,0:T(8,128)(2,1)S(1)} %add_convert_fusion.1.p_ref), channel_id=1, source_target_pairs={{0,6},{1,7},{2,4},{3,5},{4,2},{5,3},{6,0},{7,1},{8,14},{9,15},{10,... | collective-permute-start | bytes 98312 | tf_op jit(solution)/shard_map/ppermute | solution.py:22
  25.1 27.9 %collective-permute-start.13 = (bf16[2304,128]{1,0:T(8,128)(2,1)S(1)}, bf16[2304,128]{1,0:T(8,128)(2,1)S(1)}, u32[]{:S(2)}, u32[]{:S(2)}) collective-permute-start(bf16[2304,128]{1,0:T(8,128)(2,1)S(1)} %get-tuple-element.58), channel_id=1, source_target_pairs={{0,128},{8,136},{16,144},{24,152},{32,160},{40,168},{48,176},{56,1... | collective-permute-start | bytes 1769480 | tf_op jit(solution)/shard_map/ppermute | solution.py:22
  31.5 3.8 %collective-permute-start.6 = (f32[16,256]{1,0:T(8,128)S(1)}, f32[16,256]{1,0:T(8,128)S(1)}, u32[]{:S(2)}, u32[]{:S(2)}) collective-permute-start(f32[16,256]{1,0:T(8,128)S(1)} %get-tuple-element.50.state_ref), channel_id=1, source_target_pairs={{0,8},{8,0},{16,24},{24,16},{32,40},{40,32},{48,56},{56,48},{64,72... | collective-permute-start | bytes 49160 | tf_op jit(solution)/shard_map/ppermute | solution.py:22
  35.9 1.3 %collective-permute-start.7 = (f32[8,2048]{1,0:T(8,128)S(1)}, f32[8,2048]{1,0:T(8,128)S(1)}, u32[]{:S(2)}, u32[]{:S(2)}) collective-permute-start(f32[8,2048]{1,0:T(8,128)S(1)} %out_projection_1.1), channel_id=1, source_target_pairs={{0,1},{1,0},{2,3},{3,2},{4,5},{5,4},{6,7},{7,6},{8,9},{9,8},{10,11... | collective-permute-start | bytes 196616 | tf_op jit(solution)/shard_map/ppermute | solution.py:22
  37.2 5.2 %collective-permute-start.10 = (bf16[8,2048]{1,0:T(8,128)(2,1)S(1)}, bf16[8,2048]{1,0:T(8,128)(2,1)S(1)}, u32[]{:S(2)}, u32[]{:S(2)}) collective-permute-start(bf16[8,2048]{1,0:T(8,128)(2,1)S(1)} %add_convert_fusion.p_ref), channel_id=1, source_target_pairs={{0,6},{1,7},{2,4},{3,5},{4,2},{5,3},{6,0},{7,1},{8,14},{9,15},{10,... | collective-permute-start | bytes 98312 | tf_op jit(solution)/shard_map/ppermute | solution.py:22
  40.3 3.9 %collective-permute-start.8 = (bf16[8,2048]{1,0:T(8,128)(2,1)S(1)}, bf16[8,2048]{1,0:T(8,128)(2,1)S(1)}, u32[]{:S(2)}, u32[]{:S(2)}) collective-permute-start(bf16[8,2048]{1,0:T(8,128)(2,1)S(1)} %add_convert_fusion.p_ref), channel_id=1, source_target_pairs={{0,2},{1,3},{2,0},{3,1},{4,6},{5,7},{6,4},{7,5},{8,10},{9,11},{10,... | collective-permute-start | bytes 98312 | tf_op jit(solution)/shard_map/ppermute | solution.py:22
  40.3 5.4 %collective-permute-start.9 = (bf16[8,2048]{1,0:T(8,128)(2,1)S(1)}, bf16[8,2048]{1,0:T(8,128)(2,1)S(1)}, u32[]{:S(2)}, u32[]{:S(2)}) collective-permute-start(bf16[8,2048]{1,0:T(8,128)(2,1)S(1)} %add_convert_fusion.p_ref), channel_id=1, source_target_pairs={{0,4},{1,5},{2,6},{3,7},{4,0},{5,1},{6,2},{7,3},{8,12},{9,13},{10,... | collective-permute-start | bytes 98312 | tf_op jit(solution)/shard_map/ppermute | solution.py:22
  46.4 6.6 %collective-permute-start.11 = (f32[1,2560]{1,0:T(1,128)S(1)}, f32[1,2560]{1,0:T(1,128)S(1)}, u32[]{:S(2)}, u32[]{:S(2)}) collective-permute-start(f32[1,2560]{1,0:T(1,128)S(1)} %get-tuple-element.55), channel_id=1, source_target_pairs={{0,128},{8,136},{16,144},{24,152},{32,160},{40,168},{48,176},{56,1... | collective-permute-start | bytes 30728 | tf_op jit(solution)/shard_map/ppermute | solution.py:22

commit v8 on v7

--- a/solution.py
+++ b/solution.py
@@ -123,19 +123,21 @@
 def first_kernel(
     group_ref, lengths_ref, long_lengths_ref, tokens_ref, own_long_ref, far_long_ref, *rest
 ):
-    tables, held = rest[:5], rest[5:10]
-    state_ref, side_ref, fresh_ref, hidden_ref = rest[10:14]
-    buffers, semaphores = rest[14:21], rest[21]
+    tables, resident, held = rest[:5], rest[5:10], rest[10:12]
+    state_ref, side_ref, fresh_ref, hidden_ref = rest[12:16]
+    buffers, semaphores = rest[16:18], rest[18]
+    sources = (held[0].at[0, 1], held[1].at[0, 1, 0])
     copies = [
         pltpu.make_async_copy(source, target, semaphores.at[i])
-        for i, (source, target) in enumerate(zip(parts_of(0, *held), buffers))
+        for i, (source, target) in enumerate(zip(sources, buffers))
     ]
     for copy in copies:
         copy.start()
 
     def ready(*which):
         for i in which:
-            copies[i].wait()
+            if i >= 5:
+                copies[i - 5].wait()
 
     def hidden():
         own = own_long_ref[...].astype(jnp.float32)
@@ -148,7 +150,7 @@
         return hidden_ref[...]
 
     attention_step(
-        0, group_ref, lengths_ref, long_lengths_ref, hidden, *tables, buffers,
+        0, group_ref, lengths_ref, long_lengths_ref, hidden, *tables, (*resident, *buffers),
         state_ref, side_ref, fresh_ref, ready,
     )
 
@@ -212,7 +214,8 @@
         copy.wait()
 
 
-def store_kernel(length_ref, first_ref, stored_ref, blocks_ref, buffer, semaphores):
+def store_kernel(length_ref, first_ref, after_ref, stored_ref, blocks_ref, buffer, semaphores):
+    del after_ref
     reads, writes = [], []
     for n in range(FIRST):
         i, j, rows = plane_of(n)
@@ -300,11 +303,12 @@
     out.wait()
 
 
-def fetch_kernel(*refs):
-    held, outputs, semaphores = refs[:5], refs[5:12], refs[12]
+def fetch_kernel(layer, which, *refs):
+    held, outputs, semaphores = refs[:5], refs[6 : 6 + len(which)], refs[-1]
+    sources = parts_of(layer, *held)
     copies = [
-        pltpu.make_async_copy(source, target, semaphores.at[i])
-        for i, (source, target) in enumerate(zip(parts_of(1, *held), outputs))
+        pltpu.make_async_copy(sources[i], output, semaphores.at[n])
+        for n, (i, output) in enumerate(zip(which, outputs))
     ]
     for copy in copies:
         copy.start()
@@ -312,7 +316,8 @@
         copy.wait()
 
 
-def out_kernel(layer, state_ref, far_ref, side_ref, w_ref, out_ref, w, semaphore):
+def out_kernel(layer, state_ref, far_ref, side_ref, w_ref, after_ref, out_ref, w, semaphore):
+    del after_ref
     copy = pltpu.make_async_copy(w_ref.at[layer], w, semaphore)
     copy.start()
     is_main = lax.rem(row_of(16), 8) < 3
@@ -335,9 +340,10 @@
 
 
 def final_kernel(
-    group_ref, before_ref, p_ref, r1_ref, r2_ref, r3_ref, fresh0_ref, fresh1_ref,
+    group_ref, before_ref, p_ref, r1_ref, r2_ref, r3_ref, fresh0_ref, fresh1_ref, after_ref,
     stay_ref, long_ref, leave_ref, scratch,
 ):
+    del after_ref
     scratch[...] = before_ref[...] + total_of(p_ref, r1_ref, r2_ref, r3_ref)
     stay_ref[...] = scratch[0:2, :]
     odd = lax.rem(group_ref[0], 2) == 1
@@ -377,10 +383,11 @@
             name=name,
         )(held)
 
-    first, _ = leaving(0, FIRST, "leaving_first")
-    second, _ = leaving(FIRST, SECOND, "leaving_second")
+    leaving_first, _ = leaving(0, FIRST, "leaving_first")
+    leaving_second, _ = leaving(FIRST, SECOND, "leaving_second")
     first, second = (
-        permute(piece, "replica", lambda i: (i + groups // 2) % groups) for piece in (first, second)
+        permute(piece, "replica", lambda i: (i + groups // 2) % groups)
+        for piece in (leaving_first, leaving_second)
     )
     far_token = permute(long_tokens, "replica", lambda i: i ^ 1)
 
@@ -403,56 +410,56 @@
         jax.ShapeDtypeStruct((2, 128), jnp.float32),
         jax.ShapeDtypeStruct((ROWS, 2048), jnp.float32),
     )
-    scratch = [
-        pltpu.VMEM((2048, 256), jnp.bfloat16),
-        pltpu.VMEM((2048, 128), jnp.bfloat16),
-        pltpu.VMEM((2048, 128), jnp.bfloat16),
-        pltpu.VMEM((3, 2048, 128), jnp.bfloat16),
-        pltpu.VMEM((2, 2048, 128), jnp.bfloat16),
-        pltpu.VMEM((3, 2048, 128), jnp.bfloat16),
-        pltpu.VMEM((2, 2048, 128), jnp.bfloat16),
-        pltpu.SemaphoreType.DMA((7,)),
-    ]
     stored = (cache, long_cache, w_query, key_weight, value_weight)
     tables = (norm_gain, q_gain, k_gain, cosine, sine)
 
-    def project_out(layer, state, side):
+    def project_out(layer, state, side, after):
         far = permute(state, "replica", lambda i: i ^ 1)
         part = pl.pallas_call(
             functools.partial(out_kernel, layer),
             out_shape=jax.ShapeDtypeStruct((ROWS, 2048), jnp.float32),
-            in_specs=[VM, VM, VM, ANY],
+            in_specs=[VM, VM, VM, ANY, ANY],
             out_specs=VM,
             scratch_shapes=[pltpu.VMEM((256, 2048), jnp.bfloat16), pltpu.SemaphoreType.DMA(())],
             compiler_params=params,
             name=f"out_projection_{layer}",
-        )(state, far, side, w_out)
+        )(state, far, side, w_out, after)
         part = (part + permute(part, "tensor", lambda i: i ^ 1)).astype(jnp.bfloat16)
         received = [permute(part, "tensor", lambda i, k=k: i ^ k) for k in (2, 4, 6)]
         return (part, *received)
 
+    buffers = ((2048, 256), (2048, 128), (2048, 128)) + ((3, 2048, 128), (2, 2048, 128)) * 2
+
+    def fetch(layer, which, after, name):
+        return pl.pallas_call(
+            functools.partial(fetch_kernel, layer, which),
+            out_shape=tuple(pltpu.VMEM(buffers[i], jnp.bfloat16) for i in which),
+            in_specs=[ANY] * 6,
+            out_specs=(ANY,) * len(which),
+            scratch_shapes=[pltpu.SemaphoreType.DMA((len(which),))],
+            compiler_params=small,
+            name=name,
+        )(*map(in_hbm, stored), after)
+
     state, side, fresh_0, hidden = pl.pallas_call(
         first_kernel,
         out_shape=out_shape,
-        in_specs=[SM] * 3 + [VM] * 8 + [ANY] * 5,
+        in_specs=[SM] * 3 + [VM] * 13 + [ANY] * 2,
         out_specs=(VM,) * 4,
-        scratch_shapes=scratch,
+        scratch_shapes=[
+            pltpu.VMEM((3, 2048, 128), jnp.bfloat16),
+            pltpu.VMEM((2, 2048, 128), jnp.bfloat16),
+            pltpu.SemaphoreType.DMA((2,)),
+        ],
         compiler_params=params,
         name="attention_0",
-    )(group_1, lengths, long_lengths, tokens, long_tokens, far_token, *tables, *map(in_hbm, stored))
-    terms = project_out(0, state, side)
-    buffers = ((2048, 256), (2048, 128), (2048, 128)) + ((3, 2048, 128), (2, 2048, 128)) * 2
-    gate, *stored = lax.optimization_barrier((terms[0], *stored))
-    terms = (gate, *terms[1:])
-    stored = pl.pallas_call(
-        fetch_kernel,
-        out_shape=tuple(pltpu.VMEM(shape, jnp.bfloat16) for shape in buffers),
-        in_specs=[ANY] * 5,
-        out_specs=(ANY,) * 7,
-        scratch_shapes=[pltpu.SemaphoreType.DMA((7,))],
-        compiler_params=small,
-        name="fetch_1",
-    )(*map(in_hbm, stored))
+    )(
+        group_1, lengths, long_lengths, tokens, long_tokens, far_token, *tables,
+        *fetch(0, (0, 1, 2, 3, 4), leaving_first, "fetch_0"), in_hbm(cache), in_hbm(long_cache),
+    )
+    resident = fetch(1, (0, 1, 2, 3, 4), state, "fetch_1_keys")
+    terms = project_out(0, state, side, resident[1])
+    resident = (*resident, *fetch(1, (5, 6), terms[0], "fetch_1_values"))
     state, side, fresh_1, hidden = pl.pallas_call(
         second_kernel,
         out_shape=out_shape,
@@ -460,8 +467,25 @@
         out_specs=(VM,) * 4,
         compiler_params=params,
         name="attention_1",
-    )(group_1, lengths, long_lengths, hidden, *terms, *tables, *stored)
-    terms = project_out(1, state, side)
+    )(group_1, lengths, long_lengths, hidden, *terms, *tables, *resident)
+    terms = project_out(1, state, side, side)
+    partner = (group + groups // 2) % groups
+    arrived_len = lax.dynamic_slice_in_dim(lengths, partner * 3 + 2, 1)
+    stored_first, blocks = pl.pallas_call(
+        store_kernel,
+        out_shape=(
+            pltpu.HBM((2, 2, 2048, 128), jnp.bfloat16),
+            pltpu.VMEM((4, 16, 128), jnp.bfloat16),
+        ),
+        in_specs=[SM, ANY, ANY],
+        out_specs=(ANY, VM),
+        scratch_shapes=[
+            pltpu.VMEM((FIRST * UNIT, 128), jnp.bfloat16),
+            pltpu.SemaphoreType.DMA((2, FIRST)),
+        ],
+        compiler_params=pltpu.CompilerParams(vmem_limit_bytes=4 * 2**20),
+        name="store_first",
+    )(arrived_len, in_hbm(first), terms[0])
     stay, long_out, leave = pl.pallas_call(
         final_kernel,
         out_shape=(
@@ -469,30 +493,13 @@
             jax.ShapeDtypeStruct((1, 2048), jnp.float32),
             jax.ShapeDtypeStruct((1, 2560), jnp.float32),
         ),
-        in_specs=[SM] + [VM] * 7,
+        in_specs=[SM] + [VM] * 7 + [ANY],
         out_specs=(VM,) * 3,
         scratch_shapes=[pltpu.VMEM((ROWS, 2048), jnp.float32)],
         compiler_params=params,
         name="final_rows",
-    )(group_1, hidden, *terms, fresh_0, fresh_1)
+    )(group_1, hidden, *terms, fresh_0, fresh_1, blocks)
     arrived = permute(leave, "replica", lambda i: (i + groups // 2) % groups)
-    partner = (group + groups // 2) % groups
-    arrived_len = lax.dynamic_slice_in_dim(lengths, partner * 3 + 2, 1)
-    stored, blocks = pl.pallas_call(
-        store_kernel,
-        out_shape=(
-            pltpu.HBM((2, 2, 2048, 128), jnp.bfloat16),
-            pltpu.VMEM((4, 16, 128), jnp.bfloat16),
-        ),
-        in_specs=[SM, ANY],
-        out_specs=(ANY, VM),
-        scratch_shapes=[
-            pltpu.VMEM((FIRST * UNIT, 128), jnp.bfloat16),
-            pltpu.SemaphoreType.DMA((2, FIRST)),
-        ],
-        compiler_params=pltpu.CompilerParams(vmem_limit_bytes=4 * 2**20),
-        name="store_first",
-    )(arrived_len, in_hbm(first))
     out_hidden, moved = pl.pallas_call(
         arrival_kernel,
         out_shape=(
@@ -510,7 +517,7 @@
         ],
         compiler_params=small,
         name="arrival",
-    )(arrived_len, stay, arrived, blocks, in_vmem(second), stored)
+    )(arrived_len, stay, arrived, blocks, in_vmem(second), stored_first)
     return (out_hidden, long_out, moved[None, :, :, :, None, :])
 
 

time: 55.1 us -> 53.1 us (0.964)
  starting transfers between devices: 22.4 us -> 18.9 us
  Pallas kernels: 19 us -> 20.8 us
    ppermute x14, starting transfers between devices: 22.4 us -> 18.9 us  [permute(): return lax.ppermute(value, axis, pairs)]
    pallas_call x1 -> x3, Pallas kernels: 3.35 us -> 6.54 us  [fetch(): pl.pallas_call(functools.partial(fetch_kernel, layer, which), out_shape=t...]
    pallas_call x1, Pallas kernels: 4.51 us -> 3.16 us  [local(): pl.pallas_call(first_kernel, out_shape=out_shape, in_specs=[SM] * 3 + [VM...]
  transfers between devices with their start and end apart: 14 -> 14, of which waited for: 8 -> 7; matrix products, arithmetic and copies ran while one was open for 2% -> 2% of each run, Pallas kernels for 29% -> 34%
where the time goes in v8:
time: 53.1 us; the launch traced here: 52.8 us
  Pallas kernels  20.8 us (39%)
  starting transfers between devices  18.9 us (36%)
  waiting for transfers between devices  11.2 us (21%)
  between operations  0.91 us (2%)
  local copies, waits for them, and re-layouts  0.78 us (1%)
    ppermute x14, starting transfers between devices, permute(): return lax.ppermute(value, axis, pairs)  18.9 us
    ppermute x14, waiting for transfers between devices, permute(): return lax.ppermute(value, axis, pairs)  11.2 us
    pallas_call x3, Pallas kernels, fetch(): pl.pallas_call(functools.partial(fetch_kernel, layer, which), out_shape=t...  6.54 us
    pallas_call x1, Pallas kernels, local(): pl.pallas_call(first_kernel, out_shape=out_shape, in_specs=[SM] * 3 + [VM...  3.16 us
    pallas_call x1, Pallas kernels, local(): pl.pallas_call(store_kernel, out_shape=(pltpu.HBM((2, 2, 2048, 128), jnp....  2.99 us
    pallas_call x2, Pallas kernels, leaving(): pl.pallas_call(functools.partial(leaving_kernel, begin, begin + count), o...  2.51 us
    pallas_call x1, Pallas kernels, local(): pl.pallas_call(second_kernel, out_shape=out_shape, in_specs=[SM] * 3 + [V...  2.47 us
    pallas_call x1, Pallas kernels, local(): pl.pallas_call(arrival_kernel, out_shape=(pltpu.HBM((3, 2048), jnp.float3...  1.52 us
  transfers between devices with their start and end apart: 14, of which 7 were waited for; matrix products, arithmetic and copies ran while one was open for 2% of the time, Pallas kernels for 34%

profile of v8, /device:TPU:64, one launch (start us, length us, event | category | flops | bytes accessed | tf_op | source)
XLA Modules:
  0.0 52.8 jit_solution(1822649141163119)
XLA Ops:
  0.7 1.4 %leaving_first.1 = (bf16[5888,128]{1,0:T(8,128)(2,1)S(1)}, f32[8,128]{1,0:T(8,128)}) custom-call(bf16[2,2,3,2048,128]{4,3,2,1,0:T(8,128)(2,1)} %bitcast.6), custom_call_target="tpu_custom_call" | custom-call | tf_op jit(solution)/shard_map/leaving_first/pallas_call | solution.py:373
  2.1 3.1 %collective-permute-start.11 = (bf16[5888,128]{1,0:T(8,128)(2,1)S(1)}, bf16[5888,128]{1,0:T(8,128)(2,1)}, u32[]{:S(2)}, u32[]{:S(2)}) collective-permute-start(bf16[5888,128]{1,0:T(8,128)(2,1)S(1)} %get-tuple-element.32.refs_5_), channel_id=1, source_target_pairs={{0,128},{8,136},{16,144},{24,152},{32,160},{40,168},{48,176},{56,1... | collective-permute-start | bytes 4521992 | tf_op jit(solution)/shard_map/ppermute | solution.py:22
  5.2 1.9 %collective-permute-start = (bf16[1,2048]{1,0:T(2,128)(2,1)S(1)}, bf16[1,2048]{1,0:T(2,128)(2,1)S(1)}, u32[]{:S(2)}, u32[]{:S(2)}) collective-permute-start(bf16[1,2048]{1,0:T(2,128)(2,1)S(1)} %copy-done.3), channel_id=1, source_target_pairs={{0,8},{8,0},{16,24},{24,16},{32,40},{40,32},{48,56},{56,48},{64,72... | collective-permute-start | bytes 12296 | tf_op jit(solution)/shard_map/ppermute | solution.py:22
  7.5 2.4 %fetch_0.1 = (bf16[2048,256]{1,0:T(8,128)(2,1)S(1)}, bf16[2048,128]{1,0:T(8,128)(2,1)S(1)}, bf16[2048,128]{1,0:T(8,128)(2,1)S(1)}, bf16[3,2048,128]{2,1,0:T(8,128)(2,1)S(1)}, bf16[2,2048,128]{2,1,0:T(8,128)(2,1)S(1)}) custom-call(bf16[2,2,3,2048,128]{4,3,2,1,0:T(8,128)(2,1)} %bitcast.7, bf16[2,2,1,2,2048,128]{5,4,3,2,1,0:T(8,128)(2,1)} %bitcast.12, ...), custom_call_target="tpu_custom_call" | custom-call | tf_op jit(solution)/shard_map/fetch_0/pallas_call | solution.py:434
  10.0 3.2 %attention_0.1 = (f32[16,256]{1,0:T(8,128)S(1)}, f32[16,256]{1,0:T(8,128)S(1)}, f32[2,128]{1,0:T(2,128)S(1)}, f32[8,2048]{1,0:T(8,128)S(1)}) custom-call(s32[1]{0:T(128)} %bitcast.group_ref, s32[96]{0:T(128)S(1)} %copy-done.7, s32[32]{0:T(128)S(1)} %copy-done.6, bf16[3,2048]{1,0:T(4,128)(2,1)S(1)} %copy-done.2, bf16[1,2048]{1,0:T(2,128)(2,1)S(1)} %copy-done.3, ...), custom_call_target="tpu_custom_call" | custom-call | tf_op jit(solution)/shard_map/attention_0/pallas_call | solution.py:444
  13.1 0.9 %collective-permute-start.1 = (f32[16,256]{1,0:T(8,128)S(1)}, f32[16,256]{1,0:T(8,128)S(1)}, u32[]{:S(2)}, u32[]{:S(2)}) collective-permute-start(f32[16,256]{1,0:T(8,128)S(1)} %get-tuple-element.39.refs_5_.state_ref), channel_id=1, source_target_pairs={{0,8},{8,0},{16,24},{24,16},{32,40},{40,32},{48,56},{56,48},{64,72... | collective-permute-start | bytes 49160 | tf_op jit(solution)/shard_map/ppermute | solution.py:22
  14.1 2.4 %fetch_1_keys.1 = (bf16[2048,256]{1,0:T(8,128)(2,1)S(1)}, bf16[2048,128]{1,0:T(8,128)(2,1)S(1)}, bf16[2048,128]{1,0:T(8,128)(2,1)S(1)}, bf16[3,2048,128]{2,1,0:T(8,128)(2,1)S(1)}, bf16[2,2048,128]{2,1,0:T(8,128)(2,1)S(1)}) custom-call(bf16[2,2,3,2048,128]{4,3,2,1,0:T(8,128)(2,1)} %bitcast.9, bf16[2,2,1,2,2048,128]{5,4,3,2,1,0:T(8,128)(2,1)} %bitcast.14, ...), custom_call_target="tpu_custom_call" | custom-call | tf_op jit(solution)/shard_map/fetch_1_keys/pallas_call | solution.py:434
  17.6 1.2 %collective-permute-done.2 = f32[8,2048]{1,0:T(8,128)S(1)} collective-permute-done((f32[8,2048]{1,0:T(8,128)S(1)}, f32[8,2048]{1,0:T(8,128)S(1)}, u32[]{:S(2)}, u32[]{:S(2)}) %collective-permute-start.2) | collective-permute-done | bytes 65568 | tf_op jit(solution)/shard_map/ppermute | solution.py:22
  18.8 1.7 %collective-permute-start.3 = (bf16[8,2048]{1,0:T(8,128)(2,1)S(1)}, bf16[8,2048]{1,0:T(8,128)(2,1)S(1)}, u32[]{:S(2)}, u32[]{:S(2)}) collective-permute-start(bf16[8,2048]{1,0:T(8,128)(2,1)S(1)} %add_convert_fusion.1.refs_5_.p_ref), channel_id=1, source_target_pairs={{0,2},{1,3},{2,0},{3,1},{4,6},{5,7},{6,4},{7,5},{8,10},{9,11},{10,... | collective-permute-start | bytes 98312 | tf_op jit(solution)/shard_map/ppermute | solution.py:22
  20.5 2.9 %collective-permute-start.4 = (bf16[8,2048]{1,0:T(8,128)(2,1)S(1)}, bf16[8,2048]{1,0:T(8,128)(2,1)S(1)}, u32[]{:S(2)}, u32[]{:S(2)}) collective-permute-start(bf16[8,2048]{1,0:T(8,128)(2,1)S(1)} %add_convert_fusion.1.refs_5_.p_ref), channel_id=1, source_target_pairs={{0,4},{1,5},{2,6},{3,7},{4,0},{5,1},{6,2},{7,3},{8,12},{9,13},{10,... | collective-permute-start | bytes 98312 | tf_op jit(solution)/shard_map/ppermute | solution.py:22
  23.6 1.1 %leaving_second.1 = (bf16[2304,128]{1,0:T(8,128)(2,1)S(1)}, f32[8,128]{1,0:T(8,128)}) custom-call(bf16[2,2,3,2048,128]{4,3,2,1,0:T(8,128)(2,1)} %bitcast.10), custom_call_target="tpu_custom_call" | custom-call | tf_op jit(solution)/shard_map/leaving_second/pallas_call | solution.py:373
  25.3 1.7 %fetch_1_values.1 = (bf16[3,2048,128]{2,1,0:T(8,128)(2,1)S(1)}, bf16[2,2048,128]{2,1,0:T(8,128)(2,1)S(1)}) custom-call(bf16[2,2,3,2048,128]{4,3,2,1,0:T(8,128)(2,1)} %bitcast.11, bf16[2,2,1,2,2048,128]{5,4,3,2,1,0:T(8,128)(2,1)} %bitcast.15, bf16[2,2048,256]{2,1,0:T(8,128)(2,1)} %refs_2_.5, bf16[2,2048,128]{2,1,0:T(8,128)(2,1)} %refs_3_.5, ...), custom_call_target="tpu_custom_call" | custom-call | tf_op jit(solution)/shard_map/fetch_1_values/pallas_call | solution.py:434
  27.1 1.4 %collective-permute-done.5.r3_ref = bf16[8,2048]{1,0:T(8,128)(2,1)S(1)} collective-permute-done((bf16[8,2048]{1,0:T(8,128)(2,1)S(1)}, bf16[8,2048]{1,0:T(8,128)(2,1)S(1)}, u32[]{:S(2)}, u32[]{:S(2)}) %collective-permute-start.5) | collective-permute-done | bytes 32800 | tf_op jit(solution)/shard_map/ppermute | solution.py:22
  28.5 2.5 %attention_1.1 = (f32[16,256]{1,0:T(8,128)S(1)}, f32[16,256]{1,0:T(8,128)S(1)}, f32[2,128]{1,0:T(2,128)S(1)}, f32[8,2048]{1,0:T(8,128)S(1)}) custom-call(s32[1]{0:T(128)} %bitcast.group_ref, s32[96]{0:T(128)S(1)} %copy-done.7, s32[32]{0:T(128)S(1)} %copy-done.6, f32[8,2048]{1,0:T(8,128)S(1)} %get-tuple-element.38.before_ref, ...), custom_call_target="tpu_custom_call" | custom-call | tf_op jit(solution)/shard_map/attention_1/pallas_call | solution.py:463
  31.0 0.9 %collective-permute-start.6 = (f32[16,256]{1,0:T(8,128)S(1)}, f32[16,256]{1,0:T(8,128)S(1)}, u32[]{:S(2)}, u32[]{:S(2)}) collective-permute-start(f32[16,256]{1,0:T(8,128)S(1)} %get-tuple-element.49.state_ref), channel_id=1, source_target_pairs={{0,8},{8,0},{16,24},{24,16},{32,40},{40,32},{48,56},{56,48},{64,72... | collective-permute-start | bytes 49160 | tf_op jit(solution)/shard_map/ppermute | solution.py:22
  31.9 2.9 %collective-permute-done.6.far_ref = f32[16,256]{1,0:T(8,128)S(1)} collective-permute-done((f32[16,256]{1,0:T(8,128)S(1)}, f32[16,256]{1,0:T(8,128)S(1)}, u32[]{:S(2)}, u32[]{:S(2)}) %collective-permute-start.6) | collective-permute-done | bytes 16416 | tf_op jit(solution)/shard_map/ppermute | solution.py:22
  35.4 1.2 %collective-permute-done.7 = f32[8,2048]{1,0:T(8,128)S(1)} collective-permute-done((f32[8,2048]{1,0:T(8,128)S(1)}, f32[8,2048]{1,0:T(8,128)S(1)}, u32[]{:S(2)}, u32[]{:S(2)}) %collective-permute-start.7) | collective-permute-done | bytes 65568 | tf_op jit(solution)/shard_map/ppermute | solution.py:22
  36.7 1.7 %collective-permute-start.10 = (bf16[8,2048]{1,0:T(8,128)(2,1)S(1)}, bf16[8,2048]{1,0:T(8,128)(2,1)S(1)}, u32[]{:S(2)}, u32[]{:S(2)}) collective-permute-start(bf16[8,2048]{1,0:T(8,128)(2,1)S(1)} %add_convert_fusion.after_ref.p_ref), channel_id=1, source_target_pairs={{0,6},{1,7},{2,4},{3,5},{4,2},{5,3},{6,0},{7,1},{8,14},{9,15},{10,... | collective-permute-start | bytes 98312 | tf_op jit(solution)/shard_map/ppermute | solution.py:22
  38.4 3.1 %collective-permute-start.9 = (bf16[8,2048]{1,0:T(8,128)(2,1)S(1)}, bf16[8,2048]{1,0:T(8,128)(2,1)S(1)}, u32[]{:S(2)}, u32[]{:S(2)}) collective-permute-start(bf16[8,2048]{1,0:T(8,128)(2,1)S(1)} %add_convert_fusion.after_ref.p_ref), channel_id=1, source_target_pairs={{0,4},{1,5},{2,6},{3,7},{4,0},{5,1},{6,2},{7,3},{8,12},{9,13},{10,... | collective-permute-start | bytes 98312 | tf_op jit(solution)/shard_map/ppermute | solution.py:22
  42.0 3.0 %store_first.1 = (bf16[2,2,2048,128]{3,2,1,0:T(8,128)(2,1)}, bf16[4,16,128]{2,1,0:T(8,128)(2,1)S(1)}) custom-call(s32[1]{0:T(128)} %dynamic_slice.9.length_ref, bf16[5888,128]{1,0:T(8,128)(2,1)} %collective-permute-done.11.first_ref, bf16[8,2048]{1,0:T(8,128)(2,1)S(1)} %add_convert_fusion.after_ref.p_ref), custom_call_target="tpu_custom_call" | custom-call | tf_op jit(solution)/shard_map/store_first/pallas_call | solution.py:474
  45.1 0.6 %final_rows.1 = (f32[2,2048]{1,0:T(2,128)S(1)}, f32[1,2048]{1,0:T(1,128)}, f32[1,2560]{1,0:T(1,128)S(1)}) custom-call(s32[1]{0:T(128)} %bitcast.group_ref, f32[8,2048]{1,0:T(8,128)S(1)} %get-tuple-element.48.before_ref, bf16[8,2048]{1,0:T(8,128)(2,1)S(1)} %add_convert_fusion.after_ref.p_ref, bf16[8,2048]{1,0:T(8,128)(2,1)S(1)} %collective-permute-done.8.r1_ref, ...), custom_call_target="tpu_custom_call" | custom-call | tf_op jit(solution)/shard_map/final_rows/pallas_call | solution.py:489
  45.7 1.7 %collective-permute-start.12 = (f32[1,2560]{1,0:T(1,128)S(1)}, f32[1,2560]{1,0:T(1,128)S(1)}, u32[]{:S(2)}, u32[]{:S(2)}) collective-permute-start(f32[1,2560]{1,0:T(1,128)S(1)} %get-tuple-element.55), channel_id=1, source_target_pairs={{0,128},{8,136},{16,144},{24,152},{32,160},{40,168},{48,176},{56,1... | collective-permute-start | bytes 30728 | tf_op jit(solution)/shard_map/ppermute | solution.py:22
  47.4 3.7 %collective-permute-done.13.second_ref = bf16[2304,128]{1,0:T(8,128)(2,1)S(1)} collective-permute-done((bf16[2304,128]{1,0:T(8,128)(2,1)S(1)}, bf16[2304,128]{1,0:T(8,128)(2,1)S(1)}, u32[]{:S(2)}, u32[]{:S(2)}) %collective-permute-start.13) | collective-permute-done | bytes 589856 | tf_op jit(solution)/shard_map/ppermute | solution.py:22
  51.3 1.5 %arrival.1 = (f32[3,2048]{1,0:T(4,128)}, bf16[2,2,2048,128]{3,2,1,0:T(8,128)(2,1)}) custom-call(s32[1]{0:T(128)} %dynamic_slice.9.length_ref, f32[2,2048]{1,0:T(2,128)S(1)} %get-tuple-element.54.stay_ref, f32[1,2560]{1,0:T(1,128)S(1)} %collective-permute-done.12.arrived_ref, ...), custom_call_target="tpu_custom_call", output_to_operand_aliasing={{1}: (5, {})} | custom-call | tf_op jit(solution)/shard_map/arrival/pallas_call | solution.py:503
  (44 shorter events, 3.6 us)
Async XLA Ops:
  0.6 4.6 %copy-start.3 = (bf16[1,2048]{1,0:T(2,128)(2,1)S(1)}, bf16[1,2048]{1,0:T(2,128)(2,1)}, u32[]{:S(2)}) copy-start(bf16[1,2048]{1,0:T(2,128)(2,1)} %own_long_ref.1) | copy-start | bytes 12292
  0.6 6.5 %copy-start.6 = (s32[32]{0:T(128)S(1)}, s32[32]{0:T(128)}, u32[]{:S(2)}) copy-start(s32[32]{0:T(128)} %long_lengths_ref.3) | copy-start | bytes 388
  0.7 6.5 %copy-start.7 = (s32[96]{0:T(128)S(1)}, s32[96]{0:T(128)}, u32[]{:S(2)}) copy-start(s32[96]{0:T(128)} %lengths_ref.3) | copy-start | bytes 1156
  0.7 6.7 %copy-start.8 = (f32[128]{0:T(128)S(1)}, f32[128]{0:T(128)}, u32[]{:S(2)}) copy-start(f32[128]{0:T(128)} %constant.43.clone) | copy-start | bytes 1540
  0.7 6.7 %copy-start.9 = (f32[128]{0:T(128)S(1)}, f32[128]{0:T(128)}, u32[]{:S(2)}) copy-start(f32[128]{0:T(128)} %constant.44.clone) | copy-start | bytes 1540
  2.1 40.0 %collective-permute-start.11 = (bf16[5888,128]{1,0:T(8,128)(2,1)S(1)}, bf16[5888,128]{1,0:T(8,128)(2,1)}, u32[]{:S(2)}, u32[]{:S(2)}) collective-permute-start(bf16[5888,128]{1,0:T(8,128)(2,1)S(1)} %get-tuple-element.32.refs_5_), channel_id=1, source_target_pairs={{0,128},{8,136},{16,144},{24,152},{32,160},{40,168},{48,176},{56,1... | collective-permute-start | bytes 4521992 | tf_op jit(solution)/shard_map/ppermute | solution.py:22
  5.2 4.7 %collective-permute-start = (bf16[1,2048]{1,0:T(2,128)(2,1)S(1)}, bf16[1,2048]{1,0:T(2,128)(2,1)S(1)}, u32[]{:S(2)}, u32[]{:S(2)}) collective-permute-start(bf16[1,2048]{1,0:T(2,128)(2,1)S(1)} %copy-done.3), channel_id=1, source_target_pairs={{0,8},{8,0},{16,24},{24,16},{32,40},{40,32},{48,56},{56,48},{64,72... | collective-permute-start | bytes 12296 | tf_op jit(solution)/shard_map/ppermute | solution.py:22
  7.5 2.5 %copy-start.1 = (f32[2,2048]{1,0:T(2,128)S(1)}, f32[2,2048]{1,0:T(2,128)}, u32[]{:S(2)}) copy-start(f32[2,2048]{1,0:T(2,128)} %rest_0_.3) | copy-start | bytes 49156
  7.5 2.5 %copy-start.2 = (bf16[3,2048]{1,0:T(4,128)(2,1)S(1)}, bf16[3,2048]{1,0:T(4,128)(2,1)}, u32[]{:S(2)}) copy-start(bf16[3,2048]{1,0:T(4,128)(2,1)} %tokens_ref.1) | copy-start | bytes 36868
  7.5 2.5 %copy-start.4 = (f32[2,128]{1,0:T(2,128)S(1)}, f32[2,128]{1,0:T(2,128)}, u32[]{:S(2)}) copy-start(f32[2,128]{1,0:T(2,128)} %rest_1_.3) | copy-start | bytes 3076
  7.5 2.5 %copy-start.5 = (f32[2,128]{1,0:T(2,128)S(1)}, f32[2,128]{1,0:T(2,128)}, u32[]{:S(2)}) copy-start(f32[2,128]{1,0:T(2,128)} %rest_2_.3) | copy-start | bytes 3076
  13.1 3.8 %copy-start = (bf16[2,256,2048]{2,1,0:T(8,128)(2,1)S(1)}, bf16[2,256,2048]{2,1,0:T(8,128)(2,1)}, u32[]{:S(2)}) copy-start(bf16[2,256,2048]{2,1,0:T(8,128)(2,1)} %w_ref.3) | copy-start | bytes 6291460
  13.1 3.8 %collective-permute-start.1 = (f32[16,256]{1,0:T(8,128)S(1)}, f32[16,256]{1,0:T(8,128)S(1)}, u32[]{:S(2)}, u32[]{:S(2)}) collective-permute-start(f32[16,256]{1,0:T(8,128)S(1)} %get-tuple-element.39.refs_5_.state_ref), channel_id=1, source_target_pairs={{0,8},{8,0},{16,24},{24,16},{32,40},{40,32},{48,56},{56,48},{64,72... | collective-permute-start | bytes 49160 | tf_op jit(solution)/shard_map/ppermute | solution.py:22
  17.5 1.3 %collective-permute-start.2 = (f32[8,2048]{1,0:T(8,128)S(1)}, f32[8,2048]{1,0:T(8,128)S(1)}, u32[]{:S(2)}, u32[]{:S(2)}) collective-permute-start(f32[8,2048]{1,0:T(8,128)S(1)} %out_projection_0.1), channel_id=1, source_target_pairs={{0,1},{1,0},{2,3},{3,2},{4,5},{5,4},{6,7},{7,6},{8,9},{9,8},{10,11... | collective-permute-start | bytes 196616 | tf_op jit(solution)/shard_map/ppermute | solution.py:22
  18.8 8.2 %collective-permute-start.3 = (bf16[8,2048]{1,0:T(8,128)(2,1)S(1)}, bf16[8,2048]{1,0:T(8,128)(2,1)S(1)}, u32[]{:S(2)}, u32[]{:S(2)}) collective-permute-start(bf16[8,2048]{1,0:T(8,128)(2,1)S(1)} %add_convert_fusion.1.refs_5_.p_ref), channel_id=1, source_target_pairs={{0,2},{1,3},{2,0},{3,1},{4,6},{5,7},{6,4},{7,5},{8,10},{9,11},{10,... | collective-permute-start | bytes 98312 | tf_op jit(solution)/shard_map/ppermute | solution.py:22
  20.5 6.6 %collective-permute-start.4 = (bf16[8,2048]{1,0:T(8,128)(2,1)S(1)}, bf16[8,2048]{1,0:T(8,128)(2,1)S(1)}, u32[]{:S(2)}, u32[]{:S(2)}) collective-permute-start(bf16[8,2048]{1,0:T(8,128)(2,1)S(1)} %add_convert_fusion.1.refs_5_.p_ref), channel_id=1, source_target_pairs={{0,4},{1,5},{2,6},{3,7},{4,0},{5,1},{6,2},{7,3},{8,12},{9,13},{10,... | collective-permute-start | bytes 98312 | tf_op jit(solution)/shard_map/ppermute | solution.py:22
  23.4 5.1 %collective-permute-start.5 = (bf16[8,2048]{1,0:T(8,128)(2,1)S(1)}, bf16[8,2048]{1,0:T(8,128)(2,1)S(1)}, u32[]{:S(2)}, u32[]{:S(2)}) collective-permute-start(bf16[8,2048]{1,0:T(8,128)(2,1)S(1)} %add_convert_fusion.1.refs_5_.p_ref), channel_id=1, source_target_pairs={{0,6},{1,7},{2,4},{3,5},{4,2},{5,3},{6,0},{7,1},{8,14},{9,15},{10,... | collective-permute-start | bytes 98312 | tf_op jit(solution)/shard_map/ppermute | solution.py:22
  24.7 26.4 %collective-permute-start.13 = (bf16[2304,128]{1,0:T(8,128)(2,1)S(1)}, bf16[2304,128]{1,0:T(8,128)(2,1)S(1)}, u32[]{:S(2)}, u32[]{:S(2)}) collective-permute-start(bf16[2304,128]{1,0:T(8,128)(2,1)S(1)} %get-tuple-element.56), channel_id=1, source_target_pairs={{0,128},{8,136},{16,144},{24,152},{32,160},{40,168},{48,176},{56,1... | collective-permute-start | bytes 1769480 | tf_op jit(solution)/shard_map/ppermute | solution.py:22
  31.0 3.8 %collective-permute-start.6 = (f32[16,256]{1,0:T(8,128)S(1)}, f32[16,256]{1,0:T(8,128)S(1)}, u32[]{:S(2)}, u32[]{:S(2)}) collective-permute-start(f32[16,256]{1,0:T(8,128)S(1)} %get-tuple-element.49.state_ref), channel_id=1, source_target_pairs={{0,8},{8,0},{16,24},{24,16},{32,40},{40,32},{48,56},{56,48},{64,72... | collective-permute-start | bytes 49160 | tf_op jit(solution)/shard_map/ppermute | solution.py:22
  35.3 1.3 %collective-permute-start.7 = (f32[8,2048]{1,0:T(8,128)S(1)}, f32[8,2048]{1,0:T(8,128)S(1)}, u32[]{:S(2)}, u32[]{:S(2)}) collective-permute-start(f32[8,2048]{1,0:T(8,128)S(1)} %out_projection_1.1), channel_id=1, source_target_pairs={{0,1},{1,0},{2,3},{3,2},{4,5},{5,4},{6,7},{7,6},{8,9},{9,8},{10,11... | collective-permute-start | bytes 196616 | tf_op jit(solution)/shard_map/ppermute | solution.py:22
  36.7 8.4 %collective-permute-start.10 = (bf16[8,2048]{1,0:T(8,128)(2,1)S(1)}, bf16[8,2048]{1,0:T(8,128)(2,1)S(1)}, u32[]{:S(2)}, u32[]{:S(2)}) collective-permute-start(bf16[8,2048]{1,0:T(8,128)(2,1)S(1)} %add_convert_fusion.after_ref.p_ref), channel_id=1, source_target_pairs={{0,6},{1,7},{2,4},{3,5},{4,2},{5,3},{6,0},{7,1},{8,14},{9,15},{10,... | collective-permute-start | bytes 98312 | tf_op jit(solution)/shard_map/ppermute | solution.py:22
  38.4 6.7 %collective-permute-start.8 = (bf16[8,2048]{1,0:T(8,128)(2,1)S(1)}, bf16[8,2048]{1,0:T(8,128)(2,1)S(1)}, u32[]{:S(2)}, u32[]{:S(2)}) collective-permute-start(bf16[8,2048]{1,0:T(8,128)(2,1)S(1)} %add_convert_fusion.after_ref.p_ref), channel_id=1, source_target_pairs={{0,2},{1,3},{2,0},{3,1},{4,6},{5,7},{6,4},{7,5},{8,10},{9,11},{10,... | collective-permute-start | bytes 98312 | tf_op jit(solution)/shard_map/ppermute | solution.py:22
  38.4 6.7 %collective-permute-start.9 = (bf16[8,2048]{1,0:T(8,128)(2,1)S(1)}, bf16[8,2048]{1,0:T(8,128)(2,1)S(1)}, u32[]{:S(2)}, u32[]{:S(2)}) collective-permute-start(bf16[8,2048]{1,0:T(8,128)(2,1)S(1)} %add_convert_fusion.after_ref.p_ref), channel_id=1, source_target_pairs={{0,4},{1,5},{2,6},{3,7},{4,0},{5,1},{6,2},{7,3},{8,12},{9,13},{10,... | collective-permute-start | bytes 98312 | tf_op jit(solution)/shard_map/ppermute | solution.py:22
  45.7 5.6 %collective-permute-start.12 = (f32[1,2560]{1,0:T(1,128)S(1)}, f32[1,2560]{1,0:T(1,128)S(1)}, u32[]{:S(2)}, u32[]{:S(2)}) collective-permute-start(f32[1,2560]{1,0:T(1,128)S(1)} %get-tuple-element.55), channel_id=1, source_target_pairs={{0,128},{8,136},{16,144},{24,152},{32,160},{40,168},{48,176},{56,1... | collective-permute-start | bytes 30728 | tf_op jit(solution)/shard_map/ppermute | solution.py:22

commit v9 on v8

--- a/solution.py
+++ b/solution.py
@@ -179,7 +179,8 @@
 
 
 UNIT = 256
-FIRST = 23
+HEAD = 6
+FIRST = 24
 PER = 2048 // UNIT
 SECOND = 4 * PER - FIRST
 
@@ -214,14 +215,17 @@
         copy.wait()
 
 
-def store_kernel(length_ref, first_ref, after_ref, stored_ref, blocks_ref, buffer, semaphores):
+def store_kernel(length_ref, head_ref, first_ref, after_ref, stored_ref, blocks_ref, buffer, semaphores):
     del after_ref
     reads, writes = [], []
     for n in range(FIRST):
         i, j, rows = plane_of(n)
         piece = pl.ds(n * UNIT, UNIT)
+        ref, at = (head_ref, n) if n < HEAD else (first_ref, n - HEAD)
         reads.append(
-            pltpu.make_async_copy(first_ref.at[piece], buffer.at[piece], semaphores.at[0, n])
+            pltpu.make_async_copy(
+                ref.at[pl.ds(at * UNIT, UNIT)], buffer.at[piece], semaphores.at[0, n]
+            )
         )
         writes.append(
             pltpu.make_async_copy(buffer.at[piece], stored_ref.at[i, j, rows], semaphores.at[1, n])
@@ -316,8 +320,10 @@
         copy.wait()
 
 
-def out_kernel(layer, state_ref, far_ref, side_ref, w_ref, after_ref, out_ref, w, semaphore):
-    del after_ref
+def out_kernel(
+    layer, state_ref, far_ref, side_ref, w_ref, after_ref, also_after_ref, out_ref, w, semaphore
+):
+    del after_ref, also_after_ref
     copy = pltpu.make_async_copy(w_ref.at[layer], w, semaphore)
     copy.start()
     is_main = lax.rem(row_of(16), 8) < 3
@@ -383,11 +389,12 @@
             name=name,
         )(held)
 
-    leaving_first, _ = leaving(0, FIRST, "leaving_first")
+    leaving_head, _ = leaving(0, HEAD, "leaving_head")
+    leaving_first, _ = leaving(HEAD, FIRST - HEAD, "leaving_first")
     leaving_second, _ = leaving(FIRST, SECOND, "leaving_second")
-    first, second = (
+    head, first, second = (
         permute(piece, "replica", lambda i: (i + groups // 2) % groups)
-        for piece in (leaving_first, leaving_second)
+        for piece in (leaving_head, leaving_first, leaving_second)
     )
     far_token = permute(long_tokens, "replica", lambda i: i ^ 1)
 
@@ -413,17 +420,17 @@
     stored = (cache, long_cache, w_query, key_weight, value_weight)
     tables = (norm_gain, q_gain, k_gain, cosine, sine)
 
-    def project_out(layer, state, side, after):
+    def project_out(layer, state, side, *after):
         far = permute(state, "replica", lambda i: i ^ 1)
         part = pl.pallas_call(
             functools.partial(out_kernel, layer),
             out_shape=jax.ShapeDtypeStruct((ROWS, 2048), jnp.float32),
-            in_specs=[VM, VM, VM, ANY, ANY],
+            in_specs=[VM, VM, VM, ANY, ANY, ANY],
             out_specs=VM,
             scratch_shapes=[pltpu.VMEM((256, 2048), jnp.bfloat16), pltpu.SemaphoreType.DMA(())],
             compiler_params=params,
             name=f"out_projection_{layer}",
-        )(state, far, side, w_out, after)
+        )(state, far, side, w_out, *after)
         part = (part + permute(part, "tensor", lambda i: i ^ 1)).astype(jnp.bfloat16)
         received = [permute(part, "tensor", lambda i, k=k: i ^ k) for k in (2, 4, 6)]
         return (part, *received)
@@ -458,7 +465,7 @@
         *fetch(0, (0, 1, 2, 3, 4), leaving_first, "fetch_0"), in_hbm(cache), in_hbm(long_cache),
     )
     resident = fetch(1, (0, 1, 2, 3, 4), state, "fetch_1_keys")
-    terms = project_out(0, state, side, resident[1])
+    terms = project_out(0, state, side, resident[1], head)
     resident = (*resident, *fetch(1, (5, 6), terms[0], "fetch_1_values"))
     state, side, fresh_1, hidden = pl.pallas_call(
         second_kernel,
@@ -468,7 +475,7 @@
         compiler_params=params,
         name="attention_1",
     )(group_1, lengths, long_lengths, hidden, *terms, *tables, *resident)
-    terms = project_out(1, state, side, side)
+    terms = project_out(1, state, side, side, side)
     partner = (group + groups // 2) % groups
     arrived_len = lax.dynamic_slice_in_dim(lengths, partner * 3 + 2, 1)
     stored_first, blocks = pl.pallas_call(
@@ -477,7 +484,7 @@
             pltpu.HBM((2, 2, 2048, 128), jnp.bfloat16),
             pltpu.VMEM((4, 16, 128), jnp.bfloat16),
         ),
-        in_specs=[SM, ANY, ANY],
+        in_specs=[SM, ANY, ANY, ANY],
         out_specs=(ANY, VM),
         scratch_shapes=[
             pltpu.VMEM((FIRST * UNIT, 128), jnp.bfloat16),
@@ -485,7 +492,7 @@
         ],
         compiler_params=pltpu.CompilerParams(vmem_limit_bytes=4 * 2**20),
         name="store_first",
-    )(arrived_len, in_hbm(first), terms[0])
+    )(arrived_len, head, in_hbm(first), terms[0])
     stay, long_out, leave = pl.pallas_call(
         final_kernel,
         out_shape=(

time: 53.1 us -> 56.8 us (1.070)
  waiting for transfers between devices: 11.2 us -> 13.2 us
  Pallas kernels: 20.8 us -> 22.4 us
    ppermute x14 -> x15, waiting for transfers between devices: 11.2 us -> 13.2 us  [permute(): return lax.ppermute(value, axis, pairs)]
    pallas_call x2 -> x3, Pallas kernels: 2.51 us -> 3.42 us  [leaving(): pl.pallas_call(functools.partial(leaving_kernel, begin, begin + count), o...]
    pallas_call x1, Pallas kernels: 2.99 us -> 3.6 us  [local(): pl.pallas_call(store_kernel, out_shape=(pltpu.HBM((2, 2, 2048, 128), jnp....]
    ppermute x14 -> x15, starting transfers between devices: 18.9 us -> 18.8 us  [permute(): return lax.ppermute(value, axis, pairs)]
  transfers between devices with their start and end apart: 14 -> 15, of which waited for: 7 -> 7; matrix products, arithmetic and copies ran while one was open for 2% -> 2% of each run, Pallas kernels for 34% -> 35%
where the time goes in v9:
time: 56.8 us; the launch traced here: 56.4 us
  Pallas kernels  22.4 us (39%)
  starting transfers between devices  18.8 us (33%)
  waiting for transfers between devices  13.2 us (23%)
  between operations  0.91 us (2%)
  local copies, waits for them, and re-layouts  0.83 us (1%)
    ppermute x15, starting transfers between devices, permute(): return lax.ppermute(value, axis, pairs)  18.8 us
    ppermute x15, waiting for transfers between devices, permute(): return lax.ppermute(value, axis, pairs)  13.2 us
    pallas_call x3, Pallas kernels, fetch(): pl.pallas_call(functools.partial(fetch_kernel, layer, which), out_shape=t...  6.59 us
    pallas_call x1, Pallas kernels, local(): pl.pallas_call(store_kernel, out_shape=(pltpu.HBM((2, 2, 2048, 128), jnp....  3.6 us
    pallas_call x3, Pallas kernels, leaving(): pl.pallas_call(functools.partial(leaving_kernel, begin, begin + count), o...  3.42 us
    pallas_call x1, Pallas kernels, local(): pl.pallas_call(first_kernel, out_shape=out_shape, in_specs=[SM] * 3 + [VM...  3.16 us
    pallas_call x1, Pallas kernels, local(): pl.pallas_call(second_kernel, out_shape=out_shape, in_specs=[SM] * 3 + [V...  2.47 us
    pallas_call x1, Pallas kernels, local(): pl.pallas_call(arrival_kernel, out_shape=(pltpu.HBM((3, 2048), jnp.float3...  1.53 us
  transfers between devices with their start and end apart: 15, of which 7 were waited for; matrix products, arithmetic and copies ran while one was open for 2% of the time, Pallas kernels for 35%

profile of v9, /device:TPU:64, one launch (start us, length us, event | category | flops | bytes accessed | tf_op | source)
XLA Modules:
  0.0 56.4 jit_solution(10207211952266125839)
XLA Ops:
  0.6 1.0 %leaving_head.1 = (bf16[1536,128]{1,0:T(8,128)(2,1)S(1)}, f32[8,128]{1,0:T(8,128)}) custom-call(bf16[2,2,3,2048,128]{4,3,2,1,0:T(8,128)(2,1)} %bitcast.6), custom_call_target="tpu_custom_call" | custom-call | tf_op jit(solution)/shard_map/leaving_head/pallas_call | solution.py:379
  1.7 3.1 %collective-permute-start.2 = (bf16[1536,128]{1,0:T(8,128)(2,1)S(1)}, bf16[1536,128]{1,0:T(8,128)(2,1)S(1)}, u32[]{:S(2)}, u32[]{:S(2)}) collective-permute-start(bf16[1536,128]{1,0:T(8,128)(2,1)S(1)} %get-tuple-element.43), channel_id=1, source_target_pairs={{0,128},{8,136},{16,144},{24,152},{32,160},{40,168},{48,176},{56,1... | collective-permute-start | bytes 1179656 | tf_op jit(solution)/shard_map/ppermute | solution.py:22
  4.8 1.9 %collective-permute-start = (bf16[1,2048]{1,0:T(2,128)(2,1)S(1)}, bf16[1,2048]{1,0:T(2,128)(2,1)S(1)}, u32[]{:S(2)}, u32[]{:S(2)}) collective-permute-start(bf16[1,2048]{1,0:T(2,128)(2,1)S(1)} %copy-done.3), channel_id=1, source_target_pairs={{0,8},{8,0},{16,24},{24,16},{32,40},{40,32},{48,56},{56,48},{64,72... | collective-permute-start | bytes 12296 | tf_op jit(solution)/shard_map/ppermute | solution.py:22
  6.8 1.3 %leaving_first.1 = (bf16[4608,128]{1,0:T(8,128)(2,1)S(1)}, f32[8,128]{1,0:T(8,128)}) custom-call(bf16[2,2,3,2048,128]{4,3,2,1,0:T(8,128)(2,1)} %bitcast.7), custom_call_target="tpu_custom_call" | custom-call | tf_op jit(solution)/shard_map/leaving_first/pallas_call | solution.py:379
  9.1 2.4 %fetch_0.1 = (bf16[2048,256]{1,0:T(8,128)(2,1)S(1)}, bf16[2048,128]{1,0:T(8,128)(2,1)S(1)}, bf16[2048,128]{1,0:T(8,128)(2,1)S(1)}, bf16[3,2048,128]{2,1,0:T(8,128)(2,1)S(1)}, bf16[2,2048,128]{2,1,0:T(8,128)(2,1)S(1)}) custom-call(bf16[2,2,3,2048,128]{4,3,2,1,0:T(8,128)(2,1)} %bitcast.8, bf16[2,2,1,2,2048,128]{5,4,3,2,1,0:T(8,128)(2,1)} %bitcast.13, ...), custom_call_target="tpu_custom_call" | custom-call | tf_op jit(solution)/shard_map/fetch_0/pallas_call | solution.py:441
  11.5 3.2 %attention_0.1 = (f32[16,256]{1,0:T(8,128)S(1)}, f32[16,256]{1,0:T(8,128)S(1)}, f32[2,128]{1,0:T(2,128)S(1)}, f32[8,2048]{1,0:T(8,128)S(1)}) custom-call(s32[1]{0:T(128)} %bitcast.group_ref, s32[96]{0:T(128)S(1)} %copy-done.7, s32[32]{0:T(128)S(1)} %copy-done.6, bf16[3,2048]{1,0:T(4,128)(2,1)S(1)} %copy-done.2, bf16[1,2048]{1,0:T(2,128)(2,1)S(1)} %copy-done.3, ...), custom_call_target="tpu_custom_call" | custom-call | tf_op jit(solution)/shard_map/attention_0/pallas_call | solution.py:451
  14.9 2.5 %fetch_1_keys.1 = (bf16[2048,256]{1,0:T(8,128)(2,1)S(1)}, bf16[2048,128]{1,0:T(8,128)(2,1)S(1)}, bf16[2048,128]{1,0:T(8,128)(2,1)S(1)}, bf16[3,2048,128]{2,1,0:T(8,128)(2,1)S(1)}, bf16[2,2048,128]{2,1,0:T(8,128)(2,1)S(1)}) custom-call(bf16[2,2,3,2048,128]{4,3,2,1,0:T(8,128)(2,1)} %bitcast.10, bf16[2,2,1,2,2048,128]{5,4,3,2,1,0:T(8,128)(2,1)} %bitcast.15, ...), custom_call_target="tpu_custom_call" | custom-call | tf_op jit(solution)/shard_map/fetch_1_keys/pallas_call | solution.py:441
  17.4 1.1 %collective-permute-done.1.far_ref = f32[16,256]{1,0:T(8,128)S(1)} collective-permute-done((f32[16,256]{1,0:T(8,128)S(1)}, f32[16,256]{1,0:T(8,128)S(1)}, u32[]{:S(2)}, u32[]{:S(2)}) %collective-permute-start.1) | collective-permute-done | bytes 16416 | tf_op jit(solution)/shard_map/ppermute | solution.py:22
  19.1 1.2 %collective-permute-done.3 = f32[8,2048]{1,0:T(8,128)S(1)} collective-permute-done((f32[8,2048]{1,0:T(8,128)S(1)}, f32[8,2048]{1,0:T(8,128)S(1)}, u32[]{:S(2)}, u32[]{:S(2)}) %collective-permute-start.3) | collective-permute-done | bytes 65568 | tf_op jit(solution)/shard_map/ppermute | solution.py:22
  20.4 1.7 %collective-permute-start.4 = (bf16[8,2048]{1,0:T(8,128)(2,1)S(1)}, bf16[8,2048]{1,0:T(8,128)(2,1)S(1)}, u32[]{:S(2)}, u32[]{:S(2)}) collective-permute-start(bf16[8,2048]{1,0:T(8,128)(2,1)S(1)} %add_convert_fusion.1.refs_5_.p_ref), channel_id=1, source_target_pairs={{0,2},{1,3},{2,0},{3,1},{4,6},{5,7},{6,4},{7,5},{8,10},{9,11},{10,... | collective-permute-start | bytes 98312 | tf_op jit(solution)/shard_map/ppermute | solution.py:22
  22.1 2.9 %collective-permute-start.5 = (bf16[8,2048]{1,0:T(8,128)(2,1)S(1)}, bf16[8,2048]{1,0:T(8,128)(2,1)S(1)}, u32[]{:S(2)}, u32[]{:S(2)}) collective-permute-start(bf16[8,2048]{1,0:T(8,128)(2,1)S(1)} %add_convert_fusion.1.refs_5_.p_ref), channel_id=1, source_target_pairs={{0,4},{1,5},{2,6},{3,7},{4,0},{5,1},{6,2},{7,3},{8,12},{9,13},{10,... | collective-permute-start | bytes 98312 | tf_op jit(solution)/shard_map/ppermute | solution.py:22
  25.2 1.7 %fetch_1_values.1 = (bf16[3,2048,128]{2,1,0:T(8,128)(2,1)S(1)}, bf16[2,2048,128]{2,1,0:T(8,128)(2,1)S(1)}) custom-call(bf16[2,2,3,2048,128]{4,3,2,1,0:T(8,128)(2,1)} %bitcast.11, bf16[2,2,1,2,2048,128]{5,4,3,2,1,0:T(8,128)(2,1)} %bitcast.16, bf16[2,2048,256]{2,1,0:T(8,128)(2,1)} %refs_2_.5, bf16[2,2048,128]{2,1,0:T(8,128)(2,1)} %refs_3_.5, ...), custom_call_target="tpu_custom_call" | custom-call | tf_op jit(solution)/shard_map/fetch_1_values/pallas_call | solution.py:441
  27.5 2.6 %collective-permute-done.6.r3_ref = bf16[8,2048]{1,0:T(8,128)(2,1)S(1)} collective-permute-done((bf16[8,2048]{1,0:T(8,128)(2,1)S(1)}, bf16[8,2048]{1,0:T(8,128)(2,1)S(1)}, u32[]{:S(2)}, u32[]{:S(2)}) %collective-permute-start.6) | collective-permute-done | bytes 32800 | tf_op jit(solution)/shard_map/ppermute | solution.py:22
  30.1 2.5 %attention_1.1 = (f32[16,256]{1,0:T(8,128)S(1)}, f32[16,256]{1,0:T(8,128)S(1)}, f32[2,128]{1,0:T(2,128)S(1)}, f32[8,2048]{1,0:T(8,128)S(1)}) custom-call(s32[1]{0:T(128)} %bitcast.group_ref, s32[96]{0:T(128)S(1)} %copy-done.7, s32[32]{0:T(128)S(1)} %copy-done.6, f32[8,2048]{1,0:T(8,128)S(1)} %get-tuple-element.39.before_ref, ...), custom_call_target="tpu_custom_call" | custom-call | tf_op jit(solution)/shard_map/attention_1/pallas_call | solution.py:470
  32.6 0.8 %collective-permute-start.7 = (f32[16,256]{1,0:T(8,128)S(1)}, f32[16,256]{1,0:T(8,128)S(1)}, u32[]{:S(2)}, u32[]{:S(2)}) collective-permute-start(f32[16,256]{1,0:T(8,128)S(1)} %get-tuple-element.51.state_ref), channel_id=1, source_target_pairs={{0,8},{8,0},{16,24},{24,16},{32,40},{40,32},{48,56},{56,48},{64,72... | collective-permute-start | bytes 49160 | tf_op jit(solution)/shard_map/ppermute | solution.py:22
  33.4 3.0 %collective-permute-done.7.far_ref = f32[16,256]{1,0:T(8,128)S(1)} collective-permute-done((f32[16,256]{1,0:T(8,128)S(1)}, f32[16,256]{1,0:T(8,128)S(1)}, u32[]{:S(2)}, u32[]{:S(2)}) %collective-permute-start.7) | collective-permute-done | bytes 16416 | tf_op jit(solution)/shard_map/ppermute | solution.py:22
  37.0 1.1 %leaving_second.1 = (bf16[2048,128]{1,0:T(8,128)(2,1)S(1)}, f32[8,128]{1,0:T(8,128)}) custom-call(bf16[2,2,3,2048,128]{4,3,2,1,0:T(8,128)(2,1)} %bitcast.12), custom_call_target="tpu_custom_call" | custom-call | tf_op jit(solution)/shard_map/leaving_second/pallas_call | solution.py:379
  38.1 3.1 %collective-permute-start.14 = (bf16[2048,128]{1,0:T(8,128)(2,1)S(1)}, bf16[2048,128]{1,0:T(8,128)(2,1)S(1)}, u32[]{:S(2)}, u32[]{:S(2)}) collective-permute-start(bf16[2048,128]{1,0:T(8,128)(2,1)S(1)} %get-tuple-element.58), channel_id=1, source_target_pairs={{0,128},{8,136},{16,144},{24,152},{32,160},{40,168},{48,176},{56,1... | collective-permute-start | bytes 1572872 | tf_op jit(solution)/shard_map/ppermute | solution.py:22
  41.6 1.3 %collective-permute-start.11 = (bf16[8,2048]{1,0:T(8,128)(2,1)S(1)}, bf16[8,2048]{1,0:T(8,128)(2,1)S(1)}, u32[]{:S(2)}, u32[]{:S(2)}) collective-permute-start(bf16[8,2048]{1,0:T(8,128)(2,1)S(1)} %add_convert_fusion.after_ref.p_ref), channel_id=1, source_target_pairs={{0,6},{1,7},{2,4},{3,5},{4,2},{5,3},{6,0},{7,1},{8,14},{9,15},{10,... | collective-permute-start | bytes 98312 | tf_op jit(solution)/shard_map/ppermute | solution.py:22
  42.9 1.9 %collective-permute-start.9 = (bf16[8,2048]{1,0:T(8,128)(2,1)S(1)}, bf16[8,2048]{1,0:T(8,128)(2,1)S(1)}, u32[]{:S(2)}, u32[]{:S(2)}) collective-permute-start(bf16[8,2048]{1,0:T(8,128)(2,1)S(1)} %add_convert_fusion.after_ref.p_ref), channel_id=1, source_target_pairs={{0,2},{1,3},{2,0},{3,1},{4,6},{5,7},{6,4},{7,5},{8,10},{9,11},{10,... | collective-permute-start | bytes 98312 | tf_op jit(solution)/shard_map/ppermute | solution.py:22
  45.4 3.6 %store_first.1 = (bf16[2,2,2048,128]{3,2,1,0:T(8,128)(2,1)}, bf16[4,16,128]{2,1,0:T(8,128)(2,1)S(1)}) custom-call(s32[1]{0:T(128)} %dynamic_slice.9.length_ref, bf16[1536,128]{1,0:T(8,128)(2,1)S(1)} %collective-permute-done.2.also_after_ref.head_ref, bf16[4608,128]{1,0:T(8,128)(2,1)} %collective-permute-done.12.first_ref, ...), custom_call_target="tpu_custom_call" | custom-call | tf_op jit(solution)/shard_map/store_first/pallas_call | solution.py:481
  50.2 3.9 %collective-permute-done.14.second_ref = bf16[2048,128]{1,0:T(8,128)(2,1)S(1)} collective-permute-done((bf16[2048,128]{1,0:T(8,128)(2,1)S(1)}, bf16[2048,128]{1,0:T(8,128)(2,1)S(1)}, u32[]{:S(2)}, u32[]{:S(2)}) %collective-permute-start.14) | collective-permute-done | bytes 524320 | tf_op jit(solution)/shard_map/ppermute | solution.py:22
  54.1 0.7 %collective-permute-done.13.arrived_ref = f32[1,2560]{1,0:T(1,128)S(1)} collective-permute-done((f32[1,2560]{1,0:T(1,128)S(1)}, f32[1,2560]{1,0:T(1,128)S(1)}, u32[]{:S(2)}, u32[]{:S(2)}) %collective-permute-start.13) | collective-permute-done | bytes 10272 | tf_op jit(solution)/shard_map/ppermute | solution.py:22
  54.8 1.5 %arrival.1 = (f32[3,2048]{1,0:T(4,128)}, bf16[2,2,2048,128]{3,2,1,0:T(8,128)(2,1)}) custom-call(s32[1]{0:T(128)} %dynamic_slice.9.length_ref, f32[2,2048]{1,0:T(2,128)S(1)} %get-tuple-element.56.stay_ref, f32[1,2560]{1,0:T(1,128)S(1)} %collective-permute-done.13.arrived_ref, ...), custom_call_target="tpu_custom_call", output_to_operand_aliasing={{1}: (5, {})} | custom-call | tf_op jit(solution)/shard_map/arrival/pallas_call | solution.py:510
  (47 shorter events, 5.3 us)
Async XLA Ops:
  0.6 4.2 %copy-start.3 = (bf16[1,2048]{1,0:T(2,128)(2,1)S(1)}, bf16[1,2048]{1,0:T(2,128)(2,1)}, u32[]{:S(2)}) copy-start(bf16[1,2048]{1,0:T(2,128)(2,1)} %own_long_ref.1) | copy-start | bytes 12292
  1.7 7.0 %copy-start.6 = (s32[32]{0:T(128)S(1)}, s32[32]{0:T(128)}, u32[]{:S(2)}) copy-start(s32[32]{0:T(128)} %long_lengths_ref.3) | copy-start | bytes 388
  1.7 7.1 %copy-start.7 = (s32[96]{0:T(128)S(1)}, s32[96]{0:T(128)}, u32[]{:S(2)}) copy-start(s32[96]{0:T(128)} %lengths_ref.3) | copy-start | bytes 1156
  1.7 7.2 %copy-start.8 = (f32[128]{0:T(128)S(1)}, f32[128]{0:T(128)}, u32[]{:S(2)}) copy-start(f32[128]{0:T(128)} %constant.43.clone) | copy-start | bytes 1540
  1.7 7.2 %copy-start.9 = (f32[128]{0:T(128)S(1)}, f32[128]{0:T(128)}, u32[]{:S(2)}) copy-start(f32[128]{0:T(128)} %constant.44.clone) | copy-start | bytes 1540
  1.7 16.8 %collective-permute-start.2 = (bf16[1536,128]{1,0:T(8,128)(2,1)S(1)}, bf16[1536,128]{1,0:T(8,128)(2,1)S(1)}, u32[]{:S(2)}, u32[]{:S(2)}) collective-permute-start(bf16[1536,128]{1,0:T(8,128)(2,1)S(1)} %get-tuple-element.43), channel_id=1, source_target_pairs={{0,128},{8,136},{16,144},{24,152},{32,160},{40,168},{48,176},{56,1... | collective-permute-start | bytes 1179656 | tf_op jit(solution)/shard_map/ppermute | solution.py:22
  4.8 6.6 %collective-permute-start = (bf16[1,2048]{1,0:T(2,128)(2,1)S(1)}, bf16[1,2048]{1,0:T(2,128)(2,1)S(1)}, u32[]{:S(2)}, u32[]{:S(2)}) collective-permute-start(bf16[1,2048]{1,0:T(2,128)(2,1)S(1)} %copy-done.3), channel_id=1, source_target_pairs={{0,8},{8,0},{16,24},{24,16},{32,40},{40,32},{48,56},{56,48},{64,72... | collective-permute-start | bytes 12296 | tf_op jit(solution)/shard_map/ppermute | solution.py:22
  8.1 37.3 %collective-permute-start.12 = (bf16[4608,128]{1,0:T(8,128)(2,1)S(1)}, bf16[4608,128]{1,0:T(8,128)(2,1)}, u32[]{:S(2)}, u32[]{:S(2)}) collective-permute-start(bf16[4608,128]{1,0:T(8,128)(2,1)S(1)} %get-tuple-element.33.refs_5_), channel_id=1, source_target_pairs={{0,128},{8,136},{16,144},{24,152},{32,160},{40,168},{48,176},{56,1... | collective-permute-start | bytes 3538952 | tf_op jit(solution)/shard_map/ppermute | solution.py:22
  9.0 2.5 %copy-start.1 = (f32[2,2048]{1,0:T(2,128)S(1)}, f32[2,2048]{1,0:T(2,128)}, u32[]{:S(2)}) copy-start(f32[2,2048]{1,0:T(2,128)} %rest_0_.3) | copy-start | bytes 49156
  9.0 2.5 %copy-start.2 = (bf16[3,2048]{1,0:T(4,128)(2,1)S(1)}, bf16[3,2048]{1,0:T(4,128)(2,1)}, u32[]{:S(2)}) copy-start(bf16[3,2048]{1,0:T(4,128)(2,1)} %tokens_ref.1) | copy-start | bytes 36868
  9.0 2.5 %copy-start.4 = (f32[2,128]{1,0:T(2,128)S(1)}, f32[2,128]{1,0:T(2,128)}, u32[]{:S(2)}) copy-start(f32[2,128]{1,0:T(2,128)} %rest_1_.3) | copy-start | bytes 3076
  14.7 3.8 %copy-start = (bf16[2,256,2048]{2,1,0:T(8,128)(2,1)S(1)}, bf16[2,256,2048]{2,1,0:T(8,128)(2,1)}, u32[]{:S(2)}) copy-start(bf16[2,256,2048]{2,1,0:T(8,128)(2,1)} %w_ref.3) | copy-start | bytes 6291460
  14.7 3.8 %collective-permute-start.1 = (f32[16,256]{1,0:T(8,128)S(1)}, f32[16,256]{1,0:T(8,128)S(1)}, u32[]{:S(2)}, u32[]{:S(2)}) collective-permute-start(f32[16,256]{1,0:T(8,128)S(1)} %get-tuple-element.40.refs_5_.state_ref), channel_id=1, source_target_pairs={{0,8},{8,0},{16,24},{24,16},{32,40},{40,32},{48,56},{56,48},{64,72... | collective-permute-start | bytes 49160 | tf_op jit(solution)/shard_map/ppermute | solution.py:22
  19.0 1.3 %collective-permute-start.3 = (f32[8,2048]{1,0:T(8,128)S(1)}, f32[8,2048]{1,0:T(8,128)S(1)}, u32[]{:S(2)}, u32[]{:S(2)}) collective-permute-start(f32[8,2048]{1,0:T(8,128)S(1)} %out_projection_0.1), channel_id=1, source_target_pairs={{0,1},{1,0},{2,3},{3,2},{4,5},{5,4},{6,7},{7,6},{8,9},{9,8},{10,11... | collective-permute-start | bytes 196616 | tf_op jit(solution)/shard_map/ppermute | solution.py:22
  20.4 6.5 %collective-permute-start.4 = (bf16[8,2048]{1,0:T(8,128)(2,1)S(1)}, bf16[8,2048]{1,0:T(8,128)(2,1)S(1)}, u32[]{:S(2)}, u32[]{:S(2)}) collective-permute-start(bf16[8,2048]{1,0:T(8,128)(2,1)S(1)} %add_convert_fusion.1.refs_5_.p_ref), channel_id=1, source_target_pairs={{0,2},{1,3},{2,0},{3,1},{4,6},{5,7},{6,4},{7,5},{8,10},{9,11},{10,... | collective-permute-start | bytes 98312 | tf_op jit(solution)/shard_map/ppermute | solution.py:22
  22.1 5.4 %collective-permute-start.5 = (bf16[8,2048]{1,0:T(8,128)(2,1)S(1)}, bf16[8,2048]{1,0:T(8,128)(2,1)S(1)}, u32[]{:S(2)}, u32[]{:S(2)}) collective-permute-start(bf16[8,2048]{1,0:T(8,128)(2,1)S(1)} %add_convert_fusion.1.refs_5_.p_ref), channel_id=1, source_target_pairs={{0,4},{1,5},{2,6},{3,7},{4,0},{5,1},{6,2},{7,3},{8,12},{9,13},{10,... | collective-permute-start | bytes 98312 | tf_op jit(solution)/shard_map/ppermute | solution.py:22
  25.0 5.1 %collective-permute-start.6 = (bf16[8,2048]{1,0:T(8,128)(2,1)S(1)}, bf16[8,2048]{1,0:T(8,128)(2,1)S(1)}, u32[]{:S(2)}, u32[]{:S(2)}) collective-permute-start(bf16[8,2048]{1,0:T(8,128)(2,1)S(1)} %add_convert_fusion.1.refs_5_.p_ref), channel_id=1, source_target_pairs={{0,6},{1,7},{2,4},{3,5},{4,2},{5,3},{6,0},{7,1},{8,14},{9,15},{10,... | collective-permute-start | bytes 98312 | tf_op jit(solution)/shard_map/ppermute | solution.py:22
  32.6 3.8 %collective-permute-start.7 = (f32[16,256]{1,0:T(8,128)S(1)}, f32[16,256]{1,0:T(8,128)S(1)}, u32[]{:S(2)}, u32[]{:S(2)}) collective-permute-start(f32[16,256]{1,0:T(8,128)S(1)} %get-tuple-element.51.state_ref), channel_id=1, source_target_pairs={{0,8},{8,0},{16,24},{24,16},{32,40},{40,32},{48,56},{56,48},{64,72... | collective-permute-start | bytes 49160 | tf_op jit(solution)/shard_map/ppermute | solution.py:22
  36.9 4.3 %collective-permute-start.8 = (f32[8,2048]{1,0:T(8,128)S(1)}, f32[8,2048]{1,0:T(8,128)S(1)}, u32[]{:S(2)}, u32[]{:S(2)}) collective-permute-start(f32[8,2048]{1,0:T(8,128)S(1)} %out_projection_1.1), channel_id=1, source_target_pairs={{0,1},{1,0},{2,3},{3,2},{4,5},{5,4},{6,7},{7,6},{8,9},{9,8},{10,11... | collective-permute-start | bytes 196616 | tf_op jit(solution)/shard_map/ppermute | solution.py:22
  38.1 16.0 %collective-permute-start.14 = (bf16[2048,128]{1,0:T(8,128)(2,1)S(1)}, bf16[2048,128]{1,0:T(8,128)(2,1)S(1)}, u32[]{:S(2)}, u32[]{:S(2)}) collective-permute-start(bf16[2048,128]{1,0:T(8,128)(2,1)S(1)} %get-tuple-element.58), channel_id=1, source_target_pairs={{0,128},{8,136},{16,144},{24,152},{32,160},{40,168},{48,176},{56,1... | collective-permute-start | bytes 1572872 | tf_op jit(solution)/shard_map/ppermute | solution.py:22
  41.2 7.8 %collective-permute-start.10 = (bf16[8,2048]{1,0:T(8,128)(2,1)S(1)}, bf16[8,2048]{1,0:T(8,128)(2,1)S(1)}, u32[]{:S(2)}, u32[]{:S(2)}) collective-permute-start(bf16[8,2048]{1,0:T(8,128)(2,1)S(1)} %add_convert_fusion.after_ref.p_ref), channel_id=1, source_target_pairs={{0,4},{1,5},{2,6},{3,7},{4,0},{5,1},{6,2},{7,3},{8,12},{9,13},{10,... | collective-permute-start | bytes 98312 | tf_op jit(solution)/shard_map/ppermute | solution.py:22
  41.6 7.4 %collective-permute-start.11 = (bf16[8,2048]{1,0:T(8,128)(2,1)S(1)}, bf16[8,2048]{1,0:T(8,128)(2,1)S(1)}, u32[]{:S(2)}, u32[]{:S(2)}) collective-permute-start(bf16[8,2048]{1,0:T(8,128)(2,1)S(1)} %add_convert_fusion.after_ref.p_ref), channel_id=1, source_target_pairs={{0,6},{1,7},{2,4},{3,5},{4,2},{5,3},{6,0},{7,1},{8,14},{9,15},{10,... | collective-permute-start | bytes 98312 | tf_op jit(solution)/shard_map/ppermute | solution.py:22
  42.9 6.1 %collective-permute-start.9 = (bf16[8,2048]{1,0:T(8,128)(2,1)S(1)}, bf16[8,2048]{1,0:T(8,128)(2,1)S(1)}, u32[]{:S(2)}, u32[]{:S(2)}) collective-permute-start(bf16[8,2048]{1,0:T(8,128)(2,1)S(1)} %add_convert_fusion.after_ref.p_ref), channel_id=1, source_target_pairs={{0,2},{1,3},{2,0},{3,1},{4,6},{5,7},{6,4},{7,5},{8,10},{9,11},{10,... | collective-permute-start | bytes 98312 | tf_op jit(solution)/shard_map/ppermute | solution.py:22
  49.7 5.2 %collective-permute-start.13 = (f32[1,2560]{1,0:T(1,128)S(1)}, f32[1,2560]{1,0:T(1,128)S(1)}, u32[]{:S(2)}, u32[]{:S(2)}) collective-permute-start(f32[1,2560]{1,0:T(1,128)S(1)} %get-tuple-element.57), channel_id=1, source_target_pairs={{0,128},{8,136},{16,144},{24,152},{32,160},{40,168},{48,176},{56,1... | collective-permute-start | bytes 30728 | tf_op jit(solution)/shard_map/ppermute | solution.py:22
  (1 other events, 2.5 us)

commit v10 on v8

--- a/solution.py
+++ b/solution.py
@@ -214,8 +214,11 @@
         copy.wait()
 
 
-def store_kernel(length_ref, first_ref, after_ref, stored_ref, blocks_ref, buffer, semaphores):
+def store_kernel(
+    length_ref, first_ref, after_ref, stored_ref, blocks_ref, place_ref, buffer, semaphores
+):
     del after_ref
+    place_ref[...] = jnp.full((8, 128), length_ref[0].astype(jnp.float32))
     reads, writes = [], []
     for n in range(FIRST):
         i, j, rows = plane_of(n)
@@ -240,11 +243,11 @@
 
 
 def arrival_kernel(
-    length_ref, stay_ref, arrived_ref, blocks_ref, second_ref, stored_ref, out_ref, moved_ref,
+    place_ref, stay_ref, arrived_ref, blocks_ref, second_ref, stored_ref, out_ref, moved_ref,
     rows, blocks, patched, semaphores,
 ):
     del stored_ref
-    length = length_ref[0]
+    length = jnp.max(place_ref[...]).astype(jnp.int32)
     hit_unit = length // UNIT
     units = [(unit, *plane_of(unit)) for unit in range(FIRST, 4 * PER)]
 
@@ -471,14 +474,15 @@
     terms = project_out(1, state, side, side)
     partner = (group + groups // 2) % groups
     arrived_len = lax.dynamic_slice_in_dim(lengths, partner * 3 + 2, 1)
-    stored_first, blocks = pl.pallas_call(
+    stored_first, blocks, place = pl.pallas_call(
         store_kernel,
         out_shape=(
             pltpu.HBM((2, 2, 2048, 128), jnp.bfloat16),
             pltpu.VMEM((4, 16, 128), jnp.bfloat16),
+            pltpu.VMEM((8, 128), jnp.float32),
         ),
         in_specs=[SM, ANY, ANY],
-        out_specs=(ANY, VM),
+        out_specs=(ANY, VM, VM),
         scratch_shapes=[
             pltpu.VMEM((FIRST * UNIT, 128), jnp.bfloat16),
             pltpu.SemaphoreType.DMA((2, FIRST)),
@@ -506,7 +510,7 @@
             pltpu.HBM((3, 2048), jnp.float32),
             pltpu.HBM((2, 2, 2048, 128), jnp.bfloat16),
         ),
-        in_specs=[SM, VM, VM, VM, VM, ANY],
+        in_specs=[VM, VM, VM, VM, VM, ANY],
         out_specs=(ANY, ANY),
         input_output_aliases={5: 1},
         scratch_shapes=[
@@ -517,7 +521,7 @@
         ],
         compiler_params=small,
         name="arrival",
-    )(arrived_len, stay, arrived, blocks, in_vmem(second), stored_first)
+    )(place, stay, arrived, blocks, in_vmem(second), stored_first)
     return (out_hidden, long_out, moved[None, :, :, :, None, :])
 
 

time: 53.1 us -> 52.6 us (level)
  starting transfers between devices: 18.9 us -> 18 us
  waiting for transfers between devices: 11.2 us -> 12 us
    ppermute x14, starting transfers between devices: 18.9 us -> 18 us  [permute(): return lax.ppermute(value, axis, pairs)]
    ppermute x14, waiting for transfers between devices: 11.2 us -> 12 us  [permute(): return lax.ppermute(value, axis, pairs)]
where the time goes in v10:
time: 52.6 us; the launch traced here: 52.3 us
  Pallas kernels  20.4 us (39%)
  starting transfers between devices  18 us (34%)
  waiting for transfers between devices  12 us (23%)
  between operations  0.91 us (2%)
  local copies, waits for them, and re-layouts  0.79 us (2%)
    ppermute x14, starting transfers between devices, permute(): return lax.ppermute(value, axis, pairs)  18 us
    ppermute x14, waiting for transfers between devices, permute(): return lax.ppermute(value, axis, pairs)  12 us
    pallas_call x3, Pallas kernels, fetch(): pl.pallas_call(functools.partial(fetch_kernel, layer, which), out_shape=t...  6.54 us
    pallas_call x1, Pallas kernels, local(): pl.pallas_call(first_kernel, out_shape=out_shape, in_specs=[SM] * 3 + [VM...  3.16 us
    pallas_call x1, Pallas kernels, local(): pl.pallas_call(store_kernel, out_shape=(pltpu.HBM((2, 2, 2048, 128), jnp....  3.07 us
    pallas_call x2, Pallas kernels, leaving(): pl.pallas_call(functools.partial(leaving_kernel, begin, begin + count), o...  2.51 us
    pallas_call x1, Pallas kernels, local(): pl.pallas_call(second_kernel, out_shape=out_shape, in_specs=[SM] * 3 + [V...  2.47 us
    pallas_call x1, Pallas kernels, local(): pl.pallas_call(arrival_kernel, out_shape=(pltpu.HBM((3, 2048), jnp.float3...  1.07 us
  transfers between devices with their start and end apart: 14, of which 7 were waited for; matrix products, arithmetic and copies ran while one was open for 2% of the time, Pallas kernels for 34%

profile of v10, /device:TPU:64, one launch (start us, length us, event | category | flops | bytes accessed | tf_op | source)
XLA Modules:
  0.0 52.3 jit_solution(6632145268107247564)
XLA Ops:
  0.7 1.4 %leaving_first.1 = (bf16[5888,128]{1,0:T(8,128)(2,1)S(1)}, f32[8,128]{1,0:T(8,128)}) custom-call(bf16[2,2,3,2048,128]{4,3,2,1,0:T(8,128)(2,1)} %bitcast.6), custom_call_target="tpu_custom_call" | custom-call | tf_op jit(solution)/shard_map/leaving_first/pallas_call | solution.py:376
  2.1 3.1 %collective-permute-start = (bf16[5888,128]{1,0:T(8,128)(2,1)S(1)}, bf16[5888,128]{1,0:T(8,128)(2,1)}, u32[]{:S(2)}, u32[]{:S(2)}) collective-permute-start(bf16[5888,128]{1,0:T(8,128)(2,1)S(1)} %get-tuple-element.33.refs_5_), channel_id=1, source_target_pairs={{0,128},{8,136},{16,144},{24,152},{32,160},{40,168},{48,176},{56,1... | collective-permute-start | bytes 4521992 | tf_op jit(solution)/shard_map/ppermute | solution.py:22
  5.2 1.9 %collective-permute-start.1 = (bf16[1,2048]{1,0:T(2,128)(2,1)S(1)}, bf16[1,2048]{1,0:T(2,128)(2,1)S(1)}, u32[]{:S(2)}, u32[]{:S(2)}) collective-permute-start(bf16[1,2048]{1,0:T(2,128)(2,1)S(1)} %copy-done.3), channel_id=1, source_target_pairs={{0,8},{8,0},{16,24},{24,16},{32,40},{40,32},{48,56},{56,48},{64,72... | collective-permute-start | bytes 12296 | tf_op jit(solution)/shard_map/ppermute | solution.py:22
  7.5 2.4 %fetch_0.1 = (bf16[2048,256]{1,0:T(8,128)(2,1)S(1)}, bf16[2048,128]{1,0:T(8,128)(2,1)S(1)}, bf16[2048,128]{1,0:T(8,128)(2,1)S(1)}, bf16[3,2048,128]{2,1,0:T(8,128)(2,1)S(1)}, bf16[2,2048,128]{2,1,0:T(8,128)(2,1)S(1)}) custom-call(bf16[2,2,3,2048,128]{4,3,2,1,0:T(8,128)(2,1)} %bitcast.7, bf16[2,2,1,2,2048,128]{5,4,3,2,1,0:T(8,128)(2,1)} %bitcast.12, ...), custom_call_target="tpu_custom_call" | custom-call | tf_op jit(solution)/shard_map/fetch_0/pallas_call | solution.py:437
  10.0 3.2 %attention_0.1 = (f32[16,256]{1,0:T(8,128)S(1)}, f32[16,256]{1,0:T(8,128)S(1)}, f32[2,128]{1,0:T(2,128)S(1)}, f32[8,2048]{1,0:T(8,128)S(1)}) custom-call(s32[1]{0:T(128)} %bitcast.1.group_ref, s32[96]{0:T(128)S(1)} %copy-done.7, s32[32]{0:T(128)S(1)} %copy-done.6, bf16[3,2048]{1,0:T(4,128)(2,1)S(1)} %copy-done.2, bf16[1,2048]{1,0:T(2,128)(2,1)S(1)} %copy-done.3, ...), custom_call_target="tpu_custom_call" | custom-call | tf_op jit(solution)/shard_map/attention_0/pallas_call | solution.py:447
  13.1 0.9 %collective-permute-start.2 = (f32[16,256]{1,0:T(8,128)S(1)}, f32[16,256]{1,0:T(8,128)S(1)}, u32[]{:S(2)}, u32[]{:S(2)}) collective-permute-start(f32[16,256]{1,0:T(8,128)S(1)} %get-tuple-element.40.refs_5_.state_ref), channel_id=1, source_target_pairs={{0,8},{8,0},{16,24},{24,16},{32,40},{40,32},{48,56},{56,48},{64,72... | collective-permute-start | bytes 49160 | tf_op jit(solution)/shard_map/ppermute | solution.py:22
  14.1 2.4 %fetch_1_keys.1 = (bf16[2048,256]{1,0:T(8,128)(2,1)S(1)}, bf16[2048,128]{1,0:T(8,128)(2,1)S(1)}, bf16[2048,128]{1,0:T(8,128)(2,1)S(1)}, bf16[3,2048,128]{2,1,0:T(8,128)(2,1)S(1)}, bf16[2,2048,128]{2,1,0:T(8,128)(2,1)S(1)}) custom-call(bf16[2,2,3,2048,128]{4,3,2,1,0:T(8,128)(2,1)} %bitcast.9, bf16[2,2,1,2,2048,128]{5,4,3,2,1,0:T(8,128)(2,1)} %bitcast.14, ...), custom_call_target="tpu_custom_call" | custom-call | tf_op jit(solution)/shard_map/fetch_1_keys/pallas_call | solution.py:437
  17.6 1.2 %collective-permute-done.3 = f32[8,2048]{1,0:T(8,128)S(1)} collective-permute-done((f32[8,2048]{1,0:T(8,128)S(1)}, f32[8,2048]{1,0:T(8,128)S(1)}, u32[]{:S(2)}, u32[]{:S(2)}) %collective-permute-start.3) | collective-permute-done | bytes 65568 | tf_op jit(solution)/shard_map/ppermute | solution.py:22
  18.8 1.7 %collective-permute-start.4 = (bf16[8,2048]{1,0:T(8,128)(2,1)S(1)}, bf16[8,2048]{1,0:T(8,128)(2,1)S(1)}, u32[]{:S(2)}, u32[]{:S(2)}) collective-permute-start(bf16[8,2048]{1,0:T(8,128)(2,1)S(1)} %add_convert_fusion.1.refs_5_.p_ref), channel_id=1, source_target_pairs={{0,2},{1,3},{2,0},{3,1},{4,6},{5,7},{6,4},{7,5},{8,10},{9,11},{10,... | collective-permute-start | bytes 98312 | tf_op jit(solution)/shard_map/ppermute | solution.py:22
  20.5 2.9 %collective-permute-start.5 = (bf16[8,2048]{1,0:T(8,128)(2,1)S(1)}, bf16[8,2048]{1,0:T(8,128)(2,1)S(1)}, u32[]{:S(2)}, u32[]{:S(2)}) collective-permute-start(bf16[8,2048]{1,0:T(8,128)(2,1)S(1)} %add_convert_fusion.1.refs_5_.p_ref), channel_id=1, source_target_pairs={{0,4},{1,5},{2,6},{3,7},{4,0},{5,1},{6,2},{7,3},{8,12},{9,13},{10,... | collective-permute-start | bytes 98312 | tf_op jit(solution)/shard_map/ppermute | solution.py:22
  23.6 1.1 %leaving_second.1 = (bf16[2304,128]{1,0:T(8,128)(2,1)S(1)}, f32[8,128]{1,0:T(8,128)}) custom-call(bf16[2,2,3,2048,128]{4,3,2,1,0:T(8,128)(2,1)} %bitcast.10), custom_call_target="tpu_custom_call" | custom-call | tf_op jit(solution)/shard_map/leaving_second/pallas_call | solution.py:376
  25.3 1.7 %fetch_1_values.1 = (bf16[3,2048,128]{2,1,0:T(8,128)(2,1)S(1)}, bf16[2,2048,128]{2,1,0:T(8,128)(2,1)S(1)}) custom-call(bf16[2,2,3,2048,128]{4,3,2,1,0:T(8,128)(2,1)} %bitcast.11, bf16[2,2,1,2,2048,128]{5,4,3,2,1,0:T(8,128)(2,1)} %bitcast.15, bf16[2,2048,256]{2,1,0:T(8,128)(2,1)} %refs_2_.5, bf16[2,2048,128]{2,1,0:T(8,128)(2,1)} %refs_3_.5, ...), custom_call_target="tpu_custom_call" | custom-call | tf_op jit(solution)/shard_map/fetch_1_values/pallas_call | solution.py:437
  27.1 1.4 %collective-permute-done.6.r3_ref = bf16[8,2048]{1,0:T(8,128)(2,1)S(1)} collective-permute-done((bf16[8,2048]{1,0:T(8,128)(2,1)S(1)}, bf16[8,2048]{1,0:T(8,128)(2,1)S(1)}, u32[]{:S(2)}, u32[]{:S(2)}) %collective-permute-start.6) | collective-permute-done | bytes 32800 | tf_op jit(solution)/shard_map/ppermute | solution.py:22
  28.5 2.5 %attention_1.1 = (f32[16,256]{1,0:T(8,128)S(1)}, f32[16,256]{1,0:T(8,128)S(1)}, f32[2,128]{1,0:T(2,128)S(1)}, f32[8,2048]{1,0:T(8,128)S(1)}) custom-call(s32[1]{0:T(128)} %bitcast.1.group_ref, s32[96]{0:T(128)S(1)} %copy-done.7, s32[32]{0:T(128)S(1)} %copy-done.6, f32[8,2048]{1,0:T(8,128)S(1)} %get-tuple-element.39.before_ref, ...), custom_call_target="tpu_custom_call" | custom-call | tf_op jit(solution)/shard_map/attention_1/pallas_call | solution.py:466
  31.0 0.9 %collective-permute-start.7 = (f32[16,256]{1,0:T(8,128)S(1)}, f32[16,256]{1,0:T(8,128)S(1)}, u32[]{:S(2)}, u32[]{:S(2)}) collective-permute-start(f32[16,256]{1,0:T(8,128)S(1)} %get-tuple-element.49.state_ref), channel_id=1, source_target_pairs={{0,8},{8,0},{16,24},{24,16},{32,40},{40,32},{48,56},{56,48},{64,72... | collective-permute-start | bytes 49160 | tf_op jit(solution)/shard_map/ppermute | solution.py:22
  31.9 2.9 %collective-permute-done.7.far_ref = f32[16,256]{1,0:T(8,128)S(1)} collective-permute-done((f32[16,256]{1,0:T(8,128)S(1)}, f32[16,256]{1,0:T(8,128)S(1)}, u32[]{:S(2)}, u32[]{:S(2)}) %collective-permute-start.7) | collective-permute-done | bytes 16416 | tf_op jit(solution)/shard_map/ppermute | solution.py:22
  35.4 1.2 %collective-permute-done.8 = f32[8,2048]{1,0:T(8,128)S(1)} collective-permute-done((f32[8,2048]{1,0:T(8,128)S(1)}, f32[8,2048]{1,0:T(8,128)S(1)}, u32[]{:S(2)}, u32[]{:S(2)}) %collective-permute-start.8) | collective-permute-done | bytes 65568 | tf_op jit(solution)/shard_map/ppermute | solution.py:22
  36.7 0.7 %collective-permute-start.10 = (bf16[8,2048]{1,0:T(8,128)(2,1)S(1)}, bf16[8,2048]{1,0:T(8,128)(2,1)S(1)}, u32[]{:S(2)}, u32[]{:S(2)}) collective-permute-start(bf16[8,2048]{1,0:T(8,128)(2,1)S(1)} %add_convert_fusion.after_ref.p_ref), channel_id=1, source_target_pairs={{0,4},{1,5},{2,6},{3,7},{4,0},{5,1},{6,2},{7,3},{8,12},{9,13},{10,... | collective-permute-start | bytes 98312 | tf_op jit(solution)/shard_map/ppermute | solution.py:22
  37.3 1.1 %collective-permute-start.11 = (bf16[8,2048]{1,0:T(8,128)(2,1)S(1)}, bf16[8,2048]{1,0:T(8,128)(2,1)S(1)}, u32[]{:S(2)}, u32[]{:S(2)}) collective-permute-start(bf16[8,2048]{1,0:T(8,128)(2,1)S(1)} %add_convert_fusion.after_ref.p_ref), channel_id=1, source_target_pairs={{0,6},{1,7},{2,4},{3,5},{4,2},{5,3},{6,0},{7,1},{8,14},{9,15},{10,... | collective-permute-start | bytes 98312 | tf_op jit(solution)/shard_map/ppermute | solution.py:22
  38.5 1.8 %collective-permute-start.9 = (bf16[8,2048]{1,0:T(8,128)(2,1)S(1)}, bf16[8,2048]{1,0:T(8,128)(2,1)S(1)}, u32[]{:S(2)}, u32[]{:S(2)}) collective-permute-start(bf16[8,2048]{1,0:T(8,128)(2,1)S(1)} %add_convert_fusion.after_ref.p_ref), channel_id=1, source_target_pairs={{0,2},{1,3},{2,0},{3,1},{4,6},{5,7},{6,4},{7,5},{8,10},{9,11},{10,... | collective-permute-start | bytes 98312 | tf_op jit(solution)/shard_map/ppermute | solution.py:22
  40.8 3.1 %store_first.1 = (bf16[2,2,2048,128]{3,2,1,0:T(8,128)(2,1)}, bf16[4,16,128]{2,1,0:T(8,128)(2,1)S(1)}, f32[8,128]{1,0:T(8,128)S(1)}) custom-call(s32[1]{0:T(128)} %dynamic_slice.9.length_ref, bf16[5888,128]{1,0:T(8,128)(2,1)} %collective-permute-done.first_ref, bf16[8,2048]{1,0:T(8,128)(2,1)S(1)} %add_convert_fusion.after_ref.p_ref), custom_call_target="tpu_custom_call" | custom-call | tf_op jit(solution)/shard_map/store_first/pallas_call | solution.py:477
  44.6 2.0 %collective-permute-start.12 = (f32[1,2560]{1,0:T(1,128)S(1)}, f32[1,2560]{1,0:T(1,128)S(1)}, u32[]{:S(2)}, u32[]{:S(2)}) collective-permute-start(f32[1,2560]{1,0:T(1,128)S(1)} %get-tuple-element.57), channel_id=1, source_target_pairs={{0,128},{8,136},{16,144},{24,152},{32,160},{40,168},{48,176},{56,1... | collective-permute-start | bytes 30728 | tf_op jit(solution)/shard_map/ppermute | solution.py:22
  46.6 4.6 %collective-permute-done.13.second_ref = bf16[2304,128]{1,0:T(8,128)(2,1)S(1)} collective-permute-done((bf16[2304,128]{1,0:T(8,128)(2,1)S(1)}, bf16[2304,128]{1,0:T(8,128)(2,1)S(1)}, u32[]{:S(2)}, u32[]{:S(2)}) %collective-permute-start.13) | collective-permute-done | bytes 589856 | tf_op jit(solution)/shard_map/ppermute | solution.py:22
  51.3 1.1 %arrival.1 = (f32[3,2048]{1,0:T(4,128)}, bf16[2,2,2048,128]{3,2,1,0:T(8,128)(2,1)}) custom-call(f32[8,128]{1,0:T(8,128)S(1)} %get-tuple-element.51.place_ref, f32[2,2048]{1,0:T(2,128)S(1)} %get-tuple-element.56.stay_ref, f32[1,2560]{1,0:T(1,128)S(1)} %collective-permute-done.12.arrived_ref, ...), custom_call_target="tpu_custom_call", output_to_operand_aliasing={{1}: (5, {})} | custom-call | tf_op jit(solution)/shard_map/arrival/pallas_call | solution.py:507
  (44 shorter events, 4.2 us)
Async XLA Ops:
  0.6 4.6 %copy-start.3 = (bf16[1,2048]{1,0:T(2,128)(2,1)S(1)}, bf16[1,2048]{1,0:T(2,128)(2,1)}, u32[]{:S(2)}) copy-start(bf16[1,2048]{1,0:T(2,128)(2,1)} %own_long_ref.1) | copy-start | bytes 12292
  0.6 6.5 %copy-start.6 = (s32[32]{0:T(128)S(1)}, s32[32]{0:T(128)}, u32[]{:S(2)}) copy-start(s32[32]{0:T(128)} %long_lengths_ref.3) | copy-start | bytes 388
  0.7 6.5 %copy-start.7 = (s32[96]{0:T(128)S(1)}, s32[96]{0:T(128)}, u32[]{:S(2)}) copy-start(s32[96]{0:T(128)} %lengths_ref.3) | copy-start | bytes 1156
  0.7 6.7 %copy-start.8 = (f32[128]{0:T(128)S(1)}, f32[128]{0:T(128)}, u32[]{:S(2)}) copy-start(f32[128]{0:T(128)} %constant.43.clone) | copy-start | bytes 1540
  0.7 6.7 %copy-start.9 = (f32[128]{0:T(128)S(1)}, f32[128]{0:T(128)}, u32[]{:S(2)}) copy-start(f32[128]{0:T(128)} %constant.44.clone) | copy-start | bytes 1540
  2.1 38.8 %collective-permute-start = (bf16[5888,128]{1,0:T(8,128)(2,1)S(1)}, bf16[5888,128]{1,0:T(8,128)(2,1)}, u32[]{:S(2)}, u32[]{:S(2)}) collective-permute-start(bf16[5888,128]{1,0:T(8,128)(2,1)S(1)} %get-tuple-element.33.refs_5_), channel_id=1, source_target_pairs={{0,128},{8,136},{16,144},{24,152},{32,160},{40,168},{48,176},{56,1... | collective-permute-start | bytes 4521992 | tf_op jit(solution)/shard_map/ppermute | solution.py:22
  5.2 4.7 %collective-permute-start.1 = (bf16[1,2048]{1,0:T(2,128)(2,1)S(1)}, bf16[1,2048]{1,0:T(2,128)(2,1)S(1)}, u32[]{:S(2)}, u32[]{:S(2)}) collective-permute-start(bf16[1,2048]{1,0:T(2,128)(2,1)S(1)} %copy-done.3), channel_id=1, source_target_pairs={{0,8},{8,0},{16,24},{24,16},{32,40},{40,32},{48,56},{56,48},{64,72... | collective-permute-start | bytes 12296 | tf_op jit(solution)/shard_map/ppermute | solution.py:22
  7.5 2.5 %copy-start.1 = (f32[2,2048]{1,0:T(2,128)S(1)}, f32[2,2048]{1,0:T(2,128)}, u32[]{:S(2)}) copy-start(f32[2,2048]{1,0:T(2,128)} %rest_0_.3) | copy-start | bytes 49156
  7.5 2.5 %copy-start.2 = (bf16[3,2048]{1,0:T(4,128)(2,1)S(1)}, bf16[3,2048]{1,0:T(4,128)(2,1)}, u32[]{:S(2)}) copy-start(bf16[3,2048]{1,0:T(4,128)(2,1)} %tokens_ref.1) | copy-start | bytes 36868
  7.5 2.5 %copy-start.4 = (f32[2,128]{1,0:T(2,128)S(1)}, f32[2,128]{1,0:T(2,128)}, u32[]{:S(2)}) copy-start(f32[2,128]{1,0:T(2,128)} %rest_1_.3) | copy-start | bytes 3076
  7.5 2.5 %copy-start.5 = (f32[2,128]{1,0:T(2,128)S(1)}, f32[2,128]{1,0:T(2,128)}, u32[]{:S(2)}) copy-start(f32[2,128]{1,0:T(2,128)} %rest_2_.3) | copy-start | bytes 3076
  13.1 3.8 %copy-start = (bf16[2,256,2048]{2,1,0:T(8,128)(2,1)S(1)}, bf16[2,256,2048]{2,1,0:T(8,128)(2,1)}, u32[]{:S(2)}) copy-start(bf16[2,256,2048]{2,1,0:T(8,128)(2,1)} %w_ref.3) | copy-start | bytes 6291460
  13.1 3.8 %collective-permute-start.2 = (f32[16,256]{1,0:T(8,128)S(1)}, f32[16,256]{1,0:T(8,128)S(1)}, u32[]{:S(2)}, u32[]{:S(2)}) collective-permute-start(f32[16,256]{1,0:T(8,128)S(1)} %get-tuple-element.40.refs_5_.state_ref), channel_id=1, source_target_pairs={{0,8},{8,0},{16,24},{24,16},{32,40},{40,32},{48,56},{56,48},{64,72... | collective-permute-start | bytes 49160 | tf_op jit(solution)/shard_map/ppermute | solution.py:22
  17.5 1.3 %collective-permute-start.3 = (f32[8,2048]{1,0:T(8,128)S(1)}, f32[8,2048]{1,0:T(8,128)S(1)}, u32[]{:S(2)}, u32[]{:S(2)}) collective-permute-start(f32[8,2048]{1,0:T(8,128)S(1)} %out_projection_0.1), channel_id=1, source_target_pairs={{0,1},{1,0},{2,3},{3,2},{4,5},{5,4},{6,7},{7,6},{8,9},{9,8},{10,11... | collective-permute-start | bytes 196616 | tf_op jit(solution)/shard_map/ppermute | solution.py:22
  18.8 8.2 %collective-permute-start.4 = (bf16[8,2048]{1,0:T(8,128)(2,1)S(1)}, bf16[8,2048]{1,0:T(8,128)(2,1)S(1)}, u32[]{:S(2)}, u32[]{:S(2)}) collective-permute-start(bf16[8,2048]{1,0:T(8,128)(2,1)S(1)} %add_convert_fusion.1.refs_5_.p_ref), channel_id=1, source_target_pairs={{0,2},{1,3},{2,0},{3,1},{4,6},{5,7},{6,4},{7,5},{8,10},{9,11},{10,... | collective-permute-start | bytes 98312 | tf_op jit(solution)/shard_map/ppermute | solution.py:22
  20.5 6.6 %collective-permute-start.5 = (bf16[8,2048]{1,0:T(8,128)(2,1)S(1)}, bf16[8,2048]{1,0:T(8,128)(2,1)S(1)}, u32[]{:S(2)}, u32[]{:S(2)}) collective-permute-start(bf16[8,2048]{1,0:T(8,128)(2,1)S(1)} %add_convert_fusion.1.refs_5_.p_ref), channel_id=1, source_target_pairs={{0,4},{1,5},{2,6},{3,7},{4,0},{5,1},{6,2},{7,3},{8,12},{9,13},{10,... | collective-permute-start | bytes 98312 | tf_op jit(solution)/shard_map/ppermute | solution.py:22
  23.4 5.1 %collective-permute-start.6 = (bf16[8,2048]{1,0:T(8,128)(2,1)S(1)}, bf16[8,2048]{1,0:T(8,128)(2,1)S(1)}, u32[]{:S(2)}, u32[]{:S(2)}) collective-permute-start(bf16[8,2048]{1,0:T(8,128)(2,1)S(1)} %add_convert_fusion.1.refs_5_.p_ref), channel_id=1, source_target_pairs={{0,6},{1,7},{2,4},{3,5},{4,2},{5,3},{6,0},{7,1},{8,14},{9,15},{10,... | collective-permute-start | bytes 98312 | tf_op jit(solution)/shard_map/ppermute | solution.py:22
  24.7 26.4 %collective-permute-start.13 = (bf16[2304,128]{1,0:T(8,128)(2,1)S(1)}, bf16[2304,128]{1,0:T(8,128)(2,1)S(1)}, u32[]{:S(2)}, u32[]{:S(2)}) collective-permute-start(bf16[2304,128]{1,0:T(8,128)(2,1)S(1)} %get-tuple-element.58), channel_id=1, source_target_pairs={{0,128},{8,136},{16,144},{24,152},{32,160},{40,168},{48,176},{56,1... | collective-permute-start | bytes 1769480 | tf_op jit(solution)/shard_map/ppermute | solution.py:22
  31.0 3.8 %collective-permute-start.7 = (f32[16,256]{1,0:T(8,128)S(1)}, f32[16,256]{1,0:T(8,128)S(1)}, u32[]{:S(2)}, u32[]{:S(2)}) collective-permute-start(f32[16,256]{1,0:T(8,128)S(1)} %get-tuple-element.49.state_ref), channel_id=1, source_target_pairs={{0,8},{8,0},{16,24},{24,16},{32,40},{40,32},{48,56},{56,48},{64,72... | collective-permute-start | bytes 49160 | tf_op jit(solution)/shard_map/ppermute | solution.py:22
  35.3 1.3 %collective-permute-start.8 = (f32[8,2048]{1,0:T(8,128)S(1)}, f32[8,2048]{1,0:T(8,128)S(1)}, u32[]{:S(2)}, u32[]{:S(2)}) collective-permute-start(f32[8,2048]{1,0:T(8,128)S(1)} %out_projection_1.1), channel_id=1, source_target_pairs={{0,1},{1,0},{2,3},{3,2},{4,5},{5,4},{6,7},{7,6},{8,9},{9,8},{10,11... | collective-permute-start | bytes 196616 | tf_op jit(solution)/shard_map/ppermute | solution.py:22
  36.7 7.2 %collective-permute-start.10 = (bf16[8,2048]{1,0:T(8,128)(2,1)S(1)}, bf16[8,2048]{1,0:T(8,128)(2,1)S(1)}, u32[]{:S(2)}, u32[]{:S(2)}) collective-permute-start(bf16[8,2048]{1,0:T(8,128)(2,1)S(1)} %add_convert_fusion.after_ref.p_ref), channel_id=1, source_target_pairs={{0,4},{1,5},{2,6},{3,7},{4,0},{5,1},{6,2},{7,3},{8,12},{9,13},{10,... | collective-permute-start | bytes 98312 | tf_op jit(solution)/shard_map/ppermute | solution.py:22
  37.3 6.6 %collective-permute-start.11 = (bf16[8,2048]{1,0:T(8,128)(2,1)S(1)}, bf16[8,2048]{1,0:T(8,128)(2,1)S(1)}, u32[]{:S(2)}, u32[]{:S(2)}) collective-permute-start(bf16[8,2048]{1,0:T(8,128)(2,1)S(1)} %add_convert_fusion.after_ref.p_ref), channel_id=1, source_target_pairs={{0,6},{1,7},{2,4},{3,5},{4,2},{5,3},{6,0},{7,1},{8,14},{9,15},{10,... | collective-permute-start | bytes 98312 | tf_op jit(solution)/shard_map/ppermute | solution.py:22
  38.5 5.5 %collective-permute-start.9 = (bf16[8,2048]{1,0:T(8,128)(2,1)S(1)}, bf16[8,2048]{1,0:T(8,128)(2,1)S(1)}, u32[]{:S(2)}, u32[]{:S(2)}) collective-permute-start(bf16[8,2048]{1,0:T(8,128)(2,1)S(1)} %add_convert_fusion.after_ref.p_ref), channel_id=1, source_target_pairs={{0,2},{1,3},{2,0},{3,1},{4,6},{5,7},{6,4},{7,5},{8,10},{9,11},{10,... | collective-permute-start | bytes 98312 | tf_op jit(solution)/shard_map/ppermute | solution.py:22
  44.6 6.7 %collective-permute-start.12 = (f32[1,2560]{1,0:T(1,128)S(1)}, f32[1,2560]{1,0:T(1,128)S(1)}, u32[]{:S(2)}, u32[]{:S(2)}) collective-permute-start(f32[1,2560]{1,0:T(1,128)S(1)} %get-tuple-element.57), channel_id=1, source_target_pairs={{0,128},{8,136},{16,144},{24,152},{32,160},{40,168},{48,176},{56,1... | collective-permute-start | bytes 30728 | tf_op jit(solution)/shard_map/ppermute | solution.py:22

commit v11 on v10

--- a/solution.py
+++ b/solution.py
@@ -214,6 +214,27 @@
         copy.wait()
 
 
+def leaving_second_kernel(begin, end, cache_ref, out_ref, buffer, semaphores):
+    copies = []
+    for n, (i, j, place, size, at) in enumerate(runs(begin, end)):
+        piece = pl.ds(at, size)
+        copies.append(
+            (
+                pltpu.make_async_copy(
+                    cache_ref.at[i, j, 2, pl.ds(place, size)], buffer.at[piece], semaphores.at[0, n]
+                ),
+                pltpu.make_async_copy(buffer.at[piece], out_ref.at[piece], semaphores.at[1, n]),
+            )
+        )
+    for read, _ in copies:
+        read.start()
+    for read, write in copies:
+        read.wait()
+        write.start()
+    for _, write in copies:
+        write.wait()
+
+
 def store_kernel(
     length_ref, first_ref, after_ref, stored_ref, blocks_ref, place_ref, buffer, semaphores
 ):
@@ -387,7 +408,18 @@
         )(held)
 
     leaving_first, _ = leaving(0, FIRST, "leaving_first")
-    leaving_second, _ = leaving(FIRST, SECOND, "leaving_second")
+    leaving_second = pl.pallas_call(
+        functools.partial(leaving_second_kernel, FIRST, 4 * PER),
+        out_shape=pltpu.HBM((SECOND * UNIT, 128), jnp.bfloat16),
+        in_specs=[ANY],
+        out_specs=ANY,
+        scratch_shapes=[
+            pltpu.VMEM((SECOND * UNIT, 128), jnp.bfloat16),
+            pltpu.SemaphoreType.DMA((2, 4)),
+        ],
+        compiler_params=small,
+        name="leaving_second",
+    )(held)
     first, second = (
         permute(piece, "replica", lambda i: (i + groups // 2) % groups)
         for piece in (leaving_first, leaving_second)
@@ -489,7 +521,7 @@
         ],
         compiler_params=pltpu.CompilerParams(vmem_limit_bytes=4 * 2**20),
         name="store_first",
-    )(arrived_len, in_hbm(first), terms[0])
+    )(arrived_len, in_vmem(first), terms[0])
     stay, long_out, leave = pl.pallas_call(
         final_kernel,
         out_shape=(

time: 52.6 us -> 53.7 us (1.021)
  Pallas kernels: 20.4 us -> 23.4 us
  waiting for transfers between devices: 12 us -> 9.34 us
  starting transfers between devices: 18 us -> 18.8 us
    ppermute x14, waiting for transfers between devices: 12 us -> 9.34 us  [permute(): return lax.ppermute(value, axis, pairs)]
    pallas_call x0 -> x1, Pallas kernels: none -> 1.94 us  [local(): pl.pallas_call(functools.partial(leaving_second_kernel, FIRST, 4 * PER),...]
    pallas_call x2 -> x1, Pallas kernels: 2.51 us -> 1.39 us  [leaving(): pl.pallas_call(functools.partial(leaving_kernel, begin, begin + count), o...]
    pallas_call x1, Pallas kernels: 1.07 us -> 2.14 us  [local(): pl.pallas_call(arrival_kernel, out_shape=(pltpu.HBM((3, 2048), jnp.float3...]
    pallas_call x1, Pallas kernels: 3.07 us -> 4.1 us  [local(): pl.pallas_call(store_kernel, out_shape=(pltpu.HBM((2, 2, 2048, 128), jnp....]
    ppermute x14, starting transfers between devices: 18 us -> 18.8 us  [permute(): return lax.ppermute(value, axis, pairs)]
  transfers between devices with their start and end apart: 14 -> 14, of which waited for: 7 -> 6; matrix products, arithmetic and copies ran while one was open for 2% -> 2% of each run, Pallas kernels for 34% -> 37%
where the time goes in v11:
time: 53.7 us; the launch traced here: 53.4 us
  Pallas kernels  23.4 us (44%)
  starting transfers between devices  18.8 us (35%)
  waiting for transfers between devices  9.34 us (17%)
  between operations  0.9 us (2%)
  local copies, waits for them, and re-layouts  0.79 us (1%)
    ppermute x14, starting transfers between devices, permute(): return lax.ppermute(value, axis, pairs)  18.8 us
    ppermute x14, waiting for transfers between devices, permute(): return lax.ppermute(value, axis, pairs)  9.34 us
    pallas_call x3, Pallas kernels, fetch(): pl.pallas_call(functools.partial(fetch_kernel, layer, which), out_shape=t...  6.54 us
    pallas_call x1, Pallas kernels, local(): pl.pallas_call(store_kernel, out_shape=(pltpu.HBM((2, 2, 2048, 128), jnp....  4.1 us
    pallas_call x1, Pallas kernels, local(): pl.pallas_call(first_kernel, out_shape=out_shape, in_specs=[SM] * 3 + [VM...  3.16 us
    pallas_call x1, Pallas kernels, local(): pl.pallas_call(second_kernel, out_shape=out_shape, in_specs=[SM] * 3 + [V...  2.47 us
    pallas_call x1, Pallas kernels, local(): pl.pallas_call(arrival_kernel, out_shape=(pltpu.HBM((3, 2048), jnp.float3...  2.14 us
    pallas_call x1, Pallas kernels, local(): pl.pallas_call(functools.partial(leaving_second_kernel, FIRST, 4 * PER),...  1.94 us
  transfers between devices with their start and end apart: 14, of which 6 were waited for; matrix products, arithmetic and copies ran while one was open for 2% of the time, Pallas kernels for 37%

profile of v11, /device:TPU:64, one launch (start us, length us, event | category | flops | bytes accessed | tf_op | source)
XLA Modules:
  0.0 53.4 jit_solution(1748621111589775037)
XLA Ops:
  0.7 1.4 %leaving_first.1 = (bf16[5888,128]{1,0:T(8,128)(2,1)S(1)}, f32[8,128]{1,0:T(8,128)}) custom-call(bf16[2,2,3,2048,128]{4,3,2,1,0:T(8,128)(2,1)} %bitcast.6), custom_call_target="tpu_custom_call" | custom-call | tf_op jit(solution)/shard_map/leaving_first/pallas_call | solution.py:397
  2.1 3.1 %collective-permute-start = (bf16[5888,128]{1,0:T(8,128)(2,1)S(1)}, bf16[5888,128]{1,0:T(8,128)(2,1)S(1)}, u32[]{:S(2)}, u32[]{:S(2)}) collective-permute-start(bf16[5888,128]{1,0:T(8,128)(2,1)S(1)} %get-tuple-element.32.refs_5_), channel_id=1, source_target_pairs={{0,128},{8,136},{16,144},{24,152},{32,160},{40,168},{48,176},{56,1... | collective-permute-start | bytes 4521992 | tf_op jit(solution)/shard_map/ppermute | solution.py:22
  5.2 1.9 %collective-permute-start.1 = (bf16[1,2048]{1,0:T(2,128)(2,1)S(1)}, bf16[1,2048]{1,0:T(2,128)(2,1)S(1)}, u32[]{:S(2)}, u32[]{:S(2)}) collective-permute-start(bf16[1,2048]{1,0:T(2,128)(2,1)S(1)} %copy-done.3), channel_id=1, source_target_pairs={{0,8},{8,0},{16,24},{24,16},{32,40},{40,32},{48,56},{56,48},{64,72... | collective-permute-start | bytes 12296 | tf_op jit(solution)/shard_map/ppermute | solution.py:22
  7.5 2.4 %fetch_0.1 = (bf16[2048,256]{1,0:T(8,128)(2,1)S(1)}, bf16[2048,128]{1,0:T(8,128)(2,1)S(1)}, bf16[2048,128]{1,0:T(8,128)(2,1)S(1)}, bf16[3,2048,128]{2,1,0:T(8,128)(2,1)S(1)}, bf16[2,2048,128]{2,1,0:T(8,128)(2,1)S(1)}) custom-call(bf16[2,2,3,2048,128]{4,3,2,1,0:T(8,128)(2,1)} %bitcast.7, bf16[2,2,1,2,2048,128]{5,4,3,2,1,0:T(8,128)(2,1)} %bitcast.12, ...), custom_call_target="tpu_custom_call" | custom-call | tf_op jit(solution)/shard_map/fetch_0/pallas_call | solution.py:469
  10.0 3.2 %attention_0.1 = (f32[16,256]{1,0:T(8,128)S(1)}, f32[16,256]{1,0:T(8,128)S(1)}, f32[2,128]{1,0:T(2,128)S(1)}, f32[8,2048]{1,0:T(8,128)S(1)}) custom-call(s32[1]{0:T(128)} %bitcast.1.group_ref, s32[96]{0:T(128)S(1)} %copy-done.7, s32[32]{0:T(128)S(1)} %copy-done.6, bf16[3,2048]{1,0:T(4,128)(2,1)S(1)} %copy-done.2, bf16[1,2048]{1,0:T(2,128)(2,1)S(1)} %copy-done.3, ...), custom_call_target="tpu_custom_call" | custom-call | tf_op jit(solution)/shard_map/attention_0/pallas_call | solution.py:479
  13.1 0.9 %collective-permute-start.2 = (f32[16,256]{1,0:T(8,128)S(1)}, f32[16,256]{1,0:T(8,128)S(1)}, u32[]{:S(2)}, u32[]{:S(2)}) collective-permute-start(f32[16,256]{1,0:T(8,128)S(1)} %get-tuple-element.39.refs_5_.state_ref), channel_id=1, source_target_pairs={{0,8},{8,0},{16,24},{24,16},{32,40},{40,32},{48,56},{56,48},{64,72... | collective-permute-start | bytes 49160 | tf_op jit(solution)/shard_map/ppermute | solution.py:22
  14.1 2.4 %fetch_1_keys.1 = (bf16[2048,256]{1,0:T(8,128)(2,1)S(1)}, bf16[2048,128]{1,0:T(8,128)(2,1)S(1)}, bf16[2048,128]{1,0:T(8,128)(2,1)S(1)}, bf16[3,2048,128]{2,1,0:T(8,128)(2,1)S(1)}, bf16[2,2048,128]{2,1,0:T(8,128)(2,1)S(1)}) custom-call(bf16[2,2,3,2048,128]{4,3,2,1,0:T(8,128)(2,1)} %bitcast.9, bf16[2,2,1,2,2048,128]{5,4,3,2,1,0:T(8,128)(2,1)} %bitcast.14, ...), custom_call_target="tpu_custom_call" | custom-call | tf_op jit(solution)/shard_map/fetch_1_keys/pallas_call | solution.py:469
  17.6 1.2 %collective-permute-done.3 = f32[8,2048]{1,0:T(8,128)S(1)} collective-permute-done((f32[8,2048]{1,0:T(8,128)S(1)}, f32[8,2048]{1,0:T(8,128)S(1)}, u32[]{:S(2)}, u32[]{:S(2)}) %collective-permute-start.3) | collective-permute-done | bytes 65568 | tf_op jit(solution)/shard_map/ppermute | solution.py:22
  18.8 1.7 %collective-permute-start.4 = (bf16[8,2048]{1,0:T(8,128)(2,1)S(1)}, bf16[8,2048]{1,0:T(8,128)(2,1)S(1)}, u32[]{:S(2)}, u32[]{:S(2)}) collective-permute-start(bf16[8,2048]{1,0:T(8,128)(2,1)S(1)} %add_convert_fusion.1.refs_5_.p_ref), channel_id=1, source_target_pairs={{0,2},{1,3},{2,0},{3,1},{4,6},{5,7},{6,4},{7,5},{8,10},{9,11},{10,... | collective-permute-start | bytes 98312 | tf_op jit(solution)/shard_map/ppermute | solution.py:22
  20.5 2.9 %collective-permute-start.5 = (bf16[8,2048]{1,0:T(8,128)(2,1)S(1)}, bf16[8,2048]{1,0:T(8,128)(2,1)S(1)}, u32[]{:S(2)}, u32[]{:S(2)}) collective-permute-start(bf16[8,2048]{1,0:T(8,128)(2,1)S(1)} %add_convert_fusion.1.refs_5_.p_ref), channel_id=1, source_target_pairs={{0,4},{1,5},{2,6},{3,7},{4,0},{5,1},{6,2},{7,3},{8,12},{9,13},{10,... | collective-permute-start | bytes 98312 | tf_op jit(solution)/shard_map/ppermute | solution.py:22
  23.6 1.9 %leaving_second.1 = bf16[2304,128]{1,0:T(8,128)(2,1)} custom-call(bf16[2,2,3,2048,128]{4,3,2,1,0:T(8,128)(2,1)} %bitcast.10), custom_call_target="tpu_custom_call" | custom-call | tf_op jit(solution)/shard_map/leaving_second/pallas_call | solution.py:411
  26.2 1.7 %fetch_1_values.1 = (bf16[3,2048,128]{2,1,0:T(8,128)(2,1)S(1)}, bf16[2,2048,128]{2,1,0:T(8,128)(2,1)S(1)}) custom-call(bf16[2,2,3,2048,128]{4,3,2,1,0:T(8,128)(2,1)} %bitcast.11, bf16[2,2,1,2,2048,128]{5,4,3,2,1,0:T(8,128)(2,1)} %bitcast.15, bf16[2,2048,256]{2,1,0:T(8,128)(2,1)} %refs_2_.5, bf16[2,2048,128]{2,1,0:T(8,128)(2,1)} %refs_3_.5, ...), custom_call_target="tpu_custom_call" | custom-call | tf_op jit(solution)/shard_map/fetch_1_values/pallas_call | solution.py:469
  28.5 2.5 %attention_1.1 = (f32[16,256]{1,0:T(8,128)S(1)}, f32[16,256]{1,0:T(8,128)S(1)}, f32[2,128]{1,0:T(2,128)S(1)}, f32[8,2048]{1,0:T(8,128)S(1)}) custom-call(s32[1]{0:T(128)} %bitcast.1.group_ref, s32[96]{0:T(128)S(1)} %copy-done.7, s32[32]{0:T(128)S(1)} %copy-done.6, f32[8,2048]{1,0:T(8,128)S(1)} %get-tuple-element.38.before_ref, ...), custom_call_target="tpu_custom_call" | custom-call | tf_op jit(solution)/shard_map/attention_1/pallas_call | solution.py:498
  31.0 0.9 %collective-permute-start.7 = (f32[16,256]{1,0:T(8,128)S(1)}, f32[16,256]{1,0:T(8,128)S(1)}, u32[]{:S(2)}, u32[]{:S(2)}) collective-permute-start(f32[16,256]{1,0:T(8,128)S(1)} %get-tuple-element.48.state_ref), channel_id=1, source_target_pairs={{0,8},{8,0},{16,24},{24,16},{32,40},{40,32},{48,56},{56,48},{64,72... | collective-permute-start | bytes 49160 | tf_op jit(solution)/shard_map/ppermute | solution.py:22
  31.9 2.9 %collective-permute-done.7.far_ref = f32[16,256]{1,0:T(8,128)S(1)} collective-permute-done((f32[16,256]{1,0:T(8,128)S(1)}, f32[16,256]{1,0:T(8,128)S(1)}, u32[]{:S(2)}, u32[]{:S(2)}) %collective-permute-start.7) | collective-permute-done | bytes 16416 | tf_op jit(solution)/shard_map/ppermute | solution.py:22
  35.4 1.2 %collective-permute-done.8 = f32[8,2048]{1,0:T(8,128)S(1)} collective-permute-done((f32[8,2048]{1,0:T(8,128)S(1)}, f32[8,2048]{1,0:T(8,128)S(1)}, u32[]{:S(2)}, u32[]{:S(2)}) %collective-permute-start.8) | collective-permute-done | bytes 65568 | tf_op jit(solution)/shard_map/ppermute | solution.py:22
  36.7 1.5 %collective-permute-start.10 = (bf16[8,2048]{1,0:T(8,128)(2,1)S(1)}, bf16[8,2048]{1,0:T(8,128)(2,1)S(1)}, u32[]{:S(2)}, u32[]{:S(2)}) collective-permute-start(bf16[8,2048]{1,0:T(8,128)(2,1)S(1)} %add_convert_fusion.after_ref.p_ref), channel_id=1, source_target_pairs={{0,4},{1,5},{2,6},{3,7},{4,0},{5,1},{6,2},{7,3},{8,12},{9,13},{10,... | collective-permute-start | bytes 98312 | tf_op jit(solution)/shard_map/ppermute | solution.py:22
  38.2 1.1 %collective-permute-start.11 = (bf16[8,2048]{1,0:T(8,128)(2,1)S(1)}, bf16[8,2048]{1,0:T(8,128)(2,1)S(1)}, u32[]{:S(2)}, u32[]{:S(2)}) collective-permute-start(bf16[8,2048]{1,0:T(8,128)(2,1)S(1)} %add_convert_fusion.after_ref.p_ref), channel_id=1, source_target_pairs={{0,6},{1,7},{2,4},{3,5},{4,2},{5,3},{6,0},{7,1},{8,14},{9,15},{10,... | collective-permute-start | bytes 98312 | tf_op jit(solution)/shard_map/ppermute | solution.py:22
  39.3 1.0 %collective-permute-start.9 = (bf16[8,2048]{1,0:T(8,128)(2,1)S(1)}, bf16[8,2048]{1,0:T(8,128)(2,1)S(1)}, u32[]{:S(2)}, u32[]{:S(2)}) collective-permute-start(bf16[8,2048]{1,0:T(8,128)(2,1)S(1)} %add_convert_fusion.after_ref.p_ref), channel_id=1, source_target_pairs={{0,2},{1,3},{2,0},{3,1},{4,6},{5,7},{6,4},{7,5},{8,10},{9,11},{10,... | collective-permute-start | bytes 98312 | tf_op jit(solution)/shard_map/ppermute | solution.py:22
  40.8 4.1 %store_first.1 = (bf16[2,2,2048,128]{3,2,1,0:T(8,128)(2,1)}, bf16[4,16,128]{2,1,0:T(8,128)(2,1)S(1)}, f32[8,128]{1,0:T(8,128)S(1)}) custom-call(s32[1]{0:T(128)} %dynamic_slice.9.length_ref, bf16[5888,128]{1,0:T(8,128)(2,1)S(1)} %collective-permute-done.first_ref, bf16[8,2048]{1,0:T(8,128)(2,1)S(1)} %add_convert_fusion.after_ref.p_ref), custom_call_target="tpu_custom_call" | custom-call | tf_op jit(solution)/shard_map/store_first/pallas_call | solution.py:509
  45.0 0.6 %final_rows.1 = (f32[2,2048]{1,0:T(2,128)S(1)}, f32[1,2048]{1,0:T(1,128)}, f32[1,2560]{1,0:T(1,128)S(1)}) custom-call(s32[1]{0:T(128)} %bitcast.1.group_ref, f32[8,2048]{1,0:T(8,128)S(1)} %get-tuple-element.51.before_ref, bf16[8,2048]{1,0:T(8,128)(2,1)S(1)} %add_convert_fusion.after_ref.p_ref, bf16[8,2048]{1,0:T(8,128)(2,1)S(1)} %collective-permute-done.9.r1_ref, ...), custom_call_target="tpu_custom_call" | custom-call | tf_op jit(solution)/shard_map/final_rows/pallas_call | solution.py:525
  45.6 2.8 %collective-permute-start.12 = (f32[1,2560]{1,0:T(1,128)S(1)}, f32[1,2560]{1,0:T(1,128)S(1)}, u32[]{:S(2)}, u32[]{:S(2)}) collective-permute-start(f32[1,2560]{1,0:T(1,128)S(1)} %get-tuple-element.56), channel_id=1, source_target_pairs={{0,128},{8,136},{16,144},{24,152},{32,160},{40,168},{48,176},{56,1... | collective-permute-start | bytes 30728 | tf_op jit(solution)/shard_map/ppermute | solution.py:22
  48.4 2.8 %collective-permute-done.13.second_ref = bf16[2304,128]{1,0:T(8,128)(2,1)} collective-permute-done((bf16[2304,128]{1,0:T(8,128)(2,1)}, bf16[2304,128]{1,0:T(8,128)(2,1)}, u32[]{:S(2)}, u32[]{:S(2)}) %collective-permute-start.13) | collective-permute-done | bytes 589856 | tf_op jit(solution)/shard_map/ppermute | solution.py:22
  51.3 2.1 %arrival.1 = (f32[3,2048]{1,0:T(4,128)}, bf16[2,2,2048,128]{3,2,1,0:T(8,128)(2,1)}) custom-call(f32[8,128]{1,0:T(8,128)S(1)} %get-tuple-element.50.place_ref, f32[2,2048]{1,0:T(2,128)S(1)} %get-tuple-element.55.stay_ref, f32[1,2560]{1,0:T(1,128)S(1)} %collective-permute-done.12.arrived_ref, ...), custom_call_target="tpu_custom_call", output_to_operand_aliasing={{1}: (5, {})} | custom-call | tf_op jit(solution)/shard_map/arrival/pallas_call | solution.py:539
  (44 shorter events, 4.1 us)
Async XLA Ops:
  0.6 4.6 %copy-start.3 = (bf16[1,2048]{1,0:T(2,128)(2,1)S(1)}, bf16[1,2048]{1,0:T(2,128)(2,1)}, u32[]{:S(2)}) copy-start(bf16[1,2048]{1,0:T(2,128)(2,1)} %own_long_ref.1) | copy-start | bytes 12292
  0.6 6.5 %copy-start.6 = (s32[32]{0:T(128)S(1)}, s32[32]{0:T(128)}, u32[]{:S(2)}) copy-start(s32[32]{0:T(128)} %long_lengths_ref.3) | copy-start | bytes 388
  0.7 6.5 %copy-start.7 = (s32[96]{0:T(128)S(1)}, s32[96]{0:T(128)}, u32[]{:S(2)}) copy-start(s32[96]{0:T(128)} %lengths_ref.3) | copy-start | bytes 1156
  0.7 6.7 %copy-start.8 = (f32[128]{0:T(128)S(1)}, f32[128]{0:T(128)}, u32[]{:S(2)}) copy-start(f32[128]{0:T(128)} %constant.43.clone) | copy-start | bytes 1540
  0.7 6.7 %copy-start.9 = (f32[128]{0:T(128)S(1)}, f32[128]{0:T(128)}, u32[]{:S(2)}) copy-start(f32[128]{0:T(128)} %constant.44.clone) | copy-start | bytes 1540
  2.1 38.8 %collective-permute-start = (bf16[5888,128]{1,0:T(8,128)(2,1)S(1)}, bf16[5888,128]{1,0:T(8,128)(2,1)S(1)}, u32[]{:S(2)}, u32[]{:S(2)}) collective-permute-start(bf16[5888,128]{1,0:T(8,128)(2,1)S(1)} %get-tuple-element.32.refs_5_), channel_id=1, source_target_pairs={{0,128},{8,136},{16,144},{24,152},{32,160},{40,168},{48,176},{56,1... | collective-permute-start | bytes 4521992 | tf_op jit(solution)/shard_map/ppermute | solution.py:22
  5.2 4.7 %collective-permute-start.1 = (bf16[1,2048]{1,0:T(2,128)(2,1)S(1)}, bf16[1,2048]{1,0:T(2,128)(2,1)S(1)}, u32[]{:S(2)}, u32[]{:S(2)}) collective-permute-start(bf16[1,2048]{1,0:T(2,128)(2,1)S(1)} %copy-done.3), channel_id=1, source_target_pairs={{0,8},{8,0},{16,24},{24,16},{32,40},{40,32},{48,56},{56,48},{64,72... | collective-permute-start | bytes 12296 | tf_op jit(solution)/shard_map/ppermute | solution.py:22
  7.5 2.5 %copy-start.1 = (f32[2,2048]{1,0:T(2,128)S(1)}, f32[2,2048]{1,0:T(2,128)}, u32[]{:S(2)}) copy-start(f32[2,2048]{1,0:T(2,128)} %rest_0_.3) | copy-start | bytes 49156
  7.5 2.5 %copy-start.2 = (bf16[3,2048]{1,0:T(4,128)(2,1)S(1)}, bf16[3,2048]{1,0:T(4,128)(2,1)}, u32[]{:S(2)}) copy-start(bf16[3,2048]{1,0:T(4,128)(2,1)} %tokens_ref.1) | copy-start | bytes 36868
  7.5 2.5 %copy-start.4 = (f32[2,128]{1,0:T(2,128)S(1)}, f32[2,128]{1,0:T(2,128)}, u32[]{:S(2)}) copy-start(f32[2,128]{1,0:T(2,128)} %rest_1_.3) | copy-start | bytes 3076
  7.5 2.5 %copy-start.5 = (f32[2,128]{1,0:T(2,128)S(1)}, f32[2,128]{1,0:T(2,128)}, u32[]{:S(2)}) copy-start(f32[2,128]{1,0:T(2,128)} %rest_2_.3) | copy-start | bytes 3076
  13.1 3.8 %copy-start = (bf16[2,256,2048]{2,1,0:T(8,128)(2,1)S(1)}, bf16[2,256,2048]{2,1,0:T(8,128)(2,1)}, u32[]{:S(2)}) copy-start(bf16[2,256,2048]{2,1,0:T(8,128)(2,1)} %w_ref.3) | copy-start | bytes 6291460
  13.1 3.8 %collective-permute-start.2 = (f32[16,256]{1,0:T(8,128)S(1)}, f32[16,256]{1,0:T(8,128)S(1)}, u32[]{:S(2)}, u32[]{:S(2)}) collective-permute-start(f32[16,256]{1,0:T(8,128)S(1)} %get-tuple-element.39.refs_5_.state_ref), channel_id=1, source_target_pairs={{0,8},{8,0},{16,24},{24,16},{32,40},{40,32},{48,56},{56,48},{64,72... | collective-permute-start | bytes 49160 | tf_op jit(solution)/shard_map/ppermute | solution.py:22
  17.5 1.3 %collective-permute-start.3 = (f32[8,2048]{1,0:T(8,128)S(1)}, f32[8,2048]{1,0:T(8,128)S(1)}, u32[]{:S(2)}, u32[]{:S(2)}) collective-permute-start(f32[8,2048]{1,0:T(8,128)S(1)} %out_projection_0.1), channel_id=1, source_target_pairs={{0,1},{1,0},{2,3},{3,2},{4,5},{5,4},{6,7},{7,6},{8,9},{9,8},{10,11... | collective-permute-start | bytes 196616 | tf_op jit(solution)/shard_map/ppermute | solution.py:22
  18.8 9.1 %collective-permute-start.4 = (bf16[8,2048]{1,0:T(8,128)(2,1)S(1)}, bf16[8,2048]{1,0:T(8,128)(2,1)S(1)}, u32[]{:S(2)}, u32[]{:S(2)}) collective-permute-start(bf16[8,2048]{1,0:T(8,128)(2,1)S(1)} %add_convert_fusion.1.refs_5_.p_ref), channel_id=1, source_target_pairs={{0,2},{1,3},{2,0},{3,1},{4,6},{5,7},{6,4},{7,5},{8,10},{9,11},{10,... | collective-permute-start | bytes 98312 | tf_op jit(solution)/shard_map/ppermute | solution.py:22
  20.5 7.4 %collective-permute-start.5 = (bf16[8,2048]{1,0:T(8,128)(2,1)S(1)}, bf16[8,2048]{1,0:T(8,128)(2,1)S(1)}, u32[]{:S(2)}, u32[]{:S(2)}) collective-permute-start(bf16[8,2048]{1,0:T(8,128)(2,1)S(1)} %add_convert_fusion.1.refs_5_.p_ref), channel_id=1, source_target_pairs={{0,4},{1,5},{2,6},{3,7},{4,0},{5,1},{6,2},{7,3},{8,12},{9,13},{10,... | collective-permute-start | bytes 98312 | tf_op jit(solution)/shard_map/ppermute | solution.py:22
  23.4 5.1 %collective-permute-start.6 = (bf16[8,2048]{1,0:T(8,128)(2,1)S(1)}, bf16[8,2048]{1,0:T(8,128)(2,1)S(1)}, u32[]{:S(2)}, u32[]{:S(2)}) collective-permute-start(bf16[8,2048]{1,0:T(8,128)(2,1)S(1)} %add_convert_fusion.1.refs_5_.p_ref), channel_id=1, source_target_pairs={{0,6},{1,7},{2,4},{3,5},{4,2},{5,3},{6,0},{7,1},{8,14},{9,15},{10,... | collective-permute-start | bytes 98312 | tf_op jit(solution)/shard_map/ppermute | solution.py:22
  25.6 25.7 %collective-permute-start.13 = (bf16[2304,128]{1,0:T(8,128)(2,1)}, bf16[2304,128]{1,0:T(8,128)(2,1)}, u32[]{:S(2)}, u32[]{:S(2)}) collective-permute-start(bf16[2304,128]{1,0:T(8,128)(2,1)} %leaving_second.1), channel_id=1, source_target_pairs={{0,128},{8,136},{16,144},{24,152},{32,160},{40,168},{48,176},{56,1... | collective-permute-start | bytes 1769480 | tf_op jit(solution)/shard_map/ppermute | solution.py:22
  31.0 3.8 %collective-permute-start.7 = (f32[16,256]{1,0:T(8,128)S(1)}, f32[16,256]{1,0:T(8,128)S(1)}, u32[]{:S(2)}, u32[]{:S(2)}) collective-permute-start(f32[16,256]{1,0:T(8,128)S(1)} %get-tuple-element.48.state_ref), channel_id=1, source_target_pairs={{0,8},{8,0},{16,24},{24,16},{32,40},{40,32},{48,56},{56,48},{64,72... | collective-permute-start | bytes 49160 | tf_op jit(solution)/shard_map/ppermute | solution.py:22
  35.3 1.3 %collective-permute-start.8 = (f32[8,2048]{1,0:T(8,128)S(1)}, f32[8,2048]{1,0:T(8,128)S(1)}, u32[]{:S(2)}, u32[]{:S(2)}) collective-permute-start(f32[8,2048]{1,0:T(8,128)S(1)} %out_projection_1.1), channel_id=1, source_target_pairs={{0,1},{1,0},{2,3},{3,2},{4,5},{5,4},{6,7},{7,6},{8,9},{9,8},{10,11... | collective-permute-start | bytes 196616 | tf_op jit(solution)/shard_map/ppermute | solution.py:22
  36.7 8.3 %collective-permute-start.10 = (bf16[8,2048]{1,0:T(8,128)(2,1)S(1)}, bf16[8,2048]{1,0:T(8,128)(2,1)S(1)}, u32[]{:S(2)}, u32[]{:S(2)}) collective-permute-start(bf16[8,2048]{1,0:T(8,128)(2,1)S(1)} %add_convert_fusion.after_ref.p_ref), channel_id=1, source_target_pairs={{0,4},{1,5},{2,6},{3,7},{4,0},{5,1},{6,2},{7,3},{8,12},{9,13},{10,... | collective-permute-start | bytes 98312 | tf_op jit(solution)/shard_map/ppermute | solution.py:22
  38.2 6.8 %collective-permute-start.11 = (bf16[8,2048]{1,0:T(8,128)(2,1)S(1)}, bf16[8,2048]{1,0:T(8,128)(2,1)S(1)}, u32[]{:S(2)}, u32[]{:S(2)}) collective-permute-start(bf16[8,2048]{1,0:T(8,128)(2,1)S(1)} %add_convert_fusion.after_ref.p_ref), channel_id=1, source_target_pairs={{0,6},{1,7},{2,4},{3,5},{4,2},{5,3},{6,0},{7,1},{8,14},{9,15},{10,... | collective-permute-start | bytes 98312 | tf_op jit(solution)/shard_map/ppermute | solution.py:22
  39.3 5.7 %collective-permute-start.9 = (bf16[8,2048]{1,0:T(8,128)(2,1)S(1)}, bf16[8,2048]{1,0:T(8,128)(2,1)S(1)}, u32[]{:S(2)}, u32[]{:S(2)}) collective-permute-start(bf16[8,2048]{1,0:T(8,128)(2,1)S(1)} %add_convert_fusion.after_ref.p_ref), channel_id=1, source_target_pairs={{0,2},{1,3},{2,0},{3,1},{4,6},{5,7},{6,4},{7,5},{8,10},{9,11},{10,... | collective-permute-start | bytes 98312 | tf_op jit(solution)/shard_map/ppermute | solution.py:22
  45.6 5.7 %collective-permute-start.12 = (f32[1,2560]{1,0:T(1,128)S(1)}, f32[1,2560]{1,0:T(1,128)S(1)}, u32[]{:S(2)}, u32[]{:S(2)}) collective-permute-start(f32[1,2560]{1,0:T(1,128)S(1)} %get-tuple-element.56), channel_id=1, source_target_pairs={{0,128},{8,136},{16,144},{24,152},{32,160},{40,168},{48,176},{56,1... | collective-permute-start | bytes 30728 | tf_op jit(solution)/shard_map/ppermute | solution.py:22

commit v12 on v10

--- a/solution.py
+++ b/solution.py
@@ -247,6 +247,10 @@
     rows, blocks, patched, semaphores,
 ):
     del stored_ref
+    rows[0:2, :] = stay_ref[...]
+    rows[2:3, :] = arrived_ref[0:1, 0:2048]
+    out = pltpu.make_async_copy(rows, out_ref, semaphores.at[SECOND + 4])
+    out.start()
     length = jnp.max(place_ref[...]).astype(jnp.int32)
     hit_unit = length // UNIT
     units = [(unit, *plane_of(unit)) for unit in range(FIRST, 4 * PER)]
@@ -295,10 +299,6 @@
         def _():
             changed(*unit).start()
 
-    rows[0:2, :] = stay_ref[...]
-    rows[2:3, :] = arrived_ref[0:1, 0:2048]
-    out = pltpu.make_async_copy(rows, out_ref, semaphores.at[SECOND + 4])
-    out.start()
     for unit in units:
         straight(*unit).wait()
     for inside, write in early:

time: 52.6 us -> 52.6 us (level)
  no operation moved by 1% of the time
where the time goes in v12:
time: 52.6 us; the launch traced here: 52.3 us
  Pallas kernels  20.4 us (39%)
  starting transfers between devices  18 us (34%)
  waiting for transfers between devices  12 us (23%)
  between operations  0.91 us (2%)
  local copies, waits for them, and re-layouts  0.79 us (2%)
    ppermute x14, starting transfers between devices, permute(): return lax.ppermute(value, axis, pairs)  18 us
    ppermute x14, waiting for transfers between devices, permute(): return lax.ppermute(value, axis, pairs)  12 us
    pallas_call x3, Pallas kernels, fetch(): pl.pallas_call(functools.partial(fetch_kernel, layer, which), out_shape=t...  6.54 us
    pallas_call x1, Pallas kernels, local(): pl.pallas_call(first_kernel, out_shape=out_shape, in_specs=[SM] * 3 + [VM...  3.16 us
    pallas_call x1, Pallas kernels, local(): pl.pallas_call(store_kernel, out_shape=(pltpu.HBM((2, 2, 2048, 128), jnp....  3.07 us
    pallas_call x2, Pallas kernels, leaving(): pl.pallas_call(functools.partial(leaving_kernel, begin, begin + count), o...  2.51 us
    pallas_call x1, Pallas kernels, local(): pl.pallas_call(second_kernel, out_shape=out_shape, in_specs=[SM] * 3 + [V...  2.47 us
    pallas_call x1, Pallas kernels, local(): pl.pallas_call(arrival_kernel, out_shape=(pltpu.HBM((3, 2048), jnp.float3...  1.07 us
  transfers between devices with their start and end apart: 14, of which 7 were waited for; matrix products, arithmetic and copies ran while one was open for 2% of the time, Pallas kernels for 34%

profile of v12, /device:TPU:64, one launch (start us, length us, event | category | flops | bytes accessed | tf_op | source)
XLA Modules:
  0.0 52.3 jit_solution(14756873838373905698)
XLA Ops:
  0.7 1.4 %leaving_first.1 = (bf16[5888,128]{1,0:T(8,128)(2,1)S(1)}, f32[8,128]{1,0:T(8,128)}) custom-call(bf16[2,2,3,2048,128]{4,3,2,1,0:T(8,128)(2,1)} %bitcast.6), custom_call_target="tpu_custom_call" | custom-call | tf_op jit(solution)/shard_map/leaving_first/pallas_call | solution.py:376
  2.1 3.1 %collective-permute-start = (bf16[5888,128]{1,0:T(8,128)(2,1)S(1)}, bf16[5888,128]{1,0:T(8,128)(2,1)}, u32[]{:S(2)}, u32[]{:S(2)}) collective-permute-start(bf16[5888,128]{1,0:T(8,128)(2,1)S(1)} %get-tuple-element.33.refs_5_), channel_id=1, source_target_pairs={{0,128},{8,136},{16,144},{24,152},{32,160},{40,168},{48,176},{56,1... | collective-permute-start | bytes 4521992 | tf_op jit(solution)/shard_map/ppermute | solution.py:22
  5.2 1.9 %collective-permute-start.1 = (bf16[1,2048]{1,0:T(2,128)(2,1)S(1)}, bf16[1,2048]{1,0:T(2,128)(2,1)S(1)}, u32[]{:S(2)}, u32[]{:S(2)}) collective-permute-start(bf16[1,2048]{1,0:T(2,128)(2,1)S(1)} %copy-done.3), channel_id=1, source_target_pairs={{0,8},{8,0},{16,24},{24,16},{32,40},{40,32},{48,56},{56,48},{64,72... | collective-permute-start | bytes 12296 | tf_op jit(solution)/shard_map/ppermute | solution.py:22
  7.5 2.4 %fetch_0.1 = (bf16[2048,256]{1,0:T(8,128)(2,1)S(1)}, bf16[2048,128]{1,0:T(8,128)(2,1)S(1)}, bf16[2048,128]{1,0:T(8,128)(2,1)S(1)}, bf16[3,2048,128]{2,1,0:T(8,128)(2,1)S(1)}, bf16[2,2048,128]{2,1,0:T(8,128)(2,1)S(1)}) custom-call(bf16[2,2,3,2048,128]{4,3,2,1,0:T(8,128)(2,1)} %bitcast.7, bf16[2,2,1,2,2048,128]{5,4,3,2,1,0:T(8,128)(2,1)} %bitcast.12, ...), custom_call_target="tpu_custom_call" | custom-call | tf_op jit(solution)/shard_map/fetch_0/pallas_call | solution.py:437
  10.0 3.2 %attention_0.1 = (f32[16,256]{1,0:T(8,128)S(1)}, f32[16,256]{1,0:T(8,128)S(1)}, f32[2,128]{1,0:T(2,128)S(1)}, f32[8,2048]{1,0:T(8,128)S(1)}) custom-call(s32[1]{0:T(128)} %bitcast.1.group_ref, s32[96]{0:T(128)S(1)} %copy-done.7, s32[32]{0:T(128)S(1)} %copy-done.6, bf16[3,2048]{1,0:T(4,128)(2,1)S(1)} %copy-done.2, bf16[1,2048]{1,0:T(2,128)(2,1)S(1)} %copy-done.3, ...), custom_call_target="tpu_custom_call" | custom-call | tf_op jit(solution)/shard_map/attention_0/pallas_call | solution.py:447
  13.1 0.9 %collective-permute-start.2 = (f32[16,256]{1,0:T(8,128)S(1)}, f32[16,256]{1,0:T(8,128)S(1)}, u32[]{:S(2)}, u32[]{:S(2)}) collective-permute-start(f32[16,256]{1,0:T(8,128)S(1)} %get-tuple-element.40.refs_5_.state_ref), channel_id=1, source_target_pairs={{0,8},{8,0},{16,24},{24,16},{32,40},{40,32},{48,56},{56,48},{64,72... | collective-permute-start | bytes 49160 | tf_op jit(solution)/shard_map/ppermute | solution.py:22
  14.1 2.4 %fetch_1_keys.1 = (bf16[2048,256]{1,0:T(8,128)(2,1)S(1)}, bf16[2048,128]{1,0:T(8,128)(2,1)S(1)}, bf16[2048,128]{1,0:T(8,128)(2,1)S(1)}, bf16[3,2048,128]{2,1,0:T(8,128)(2,1)S(1)}, bf16[2,2048,128]{2,1,0:T(8,128)(2,1)S(1)}) custom-call(bf16[2,2,3,2048,128]{4,3,2,1,0:T(8,128)(2,1)} %bitcast.9, bf16[2,2,1,2,2048,128]{5,4,3,2,1,0:T(8,128)(2,1)} %bitcast.14, ...), custom_call_target="tpu_custom_call" | custom-call | tf_op jit(solution)/shard_map/fetch_1_keys/pallas_call | solution.py:437
  17.6 1.2 %collective-permute-done.3 = f32[8,2048]{1,0:T(8,128)S(1)} collective-permute-done((f32[8,2048]{1,0:T(8,128)S(1)}, f32[8,2048]{1,0:T(8,128)S(1)}, u32[]{:S(2)}, u32[]{:S(2)}) %collective-permute-start.3) | collective-permute-done | bytes 65568 | tf_op jit(solution)/shard_map/ppermute | solution.py:22
  18.8 1.7 %collective-permute-start.4 = (bf16[8,2048]{1,0:T(8,128)(2,1)S(1)}, bf16[8,2048]{1,0:T(8,128)(2,1)S(1)}, u32[]{:S(2)}, u32[]{:S(2)}) collective-permute-start(bf16[8,2048]{1,0:T(8,128)(2,1)S(1)} %add_convert_fusion.1.refs_5_.p_ref), channel_id=1, source_target_pairs={{0,2},{1,3},{2,0},{3,1},{4,6},{5,7},{6,4},{7,5},{8,10},{9,11},{10,... | collective-permute-start | bytes 98312 | tf_op jit(solution)/shard_map/ppermute | solution.py:22
  20.5 2.9 %collective-permute-start.5 = (bf16[8,2048]{1,0:T(8,128)(2,1)S(1)}, bf16[8,2048]{1,0:T(8,128)(2,1)S(1)}, u32[]{:S(2)}, u32[]{:S(2)}) collective-permute-start(bf16[8,2048]{1,0:T(8,128)(2,1)S(1)} %add_convert_fusion.1.refs_5_.p_ref), channel_id=1, source_target_pairs={{0,4},{1,5},{2,6},{3,7},{4,0},{5,1},{6,2},{7,3},{8,12},{9,13},{10,... | collective-permute-start | bytes 98312 | tf_op jit(solution)/shard_map/ppermute | solution.py:22
  23.6 1.1 %leaving_second.1 = (bf16[2304,128]{1,0:T(8,128)(2,1)S(1)}, f32[8,128]{1,0:T(8,128)}) custom-call(bf16[2,2,3,2048,128]{4,3,2,1,0:T(8,128)(2,1)} %bitcast.10), custom_call_target="tpu_custom_call" | custom-call | tf_op jit(solution)/shard_map/leaving_second/pallas_call | solution.py:376
  25.3 1.7 %fetch_1_values.1 = (bf16[3,2048,128]{2,1,0:T(8,128)(2,1)S(1)}, bf16[2,2048,128]{2,1,0:T(8,128)(2,1)S(1)}) custom-call(bf16[2,2,3,2048,128]{4,3,2,1,0:T(8,128)(2,1)} %bitcast.11, bf16[2,2,1,2,2048,128]{5,4,3,2,1,0:T(8,128)(2,1)} %bitcast.15, bf16[2,2048,256]{2,1,0:T(8,128)(2,1)} %refs_2_.5, bf16[2,2048,128]{2,1,0:T(8,128)(2,1)} %refs_3_.5, ...), custom_call_target="tpu_custom_call" | custom-call | tf_op jit(solution)/shard_map/fetch_1_values/pallas_call | solution.py:437
  27.1 1.4 %collective-permute-done.6.r3_ref = bf16[8,2048]{1,0:T(8,128)(2,1)S(1)} collective-permute-done((bf16[8,2048]{1,0:T(8,128)(2,1)S(1)}, bf16[8,2048]{1,0:T(8,128)(2,1)S(1)}, u32[]{:S(2)}, u32[]{:S(2)}) %collective-permute-start.6) | collective-permute-done | bytes 32800 | tf_op jit(solution)/shard_map/ppermute | solution.py:22
  28.5 2.5 %attention_1.1 = (f32[16,256]{1,0:T(8,128)S(1)}, f32[16,256]{1,0:T(8,128)S(1)}, f32[2,128]{1,0:T(2,128)S(1)}, f32[8,2048]{1,0:T(8,128)S(1)}) custom-call(s32[1]{0:T(128)} %bitcast.1.group_ref, s32[96]{0:T(128)S(1)} %copy-done.7, s32[32]{0:T(128)S(1)} %copy-done.6, f32[8,2048]{1,0:T(8,128)S(1)} %get-tuple-element.39.before_ref, ...), custom_call_target="tpu_custom_call" | custom-call | tf_op jit(solution)/shard_map/attention_1/pallas_call | solution.py:466
  31.0 0.9 %collective-permute-start.7 = (f32[16,256]{1,0:T(8,128)S(1)}, f32[16,256]{1,0:T(8,128)S(1)}, u32[]{:S(2)}, u32[]{:S(2)}) collective-permute-start(f32[16,256]{1,0:T(8,128)S(1)} %get-tuple-element.49.state_ref), channel_id=1, source_target_pairs={{0,8},{8,0},{16,24},{24,16},{32,40},{40,32},{48,56},{56,48},{64,72... | collective-permute-start | bytes 49160 | tf_op jit(solution)/shard_map/ppermute | solution.py:22
  31.9 2.9 %collective-permute-done.7.far_ref = f32[16,256]{1,0:T(8,128)S(1)} collective-permute-done((f32[16,256]{1,0:T(8,128)S(1)}, f32[16,256]{1,0:T(8,128)S(1)}, u32[]{:S(2)}, u32[]{:S(2)}) %collective-permute-start.7) | collective-permute-done | bytes 16416 | tf_op jit(solution)/shard_map/ppermute | solution.py:22
  35.4 1.2 %collective-permute-done.8 = f32[8,2048]{1,0:T(8,128)S(1)} collective-permute-done((f32[8,2048]{1,0:T(8,128)S(1)}, f32[8,2048]{1,0:T(8,128)S(1)}, u32[]{:S(2)}, u32[]{:S(2)}) %collective-permute-start.8) | collective-permute-done | bytes 65568 | tf_op jit(solution)/shard_map/ppermute | solution.py:22
  36.7 0.7 %collective-permute-start.10 = (bf16[8,2048]{1,0:T(8,128)(2,1)S(1)}, bf16[8,2048]{1,0:T(8,128)(2,1)S(1)}, u32[]{:S(2)}, u32[]{:S(2)}) collective-permute-start(bf16[8,2048]{1,0:T(8,128)(2,1)S(1)} %add_convert_fusion.after_ref.p_ref), channel_id=1, source_target_pairs={{0,4},{1,5},{2,6},{3,7},{4,0},{5,1},{6,2},{7,3},{8,12},{9,13},{10,... | collective-permute-start | bytes 98312 | tf_op jit(solution)/shard_map/ppermute | solution.py:22
  37.3 1.1 %collective-permute-start.11 = (bf16[8,2048]{1,0:T(8,128)(2,1)S(1)}, bf16[8,2048]{1,0:T(8,128)(2,1)S(1)}, u32[]{:S(2)}, u32[]{:S(2)}) collective-permute-start(bf16[8,2048]{1,0:T(8,128)(2,1)S(1)} %add_convert_fusion.after_ref.p_ref), channel_id=1, source_target_pairs={{0,6},{1,7},{2,4},{3,5},{4,2},{5,3},{6,0},{7,1},{8,14},{9,15},{10,... | collective-permute-start | bytes 98312 | tf_op jit(solution)/shard_map/ppermute | solution.py:22
  38.5 1.8 %collective-permute-start.9 = (bf16[8,2048]{1,0:T(8,128)(2,1)S(1)}, bf16[8,2048]{1,0:T(8,128)(2,1)S(1)}, u32[]{:S(2)}, u32[]{:S(2)}) collective-permute-start(bf16[8,2048]{1,0:T(8,128)(2,1)S(1)} %add_convert_fusion.after_ref.p_ref), channel_id=1, source_target_pairs={{0,2},{1,3},{2,0},{3,1},{4,6},{5,7},{6,4},{7,5},{8,10},{9,11},{10,... | collective-permute-start | bytes 98312 | tf_op jit(solution)/shard_map/ppermute | solution.py:22
  40.8 3.1 %store_first.1 = (bf16[2,2,2048,128]{3,2,1,0:T(8,128)(2,1)}, bf16[4,16,128]{2,1,0:T(8,128)(2,1)S(1)}, f32[8,128]{1,0:T(8,128)S(1)}) custom-call(s32[1]{0:T(128)} %dynamic_slice.9.length_ref, bf16[5888,128]{1,0:T(8,128)(2,1)} %collective-permute-done.first_ref, bf16[8,2048]{1,0:T(8,128)(2,1)S(1)} %add_convert_fusion.after_ref.p_ref), custom_call_target="tpu_custom_call" | custom-call | tf_op jit(solution)/shard_map/store_first/pallas_call | solution.py:477
  44.6 2.0 %collective-permute-start.12 = (f32[1,2560]{1,0:T(1,128)S(1)}, f32[1,2560]{1,0:T(1,128)S(1)}, u32[]{:S(2)}, u32[]{:S(2)}) collective-permute-start(f32[1,2560]{1,0:T(1,128)S(1)} %get-tuple-element.57), channel_id=1, source_target_pairs={{0,128},{8,136},{16,144},{24,152},{32,160},{40,168},{48,176},{56,1... | collective-permute-start | bytes 30728 | tf_op jit(solution)/shard_map/ppermute | solution.py:22
  46.6 4.6 %collective-permute-done.13.second_ref = bf16[2304,128]{1,0:T(8,128)(2,1)S(1)} collective-permute-done((bf16[2304,128]{1,0:T(8,128)(2,1)S(1)}, bf16[2304,128]{1,0:T(8,128)(2,1)S(1)}, u32[]{:S(2)}, u32[]{:S(2)}) %collective-permute-start.13) | collective-permute-done | bytes 589856 | tf_op jit(solution)/shard_map/ppermute | solution.py:22
  51.3 1.1 %arrival.1 = (f32[3,2048]{1,0:T(4,128)}, bf16[2,2,2048,128]{3,2,1,0:T(8,128)(2,1)}) custom-call(f32[8,128]{1,0:T(8,128)S(1)} %get-tuple-element.51.place_ref, f32[2,2048]{1,0:T(2,128)S(1)} %get-tuple-element.56.stay_ref, f32[1,2560]{1,0:T(1,128)S(1)} %collective-permute-done.12.arrived_ref, ...), custom_call_target="tpu_custom_call", output_to_operand_aliasing={{1}: (5, {})} | custom-call | tf_op jit(solution)/shard_map/arrival/pallas_call | solution.py:507
  (44 shorter events, 4.2 us)
Async XLA Ops:
  0.6 4.6 %copy-start.3 = (bf16[1,2048]{1,0:T(2,128)(2,1)S(1)}, bf16[1,2048]{1,0:T(2,128)(2,1)}, u32[]{:S(2)}) copy-start(bf16[1,2048]{1,0:T(2,128)(2,1)} %own_long_ref.1) | copy-start | bytes 12292
  0.6 6.5 %copy-start.6 = (s32[32]{0:T(128)S(1)}, s32[32]{0:T(128)}, u32[]{:S(2)}) copy-start(s32[32]{0:T(128)} %long_lengths_ref.3) | copy-start | bytes 388
  0.7 6.5 %copy-start.7 = (s32[96]{0:T(128)S(1)}, s32[96]{0:T(128)}, u32[]{:S(2)}) copy-start(s32[96]{0:T(128)} %lengths_ref.3) | copy-start | bytes 1156
  0.7 6.7 %copy-start.8 = (f32[128]{0:T(128)S(1)}, f32[128]{0:T(128)}, u32[]{:S(2)}) copy-start(f32[128]{0:T(128)} %constant.43.clone) | copy-start | bytes 1540
  0.7 6.7 %copy-start.9 = (f32[128]{0:T(128)S(1)}, f32[128]{0:T(128)}, u32[]{:S(2)}) copy-start(f32[128]{0:T(128)} %constant.44.clone) | copy-start | bytes 1540
  2.1 38.8 %collective-permute-start = (bf16[5888,128]{1,0:T(8,128)(2,1)S(1)}, bf16[5888,128]{1,0:T(8,128)(2,1)}, u32[]{:S(2)}, u32[]{:S(2)}) collective-permute-start(bf16[5888,128]{1,0:T(8,128)(2,1)S(1)} %get-tuple-element.33.refs_5_), channel_id=1, source_target_pairs={{0,128},{8,136},{16,144},{24,152},{32,160},{40,168},{48,176},{56,1... | collective-permute-start | bytes 4521992 | tf_op jit(solution)/shard_map/ppermute | solution.py:22
  5.2 4.7 %collective-permute-start.1 = (bf16[1,2048]{1,0:T(2,128)(2,1)S(1)}, bf16[1,2048]{1,0:T(2,128)(2,1)S(1)}, u32[]{:S(2)}, u32[]{:S(2)}) collective-permute-start(bf16[1,2048]{1,0:T(2,128)(2,1)S(1)} %copy-done.3), channel_id=1, source_target_pairs={{0,8},{8,0},{16,24},{24,16},{32,40},{40,32},{48,56},{56,48},{64,72... | collective-permute-start | bytes 12296 | tf_op jit(solution)/shard_map/ppermute | solution.py:22
  7.5 2.5 %copy-start.1 = (f32[2,2048]{1,0:T(2,128)S(1)}, f32[2,2048]{1,0:T(2,128)}, u32[]{:S(2)}) copy-start(f32[2,2048]{1,0:T(2,128)} %rest_0_.3) | copy-start | bytes 49156
  7.5 2.5 %copy-start.2 = (bf16[3,2048]{1,0:T(4,128)(2,1)S(1)}, bf16[3,2048]{1,0:T(4,128)(2,1)}, u32[]{:S(2)}) copy-start(bf16[3,2048]{1,0:T(4,128)(2,1)} %tokens_ref.1) | copy-start | bytes 36868
  7.5 2.5 %copy-start.4 = (f32[2,128]{1,0:T(2,128)S(1)}, f32[2,128]{1,0:T(2,128)}, u32[]{:S(2)}) copy-start(f32[2,128]{1,0:T(2,128)} %rest_1_.3) | copy-start | bytes 3076
  7.5 2.5 %copy-start.5 = (f32[2,128]{1,0:T(2,128)S(1)}, f32[2,128]{1,0:T(2,128)}, u32[]{:S(2)}) copy-start(f32[2,128]{1,0:T(2,128)} %rest_2_.3) | copy-start | bytes 3076
  13.1 3.8 %copy-start = (bf16[2,256,2048]{2,1,0:T(8,128)(2,1)S(1)}, bf16[2,256,2048]{2,1,0:T(8,128)(2,1)}, u32[]{:S(2)}) copy-start(bf16[2,256,2048]{2,1,0:T(8,128)(2,1)} %w_ref.3) | copy-start | bytes 6291460
  13.1 3.8 %collective-permute-start.2 = (f32[16,256]{1,0:T(8,128)S(1)}, f32[16,256]{1,0:T(8,128)S(1)}, u32[]{:S(2)}, u32[]{:S(2)}) collective-permute-start(f32[16,256]{1,0:T(8,128)S(1)} %get-tuple-element.40.refs_5_.state_ref), channel_id=1, source_target_pairs={{0,8},{8,0},{16,24},{24,16},{32,40},{40,32},{48,56},{56,48},{64,72... | collective-permute-start | bytes 49160 | tf_op jit(solution)/shard_map/ppermute | solution.py:22
  17.5 1.3 %collective-permute-start.3 = (f32[8,2048]{1,0:T(8,128)S(1)}, f32[8,2048]{1,0:T(8,128)S(1)}, u32[]{:S(2)}, u32[]{:S(2)}) collective-permute-start(f32[8,2048]{1,0:T(8,128)S(1)} %out_projection_0.1), channel_id=1, source_target_pairs={{0,1},{1,0},{2,3},{3,2},{4,5},{5,4},{6,7},{7,6},{8,9},{9,8},{10,11... | collective-permute-start | bytes 196616 | tf_op jit(solution)/shard_map/ppermute | solution.py:22
  18.8 8.2 %collective-permute-start.4 = (bf16[8,2048]{1,0:T(8,128)(2,1)S(1)}, bf16[8,2048]{1,0:T(8,128)(2,1)S(1)}, u32[]{:S(2)}, u32[]{:S(2)}) collective-permute-start(bf16[8,2048]{1,0:T(8,128)(2,1)S(1)} %add_convert_fusion.1.refs_5_.p_ref), channel_id=1, source_target_pairs={{0,2},{1,3},{2,0},{3,1},{4,6},{5,7},{6,4},{7,5},{8,10},{9,11},{10,... | collective-permute-start | bytes 98312 | tf_op jit(solution)/shard_map/ppermute | solution.py:22
  20.5 6.6 %collective-permute-start.5 = (bf16[8,2048]{1,0:T(8,128)(2,1)S(1)}, bf16[8,2048]{1,0:T(8,128)(2,1)S(1)}, u32[]{:S(2)}, u32[]{:S(2)}) collective-permute-start(bf16[8,2048]{1,0:T(8,128)(2,1)S(1)} %add_convert_fusion.1.refs_5_.p_ref), channel_id=1, source_target_pairs={{0,4},{1,5},{2,6},{3,7},{4,0},{5,1},{6,2},{7,3},{8,12},{9,13},{10,... | collective-permute-start | bytes 98312 | tf_op jit(solution)/shard_map/ppermute | solution.py:22
  23.4 5.1 %collective-permute-start.6 = (bf16[8,2048]{1,0:T(8,128)(2,1)S(1)}, bf16[8,2048]{1,0:T(8,128)(2,1)S(1)}, u32[]{:S(2)}, u32[]{:S(2)}) collective-permute-start(bf16[8,2048]{1,0:T(8,128)(2,1)S(1)} %add_convert_fusion.1.refs_5_.p_ref), channel_id=1, source_target_pairs={{0,6},{1,7},{2,4},{3,5},{4,2},{5,3},{6,0},{7,1},{8,14},{9,15},{10,... | collective-permute-start | bytes 98312 | tf_op jit(solution)/shard_map/ppermute | solution.py:22
  24.7 26.4 %collective-permute-start.13 = (bf16[2304,128]{1,0:T(8,128)(2,1)S(1)}, bf16[2304,128]{1,0:T(8,128)(2,1)S(1)}, u32[]{:S(2)}, u32[]{:S(2)}) collective-permute-start(bf16[2304,128]{1,0:T(8,128)(2,1)S(1)} %get-tuple-element.58), channel_id=1, source_target_pairs={{0,128},{8,136},{16,144},{24,152},{32,160},{40,168},{48,176},{56,1... | collective-permute-start | bytes 1769480 | tf_op jit(solution)/shard_map/ppermute | solution.py:22
  31.0 3.8 %collective-permute-start.7 = (f32[16,256]{1,0:T(8,128)S(1)}, f32[16,256]{1,0:T(8,128)S(1)}, u32[]{:S(2)}, u32[]{:S(2)}) collective-permute-start(f32[16,256]{1,0:T(8,128)S(1)} %get-tuple-element.49.state_ref), channel_id=1, source_target_pairs={{0,8},{8,0},{16,24},{24,16},{32,40},{40,32},{48,56},{56,48},{64,72... | collective-permute-start | bytes 49160 | tf_op jit(solution)/shard_map/ppermute | solution.py:22
  35.3 1.3 %collective-permute-start.8 = (f32[8,2048]{1,0:T(8,128)S(1)}, f32[8,2048]{1,0:T(8,128)S(1)}, u32[]{:S(2)}, u32[]{:S(2)}) collective-permute-start(f32[8,2048]{1,0:T(8,128)S(1)} %out_projection_1.1), channel_id=1, source_target_pairs={{0,1},{1,0},{2,3},{3,2},{4,5},{5,4},{6,7},{7,6},{8,9},{9,8},{10,11... | collective-permute-start | bytes 196616 | tf_op jit(solution)/shard_map/ppermute | solution.py:22
  36.7 7.2 %collective-permute-start.10 = (bf16[8,2048]{1,0:T(8,128)(2,1)S(1)}, bf16[8,2048]{1,0:T(8,128)(2,1)S(1)}, u32[]{:S(2)}, u32[]{:S(2)}) collective-permute-start(bf16[8,2048]{1,0:T(8,128)(2,1)S(1)} %add_convert_fusion.after_ref.p_ref), channel_id=1, source_target_pairs={{0,4},{1,5},{2,6},{3,7},{4,0},{5,1},{6,2},{7,3},{8,12},{9,13},{10,... | collective-permute-start | bytes 98312 | tf_op jit(solution)/shard_map/ppermute | solution.py:22
  37.3 6.6 %collective-permute-start.11 = (bf16[8,2048]{1,0:T(8,128)(2,1)S(1)}, bf16[8,2048]{1,0:T(8,128)(2,1)S(1)}, u32[]{:S(2)}, u32[]{:S(2)}) collective-permute-start(bf16[8,2048]{1,0:T(8,128)(2,1)S(1)} %add_convert_fusion.after_ref.p_ref), channel_id=1, source_target_pairs={{0,6},{1,7},{2,4},{3,5},{4,2},{5,3},{6,0},{7,1},{8,14},{9,15},{10,... | collective-permute-start | bytes 98312 | tf_op jit(solution)/shard_map/ppermute | solution.py:22
  38.5 5.5 %collective-permute-start.9 = (bf16[8,2048]{1,0:T(8,128)(2,1)S(1)}, bf16[8,2048]{1,0:T(8,128)(2,1)S(1)}, u32[]{:S(2)}, u32[]{:S(2)}) collective-permute-start(bf16[8,2048]{1,0:T(8,128)(2,1)S(1)} %add_convert_fusion.after_ref.p_ref), channel_id=1, source_target_pairs={{0,2},{1,3},{2,0},{3,1},{4,6},{5,7},{6,4},{7,5},{8,10},{9,11},{10,... | collective-permute-start | bytes 98312 | tf_op jit(solution)/shard_map/ppermute | solution.py:22
  44.6 6.7 %collective-permute-start.12 = (f32[1,2560]{1,0:T(1,128)S(1)}, f32[1,2560]{1,0:T(1,128)S(1)}, u32[]{:S(2)}, u32[]{:S(2)}) collective-permute-start(f32[1,2560]{1,0:T(1,128)S(1)} %get-tuple-element.57), channel_id=1, source_target_pairs={{0,128},{8,136},{16,144},{24,152},{32,160},{40,168},{48,176},{56,1... | collective-permute-start | bytes 30728 | tf_op jit(solution)/shard_map/ppermute | solution.py:22

commit v13 on v10

--- a/solution.py
+++ b/solution.py
@@ -280,9 +280,9 @@
             blocks.at[plane], moved_ref.at[plane // 2, plane % 2, pl.ds(start, 16)],
             semaphores.at[SECOND + plane],
         )
-        early.append((plane * PER + hit_unit < FIRST, write))
+        early.append((None if plane < FIRST // PER else plane * PER + hit_unit < FIRST, write))
     for inside, write in early:
-        pl.when(inside)(write.start)
+        write.start() if inside is None else pl.when(inside)(write.start)
     for plane in range(FIRST // PER, 4):
         at = jnp.maximum(plane * PER + hit_unit - FIRST, 0) * UNIT
         whole = second_ref[pl.ds(pl.multiple_of(at, UNIT), UNIT), :].astype(jnp.float32)
@@ -302,7 +302,7 @@
     for unit in units:
         straight(*unit).wait()
     for inside, write in early:
-        pl.when(inside)(write.wait)
+        write.wait() if inside is None else pl.when(inside)(write.wait)
     out.wait()
 
 

time: 52.6 us -> 52.6 us (level)
  no operation moved by 1% of the time
where the time goes in v13:
time: 52.6 us; the launch traced here: 52.3 us
  Pallas kernels  20.4 us (39%)
  starting transfers between devices  18 us (34%)
  waiting for transfers between devices  12 us (23%)
  between operations  0.91 us (2%)
  local copies, waits for them, and re-layouts  0.79 us (2%)
    ppermute x14, starting transfers between devices, permute(): return lax.ppermute(value, axis, pairs)  18 us
    ppermute x14, waiting for transfers between devices, permute(): return lax.ppermute(value, axis, pairs)  12 us
    pallas_call x3, Pallas kernels, fetch(): pl.pallas_call(functools.partial(fetch_kernel, layer, which), out_shape=t...  6.54 us
    pallas_call x1, Pallas kernels, local(): pl.pallas_call(first_kernel, out_shape=out_shape, in_specs=[SM] * 3 + [VM...  3.16 us
    pallas_call x1, Pallas kernels, local(): pl.pallas_call(store_kernel, out_shape=(pltpu.HBM((2, 2, 2048, 128), jnp....  3.07 us
    pallas_call x2, Pallas kernels, leaving(): pl.pallas_call(functools.partial(leaving_kernel, begin, begin + count), o...  2.51 us
    pallas_call x1, Pallas kernels, local(): pl.pallas_call(second_kernel, out_shape=out_shape, in_specs=[SM] * 3 + [V...  2.47 us
    pallas_call x1, Pallas kernels, local(): pl.pallas_call(arrival_kernel, out_shape=(pltpu.HBM((3, 2048), jnp.float3...  1.07 us
  transfers between devices with their start and end apart: 14, of which 7 were waited for; matrix products, arithmetic and copies ran while one was open for 2% of the time, Pallas kernels for 34%

profile of v13, /device:TPU:64, one launch (start us, length us, event | category | flops | bytes accessed | tf_op | source)
XLA Modules:
  0.0 52.3 jit_solution(17235099562438374275)
XLA Ops:
  0.7 1.4 %leaving_first.1 = (bf16[5888,128]{1,0:T(8,128)(2,1)S(1)}, f32[8,128]{1,0:T(8,128)}) custom-call(bf16[2,2,3,2048,128]{4,3,2,1,0:T(8,128)(2,1)} %bitcast.6), custom_call_target="tpu_custom_call" | custom-call | tf_op jit(solution)/shard_map/leaving_first/pallas_call | solution.py:376
  2.1 3.1 %collective-permute-start = (bf16[5888,128]{1,0:T(8,128)(2,1)S(1)}, bf16[5888,128]{1,0:T(8,128)(2,1)}, u32[]{:S(2)}, u32[]{:S(2)}) collective-permute-start(bf16[5888,128]{1,0:T(8,128)(2,1)S(1)} %get-tuple-element.33.refs_5_), channel_id=1, source_target_pairs={{0,128},{8,136},{16,144},{24,152},{32,160},{40,168},{48,176},{56,1... | collective-permute-start | bytes 4521992 | tf_op jit(solution)/shard_map/ppermute | solution.py:22
  5.2 1.9 %collective-permute-start.1 = (bf16[1,2048]{1,0:T(2,128)(2,1)S(1)}, bf16[1,2048]{1,0:T(2,128)(2,1)S(1)}, u32[]{:S(2)}, u32[]{:S(2)}) collective-permute-start(bf16[1,2048]{1,0:T(2,128)(2,1)S(1)} %copy-done.3), channel_id=1, source_target_pairs={{0,8},{8,0},{16,24},{24,16},{32,40},{40,32},{48,56},{56,48},{64,72... | collective-permute-start | bytes 12296 | tf_op jit(solution)/shard_map/ppermute | solution.py:22
  7.5 2.4 %fetch_0.1 = (bf16[2048,256]{1,0:T(8,128)(2,1)S(1)}, bf16[2048,128]{1,0:T(8,128)(2,1)S(1)}, bf16[2048,128]{1,0:T(8,128)(2,1)S(1)}, bf16[3,2048,128]{2,1,0:T(8,128)(2,1)S(1)}, bf16[2,2048,128]{2,1,0:T(8,128)(2,1)S(1)}) custom-call(bf16[2,2,3,2048,128]{4,3,2,1,0:T(8,128)(2,1)} %bitcast.7, bf16[2,2,1,2,2048,128]{5,4,3,2,1,0:T(8,128)(2,1)} %bitcast.12, ...), custom_call_target="tpu_custom_call" | custom-call | tf_op jit(solution)/shard_map/fetch_0/pallas_call | solution.py:437
  10.0 3.2 %attention_0.1 = (f32[16,256]{1,0:T(8,128)S(1)}, f32[16,256]{1,0:T(8,128)S(1)}, f32[2,128]{1,0:T(2,128)S(1)}, f32[8,2048]{1,0:T(8,128)S(1)}) custom-call(s32[1]{0:T(128)} %bitcast.1.group_ref, s32[96]{0:T(128)S(1)} %copy-done.7, s32[32]{0:T(128)S(1)} %copy-done.6, bf16[3,2048]{1,0:T(4,128)(2,1)S(1)} %copy-done.2, bf16[1,2048]{1,0:T(2,128)(2,1)S(1)} %copy-done.3, ...), custom_call_target="tpu_custom_call" | custom-call | tf_op jit(solution)/shard_map/attention_0/pallas_call | solution.py:447
  13.1 0.9 %collective-permute-start.2 = (f32[16,256]{1,0:T(8,128)S(1)}, f32[16,256]{1,0:T(8,128)S(1)}, u32[]{:S(2)}, u32[]{:S(2)}) collective-permute-start(f32[16,256]{1,0:T(8,128)S(1)} %get-tuple-element.40.refs_5_.state_ref), channel_id=1, source_target_pairs={{0,8},{8,0},{16,24},{24,16},{32,40},{40,32},{48,56},{56,48},{64,72... | collective-permute-start | bytes 49160 | tf_op jit(solution)/shard_map/ppermute | solution.py:22
  14.1 2.4 %fetch_1_keys.1 = (bf16[2048,256]{1,0:T(8,128)(2,1)S(1)}, bf16[2048,128]{1,0:T(8,128)(2,1)S(1)}, bf16[2048,128]{1,0:T(8,128)(2,1)S(1)}, bf16[3,2048,128]{2,1,0:T(8,128)(2,1)S(1)}, bf16[2,2048,128]{2,1,0:T(8,128)(2,1)S(1)}) custom-call(bf16[2,2,3,2048,128]{4,3,2,1,0:T(8,128)(2,1)} %bitcast.9, bf16[2,2,1,2,2048,128]{5,4,3,2,1,0:T(8,128)(2,1)} %bitcast.14, ...), custom_call_target="tpu_custom_call" | custom-call | tf_op jit(solution)/shard_map/fetch_1_keys/pallas_call | solution.py:437
  17.6 1.2 %collective-permute-done.3 = f32[8,2048]{1,0:T(8,128)S(1)} collective-permute-done((f32[8,2048]{1,0:T(8,128)S(1)}, f32[8,2048]{1,0:T(8,128)S(1)}, u32[]{:S(2)}, u32[]{:S(2)}) %collective-permute-start.3) | collective-permute-done | bytes 65568 | tf_op jit(solution)/shard_map/ppermute | solution.py:22
  18.8 1.7 %collective-permute-start.4 = (bf16[8,2048]{1,0:T(8,128)(2,1)S(1)}, bf16[8,2048]{1,0:T(8,128)(2,1)S(1)}, u32[]{:S(2)}, u32[]{:S(2)}) collective-permute-start(bf16[8,2048]{1,0:T(8,128)(2,1)S(1)} %add_convert_fusion.1.refs_5_.p_ref), channel_id=1, source_target_pairs={{0,2},{1,3},{2,0},{3,1},{4,6},{5,7},{6,4},{7,5},{8,10},{9,11},{10,... | collective-permute-start | bytes 98312 | tf_op jit(solution)/shard_map/ppermute | solution.py:22
  20.5 2.9 %collective-permute-start.5 = (bf16[8,2048]{1,0:T(8,128)(2,1)S(1)}, bf16[8,2048]{1,0:T(8,128)(2,1)S(1)}, u32[]{:S(2)}, u32[]{:S(2)}) collective-permute-start(bf16[8,2048]{1,0:T(8,128)(2,1)S(1)} %add_convert_fusion.1.refs_5_.p_ref), channel_id=1, source_target_pairs={{0,4},{1,5},{2,6},{3,7},{4,0},{5,1},{6,2},{7,3},{8,12},{9,13},{10,... | collective-permute-start | bytes 98312 | tf_op jit(solution)/shard_map/ppermute | solution.py:22
  23.6 1.1 %leaving_second.1 = (bf16[2304,128]{1,0:T(8,128)(2,1)S(1)}, f32[8,128]{1,0:T(8,128)}) custom-call(bf16[2,2,3,2048,128]{4,3,2,1,0:T(8,128)(2,1)} %bitcast.10), custom_call_target="tpu_custom_call" | custom-call | tf_op jit(solution)/shard_map/leaving_second/pallas_call | solution.py:376
  25.3 1.7 %fetch_1_values.1 = (bf16[3,2048,128]{2,1,0:T(8,128)(2,1)S(1)}, bf16[2,2048,128]{2,1,0:T(8,128)(2,1)S(1)}) custom-call(bf16[2,2,3,2048,128]{4,3,2,1,0:T(8,128)(2,1)} %bitcast.11, bf16[2,2,1,2,2048,128]{5,4,3,2,1,0:T(8,128)(2,1)} %bitcast.15, bf16[2,2048,256]{2,1,0:T(8,128)(2,1)} %refs_2_.5, bf16[2,2048,128]{2,1,0:T(8,128)(2,1)} %refs_3_.5, ...), custom_call_target="tpu_custom_call" | custom-call | tf_op jit(solution)/shard_map/fetch_1_values/pallas_call | solution.py:437
  27.1 1.4 %collective-permute-done.6.r3_ref = bf16[8,2048]{1,0:T(8,128)(2,1)S(1)} collective-permute-done((bf16[8,2048]{1,0:T(8,128)(2,1)S(1)}, bf16[8,2048]{1,0:T(8,128)(2,1)S(1)}, u32[]{:S(2)}, u32[]{:S(2)}) %collective-permute-start.6) | collective-permute-done | bytes 32800 | tf_op jit(solution)/shard_map/ppermute | solution.py:22
  28.5 2.5 %attention_1.1 = (f32[16,256]{1,0:T(8,128)S(1)}, f32[16,256]{1,0:T(8,128)S(1)}, f32[2,128]{1,0:T(2,128)S(1)}, f32[8,2048]{1,0:T(8,128)S(1)}) custom-call(s32[1]{0:T(128)} %bitcast.1.group_ref, s32[96]{0:T(128)S(1)} %copy-done.7, s32[32]{0:T(128)S(1)} %copy-done.6, f32[8,2048]{1,0:T(8,128)S(1)} %get-tuple-element.39.before_ref, ...), custom_call_target="tpu_custom_call" | custom-call | tf_op jit(solution)/shard_map/attention_1/pallas_call | solution.py:466
  31.0 0.9 %collective-permute-start.7 = (f32[16,256]{1,0:T(8,128)S(1)}, f32[16,256]{1,0:T(8,128)S(1)}, u32[]{:S(2)}, u32[]{:S(2)}) collective-permute-start(f32[16,256]{1,0:T(8,128)S(1)} %get-tuple-element.49.state_ref), channel_id=1, source_target_pairs={{0,8},{8,0},{16,24},{24,16},{32,40},{40,32},{48,56},{56,48},{64,72... | collective-permute-start | bytes 49160 | tf_op jit(solution)/shard_map/ppermute | solution.py:22
  31.9 2.9 %collective-permute-done.7.far_ref = f32[16,256]{1,0:T(8,128)S(1)} collective-permute-done((f32[16,256]{1,0:T(8,128)S(1)}, f32[16,256]{1,0:T(8,128)S(1)}, u32[]{:S(2)}, u32[]{:S(2)}) %collective-permute-start.7) | collective-permute-done | bytes 16416 | tf_op jit(solution)/shard_map/ppermute | solution.py:22
  35.4 1.2 %collective-permute-done.8 = f32[8,2048]{1,0:T(8,128)S(1)} collective-permute-done((f32[8,2048]{1,0:T(8,128)S(1)}, f32[8,2048]{1,0:T(8,128)S(1)}, u32[]{:S(2)}, u32[]{:S(2)}) %collective-permute-start.8) | collective-permute-done | bytes 65568 | tf_op jit(solution)/shard_map/ppermute | solution.py:22
  36.7 0.7 %collective-permute-start.10 = (bf16[8,2048]{1,0:T(8,128)(2,1)S(1)}, bf16[8,2048]{1,0:T(8,128)(2,1)S(1)}, u32[]{:S(2)}, u32[]{:S(2)}) collective-permute-start(bf16[8,2048]{1,0:T(8,128)(2,1)S(1)} %add_convert_fusion.after_ref.p_ref), channel_id=1, source_target_pairs={{0,4},{1,5},{2,6},{3,7},{4,0},{5,1},{6,2},{7,3},{8,12},{9,13},{10,... | collective-permute-start | bytes 98312 | tf_op jit(solution)/shard_map/ppermute | solution.py:22
  37.3 1.1 %collective-permute-start.11 = (bf16[8,2048]{1,0:T(8,128)(2,1)S(1)}, bf16[8,2048]{1,0:T(8,128)(2,1)S(1)}, u32[]{:S(2)}, u32[]{:S(2)}) collective-permute-start(bf16[8,2048]{1,0:T(8,128)(2,1)S(1)} %add_convert_fusion.after_ref.p_ref), channel_id=1, source_target_pairs={{0,6},{1,7},{2,4},{3,5},{4,2},{5,3},{6,0},{7,1},{8,14},{9,15},{10,... | collective-permute-start | bytes 98312 | tf_op jit(solution)/shard_map/ppermute | solution.py:22
  38.5 1.8 %collective-permute-start.9 = (bf16[8,2048]{1,0:T(8,128)(2,1)S(1)}, bf16[8,2048]{1,0:T(8,128)(2,1)S(1)}, u32[]{:S(2)}, u32[]{:S(2)}) collective-permute-start(bf16[8,2048]{1,0:T(8,128)(2,1)S(1)} %add_convert_fusion.after_ref.p_ref), channel_id=1, source_target_pairs={{0,2},{1,3},{2,0},{3,1},{4,6},{5,7},{6,4},{7,5},{8,10},{9,11},{10,... | collective-permute-start | bytes 98312 | tf_op jit(solution)/shard_map/ppermute | solution.py:22
  40.8 3.1 %store_first.1 = (bf16[2,2,2048,128]{3,2,1,0:T(8,128)(2,1)}, bf16[4,16,128]{2,1,0:T(8,128)(2,1)S(1)}, f32[8,128]{1,0:T(8,128)S(1)}) custom-call(s32[1]{0:T(128)} %dynamic_slice.9.length_ref, bf16[5888,128]{1,0:T(8,128)(2,1)} %collective-permute-done.first_ref, bf16[8,2048]{1,0:T(8,128)(2,1)S(1)} %add_convert_fusion.after_ref.p_ref), custom_call_target="tpu_custom_call" | custom-call | tf_op jit(solution)/shard_map/store_first/pallas_call | solution.py:477
  44.6 2.0 %collective-permute-start.12 = (f32[1,2560]{1,0:T(1,128)S(1)}, f32[1,2560]{1,0:T(1,128)S(1)}, u32[]{:S(2)}, u32[]{:S(2)}) collective-permute-start(f32[1,2560]{1,0:T(1,128)S(1)} %get-tuple-element.57), channel_id=1, source_target_pairs={{0,128},{8,136},{16,144},{24,152},{32,160},{40,168},{48,176},{56,1... | collective-permute-start | bytes 30728 | tf_op jit(solution)/shard_map/ppermute | solution.py:22
  46.6 4.6 %collective-permute-done.13.second_ref = bf16[2304,128]{1,0:T(8,128)(2,1)S(1)} collective-permute-done((bf16[2304,128]{1,0:T(8,128)(2,1)S(1)}, bf16[2304,128]{1,0:T(8,128)(2,1)S(1)}, u32[]{:S(2)}, u32[]{:S(2)}) %collective-permute-start.13) | collective-permute-done | bytes 589856 | tf_op jit(solution)/shard_map/ppermute | solution.py:22
  51.3 1.1 %arrival.1 = (f32[3,2048]{1,0:T(4,128)}, bf16[2,2,2048,128]{3,2,1,0:T(8,128)(2,1)}) custom-call(f32[8,128]{1,0:T(8,128)S(1)} %get-tuple-element.51.place_ref, f32[2,2048]{1,0:T(2,128)S(1)} %get-tuple-element.56.stay_ref, f32[1,2560]{1,0:T(1,128)S(1)} %collective-permute-done.12.arrived_ref, ...), custom_call_target="tpu_custom_call", output_to_operand_aliasing={{1}: (5, {})} | custom-call | tf_op jit(solution)/shard_map/arrival/pallas_call | solution.py:507
  (44 shorter events, 4.2 us)
Async XLA Ops:
  0.6 4.6 %copy-start.3 = (bf16[1,2048]{1,0:T(2,128)(2,1)S(1)}, bf16[1,2048]{1,0:T(2,128)(2,1)}, u32[]{:S(2)}) copy-start(bf16[1,2048]{1,0:T(2,128)(2,1)} %own_long_ref.1) | copy-start | bytes 12292
  0.6 6.5 %copy-start.6 = (s32[32]{0:T(128)S(1)}, s32[32]{0:T(128)}, u32[]{:S(2)}) copy-start(s32[32]{0:T(128)} %long_lengths_ref.3) | copy-start | bytes 388
  0.7 6.5 %copy-start.7 = (s32[96]{0:T(128)S(1)}, s32[96]{0:T(128)}, u32[]{:S(2)}) copy-start(s32[96]{0:T(128)} %lengths_ref.3) | copy-start | bytes 1156
  0.7 6.7 %copy-start.8 = (f32[128]{0:T(128)S(1)}, f32[128]{0:T(128)}, u32[]{:S(2)}) copy-start(f32[128]{0:T(128)} %constant.43.clone) | copy-start | bytes 1540
  0.7 6.7 %copy-start.9 = (f32[128]{0:T(128)S(1)}, f32[128]{0:T(128)}, u32[]{:S(2)}) copy-start(f32[128]{0:T(128)} %constant.44.clone) | copy-start | bytes 1540
  2.1 38.8 %collective-permute-start = (bf16[5888,128]{1,0:T(8,128)(2,1)S(1)}, bf16[5888,128]{1,0:T(8,128)(2,1)}, u32[]{:S(2)}, u32[]{:S(2)}) collective-permute-start(bf16[5888,128]{1,0:T(8,128)(2,1)S(1)} %get-tuple-element.33.refs_5_), channel_id=1, source_target_pairs={{0,128},{8,136},{16,144},{24,152},{32,160},{40,168},{48,176},{56,1... | collective-permute-start | bytes 4521992 | tf_op jit(solution)/shard_map/ppermute | solution.py:22
  5.2 4.7 %collective-permute-start.1 = (bf16[1,2048]{1,0:T(2,128)(2,1)S(1)}, bf16[1,2048]{1,0:T(2,128)(2,1)S(1)}, u32[]{:S(2)}, u32[]{:S(2)}) collective-permute-start(bf16[1,2048]{1,0:T(2,128)(2,1)S(1)} %copy-done.3), channel_id=1, source_target_pairs={{0,8},{8,0},{16,24},{24,16},{32,40},{40,32},{48,56},{56,48},{64,72... | collective-permute-start | bytes 12296 | tf_op jit(solution)/shard_map/ppermute | solution.py:22
  7.5 2.5 %copy-start.1 = (f32[2,2048]{1,0:T(2,128)S(1)}, f32[2,2048]{1,0:T(2,128)}, u32[]{:S(2)}) copy-start(f32[2,2048]{1,0:T(2,128)} %rest_0_.3) | copy-start | bytes 49156
  7.5 2.5 %copy-start.2 = (bf16[3,2048]{1,0:T(4,128)(2,1)S(1)}, bf16[3,2048]{1,0:T(4,128)(2,1)}, u32[]{:S(2)}) copy-start(bf16[3,2048]{1,0:T(4,128)(2,1)} %tokens_ref.1) | copy-start | bytes 36868
  7.5 2.5 %copy-start.4 = (f32[2,128]{1,0:T(2,128)S(1)}, f32[2,128]{1,0:T(2,128)}, u32[]{:S(2)}) copy-start(f32[2,128]{1,0:T(2,128)} %rest_1_.3) | copy-start | bytes 3076
  7.5 2.5 %copy-start.5 = (f32[2,128]{1,0:T(2,128)S(1)}, f32[2,128]{1,0:T(2,128)}, u32[]{:S(2)}) copy-start(f32[2,128]{1,0:T(2,128)} %rest_2_.3) | copy-start | bytes 3076
  13.1 3.8 %copy-start = (bf16[2,256,2048]{2,1,0:T(8,128)(2,1)S(1)}, bf16[2,256,2048]{2,1,0:T(8,128)(2,1)}, u32[]{:S(2)}) copy-start(bf16[2,256,2048]{2,1,0:T(8,128)(2,1)} %w_ref.3) | copy-start | bytes 6291460
  13.1 3.8 %collective-permute-start.2 = (f32[16,256]{1,0:T(8,128)S(1)}, f32[16,256]{1,0:T(8,128)S(1)}, u32[]{:S(2)}, u32[]{:S(2)}) collective-permute-start(f32[16,256]{1,0:T(8,128)S(1)} %get-tuple-element.40.refs_5_.state_ref), channel_id=1, source_target_pairs={{0,8},{8,0},{16,24},{24,16},{32,40},{40,32},{48,56},{56,48},{64,72... | collective-permute-start | bytes 49160 | tf_op jit(solution)/shard_map/ppermute | solution.py:22
  17.5 1.3 %collective-permute-start.3 = (f32[8,2048]{1,0:T(8,128)S(1)}, f32[8,2048]{1,0:T(8,128)S(1)}, u32[]{:S(2)}, u32[]{:S(2)}) collective-permute-start(f32[8,2048]{1,0:T(8,128)S(1)} %out_projection_0.1), channel_id=1, source_target_pairs={{0,1},{1,0},{2,3},{3,2},{4,5},{5,4},{6,7},{7,6},{8,9},{9,8},{10,11... | collective-permute-start | bytes 196616 | tf_op jit(solution)/shard_map/ppermute | solution.py:22
  18.8 8.2 %collective-permute-start.4 = (bf16[8,2048]{1,0:T(8,128)(2,1)S(1)}, bf16[8,2048]{1,0:T(8,128)(2,1)S(1)}, u32[]{:S(2)}, u32[]{:S(2)}) collective-permute-start(bf16[8,2048]{1,0:T(8,128)(2,1)S(1)} %add_convert_fusion.1.refs_5_.p_ref), channel_id=1, source_target_pairs={{0,2},{1,3},{2,0},{3,1},{4,6},{5,7},{6,4},{7,5},{8,10},{9,11},{10,... | collective-permute-start | bytes 98312 | tf_op jit(solution)/shard_map/ppermute | solution.py:22
  20.5 6.6 %collective-permute-start.5 = (bf16[8,2048]{1,0:T(8,128)(2,1)S(1)}, bf16[8,2048]{1,0:T(8,128)(2,1)S(1)}, u32[]{:S(2)}, u32[]{:S(2)}) collective-permute-start(bf16[8,2048]{1,0:T(8,128)(2,1)S(1)} %add_convert_fusion.1.refs_5_.p_ref), channel_id=1, source_target_pairs={{0,4},{1,5},{2,6},{3,7},{4,0},{5,1},{6,2},{7,3},{8,12},{9,13},{10,... | collective-permute-start | bytes 98312 | tf_op jit(solution)/shard_map/ppermute | solution.py:22
  23.4 5.1 %collective-permute-start.6 = (bf16[8,2048]{1,0:T(8,128)(2,1)S(1)}, bf16[8,2048]{1,0:T(8,128)(2,1)S(1)}, u32[]{:S(2)}, u32[]{:S(2)}) collective-permute-start(bf16[8,2048]{1,0:T(8,128)(2,1)S(1)} %add_convert_fusion.1.refs_5_.p_ref), channel_id=1, source_target_pairs={{0,6},{1,7},{2,4},{3,5},{4,2},{5,3},{6,0},{7,1},{8,14},{9,15},{10,... | collective-permute-start | bytes 98312 | tf_op jit(solution)/shard_map/ppermute | solution.py:22
  24.7 26.4 %collective-permute-start.13 = (bf16[2304,128]{1,0:T(8,128)(2,1)S(1)}, bf16[2304,128]{1,0:T(8,128)(2,1)S(1)}, u32[]{:S(2)}, u32[]{:S(2)}) collective-permute-start(bf16[2304,128]{1,0:T(8,128)(2,1)S(1)} %get-tuple-element.58), channel_id=1, source_target_pairs={{0,128},{8,136},{16,144},{24,152},{32,160},{40,168},{48,176},{56,1... | collective-permute-start | bytes 1769480 | tf_op jit(solution)/shard_map/ppermute | solution.py:22
  31.0 3.8 %collective-permute-start.7 = (f32[16,256]{1,0:T(8,128)S(1)}, f32[16,256]{1,0:T(8,128)S(1)}, u32[]{:S(2)}, u32[]{:S(2)}) collective-permute-start(f32[16,256]{1,0:T(8,128)S(1)} %get-tuple-element.49.state_ref), channel_id=1, source_target_pairs={{0,8},{8,0},{16,24},{24,16},{32,40},{40,32},{48,56},{56,48},{64,72... | collective-permute-start | bytes 49160 | tf_op jit(solution)/shard_map/ppermute | solution.py:22
  35.3 1.3 %collective-permute-start.8 = (f32[8,2048]{1,0:T(8,128)S(1)}, f32[8,2048]{1,0:T(8,128)S(1)}, u32[]{:S(2)}, u32[]{:S(2)}) collective-permute-start(f32[8,2048]{1,0:T(8,128)S(1)} %out_projection_1.1), channel_id=1, source_target_pairs={{0,1},{1,0},{2,3},{3,2},{4,5},{5,4},{6,7},{7,6},{8,9},{9,8},{10,11... | collective-permute-start | bytes 196616 | tf_op jit(solution)/shard_map/ppermute | solution.py:22
  36.7 7.2 %collective-permute-start.10 = (bf16[8,2048]{1,0:T(8,128)(2,1)S(1)}, bf16[8,2048]{1,0:T(8,128)(2,1)S(1)}, u32[]{:S(2)}, u32[]{:S(2)}) collective-permute-start(bf16[8,2048]{1,0:T(8,128)(2,1)S(1)} %add_convert_fusion.after_ref.p_ref), channel_id=1, source_target_pairs={{0,4},{1,5},{2,6},{3,7},{4,0},{5,1},{6,2},{7,3},{8,12},{9,13},{10,... | collective-permute-start | bytes 98312 | tf_op jit(solution)/shard_map/ppermute | solution.py:22
  37.3 6.6 %collective-permute-start.11 = (bf16[8,2048]{1,0:T(8,128)(2,1)S(1)}, bf16[8,2048]{1,0:T(8,128)(2,1)S(1)}, u32[]{:S(2)}, u32[]{:S(2)}) collective-permute-start(bf16[8,2048]{1,0:T(8,128)(2,1)S(1)} %add_convert_fusion.after_ref.p_ref), channel_id=1, source_target_pairs={{0,6},{1,7},{2,4},{3,5},{4,2},{5,3},{6,0},{7,1},{8,14},{9,15},{10,... | collective-permute-start | bytes 98312 | tf_op jit(solution)/shard_map/ppermute | solution.py:22
  38.5 5.5 %collective-permute-start.9 = (bf16[8,2048]{1,0:T(8,128)(2,1)S(1)}, bf16[8,2048]{1,0:T(8,128)(2,1)S(1)}, u32[]{:S(2)}, u32[]{:S(2)}) collective-permute-start(bf16[8,2048]{1,0:T(8,128)(2,1)S(1)} %add_convert_fusion.after_ref.p_ref), channel_id=1, source_target_pairs={{0,2},{1,3},{2,0},{3,1},{4,6},{5,7},{6,4},{7,5},{8,10},{9,11},{10,... | collective-permute-start | bytes 98312 | tf_op jit(solution)/shard_map/ppermute | solution.py:22
  44.6 6.7 %collective-permute-start.12 = (f32[1,2560]{1,0:T(1,128)S(1)}, f32[1,2560]{1,0:T(1,128)S(1)}, u32[]{:S(2)}, u32[]{:S(2)}) collective-permute-start(f32[1,2560]{1,0:T(1,128)S(1)} %get-tuple-element.57), channel_id=1, source_target_pairs={{0,128},{8,136},{16,144},{24,152},{32,160},{40,168},{48,176},{56,1... | collective-permute-start | bytes 30728 | tf_op jit(solution)/shard_map/ppermute | solution.py:22
